TPU v7x, 32 devices: a whole 2x2x4 slice. The times are simulated.
32 devices in a mesh: groups: 2 (over x), height: 16 (over z, y, core).
Axes of the slice: x: 2, y: 2, z: 4, core: 2. Of those that a mesh axis runs over, the one named last changes fastest.
Arguments:
- frames: bfloat16 [4, 128, 32, 128], P('groups', 'height'), parts along dimension 0, may hold values from -6 to 6
- weight_a: bfloat16 [3, 3, 3, 128, 128], replicated, may hold values from -0.109375 to 0.109375
- weight_b: bfloat16 [3, 3, 3, 128, 256], replicated, may hold values from -0.109375 to 0.109375
- cotangent: bfloat16 [4, 64, 16, 256], P('groups', 'height'), parts along dimension 0, may hold values from -6 to 6
Outputs:
- encoded: bfloat16 [4, 64, 16, 256], P('groups', 'height'), parts along dimension 0
- frames_grad: bfloat16 [4, 128, 32, 128], P('groups', 'height'), parts along dimension 0
- weight_a_grad: bfloat16 [6, 3, 3, 128, 128], P('groups'), parts along dimension 0
- weight_b_grad: bfloat16 [6, 3, 3, 128, 256], P('groups'), parts along dimension 0
There are 2 independent parts, one for each index of `groups`. A program takes and returns all parts, laid end to end along the dimension named above; an argument that names none is the same for every part. Nothing has to cross between parts.
All inputs are finite; a program needn't handle non-finite values.
Results may differ from a plain program's by a relative error of at most 0.0053.
Values may be sent and summed in bfloat16 or wider, within the bound.
No kernel may reach another device: no remote copies, remote signals or barrier semaphores. Data moves between devices by JAX's collectives and lax.ppermute only.
A program may use at most 64 MiB of HBM per device.

v0:
```python
import jax
import jax.numpy as jnp
from jax import lax
from jax.sharding import PartitionSpec as P


def with_halo(shard, sides, width):
    for axis, dim in sides:
        count, length = (lax.axis_size(axis), shard.shape[dim])
        up = [(i, (i + 1) % count) for i in range(count - 1)]
        down = [(j, i) for i, j in up]
        last = lax.slice_in_dim(shard, length - width, length, axis=dim)
        first = lax.slice_in_dim(shard, 0, width, axis=dim)
        before = lax.ppermute(last, axis, up)
        after = lax.ppermute(first, axis, down)
        shard = jnp.concatenate([before, shard, after], axis=dim)
    return shard


def passed_along(value, axis, steps):
    count = lax.axis_size(axis)
    first, last = (max(0, -steps), min(count, count - steps))
    return lax.ppermute(value, axis, [(source, source + steps) for source in range(first, last)])


def pad_time(field):
    return jnp.concatenate([field[:1], field[:1], field], axis=0)


def fold_time(grads):
    return grads[2:].at[0].add(grads[0] + grads[1])


def widen_full(field):
    padded = pad_time(field)
    zero_col = jnp.zeros_like(padded[:, :, :1])
    padded = jnp.concatenate([zero_col, padded, zero_col], axis=2)
    width = field.shape[2]
    return jnp.concatenate(
        [padded[:, :, 0:width], padded[:, :, 1 : width + 1], padded[:, :, 2 : width + 2]], axis=3
    )


def widen_half(field):
    padded = pad_time(field)
    zero_col = jnp.zeros_like(padded[:, :, :1])
    padded = jnp.concatenate([zero_col, padded], axis=2)
    width = field.shape[2]
    return jnp.concatenate([padded[:, :, k : k + width - 1 : 2] for k in range(3)], axis=3)


def forward_a(stacked, kernel, rows):
    frames = stacked.shape[0] - 2
    width = stacked.shape[2]
    total = jnp.zeros((frames * rows * width, kernel.shape[-1]), jnp.float32)
    for kt in range(3):
        for kh in range(3):
            piece = stacked[kt : kt + frames, kh : kh + rows]
            total = total + jnp.dot(
                piece.reshape(-1, piece.shape[-1]),
                kernel[kt, kh],
                preferred_element_type=jnp.float32,
            )
    return total.reshape(frames, rows, width, kernel.shape[-1])


def forward_b(stacked, kernel, rows):
    frames = stacked.shape[0] - 2
    width = stacked.shape[2]
    total = jnp.zeros((frames * rows * width, kernel.shape[-1]), jnp.float32)
    for kt in range(3):
        for kh in range(3):
            piece = stacked[kt : kt + frames, kh : kh + 2 * rows - 1 : 2]
            total = total + jnp.dot(
                piece.reshape(-1, piece.shape[-1]),
                kernel[kt, kh],
                preferred_element_type=jnp.float32,
            )
    return total.reshape(frames, rows, width, kernel.shape[-1])


def backward_a(stacked, kernel, grad, rows):
    frames = stacked.shape[0] - 2
    width = stacked.shape[2]
    chans = grad.shape[-1]
    flat = grad.reshape(-1, chans)
    wgrad = []
    dstack = jnp.zeros(stacked.shape, jnp.float32)
    for kt in range(3):
        for kh in range(3):
            piece = stacked[kt : kt + frames, kh : kh + rows]
            wgrad.append(
                lax.dot_general(
                    piece.reshape(-1, piece.shape[-1]),
                    flat,
                    (((0,), (0,)), ((), ())),
                    preferred_element_type=jnp.float32,
                )
            )
            back = lax.dot_general(
                flat, kernel[kt, kh], (((1,), (1,)), ((), ())), preferred_element_type=jnp.float32
            )
            dstack = dstack.at[kt : kt + frames, kh : kh + rows].add(
                back.reshape(frames, rows, width, -1)
            )
    return (jnp.stack(wgrad).reshape(kernel.shape), dstack)


def backward_b(stacked, kernel, grad, rows):
    frames = stacked.shape[0] - 2
    width = stacked.shape[2]
    flat = grad.reshape(-1, grad.shape[-1])
    wgrad = []
    dstack = jnp.zeros(stacked.shape, jnp.float32)
    for kt in range(3):
        for kh in range(3):
            piece = stacked[kt : kt + frames, kh : kh + 2 * rows - 1 : 2]
            wgrad.append(
                lax.dot_general(
                    piece.reshape(-1, piece.shape[-1]),
                    flat,
                    (((0,), (0,)), ((), ())),
                    preferred_element_type=jnp.float32,
                )
            )
            back = lax.dot_general(
                flat, kernel[kt, kh], (((1,), (1,)), ((), ())), preferred_element_type=jnp.float32
            )
            dstack = dstack.at[kt : kt + frames, kh : kh + 2 * rows - 1 : 2].add(
                back.reshape(frames, rows, width, -1)
            )
    return (jnp.stack(wgrad).reshape(kernel.shape), dstack)


def unstack_full(dstack, chans):
    width = dstack.shape[2]
    shape = (dstack.shape[0], dstack.shape[1], width + 2, chans)
    total = jnp.zeros(shape, jnp.float32)
    for k in range(3):
        total = total.at[:, :, k : k + width].add(dstack[..., k * chans : (k + 1) * chans])
    return fold_time(total[:, :, 1 : width + 1])


def unstack_half(dstack, chans, width):
    shape = (dstack.shape[0], dstack.shape[1], width + 1, chans)
    total = jnp.zeros(shape, jnp.float32)
    for k in range(3):
        total = total.at[:, :, k : k + width - 1 : 2].add(dstack[..., k * chans : (k + 1) * chans])
    return fold_time(total[:, :, 1:])


def on_device(frames, weight_a, weight_b, cotangent):
    chans = frames.shape[-1]
    rows = frames.shape[1]
    width = frames.shape[2]
    kernel_a = weight_a.reshape(3, 3, 3 * chans, chans)
    kernel_b = weight_b.reshape(3, 3, 3 * chans, weight_b.shape[-1])
    rows_ext = with_halo(frames, (("height", 1),), 1)
    stacked_a = widen_full(rows_ext)
    pre = frames.astype(jnp.float32) + forward_a(stacked_a, kernel_a, rows)
    sig = jax.nn.sigmoid(pre)
    act = (pre * sig).astype(jnp.bfloat16)
    lower = passed_along(act[:, rows - 1 : rows], "height", 1)
    act_ext = jnp.concatenate([lower, act], axis=1)
    stacked_b = widen_half(act_ext)
    encoded = forward_b(stacked_b, kernel_b, rows // 2).astype(jnp.bfloat16)
    wgrad_b, dstack_b = backward_b(stacked_b, kernel_b, cotangent, rows // 2)
    act_full = unstack_half(dstack_b, chans, width)
    incoming = passed_along(act_full[:, 0:1], "height", -1)
    act_grad = act_full[:, 1:].at[:, rows - 1 : rows].add(incoming)
    pre_grad = (act_grad * sig * (1.0 + pre * (1.0 - sig))).astype(jnp.bfloat16)
    wgrad_a, dstack_a = backward_a(stacked_a, kernel_a, pre_grad, rows)
    field_grad = unstack_full(dstack_a, chans)
    edges = jnp.concatenate([field_grad[:, 0:1], field_grad[:, rows + 1 : rows + 2]], axis=1)
    edges_ext = with_halo(edges, (("height", 1),), 1)
    summed = pre_grad.astype(jnp.float32) + field_grad[:, 1 : rows + 1]
    summed = summed.at[:, 0:1].add(edges_ext[:, 0:1])
    summed = summed.at[:, rows - 1 : rows].add(edges_ext[:, 3:4])
    frames_grad = summed.astype(jnp.bfloat16)
    scale = (frames.shape[0] * rows * lax.axis_size("height") * width) ** (-0.5)
    flat_a = (wgrad_a * scale).reshape(-1)
    flat_b = (wgrad_b * scale).reshape(-1)
    total_a, total_b = lax.psum((flat_a, flat_b), "height")
    grad_a = total_a.astype(jnp.bfloat16)
    grad_b = total_b.astype(jnp.bfloat16)
    weight_a_grad = grad_a.reshape(weight_a.shape)
    weight_b_grad = grad_b.reshape(weight_b.shape)
    return (encoded, frames_grad, weight_a_grad, weight_b_grad)


def solution(mesh):
    in_specs = (P("groups", "height", None, None), P(), P(), P("groups", "height", None, None))
    out_specs = (
        P("groups", "height", None, None),
        P("groups", "height", None, None),
        P("groups", None, None, None, None),
        P("groups", None, None, None, None),
    )
    return jax.shard_map(
        on_device, mesh=mesh, in_specs=in_specs, out_specs=out_specs, check_vma=False
    )
```

profile of v0, /device:TPU:0, one launch (start us, length us, event | category | flops | bytes accessed | tf_op | source)
XLA Modules:
  0.0 359.8 jit_solution(13735289720688127811)
XLA Ops:
  2.8 3.0 collective-permute-start
  12.4 20.8 %while.26 = (s32[]{:T(128)}, f32[4,9,16,384]{3,2,1,0:T(8,128)S(1)}, s32[4,2]{0,1:T(2,128)S(1)}, f32[4,2,16,384]{3,2,0,1:T(8,128)}, s32[]{:T(128)}, /*index=5*/s32[4]{0:T(128)S(1)}, s32[1]{0:T(128)}) while((s32[]{:T(128)}, f32[4,9,16,384]{3,2,1,0:T(8,128)S(1)}, s32[4,2]{0,1:T(2,128)S(1)}, f32[4,2,16,384]{3,2,0,1:T(8,128)}, s32[]{:T(128)}, ...), condition=%wide.while_cond.17, body=%wide.while_body.17.sunk | while | flops 24605 | bytes 147619 | solution.py:129
  15.0 2.6 fusion.219
  20.2 2.6 fusion.219
  25.4 2.6 fusion.219
  30.6 2.6 fusion.219
  33.2 18.4 %while.27 = (s32[]{:T(128)}, f32[4,9,16,384]{3,2,1,0:T(8,128)S(1)}, s32[4,2]{0,1:T(2,128)S(1)}, f32[4,2,16,384]{3,2,0,1:T(8,128)S(1)}, s32[]{:T(128)}, /*index=5*/s32[4]{0:T(128)S(1)}, s32[1]{0:T(128)}) while((s32[]{:T(128)}, f32[4,9,16,384]{3,2,1,0:T(8,128)S(1)}, s32[4,2]{0,1:T(2,128)S(1)}, f32[4,2,16,384]{3,2,0,1:T(8,128)S(1)}, s32[]{:T(128)}, ...), condition=%wide.while_cond.18, body=%wide.while_body.18.sunk | while | flops 24605 | bytes 147619 | solution.py:129
  33.8 2.0 and_reduce_fusion.20
  38.5 2.0 and_reduce_fusion.20
  43.1 2.0 and_reduce_fusion.20
  47.7 2.0 and_reduce_fusion.20
  51.6 17.7 %while.28 = (s32[]{:T(128)}, f32[4,9,16,384]{3,2,1,0:T(8,128)S(1)}, s32[4,2]{0,1:T(2,128)S(1)}, f32[4,2,16,384]{3,2,0,1:T(8,128)S(1)}, s32[]{:T(128)}, /*index=5*/s32[4]{0:T(128)S(1)}, s32[1]{0:T(128)}) while((s32[]{:T(128)}, f32[4,9,16,384]{3,2,1,0:T(8,128)S(1)}, s32[4,2]{0,1:T(2,128)S(1)}, f32[4,2,16,384]{3,2,0,1:T(8,128)S(1)}, s32[]{:T(128)}, ...), condition=%wide.while_cond.19, body=%wide.while_body.19.sunk | while | flops 24605 | bytes 147619 | solution.py:129
  69.3 17.9 %while.29 = (s32[]{:T(128)}, f32[4,9,16,384]{3,2,1,0:T(8,128)S(1)}, s32[4,2]{0,1:T(2,128)S(1)}, f32[4,2,16,384]{3,2,0,1:T(8,128)S(1)}, s32[]{:T(128)}, /*index=5*/s32[4]{0:T(128)S(1)}, s32[1]{0:T(128)}) while((s32[]{:T(128)}, f32[4,9,16,384]{3,2,1,0:T(8,128)S(1)}, s32[4,2]{0,1:T(2,128)S(1)}, f32[4,2,16,384]{3,2,0,1:T(8,128)S(1)}, s32[]{:T(128)}, ...), condition=%wide.while_cond.20, body=%wide.while_body.20.sunk | while | flops 24605 | bytes 147619 | solution.py:129
  74.4 2.0 and_reduce_fusion.22
  83.4 2.0 and_reduce_fusion.22
  87.2 18.4 %while.30 = (s32[]{:T(128)}, f32[4,9,16,384]{3,2,1,0:T(8,128)S(1)}, s32[4,2]{0,1:T(2,128)S(1)}, f32[4,2,16,384]{3,2,0,1:T(8,128)S(1)}, s32[]{:T(128)}, /*index=5*/s32[4]{0:T(128)S(1)}, s32[1]{0:T(128)}) while((s32[]{:T(128)}, f32[4,9,16,384]{3,2,1,0:T(8,128)S(1)}, s32[4,2]{0,1:T(2,128)S(1)}, f32[4,2,16,384]{3,2,0,1:T(8,128)S(1)}, s32[]{:T(128)}, ...), condition=%wide.while_cond.21, body=%wide.while_body.21.sunk | while | flops 24605 | bytes 147619 | solution.py:129
  87.9 2.0 and_reduce_fusion.23
  92.5 2.0 and_reduce_fusion.23
  97.1 2.0 and_reduce_fusion.23
  101.7 2.0 and_reduce_fusion.23
  105.6 18.4 %while.31 = (s32[]{:T(128)}, f32[4,9,16,384]{3,2,1,0:T(8,128)S(1)}, s32[4,2]{0,1:T(2,128)S(1)}, f32[4,2,16,384]{3,2,0,1:T(8,128)S(1)}, s32[]{:T(128)}, /*index=5*/s32[4]{0:T(128)S(1)}, s32[1]{0:T(128)}) while((s32[]{:T(128)}, f32[4,9,16,384]{3,2,1,0:T(8,128)S(1)}, s32[4,2]{0,1:T(2,128)S(1)}, f32[4,2,16,384]{3,2,0,1:T(8,128)S(1)}, s32[]{:T(128)}, ...), condition=%wide.while_cond.22, body=%wide.while_body.22.sunk | while | flops 24605 | bytes 147619 | solution.py:129
  106.2 2.0 and_reduce_fusion.24
  110.9 2.0 and_reduce_fusion.24
  115.5 2.0 and_reduce_fusion.24
  120.1 2.0 and_reduce_fusion.24
  124.0 18.3 %while.32 = (s32[]{:T(128)}, f32[4,9,16,384]{3,2,1,0:T(8,128)S(1)}, s32[4,2]{0,1:T(2,128)S(1)}, f32[4,2,16,384]{3,2,0,1:T(8,128)S(1)}, s32[]{:T(128)}, /*index=5*/s32[4]{0:T(128)S(1)}, s32[1]{0:T(128)}) while((s32[]{:T(128)}, f32[4,9,16,384]{3,2,1,0:T(8,128)S(1)}, s32[4,2]{0,1:T(2,128)S(1)}, f32[4,2,16,384]{3,2,0,1:T(8,128)S(1)}, s32[]{:T(128)}, ...), condition=%wide.while_cond.23, body=%wide.while_body.23.sunk | while | flops 24605 | bytes 147619 | solution.py:129
  124.7 2.0 and_reduce_fusion.25
  129.3 2.0 and_reduce_fusion.25
  133.9 2.0 and_reduce_fusion.25
  138.5 2.0 and_reduce_fusion.25
  142.4 18.4 %while.33 = (s32[]{:T(128)}, f32[4,9,16,384]{3,2,1,0:T(8,128)S(1)}, s32[4,2]{0,1:T(2,128)S(1)}, f32[4,2,16,384]{3,2,0,1:T(8,128)S(1)}, s32[]{:T(128)}, /*index=5*/s32[4]{0:T(128)S(1)}, s32[1]{0:T(128)}) while((s32[]{:T(128)}, f32[4,9,16,384]{3,2,1,0:T(8,128)S(1)}, s32[4,2]{0,1:T(2,128)S(1)}, f32[4,2,16,384]{3,2,0,1:T(8,128)S(1)}, s32[]{:T(128)}, ...), condition=%wide.while_cond.24, body=%wide.while_body.24.sunk | while | flops 24605 | bytes 147619 | solution.py:129
  143.0 2.1 and_reduce_fusion.26
  147.6 2.1 and_reduce_fusion.26
  152.2 2.1 and_reduce_fusion.26
  156.8 2.1 and_reduce_fusion.26
  160.8 18.3 %while.34 = (s32[]{:T(128)}, f32[4,9,16,384]{3,2,1,0:T(8,128)S(1)}, s32[4,2]{0,1:T(2,128)S(1)}, f32[4,2,16,384]{3,2,0,1:T(8,128)S(1)}, s32[]{:T(128)}, /*index=5*/s32[4]{0:T(128)S(1)}, s32[1]{0:T(128)}) while((s32[]{:T(128)}, f32[4,9,16,384]{3,2,1,0:T(8,128)S(1)}, s32[4,2]{0,1:T(2,128)S(1)}, f32[4,2,16,384]{3,2,0,1:T(8,128)S(1)}, s32[]{:T(128)}, ...), condition=%wide.while_cond.25, body=%wide.while_body.25.sunk | while | flops 24605 | bytes 147619 | solution.py:129
  161.4 2.0 and_reduce_fusion.27
  166.0 2.0 and_reduce_fusion.27
  170.6 2.0 and_reduce_fusion.27
  175.1 2.0 and_reduce_fusion.27
  196.2 2.2 fusion.16
  201.1 2.9 scatter-add.193
  205.0 2.9 scatter-add.194
  208.4 5.1 %collective-permute-start.2 = (bf16[2,1,32,128]{3,2,1,0:T(8,128)(2,1)S(1)}, bf16[2,1,32,128]{3,2,1,0:T(8,128)(2,1)S(1)}, u32[]{:S(2)}, u32[]{:S(2)}) collective-permute-start(bf16[2,1,32,128]{3,2,1,0:T(8,128)(2,1)S(1)} %slice.1035), channel_id=1, source_target_pairs={{0,1},{1,2},{2,3},{3,4},{4,5},{5,6},{6,7},{7,8},{8,9},{9,10},{10,1... | collective-permute-start | bytes 49160 | tf_op jit(solution)/shard_map/ppermute | solution.py:23
  214.8 4.3 %collective-permute-start.4 = (f32[2,1,32,128]{3,2,1,0:T(8,128)S(1)}, f32[2,1,32,128]{3,2,1,0:T(8,128)S(1)}, u32[]{:S(2)}, u32[]{:S(2)}) collective-permute-start(f32[2,1,32,128]{3,2,1,0:T(8,128)S(1)} %get-tuple-element.435), channel_id=1, source_target_pairs={{0,1},{1,2},{2,3},{3,4},{4,5},{5,6},{6,7},{7,8},{8,9},{9,10},{10,1... | collective-permute-start | bytes 98312 | tf_op jit(solution)/shard_map/ppermute | solution.py:14
  227.7 3.6 copy.73
  232.6 122.0 %all-reduce.16 = (bf16[442368]{0:T(1024)(128)(2,1)}, bf16[884736]{0:T(1024)(128)(2,1)}) all-reduce(f32[442368]{0:T(1024)} %bitcast.605, f32[884736]{0:T(1024)} %bitcast.586), channel_id=1, replica_groups=mesh['groups'=2,'height'=16] {'height'}, use_global_device_ids=true, to_apply=%region_13.0 | all-reduce | flops 1327104 | bytes 7962624 | tf_op jit(solution)/shard_map/psum | solution.py:183
  355.4 3.7 %reshape.847 = bf16[3,3,3,128,256]{4,3,2,1,0:T(8,128)(2,1)} reshape(bf16[884736]{0:T(1024)(128)(2,1)} %get-tuple-element.389) | data formatting | bytes 3538944 | tf_op jit(solution)/shard_map/reshape | solution.py:187
  (259 shorter events, 144.7 us)
Async XLA Ops:
  0.6 5.3 %copy-start = (bf16[2,4,16,256]{3,2,1,0:T(8,128)(2,1)S(1)}, bf16[2,4,16,256]{3,2,1,0:T(8,128)(2,1)}, u32[]{:S(2)}) copy-start(bf16[2,4,16,256]{3,2,1,0:T(8,128)(2,1)} %param.41) | copy-start | bytes 196612
  0.6 10.5 %copy-start.1 = (bf16[3,3,3,128,256]{4,3,2,1,0:T(8,128)(2,1)S(1)}, bf16[3,3,3,128,256]{4,3,2,1,0:T(8,128)(2,1)}, u32[]{:S(2)}) copy-start(bf16[3,3,3,128,256]{4,3,2,1,0:T(8,128)(2,1)} %param.40) | copy-start | bytes 5308420
  1.5 187.7 %collective-permute-start.1 = (bf16[2,1,32,128]{3,2,1,0:T(8,128)(2,1)S(1)}, bf16[2,1,32,128]{3,2,1,0:T(8,128)(2,1)S(1)}, u32[]{:S(2)}, u32[]{:S(2)}) collective-permute-start(bf16[2,1,32,128]{3,2,1,0:T(8,128)(2,1)S(1)} %get-tuple-element.438), channel_id=1, source_target_pairs={{1,0},{2,1},{3,2},{4,3},{5,4},{6,5},{7,6},{8,7},{9,8},{10,9},{11,1... | collective-permute-start | bytes 49160 | tf_op jit(solution)/shard_map/ppermute | solution.py:15
  2.8 186.3 %collective-permute-start = (bf16[2,1,32,128]{3,2,1,0:T(8,128)(2,1)S(1)}, bf16[2,1,32,128]{3,2,1,0:T(8,128)(2,1)S(1)}, u32[]{:S(2)}, u32[]{:S(2)}) collective-permute-start(bf16[2,1,32,128]{3,2,1,0:T(8,128)(2,1)S(1)} %get-tuple-element.439), channel_id=1, source_target_pairs={{0,1},{1,2},{2,3},{3,4},{4,5},{5,6},{6,7},{7,8},{8,9},{9,10},{10,1... | collective-permute-start | bytes 49160 | tf_op jit(solution)/shard_map/ppermute | solution.py:14
  8.9 3.5 copy-start.8
  183.3 4.5 %copy-start.10 = (s32[4]{0:T(128)S(1)}, s32[4]{0:T(128)}, u32[]{:S(2)}) copy-start(s32[4]{0:T(128)} %constant.480.clone.1) | copy-start | bytes 52
  183.3 5.8 %copy-start.9 = (bf16[2,8,32,128]{3,2,1,0:T(8,128)(2,1)S(1)}, bf16[2,8,32,128]{3,2,1,0:T(8,128)(2,1)}, u32[]{:S(2)}) copy-start(bf16[2,8,32,128]{3,2,1,0:T(8,128)(2,1)} %param.38) | copy-start | bytes 393220
  185.7 8.2 %collective-permute-start.3 = (f32[2,1,32,128]{3,2,1,0:T(8,128)S(1)}, f32[2,1,32,128]{3,2,1,0:T(8,128)S(1)}, u32[]{:S(2)}, u32[]{:S(2)}) collective-permute-start(f32[2,1,32,128]{3,2,1,0:T(8,128)S(1)} %slice.1051), channel_id=1, source_target_pairs={{1,0},{2,1},{3,2},{4,3},{5,4},{6,5},{7,6},{8,7},{9,8},{10,9},{11,1... | collective-permute-start | bytes 98312 | tf_op jit(solution)/shard_map/ppermute | solution.py:23
  189.2 0.7 copy-start.6
  189.5 0.7 copy-start.4
  190.3 1.2 copy-start.3
  205.0 3.1 copy-start.5
  205.0 3.1 copy-start.7
  208.4 14.6 %collective-permute-start.2 = (bf16[2,1,32,128]{3,2,1,0:T(8,128)(2,1)S(1)}, bf16[2,1,32,128]{3,2,1,0:T(8,128)(2,1)S(1)}, u32[]{:S(2)}, u32[]{:S(2)}) collective-permute-start(bf16[2,1,32,128]{3,2,1,0:T(8,128)(2,1)S(1)} %slice.1035), channel_id=1, source_target_pairs={{0,1},{1,2},{2,3},{3,4},{4,5},{5,6},{6,7},{7,8},{8,9},{9,10},{10,1... | collective-permute-start | bytes 49160 | tf_op jit(solution)/shard_map/ppermute | solution.py:23
  213.5 145.6 %collective-permute-start.5 = (f32[2,1,32,128]{3,2,1,0:T(8,128)S(1)}, f32[2,1,32,128]{3,2,1,0:T(8,128)S(1)}, u32[]{:S(2)}, u32[]{:S(2)}) collective-permute-start(f32[2,1,32,128]{3,2,1,0:T(8,128)S(1)} %get-tuple-element.434), channel_id=1, source_target_pairs={{1,0},{2,1},{3,2},{4,3},{5,4},{6,5},{7,6},{8,7},{9,8},{10,9},{11,1... | collective-permute-start | bytes 98312 | tf_op jit(solution)/shard_map/ppermute | solution.py:15
  214.8 144.3 %collective-permute-start.4 = (f32[2,1,32,128]{3,2,1,0:T(8,128)S(1)}, f32[2,1,32,128]{3,2,1,0:T(8,128)S(1)}, u32[]{:S(2)}, u32[]{:S(2)}) collective-permute-start(f32[2,1,32,128]{3,2,1,0:T(8,128)S(1)} %get-tuple-element.435), channel_id=1, source_target_pairs={{0,1},{1,2},{2,3},{3,4},{4,5},{5,6},{6,7},{7,8},{8,9},{9,10},{10,1... | collective-permute-start | bytes 98312 | tf_op jit(solution)/shard_map/ppermute | solution.py:14
  223.8 1.5 copy-start.2
where the time goes:
time: 365 us; the launch traced here: 360 us
  other arithmetic  155 us (42%)
  blocking collectives  122 us (33%)
  local copies, waits for them, and re-layouts  43 us (12%)
  matrix products  21.4 us (6%)
  starting transfers between devices  16.5 us (5%)
    scatter-add x72, other arithmetic  144 us
    psum x1, blocking collectives, on_device(): total_a, total_b = lax.psum((flat_a, flat_b), 'height')  122 us
    scatter-add x72, local copies, waits for them, and re-layouts  22.3 us
    ppermute x2, starting transfers between devices, with_halo(): before = lax.ppermute(last, axis, up)  7.31 us
  transfers between devices with their start and end apart: 6, of which 0 were waited for; matrix products, arithmetic and copies ran while one was open for 56% of the time, Pallas kernels for 0%

commit v1 on v0

v1 whole, which is shorter than its diff:
```python
import jax
import jax.numpy as jnp
from jax import lax
from jax.experimental import pallas as pl
from jax.experimental.pallas import tpu as pltpu
from jax.sharding import PartitionSpec as P

F32 = jnp.float32
BF16 = jnp.bfloat16
AXIS = "height"
VMEM_LIMIT = 48 * 1024 * 1024


def position():
    index = lax.axis_index(AXIS)
    return (index % 2, (index // 2) % 2, index // 4)


def mm(a, b):
    return lax.dot_general(a, b, (((1,), (0,)), ((), ())), preferred_element_type=F32)


def mm_nt(a, b):
    return lax.dot_general(a, b, (((1,), (1,)), ((), ())), preferred_element_type=F32)


def mm_tn(a, b):
    return lax.dot_general(a, b, (((0,), (0,)), ((), ())), preferred_element_type=F32)


def shifted(field, by, half):
    rows, _, chans = field.shape
    flat = field.reshape(rows * half, chans)
    column = lax.broadcasted_iota(jnp.int32, flat.shape, 0) % half
    moved = pltpu.roll(flat, by % (rows * half), axis=0)
    edge = 0 if by > 0 else half - 1
    return jnp.where(column == edge, 0.0, moved).reshape(field.shape)


def wide_pair(even, odd, half):
    before = shifted(odd, 1, half).astype(BF16)
    after = shifted(even, -1, half).astype(BF16)
    even, odd = (even.astype(BF16), odd.astype(BF16))
    return (
        jnp.concatenate([before, even, odd], axis=-1),
        jnp.concatenate([even, odd, after], axis=-1),
    )


def forward_kernel(
    own_f, other_f, halo_1f, halo_2f, own_g, other_g, halo_1g, halo_2g, weight_a,
    keep_b, send_b, pre_ref, stacked_a, stacked_b, cot_ref, flat,
):
    core, side, plane = position()
    frames, rows, width, chans = own_f.shape
    half = width // 2
    ext = 2 * rows + 4
    block = rows * width
    for t in range(frames):
        base = t * ext * width
        top = jnp.where(core == 0, halo_1f[t].astype(F32), halo_2f[t].astype(F32))
        low = jnp.where(core == 0, halo_2f[t].astype(F32), halo_1f[t].astype(F32))
        flat[base : base + 2 * width] = top.reshape(2 * width, chans)
        flat[base + (ext - 2) * width : base + ext * width] = low.reshape(2 * width, chans)
        at = pl.multiple_of(base + 2 * width + core * block, 2 * width)
        flat[pl.ds(at, block)] = own_f[t].astype(F32).reshape(block, chans)
        at = pl.multiple_of(base + 2 * width + (1 - core) * block, 2 * width)
        flat[pl.ds(at, block)] = other_f[t].astype(F32).reshape(block, chans)
        cot_ref[t, 0] = jnp.where(core == 0, halo_1g[t, 0], halo_2g[t, 0])
        cot_ref[t, rows + 1] = jnp.where(core == 0, halo_2g[t, 0], halo_1g[t, 0])
        cot_ref[t, pl.ds(1 + core * (rows // 2), rows // 2)] = own_g[t]
        cot_ref[t, pl.ds(1 + (1 - core) * (rows // 2), rows // 2)] = other_g[t]
    count = frames * ext
    even = flat[pl.ds(0, count * half, stride=2), :].reshape(count, half, chans)
    odd = flat[pl.ds(1, count * half, stride=2), :].reshape(count, half, chans)
    taps_even, taps_odd = wide_pair(even, odd, half)
    stacked_a[:, :, 0:half] = taps_even.reshape(frames, ext, half, 3 * chans)
    stacked_a[:, :, half:width] = taps_odd.reshape(frames, ext, half, 3 * chans)

    inner = ext - 2
    shared = jnp.zeros((inner * width, chans), F32)
    latest = [jnp.zeros((inner * width, chans), F32) for _ in range(2)]
    for kh in range(3):
        first = stacked_a[0, kh : kh + inner].reshape(inner * width, 3 * chans)
        second = stacked_a[1, kh : kh + inner].reshape(inner * width, 3 * chans)
        shared += mm(first, weight_a[0, kh]) + mm(first, weight_a[1, kh])
        latest[0] += mm(first, weight_a[2, kh])
        latest[1] += mm(second, weight_a[2, kh])
    even = even.reshape(frames, ext, half, chans)
    odd = odd.reshape(frames, ext, half, chans)
    outside = (plane == 0) & (side == 0)
    row = lax.broadcasted_iota(jnp.int32, (inner, half, chans), 0)
    hidden = outside & (row == 0)
    for t in range(frames):
        conv = (shared + latest[t]).reshape(inner, 2, half, chans)
        pre_even = even[t, 1 : ext - 1] + conv[:, 0]
        pre_odd = odd[t, 1 : ext - 1] + conv[:, 1]
        pre_ref[t, :, 0:half] = pre_even
        pre_ref[t, :, half:width] = pre_odd
        act_even = jnp.where(hidden, 0.0, pre_even * jax.nn.sigmoid(pre_even))
        act_odd = jnp.where(hidden, 0.0, pre_odd * jax.nn.sigmoid(pre_odd))
        stacked_b[t] = jnp.concatenate(
            [
                shifted(act_odd, 1, half).astype(BF16),
                act_even.astype(BF16),
                act_odd.astype(BF16),
            ],
            axis=-1,
        ).reshape(inner // 2, 2, half, 3 * chans)
    wide = own_g.shape[-1]
    grads = [cot_ref[t, 1 : rows + 1].reshape(rows * half, wide) for t in range(frames)]
    grad = jnp.concatenate(grads, axis=0)
    part = chans // 2
    for kh in range(3):
        lo, parity = divmod(kh, 2)
        piece = [
            stacked_b[t, lo : lo + rows, parity].reshape(rows * half, 3 * chans)
            for t in (0, core)
        ]
        total = mm_tn(jnp.concatenate(piece, axis=0), grad)
        for kw in range(3):
            upper = total[kw * chans : kw * chans + part].astype(BF16)
            lower = total[kw * chans + part : (kw + 1) * chans].astype(BF16)
            keep_b[kh * 3 + kw] = jnp.where(side == 0, upper, lower)
            send_b[kh * 3 + kw] = jnp.where(side == 0, lower, upper)


def backward_kernel(last, cot_ref, pre_ref, stacked_a, weight_b, keep_a, send_a, pre_grad):
    core, side, plane = position()
    frames, ext_g, half, wide = cot_ref.shape
    chans = weight_b.shape[3]
    inner = pre_ref.shape[1]
    width = 2 * half
    mid = inner // 2
    cot = cot_ref[...].reshape(frames * ext_g, half, wide)
    ahead = shifted(cot.astype(F32), -1, half).astype(BF16)
    both = jnp.concatenate([cot, ahead], axis=-1).reshape(frames, ext_g, half, 2 * wide)
    later = both[:, 1:].reshape(frames * mid * half, 2 * wide)
    sooner = both[:, :-1].reshape(frames * mid * half, 2 * wide)
    zero = jnp.zeros((chans, wide), BF16)

    def taps(kt, kh):
        return jnp.concatenate(
            [
                jnp.concatenate([weight_b[kt, kh, 1], zero], axis=1),
                jnp.concatenate([weight_b[kt, kh, 2], weight_b[kt, kh, 0]], axis=1),
            ],
            axis=0,
        )

    def rows_of(kt):
        even = mm_nt(later, taps(kt, 1))
        odd = mm_nt(later, taps(kt, 0)) + mm_nt(sooner, taps(kt, 2))
        shape = (frames, mid, half, 2 * chans)
        return (even.reshape(shape), odd.reshape(shape))

    copies = [rows_of(kt) for kt in range(3)]
    outside_low = (plane == 0) & (side == 0)
    outside_high = (plane == last // 2) & (side == last % 2)
    row = lax.broadcasted_iota(jnp.int32, (inner, half, chans), 0)
    hidden = (outside_low & (row == 0)) | (outside_high & (row == inner - 1))
    for t in range(frames):
        sums = []
        for parity in range(2):
            total = copies[2][parity][t]
            if t == 0:
                total = total + (copies[0][parity][0] + copies[1][parity][0])
                total = total + (copies[0][parity][1] + copies[1][parity][1])
            sums.append(total)
        grad = jnp.stack([sums[1], sums[0]], axis=1).reshape(inner, half, 2 * chans)
        for parity in range(2):
            act_grad = grad[:, :, parity * chans : (parity + 1) * chans]
            pre = pre_ref[t, :, parity * half : (parity + 1) * half]
            sig = jax.nn.sigmoid(pre)
            value = act_grad * sig * (1.0 + pre * (1.0 - sig))
            value = jnp.where(hidden, 0.0, value).astype(BF16)
            pre_grad[t, :, parity * half : (parity + 1) * half] = value
    rows = inner - 2
    grads = [pre_grad[t, 1 : rows + 1].reshape(rows * width, chans) for t in range(frames)]
    grad = jnp.concatenate(grads, axis=0)
    part = chans // 2
    for kh in range(3):
        piece = [
            stacked_a[t, kh + 1 : kh + 1 + rows].reshape(rows * width, 3 * chans)
            for t in (0, core)
        ]
        total = mm_tn(jnp.concatenate(piece, axis=0), grad)
        for kw in range(3):
            upper = total[kw * chans : kw * chans + part].astype(BF16)
            lower = total[kw * chans + part : (kw + 1) * chans].astype(BF16)
            keep_a[kh * 3 + kw] = jnp.where(side == 0, upper, lower)
            send_a[kh * 3 + kw] = jnp.where(side == 0, lower, upper)


def output_kernel(stacked_b, pre_grad, weight_a, weight_b, encoded, frames_grad, flat):
    core, _, _ = position()
    frames, _, _, half, _ = stacked_b.shape
    rows, width, chans = frames_grad.shape[1:]
    short = rows // 2
    wide = encoded.shape[-1]
    count = short * half
    shared = jnp.zeros((count, wide), F32)
    latest = jnp.zeros((frames * count, wide), F32)
    for kh in range(3):
        lo, parity = divmod(kh, 2)
        piece = [
            stacked_b[t, pl.ds(short * core + lo, short), parity].reshape(count, 3 * chans)
            for t in range(frames)
        ]
        shared += mm(piece[0], weight_b[0, kh]) + mm(piece[0], weight_b[1, kh])
        latest += mm(jnp.concatenate(piece, axis=0), weight_b[2, kh])
    for t in range(frames):
        value = shared + latest[t * count : (t + 1) * count]
        encoded[t] = value.astype(BF16).reshape(short, half, wide)

    ext = rows + 2
    own = pre_grad[:, pl.ds(rows * core, ext)].astype(F32)
    even = own[:, :, 0:half].reshape(frames * ext, half, chans)
    odd = own[:, :, half:width].reshape(frames * ext, half, chans)
    before = shifted(odd, 1, half).astype(BF16)
    after = shifted(even, -1, half).astype(BF16)
    even_16, odd_16 = (even.astype(BF16), odd.astype(BF16))
    stacked = jnp.stack(
        [
            jnp.concatenate([odd_16, even_16, before], axis=-1),
            jnp.concatenate([after, odd_16, even_16], axis=-1),
        ],
        axis=1,
    ).reshape(frames, ext, width, 3 * chans)
    early = jnp.zeros((frames * rows * width, chans), F32)
    late = jnp.zeros((frames * rows * width, chans), F32)
    for kh in range(3):
        piece = stacked[:, 2 - kh : 2 - kh + rows].reshape(frames * rows * width, 3 * chans)
        for kt in range(3):
            taps = jnp.concatenate([weight_a[kt, kh, kw] for kw in range(3)], axis=1)
            if kt == 2:
                late += mm_nt(piece, taps)
            else:
                early += mm_nt(piece, taps)
    early = early.reshape(frames, rows, 2, half, chans)
    late = late.reshape(frames, rows, 2, half, chans)
    even = even.reshape(frames, ext, half, chans)[:, 1 : rows + 1]
    odd = odd.reshape(frames, ext, half, chans)[:, 1 : rows + 1]
    size = rows * half
    for t in range(frames):
        total = late[t]
        if t == 0:
            total = total + (early[0] + early[1])
        for parity, value in ((0, even), (1, odd)):
            summed = value[t] + total[:, parity]
            flat[pl.ds(t * 2 * size + parity, size, stride=2), :] = summed.reshape(size, chans)
    frames_grad[...] = flat[...].reshape(frames_grad.shape).astype(BF16)


def add_kernel(keep, recv, *outs):
    _, _, plane = position()
    planes = len(outs)
    rows = keep.shape[1] // planes
    for step in range(planes):
        at = pl.multiple_of(((plane + step) % planes) * rows, rows)
        value = keep[:, pl.ds(at, rows)].astype(F32) + recv[:, pl.ds(at, rows)].astype(F32)
        outs[step][...] = value.astype(BF16)


def finish_kernel(scale, parts_a, parts_b, out):
    chans = parts_a[0].shape[-1]

    def total(parts):
        value = parts[0][...].astype(F32)
        for part in parts[1:]:
            value = value + part[...].astype(F32)
        return (value * scale).astype(BF16)

    out[:, :, 0:chans] = total(parts_a)
    out[:, :, chans:] = total(parts_b)


def assemble_kernel(planes, *refs):
    pieces, (out_a, out_b) = (refs[:-2], refs[-2:])
    core, side, plane = position()
    chans = out_a.shape[-1]
    rows = pieces[0].shape[1]
    at = 0
    for flip_core in range(2):
        for flip_side in range(2):
            for step in range(planes):
                piece = pieces[at]
                at += 1
                tap = core ^ flip_core
                source = (plane - step + planes) % planes
                start = pl.multiple_of((side ^ flip_side) * (chans // 2) + source * rows, rows)
                for slot in (2 * tap, 1 + tap):
                    out_a[slot, :, pl.ds(start, rows)] = piece[:, :, 0:chans]
                    out_b[slot, :, pl.ds(start, rows)] = piece[:, :, chans:]


def call(body, outs, args, scratch=(), flops=0):
    size = sum(a.size * a.dtype.itemsize for a in args)
    size += sum(o.size * o.dtype.itemsize for o in outs)
    return pl.pallas_call(
        body,
        out_shape=outs,
        scratch_shapes=scratch,
        compiler_params=pltpu.CompilerParams(vmem_limit_bytes=VMEM_LIMIT),
        cost_estimate=pl.CostEstimate(flops=flops, bytes_accessed=size, transcendentals=0),
    )(*args)


def on_device(frames, weight_a, weight_b, cotangent):
    count, rows, width, chans = frames.shape
    assert count == 2
    wide = weight_b.shape[-1]
    half = width // 2
    n = lax.axis_size(AXIS)
    chips = n // 2
    planes = n // 4
    core, side, plane = position()
    shape = jax.ShapeDtypeStruct

    def send(value, pairs):
        return lax.ppermute(value, AXIS, pairs)

    swap_core = [(i, i ^ 1) for i in range(n)]
    swap_side = [(i, i ^ 2) for i in range(n)]
    near = [(2 * k + 1, 2 * k + 2) for k in range(chips - 1)]
    near += [(2 * k + 2, 2 * k + 1) for k in range(chips - 1)]
    far = [(2 * k + 1, 2 * k + 3) for k in range(chips - 1)]
    far += [(2 * k + 2, 2 * k) for k in range(chips - 1)]

    edge_f = lax.dynamic_slice_in_dim(frames, core * (rows - 2), 2, axis=1)
    edge_g = lax.dynamic_slice_in_dim(cotangent, core * (rows // 2 - 1), 1, axis=1)
    edge_g = jnp.concatenate([edge_g[..., :chans], edge_g[..., chans:]], axis=1)
    edge = jnp.concatenate([edge_f, edge_g.reshape(count, 1, width, chans)], axis=1)
    halos = [send(edge, near), send(edge, far)]
    halo_f = [halo[:, 0:2] for halo in halos]
    halo_g = [
        jnp.concatenate([halo[:, 2:3, 0:half], halo[:, 2:3, half:]], axis=-1) for halo in halos
    ]
    other_f = send(frames, swap_core)
    other_g = send(cotangent, swap_core)

    inner = 2 * rows + 2
    kernel_a = weight_a.reshape(3, 3, 3 * chans, chans)
    kernel_b = weight_b.reshape(3, 3, 3 * chans, wide)
    part = chans // 2
    keep_b, send_b, pre, stacked_a, stacked_b, cot = call(
        forward_kernel,
        (
            shape((9, part, wide), BF16),
            shape((9, part, wide), BF16),
            shape((count, inner, width, chans), F32),
            shape((count, inner + 2, width, 3 * chans), BF16),
            shape((count, inner // 2, 2, half, 3 * chans), BF16),
            shape((count, rows + 2, half, wide), BF16),
        ),
        (frames, other_f, *halo_f, cotangent, other_g, *halo_g, kernel_a),
        [pltpu.VMEM((count * (inner + 2) * width, chans), F32)],
        flops=10**9,
    )
    recv_b = send(send_b, swap_side)

    def backward(*refs):
        backward_kernel(chips - 1, *refs)

    keep_a, send_a, pre_grad = call(
        backward,
        (
            shape((9, part, chans), BF16),
            shape((9, part, chans), BF16),
            shape((count, inner, width, chans), BF16),
        ),
        (cot, pre, stacked_a, weight_b),
        flops=10**9,
    )
    recv_a = send(send_a, swap_side)
    encoded, frames_grad = call(
        output_kernel,
        (shape(cotangent.shape, BF16), shape(frames.shape, BF16)),
        (stacked_b, pre_grad, weight_a, kernel_b),
        [pltpu.VMEM((count * rows * width, chans), F32)],
        flops=10**9,
    )

    scale = (count * rows * n * width) ** (-0.5)
    if part % (8 * planes):
        taps = jnp.arange(2)[:, None, None, None, None] == core
        sides = jnp.arange(2)[None, None, :, None, None] == side
        both = []
        for keep, recv in ((keep_a, recv_a), (keep_b, recv_b)):
            value = keep.astype(F32) + recv.astype(F32)
            slots = jnp.where(taps & sides, value[None, :, None], 0.0)
            total = lax.psum(slots, AXIS) * scale
            total = total.astype(BF16).reshape(2, 3, 3, chans, -1)
            both.append(jnp.concatenate([total[:1], total], axis=0))
        return (encoded, frames_grad, both[0], both[1])

    parts = []
    for keep, recv in ((keep_b, recv_b), (keep_a, recv_a)):
        piece = shape((9, part // planes, keep.shape[-1]), BF16)
        pieces = call(add_kernel, (piece,) * planes, (keep, recv))
        got = [pieces[0]]
        for step in range(1, planes):
            to = [(i, (i + 4 * step) % n) for i in range(n)]
            got.append(send(pieces[step], to))
        parts.append(got)

    def finish(*refs):
        finish_kernel(scale, refs[:planes], refs[planes : 2 * planes], refs[-1])

    (own,) = call(
        finish,
        (shape((9, part // planes, chans + wide), BF16),),
        (*parts[1], *parts[0]),
    )
    pieces = [own]
    for step in range(1, planes):
        pieces.append(send(own, [(i, (i + 4 * step) % n) for i in range(n)]))
    pieces += [send(piece, swap_side) for piece in pieces]
    pieces += [send(piece, swap_core) for piece in pieces]

    def assemble(*refs):
        assemble_kernel(planes, *refs)

    grad_a, grad_b = call(
        assemble,
        (shape((3, 9, chans, chans), BF16), shape((3, 9, chans, wide), BF16)),
        pieces,
    )
    return (encoded, frames_grad, grad_a.reshape(weight_a.shape), grad_b.reshape(weight_b.shape))


def solution(mesh):
    in_specs = (P("groups", "height", None, None), P(), P(), P("groups", "height", None, None))
    out_specs = (
        P("groups", "height", None, None),
        P("groups", "height", None, None),
        P("groups", None, None, None, None),
        P("groups", None, None, None, None),
    )
    return jax.shard_map(
        on_device, mesh=mesh, in_specs=in_specs, out_specs=out_specs, check_vma=False
    )
```

time: 365 us -> 70.1 us (0.19); the launches traced: 360 us -> 69.7 us
  other arithmetic: 155 us -> 0.03 us
  blocking collectives: 122 us -> 0 us
  local copies, waits for them, and re-layouts: 43 us -> 4.42 us
  waiting for transfers between devices: 0.02 us -> 29.3 us
  matrix products: 21.4 us -> 0 us
  starting transfers between devices: 16.5 us -> 26.9 us
  Pallas kernels: 0 us -> 8.24 us
    scatter-add x80 -> x0, other arithmetic: 149 us -> none
    psum x1 -> x0, blocking collectives: 122 us -> none  [on_device(): total_a, total_b = lax.psum((flat_a, flat_b), 'height')]
    ppermute x6 -> x27, waiting for transfers between devices: 0.02 us -> 29.3 us  [send(): return lax.ppermute(value, AXIS, pairs)]
    scatter-add x76 -> x0, local copies, waits for them, and re-layouts: 28.4 us -> none
    dot_general x54 -> x0, matrix products: 21.4 us -> none  [the longest x9 6.27 us: backward_b(): lax.dot_general(flat, kernel[kt, kh], (((1,), (1,)), ((), ())), preferred...]
    ppermute x6 -> x27, starting transfers between devices: 16.5 us -> 26.9 us  [send(): return lax.ppermute(value, AXIS, pairs)]
    pallas_call x0 -> x7, Pallas kernels: none -> 8.24 us  [call(): pl.pallas_call(body, out_shape=outs, scratch_shapes=scratch, compiler_par...]
    reshape x1 -> x0, local copies, waits for them, and re-layouts: 3.72 us -> none  [on_device(): weight_b_grad = grad_b.reshape(weight_b.shape)]
  transfers between devices with their start and end apart: 6 -> 27, of which waited for: 0 -> 9; matrix products, arithmetic and copies ran while one was open for 56% -> 0% of each run, Pallas kernels for 0% -> 6%
where the time goes in v1:
time: 70.1 us; the launch traced here: 69.7 us
  waiting for transfers between devices  29.3 us (42%)
  starting transfers between devices  26.9 us (38%)
  Pallas kernels  8.24 us (12%)
  local copies, waits for them, and re-layouts  4.42 us (6%)
  between operations  0.8 us (1%)
    ppermute x27, waiting for transfers between devices, send(): return lax.ppermute(value, AXIS, pairs)  29.3 us
    ppermute x27, starting transfers between devices, send(): return lax.ppermute(value, AXIS, pairs)  26.9 us
    pallas_call x7, Pallas kernels, call(): pl.pallas_call(body, out_shape=outs, scratch_shapes=scratch, compiler_par...  8.24 us
    unnamed x10, local copies, waits for them, and re-layouts  2.92 us
  transfers between devices with their start and end apart: 27, of which 9 were waited for; matrix products, arithmetic and copies ran while one was open for 0% of the time, Pallas kernels for 6%

profile of v1, /device:TPU:0, one launch (start us, length us, event | category | flops | bytes accessed | tf_op | source)
XLA Modules:
  0.0 69.7 jit_solution(671908588790183533)
XLA Ops:
  0.7 0.7 %constant_dynamic-slice_fusion = (bf16[2,1,16,128]{3,2,1,0:T(8,128)(2,1)S(1)}, bf16[2,1,16,128]{3,2,1,0:T(8,128)(2,1)S(1)}) fusion(bf16[2,4,16,256]{3,2,1,0:T(8,128)(2,1)} %own_g.1, s32[]{:T(128)S(6)} %select_n.15, s32[]{:T(128)S(6)} %add.13), kind=kLoop, calls=%fused_computation.4 | loop fusion | bytes 32776 | tf_op jit(solution)/shard_map/slice | solution.py:332
  1.4 0.8 %constant_dynamic-slice_fusion.2 = bf16[2,2,32,128]{3,2,1,0:T(8,128)(2,1)S(1)} fusion(bf16[2,8,32,128]{3,2,1,0:T(8,128)(2,1)} %own_f.1, s32[]{:T(128)S(6)} %select_n.14), kind=kLoop, calls=%fused_computation.6 | loop fusion | bytes 65540 | tf_op jit(solution)/shard_map/dynamic_slice | solution.py:330
  2.2 1.3 %collective-permute-start.2 = (bf16[2,3,32,128]{3,2,1,0:T(8,128)(2,1)S(1)}, bf16[2,3,32,128]{3,2,1,0:T(8,128)(2,1)S(1)}, u32[]{:S(2)}, u32[]{:S(2)}) collective-permute-start(bf16[2,3,32,128]{3,2,1,0:T(8,128)(2,1)S(1)} %pad_maximum_fusion), channel_id=1, source_target_pairs={{1,3},{3,5},{5,7},{7,9},{9,11},{11,13},{13,15},{2,0},{4,2},{6,4},{... | collective-permute-start | bytes 147464 | tf_op jit(solution)/shard_map/ppermute | solution.py:321
  3.5 0.7 collective-permute-start.1
  4.1 5.0 %collective-permute-start.3 = (bf16[2,4,16,256]{3,2,1,0:T(8,128)(2,1)}, bf16[2,4,16,256]{3,2,1,0:T(8,128)(2,1)S(1)}, u32[]{:S(2)}, u32[]{:S(2)}) collective-permute-start(bf16[2,4,16,256]{3,2,1,0:T(8,128)(2,1)} %own_g.1), channel_id=1, source_target_pairs={{0,1},{1,0},{2,3},{3,2},{4,5},{5,4},{6,7},{7,6},{8,9},{9,8},{10,11... | collective-permute-start | bytes 196616 | tf_op jit(solution)/shard_map/ppermute | solution.py:321
  9.1 0.1 collective-permute-start
  9.2 0.0 collective-permute-done.2
  9.3 1.0 %collective-permute-done.3.other_g = bf16[2,4,16,256]{3,2,1,0:T(8,128)(2,1)S(1)} collective-permute-done((bf16[2,4,16,256]{3,2,1,0:T(8,128)(2,1)}, bf16[2,4,16,256]{3,2,1,0:T(8,128)(2,1)S(1)}, u32[]{:S(2)}, u32[]{:S(2)}) %collective-permute-start.3) | collective-permute-done | bytes 65568 | tf_op jit(solution)/shard_map/ppermute | solution.py:321
  10.3 0.4 collective-permute-done.other_f
  10.7 0.9 %copy-done = bf16[2,8,32,128]{3,2,1,0:T(8,128)(2,1)S(1)} copy-done((bf16[2,8,32,128]{3,2,1,0:T(8,128)(2,1)S(1)}, bf16[2,8,32,128]{3,2,1,0:T(8,128)(2,1)}, u32[]{:S(2)}) %copy-start) | copy-done | bytes 131096
  11.6 0.8 %copy-done.1 = bf16[2,4,16,256]{3,2,1,0:T(8,128)(2,1)S(1)} copy-done((bf16[2,4,16,256]{3,2,1,0:T(8,128)(2,1)S(1)}, bf16[2,4,16,256]{3,2,1,0:T(8,128)(2,1)}, u32[]{:S(2)}) %copy-start.1) | copy-done | bytes 65560
  12.5 1.2 %copy-done.3 = bf16[3,3,3,128,128]{4,3,2,1,0:T(8,128)(2,1)S(1)} copy-done((bf16[3,3,3,128,128]{4,3,2,1,0:T(8,128)(2,1)S(1)}, bf16[3,3,3,128,128]{4,3,2,1,0:T(8,128)(2,1)}, u32[]{:S(2)}) %copy-start.3) | copy-done | bytes 884760
  13.6 2.1 %shard_map.75 = (bf16[9,64,256]{2,1,0:T(8,128)(2,1)S(1)}, bf16[9,64,256]{2,1,0:T(8,128)(2,1)S(1)}, f32[2,18,32,128]{3,2,1,0:T(8,128)S(1)}, bf16[2,20,32,384]{3,2...) custom-call(bf16[2,8,32,128]{3,2,1,0:T(8,128)(2,1)S(1)} %copy-done, ...), custom_call_target="tpu_custom_call" | custom-call | flops 1000000000 | bytes 4145152 | tf_op jit(solution)/shard_map/pallas_call | solution.py:300
  15.7 3.0 %collective-permute-start.8 = (bf16[9,64,256]{2,1,0:T(8,128)(2,1)S(1)}, bf16[9,64,256]{2,1,0:T(8,128)(2,1)S(1)}, u32[]{:S(2)}, u32[]{:S(2)}) collective-permute-start(bf16[9,64,256]{2,1,0:T(8,128)(2,1)S(1)} %get-tuple-element.39), channel_id=1, source_target_pairs={{0,2},{1,3},{2,0},{3,1},{4,6},{5,7},{6,4},{7,5},{8,10},{9,11},{10,... | collective-permute-start | bytes 884744 | tf_op jit(solution)/shard_map/ppermute | solution.py:321
  18.7 2.1 %shard_map.76 = (bf16[9,64,128]{2,1,0:T(8,128)(2,1)S(1)}, bf16[9,64,128]{2,1,0:T(8,128)(2,1)S(1)}, bf16[2,18,32,128]{3,2,1,0:T(8,128)(2,1)S(1)}) custom-call(bf16[2,10,16,256]{3,2,1,0:T(8,128)(2,1)S(1)} %get-tuple-element.26.refs_0_, f32[2,18,32,128]{3,2,1,0:T(8,128)S(1)} %get-tuple-element.27.refs_1_, ...), custom_call_target="tpu_custom_call" | custom-call | flops 1000000000 | bytes 4096000 | tf_op jit(solution)/shard_map/pallas_call | solution.py:300
  20.8 0.1 collective-permute-start.4
  20.9 8.7 %collective-permute-done.4.recv = bf16[9,64,128]{2,1,0:T(8,128)(2,1)S(1)} collective-permute-done((bf16[9,64,128]{2,1,0:T(8,128)(2,1)S(1)}, bf16[9,64,128]{2,1,0:T(8,128)(2,1)S(1)}, u32[]{:S(2)}, u32[]{:S(2)}) %collective-permute-start.4) | collective-permute-done | bytes 147488 | tf_op jit(solution)/shard_map/ppermute | solution.py:321
  29.6 2.0 %collective-permute-start.5 = (bf16[9,16,128]{2,1,0:T(8,128)(2,1)S(1)}, bf16[9,16,128]{2,1,0:T(8,128)(2,1)S(1)}, u32[]{:S(2)}, u32[]{:S(2)}) collective-permute-start(bf16[9,16,128]{2,1,0:T(8,128)(2,1)S(1)} %get-tuple-element.35), channel_id=1, source_target_pairs={{0,4},{1,5},{2,6},{3,7},{4,8},{5,9},{6,10},{7,11},{8,12},{9,13},{1... | collective-permute-start | bytes 110600 | tf_op jit(solution)/shard_map/ppermute | solution.py:321
  31.6 0.0 collective-permute-done.8.recv
  31.6 0.1 shard_map.79
  31.6 1.6 %collective-permute-start.9 = (bf16[9,16,256]{2,1,0:T(8,128)(2,1)S(1)}, bf16[9,16,256]{2,1,0:T(8,128)(2,1)S(1)}, u32[]{:S(2)}, u32[]{:S(2)}) collective-permute-start(bf16[9,16,256]{2,1,0:T(8,128)(2,1)S(1)} %get-tuple-element.41), channel_id=1, source_target_pairs={{0,4},{1,5},{2,6},{3,7},{4,8},{5,9},{6,10},{7,11},{8,12},{9,13},{1... | collective-permute-start | bytes 221192 | tf_op jit(solution)/shard_map/ppermute | solution.py:321
  33.3 0.9 %collective-permute-start.10 = (bf16[9,16,256]{2,1,0:T(8,128)(2,1)S(1)}, bf16[9,16,256]{2,1,0:T(8,128)(2,1)S(1)}, u32[]{:S(2)}, u32[]{:S(2)}) collective-permute-start(bf16[9,16,256]{2,1,0:T(8,128)(2,1)S(1)} %get-tuple-element.42), channel_id=1, source_target_pairs={{0,8},{1,9},{2,10},{3,11},{4,12},{5,13},{6,14},{7,15},{8,0},{9,1},... | collective-permute-start | bytes 221192 | tf_op jit(solution)/shard_map/ppermute | solution.py:321
  34.1 2.4 %collective-permute-start.11 = (bf16[9,16,256]{2,1,0:T(8,128)(2,1)S(1)}, bf16[9,16,256]{2,1,0:T(8,128)(2,1)S(1)}, u32[]{:S(2)}, u32[]{:S(2)}) collective-permute-start(bf16[9,16,256]{2,1,0:T(8,128)(2,1)S(1)} %get-tuple-element.43), channel_id=1, source_target_pairs={{0,12},{1,13},{2,14},{3,15},{4,0},{5,1},{6,2},{7,3},{8,4},{9,5},{1... | collective-permute-start | bytes 221192 | tf_op jit(solution)/shard_map/ppermute | solution.py:321
  36.5 1.0 %collective-permute-start.6 = (bf16[9,16,128]{2,1,0:T(8,128)(2,1)S(1)}, bf16[9,16,128]{2,1,0:T(8,128)(2,1)S(1)}, u32[]{:S(2)}, u32[]{:S(2)}) collective-permute-start(bf16[9,16,128]{2,1,0:T(8,128)(2,1)S(1)} %get-tuple-element.36), channel_id=1, source_target_pairs={{0,8},{1,9},{2,10},{3,11},{4,12},{5,13},{6,14},{7,15},{8,0},{9,1},... | collective-permute-start | bytes 110600 | tf_op jit(solution)/shard_map/ppermute | solution.py:321
  37.5 0.0 collective-permute-done.5.refs_1_
  37.5 1.0 %collective-permute-start.7 = (bf16[9,16,128]{2,1,0:T(8,128)(2,1)S(1)}, bf16[9,16,128]{2,1,0:T(8,128)(2,1)S(1)}, u32[]{:S(2)}, u32[]{:S(2)}) collective-permute-start(bf16[9,16,128]{2,1,0:T(8,128)(2,1)S(1)} %get-tuple-element.37), channel_id=1, source_target_pairs={{0,12},{1,13},{2,14},{3,15},{4,0},{5,1},{6,2},{7,3},{8,4},{9,5},{1... | collective-permute-start | bytes 110600 | tf_op jit(solution)/shard_map/ppermute | solution.py:321
  38.5 5.1 %collective-permute-done.6.refs_2_ = bf16[9,16,128]{2,1,0:T(8,128)(2,1)S(1)} collective-permute-done((bf16[9,16,128]{2,1,0:T(8,128)(2,1)S(1)}, bf16[9,16,128]{2,1,0:T(8,128)(2,1)S(1)}, u32[]{:S(2)}, u32[]{:S(2)}) %collective-permute-start.6) | collective-permute-done | bytes 36896 | tf_op jit(solution)/shard_map/ppermute | solution.py:321
  43.7 0.0 collective-permute-done.7.refs_3_
  43.7 0.0 collective-permute-done.9.refs_5_
  43.7 0.0 collective-permute-done.10.refs_6_
  43.7 0.1 shard_map.80.refs_0_
  43.8 2.0 %collective-permute-start.15 = (bf16[9,16,384]{2,1,0:T(8,128)(2,1)S(1)}, bf16[9,16,384]{2,1,0:T(8,128)(2,1)S(1)}, u32[]{:S(2)}, u32[]{:S(2)}) collective-permute-start(bf16[9,16,384]{2,1,0:T(8,128)(2,1)S(1)} %shard_map.80.refs_0_), channel_id=1, source_target_pairs={{0,2},{1,3},{2,0},{3,1},{4,6},{5,7},{6,4},{7,5},{8,10},{9,11},{10,... | collective-permute-start | bytes 331784 | tf_op jit(solution)/shard_map/ppermute | solution.py:321
  45.7 1.8 %collective-permute-start.14 = (bf16[9,16,384]{2,1,0:T(8,128)(2,1)S(1)}, bf16[9,16,384]{2,1,0:T(8,128)(2,1)S(1)}, u32[]{:S(2)}, u32[]{:S(2)}) collective-permute-start(bf16[9,16,384]{2,1,0:T(8,128)(2,1)S(1)} %shard_map.80.refs_0_), channel_id=1, source_target_pairs={{0,12},{1,13},{2,14},{3,15},{4,0},{5,1},{6,2},{7,3},{8,4},{9,5},{1... | collective-permute-start | bytes 331784 | tf_op jit(solution)/shard_map/ppermute | solution.py:321
  47.5 0.0 collective-permute-start.19
  47.5 1.0 %collective-permute-start.13 = (bf16[9,16,384]{2,1,0:T(8,128)(2,1)S(1)}, bf16[9,16,384]{2,1,0:T(8,128)(2,1)S(1)}, u32[]{:S(2)}, u32[]{:S(2)}) collective-permute-start(bf16[9,16,384]{2,1,0:T(8,128)(2,1)S(1)} %shard_map.80.refs_0_), channel_id=1, source_target_pairs={{0,8},{1,9},{2,10},{3,11},{4,12},{5,13},{6,14},{7,15},{8,0},{9,1},... | collective-permute-start | bytes 331784 | tf_op jit(solution)/shard_map/ppermute | solution.py:321
  48.4 0.4 collective-permute-done.15.refs_4_
  48.9 0.0 collective-permute-start.23
  48.9 1.7 %collective-permute-done.14.refs_3_ = bf16[9,16,384]{2,1,0:T(8,128)(2,1)S(1)} collective-permute-done((bf16[9,16,384]{2,1,0:T(8,128)(2,1)S(1)}, bf16[9,16,384]{2,1,0:T(8,128)(2,1)S(1)}, u32[]{:S(2)}, u32[]{:S(2)}) %collective-permute-start.14) | collective-permute-done | bytes 110624 | tf_op jit(solution)/shard_map/ppermute | solution.py:321
  50.5 0.6 collective-permute-start.18
  51.1 7.2 %collective-permute-done.13.refs_2_ = bf16[9,16,384]{2,1,0:T(8,128)(2,1)S(1)} collective-permute-done((bf16[9,16,384]{2,1,0:T(8,128)(2,1)S(1)}, bf16[9,16,384]{2,1,0:T(8,128)(2,1)S(1)}, u32[]{:S(2)}, u32[]{:S(2)}) %collective-permute-start.13) | collective-permute-done | bytes 110624 | tf_op jit(solution)/shard_map/ppermute | solution.py:321
  58.3 0.2 collective-permute-start.17
  58.6 1.8 %collective-permute-start.16 = (bf16[9,16,384]{2,1,0:T(8,128)(2,1)S(1)}, bf16[9,16,384]{2,1,0:T(8,128)(2,1)S(1)}, u32[]{:S(2)}, u32[]{:S(2)}) collective-permute-start(bf16[9,16,384]{2,1,0:T(8,128)(2,1)S(1)} %collective-permute-done.12.refs_1_), channel_id=1, source_target_pairs={{0,2},{1,3},{2,0},{3,1},{4,6},{5,7},{6,4},{7,5},{8,10},{9,11},{10,... | collective-permute-start | bytes 331784 | tf_op jit(solution)/shard_map/ppermute | solution.py:321
  60.3 0.5 collective-permute-start.20
  60.9 0.1 collective-permute-start.26
  60.9 3.3 %collective-permute-done.17.refs_6_ = bf16[9,16,384]{2,1,0:T(8,128)(2,1)S(1)} collective-permute-done((bf16[9,16,384]{2,1,0:T(8,128)(2,1)S(1)}, bf16[9,16,384]{2,1,0:T(8,128)(2,1)S(1)}, u32[]{:S(2)}, u32[]{:S(2)}) %collective-permute-start.17) | collective-permute-done | bytes 110624 | tf_op jit(solution)/shard_map/ppermute | solution.py:321
  64.2 1.5 %collective-permute-done.16.refs_5_ = bf16[9,16,384]{2,1,0:T(8,128)(2,1)S(1)} collective-permute-done((bf16[9,16,384]{2,1,0:T(8,128)(2,1)S(1)}, bf16[9,16,384]{2,1,0:T(8,128)(2,1)S(1)}, u32[]{:S(2)}, u32[]{:S(2)}) %collective-permute-start.16) | collective-permute-done | bytes 110624 | tf_op jit(solution)/shard_map/ppermute | solution.py:321
  65.7 2.0 %shard_map.77 = (bf16[2,4,16,256]{3,2,1,0:T(8,128)(2,1)}, bf16[2,8,32,128]{3,2,1,0:T(8,128)(2,1)}) custom-call(bf16[2,9,2,16,384]{4,3,2,1,0:T(8,128)(2,1)S(1)} %get-tuple-element.25.stacked_b, bf16[2,18,32,128]{3,2,1,0:T(8,128)(2,1)S(1)} %get-tuple-element.29.pre_grad, bf16[3,3,3,128,128]{4,3,2,1,0:T(8,128)(2,1)S(1)} %copy-done.4, ...), custom_call_target="tpu_custom_call" | custom-call | flops 1000000000 | bytes 3588096 | tf_op jit(solution)/shard_map/pallas_call | solution.py:300
  67.8 1.9 %shard_map.81 = (bf16[3,9,128,128]{3,2,1,0:T(8,128)(2,1)}, bf16[3,9,128,256]{3,2,1,0:T(8,128)(2,1)}) custom-call(bf16[9,16,384]{2,1,0:T(8,128)(2,1)S(1)} %shard_map.80.refs_0_, bf16[9,16,384]{2,1,0:T(8,128)(2,1)S(1)} %collective-permute-done.12.refs_1_, bf16[9,16,384]{2,1,0:T(8,128)(2,1)S(1)} %collective-permute-done.13.refs_2_, ...), custom_call_target="tpu_custom_call" | custom-call | bytes 4423680 | tf_op jit(solution)/shard_map/pallas_call | solution.py:300
  (33 shorter events, 0.1 us)
Async XLA Ops:
  2.2 7.1 %collective-permute-start.2 = (bf16[2,3,32,128]{3,2,1,0:T(8,128)(2,1)S(1)}, bf16[2,3,32,128]{3,2,1,0:T(8,128)(2,1)S(1)}, u32[]{:S(2)}, u32[]{:S(2)}) collective-permute-start(bf16[2,3,32,128]{3,2,1,0:T(8,128)(2,1)S(1)} %pad_maximum_fusion), channel_id=1, source_target_pairs={{1,3},{3,5},{5,7},{7,9},{9,11},{11,13},{13,15},{2,0},{4,2},{6,4},{... | collective-permute-start | bytes 147464 | tf_op jit(solution)/shard_map/ppermute | solution.py:321
  3.5 5.8 %collective-permute-start.1 = (bf16[2,3,32,128]{3,2,1,0:T(8,128)(2,1)S(1)}, bf16[2,3,32,128]{3,2,1,0:T(8,128)(2,1)S(1)}, u32[]{:S(2)}, u32[]{:S(2)}) collective-permute-start(bf16[2,3,32,128]{3,2,1,0:T(8,128)(2,1)S(1)} %pad_maximum_fusion), channel_id=1, source_target_pairs={{1,2},{3,4},{5,6},{7,8},{9,10},{11,12},{13,14},{2,1},{4,3},{6,5},{... | collective-permute-start | bytes 147464 | tf_op jit(solution)/shard_map/ppermute | solution.py:321
  4.1 6.1 %collective-permute-start.3 = (bf16[2,4,16,256]{3,2,1,0:T(8,128)(2,1)}, bf16[2,4,16,256]{3,2,1,0:T(8,128)(2,1)S(1)}, u32[]{:S(2)}, u32[]{:S(2)}) collective-permute-start(bf16[2,4,16,256]{3,2,1,0:T(8,128)(2,1)} %own_g.1), channel_id=1, source_target_pairs={{0,1},{1,0},{2,3},{3,2},{4,5},{5,4},{6,7},{7,6},{8,9},{9,8},{10,11... | collective-permute-start | bytes 196616 | tf_op jit(solution)/shard_map/ppermute | solution.py:321
  9.1 1.6 %collective-permute-start = (bf16[2,8,32,128]{3,2,1,0:T(8,128)(2,1)}, bf16[2,8,32,128]{3,2,1,0:T(8,128)(2,1)S(1)}, u32[]{:S(2)}, u32[]{:S(2)}) collective-permute-start(bf16[2,8,32,128]{3,2,1,0:T(8,128)(2,1)} %own_f.1), channel_id=1, source_target_pairs={{0,1},{1,0},{2,3},{3,2},{4,5},{5,4},{6,7},{7,6},{8,9},{9,8},{10,11... | collective-permute-start | bytes 393224 | tf_op jit(solution)/shard_map/ppermute | solution.py:321
  10.7 0.9 %copy-start = (bf16[2,8,32,128]{3,2,1,0:T(8,128)(2,1)S(1)}, bf16[2,8,32,128]{3,2,1,0:T(8,128)(2,1)}, u32[]{:S(2)}) copy-start(bf16[2,8,32,128]{3,2,1,0:T(8,128)(2,1)} %own_f.1) | copy-start | bytes 393220
  11.6 0.8 %copy-start.1 = (bf16[2,4,16,256]{3,2,1,0:T(8,128)(2,1)S(1)}, bf16[2,4,16,256]{3,2,1,0:T(8,128)(2,1)}, u32[]{:S(2)}) copy-start(bf16[2,4,16,256]{3,2,1,0:T(8,128)(2,1)} %own_g.1) | copy-start | bytes 196612
  12.5 1.2 %copy-start.3 = (bf16[3,3,3,128,128]{4,3,2,1,0:T(8,128)(2,1)S(1)}, bf16[3,3,3,128,128]{4,3,2,1,0:T(8,128)(2,1)}, u32[]{:S(2)}) copy-start(bf16[3,3,3,128,128]{4,3,2,1,0:T(8,128)(2,1)} %weight_a.1) | copy-start | bytes 2654212
  13.6 5.1 %copy-start.2 = (bf16[3,3,3,128,256]{4,3,2,1,0:T(8,128)(2,1)S(1)}, bf16[3,3,3,128,256]{4,3,2,1,0:T(8,128)(2,1)}, u32[]{:S(2)}) copy-start(bf16[3,3,3,128,256]{4,3,2,1,0:T(8,128)(2,1)} %refs_3_.1) | copy-start | bytes 5308420
  15.7 15.9 %collective-permute-start.8 = (bf16[9,64,256]{2,1,0:T(8,128)(2,1)S(1)}, bf16[9,64,256]{2,1,0:T(8,128)(2,1)S(1)}, u32[]{:S(2)}, u32[]{:S(2)}) collective-permute-start(bf16[9,64,256]{2,1,0:T(8,128)(2,1)S(1)} %get-tuple-element.39), channel_id=1, source_target_pairs={{0,2},{1,3},{2,0},{3,1},{4,6},{5,7},{6,4},{7,5},{8,10},{9,11},{10,... | collective-permute-start | bytes 884744 | tf_op jit(solution)/shard_map/ppermute | solution.py:321
  18.7 47.0 %copy-start.4 = (bf16[3,3,3,128,128]{4,3,2,1,0:T(8,128)(2,1)S(1)}, bf16[3,3,3,128,128]{4,3,2,1,0:T(8,128)(2,1)}, u32[]{:S(2)}) copy-start(bf16[3,3,3,128,128]{4,3,2,1,0:T(8,128)(2,1)} %weight_a.1) | copy-start | bytes 2654212
  20.8 8.7 %collective-permute-start.4 = (bf16[9,64,128]{2,1,0:T(8,128)(2,1)S(1)}, bf16[9,64,128]{2,1,0:T(8,128)(2,1)S(1)}, u32[]{:S(2)}, u32[]{:S(2)}) collective-permute-start(bf16[9,64,128]{2,1,0:T(8,128)(2,1)S(1)} %get-tuple-element.33), channel_id=1, source_target_pairs={{0,2},{1,3},{2,0},{3,1},{4,6},{5,7},{6,4},{7,5},{8,10},{9,11},{10,... | collective-permute-start | bytes 442376 | tf_op jit(solution)/shard_map/ppermute | solution.py:321
  29.6 8.0 %collective-permute-start.5 = (bf16[9,16,128]{2,1,0:T(8,128)(2,1)S(1)}, bf16[9,16,128]{2,1,0:T(8,128)(2,1)S(1)}, u32[]{:S(2)}, u32[]{:S(2)}) collective-permute-start(bf16[9,16,128]{2,1,0:T(8,128)(2,1)S(1)} %get-tuple-element.35), channel_id=1, source_target_pairs={{0,4},{1,5},{2,6},{3,7},{4,8},{5,9},{6,10},{7,11},{8,12},{9,13},{1... | collective-permute-start | bytes 110600 | tf_op jit(solution)/shard_map/ppermute | solution.py:321
  31.6 12.0 %collective-permute-start.9 = (bf16[9,16,256]{2,1,0:T(8,128)(2,1)S(1)}, bf16[9,16,256]{2,1,0:T(8,128)(2,1)S(1)}, u32[]{:S(2)}, u32[]{:S(2)}) collective-permute-start(bf16[9,16,256]{2,1,0:T(8,128)(2,1)S(1)} %get-tuple-element.41), channel_id=1, source_target_pairs={{0,4},{1,5},{2,6},{3,7},{4,8},{5,9},{6,10},{7,11},{8,12},{9,13},{1... | collective-permute-start | bytes 221192 | tf_op jit(solution)/shard_map/ppermute | solution.py:321
  33.3 10.4 %collective-permute-start.10 = (bf16[9,16,256]{2,1,0:T(8,128)(2,1)S(1)}, bf16[9,16,256]{2,1,0:T(8,128)(2,1)S(1)}, u32[]{:S(2)}, u32[]{:S(2)}) collective-permute-start(bf16[9,16,256]{2,1,0:T(8,128)(2,1)S(1)} %get-tuple-element.42), channel_id=1, source_target_pairs={{0,8},{1,9},{2,10},{3,11},{4,12},{5,13},{6,14},{7,15},{8,0},{9,1},... | collective-permute-start | bytes 221192 | tf_op jit(solution)/shard_map/ppermute | solution.py:321
  34.1 9.5 %collective-permute-start.11 = (bf16[9,16,256]{2,1,0:T(8,128)(2,1)S(1)}, bf16[9,16,256]{2,1,0:T(8,128)(2,1)S(1)}, u32[]{:S(2)}, u32[]{:S(2)}) collective-permute-start(bf16[9,16,256]{2,1,0:T(8,128)(2,1)S(1)} %get-tuple-element.43), channel_id=1, source_target_pairs={{0,12},{1,13},{2,14},{3,15},{4,0},{5,1},{6,2},{7,3},{8,4},{9,5},{1... | collective-permute-start | bytes 221192 | tf_op jit(solution)/shard_map/ppermute | solution.py:321
  36.5 7.1 %collective-permute-start.6 = (bf16[9,16,128]{2,1,0:T(8,128)(2,1)S(1)}, bf16[9,16,128]{2,1,0:T(8,128)(2,1)S(1)}, u32[]{:S(2)}, u32[]{:S(2)}) collective-permute-start(bf16[9,16,128]{2,1,0:T(8,128)(2,1)S(1)} %get-tuple-element.36), channel_id=1, source_target_pairs={{0,8},{1,9},{2,10},{3,11},{4,12},{5,13},{6,14},{7,15},{8,0},{9,1},... | collective-permute-start | bytes 110600 | tf_op jit(solution)/shard_map/ppermute | solution.py:321
  37.5 6.1 %collective-permute-start.7 = (bf16[9,16,128]{2,1,0:T(8,128)(2,1)S(1)}, bf16[9,16,128]{2,1,0:T(8,128)(2,1)S(1)}, u32[]{:S(2)}, u32[]{:S(2)}) collective-permute-start(bf16[9,16,128]{2,1,0:T(8,128)(2,1)S(1)} %get-tuple-element.37), channel_id=1, source_target_pairs={{0,12},{1,13},{2,14},{3,15},{4,0},{5,1},{6,2},{7,3},{8,4},{9,5},{1... | collective-permute-start | bytes 110600 | tf_op jit(solution)/shard_map/ppermute | solution.py:321
  43.8 5.1 %collective-permute-start.15 = (bf16[9,16,384]{2,1,0:T(8,128)(2,1)S(1)}, bf16[9,16,384]{2,1,0:T(8,128)(2,1)S(1)}, u32[]{:S(2)}, u32[]{:S(2)}) collective-permute-start(bf16[9,16,384]{2,1,0:T(8,128)(2,1)S(1)} %shard_map.80.refs_0_), channel_id=1, source_target_pairs={{0,2},{1,3},{2,0},{3,1},{4,6},{5,7},{6,4},{7,5},{8,10},{9,11},{10,... | collective-permute-start | bytes 331784 | tf_op jit(solution)/shard_map/ppermute | solution.py:321
  45.7 4.8 %collective-permute-start.14 = (bf16[9,16,384]{2,1,0:T(8,128)(2,1)S(1)}, bf16[9,16,384]{2,1,0:T(8,128)(2,1)S(1)}, u32[]{:S(2)}, u32[]{:S(2)}) collective-permute-start(bf16[9,16,384]{2,1,0:T(8,128)(2,1)S(1)} %shard_map.80.refs_0_), channel_id=1, source_target_pairs={{0,12},{1,13},{2,14},{3,15},{4,0},{5,1},{6,2},{7,3},{8,4},{9,5},{1... | collective-permute-start | bytes 331784 | tf_op jit(solution)/shard_map/ppermute | solution.py:321
  47.5 3.1 %collective-permute-start.19 = (bf16[9,16,384]{2,1,0:T(8,128)(2,1)S(1)}, bf16[9,16,384]{2,1,0:T(8,128)(2,1)S(1)}, u32[]{:S(2)}, u32[]{:S(2)}) collective-permute-start(bf16[9,16,384]{2,1,0:T(8,128)(2,1)S(1)} %shard_map.80.refs_0_), channel_id=1, source_target_pairs={{0,1},{1,0},{2,3},{3,2},{4,5},{5,4},{6,7},{7,6},{8,9},{9,8},{10,11... | collective-permute-start | bytes 331784 | tf_op jit(solution)/shard_map/ppermute | solution.py:321
  47.5 10.8 %collective-permute-start.13 = (bf16[9,16,384]{2,1,0:T(8,128)(2,1)S(1)}, bf16[9,16,384]{2,1,0:T(8,128)(2,1)S(1)}, u32[]{:S(2)}, u32[]{:S(2)}) collective-permute-start(bf16[9,16,384]{2,1,0:T(8,128)(2,1)S(1)} %shard_map.80.refs_0_), channel_id=1, source_target_pairs={{0,8},{1,9},{2,10},{3,11},{4,12},{5,13},{6,14},{7,15},{8,0},{9,1},... | collective-permute-start | bytes 331784 | tf_op jit(solution)/shard_map/ppermute | solution.py:321
  48.4 10.1 %collective-permute-start.12 = (bf16[9,16,384]{2,1,0:T(8,128)(2,1)S(1)}, bf16[9,16,384]{2,1,0:T(8,128)(2,1)S(1)}, u32[]{:S(2)}, u32[]{:S(2)}) collective-permute-start(bf16[9,16,384]{2,1,0:T(8,128)(2,1)S(1)} %shard_map.80.refs_0_), channel_id=1, source_target_pairs={{0,4},{1,5},{2,6},{3,7},{4,8},{5,9},{6,10},{7,11},{8,12},{9,13},{1... | collective-permute-start | bytes 331784 | tf_op jit(solution)/shard_map/ppermute | solution.py:321
  48.9 11.5 %collective-permute-start.23 = (bf16[9,16,384]{2,1,0:T(8,128)(2,1)S(1)}, bf16[9,16,384]{2,1,0:T(8,128)(2,1)S(1)}, u32[]{:S(2)}, u32[]{:S(2)}) collective-permute-start(bf16[9,16,384]{2,1,0:T(8,128)(2,1)S(1)} %collective-permute-done.15.refs_4_), channel_id=1, source_target_pairs={{0,1},{1,0},{2,3},{3,2},{4,5},{5,4},{6,7},{7,6},{8,9},{9,8},{10,11... | collective-permute-start | bytes 331784 | tf_op jit(solution)/shard_map/ppermute | solution.py:321
  50.5 9.8 %collective-permute-start.22 = (bf16[9,16,384]{2,1,0:T(8,128)(2,1)S(1)}, bf16[9,16,384]{2,1,0:T(8,128)(2,1)S(1)}, u32[]{:S(2)}, u32[]{:S(2)}) collective-permute-start(bf16[9,16,384]{2,1,0:T(8,128)(2,1)S(1)} %collective-permute-done.14.refs_3_), channel_id=1, source_target_pairs={{0,1},{1,0},{2,3},{3,2},{4,5},{5,4},{6,7},{7,6},{8,9},{9,8},{10,11... | collective-permute-start | bytes 331784 | tf_op jit(solution)/shard_map/ppermute | solution.py:321
  50.5 10.3 %collective-permute-start.18 = (bf16[9,16,384]{2,1,0:T(8,128)(2,1)S(1)}, bf16[9,16,384]{2,1,0:T(8,128)(2,1)S(1)}, u32[]{:S(2)}, u32[]{:S(2)}) collective-permute-start(bf16[9,16,384]{2,1,0:T(8,128)(2,1)S(1)} %collective-permute-done.14.refs_3_), channel_id=1, source_target_pairs={{0,2},{1,3},{2,0},{3,1},{4,6},{5,7},{6,4},{7,5},{8,10},{9,11},{10,... | collective-permute-start | bytes 331784 | tf_op jit(solution)/shard_map/ppermute | solution.py:321
  58.3 5.9 %collective-permute-start.17 = (bf16[9,16,384]{2,1,0:T(8,128)(2,1)S(1)}, bf16[9,16,384]{2,1,0:T(8,128)(2,1)S(1)}, u32[]{:S(2)}, u32[]{:S(2)}) collective-permute-start(bf16[9,16,384]{2,1,0:T(8,128)(2,1)S(1)} %collective-permute-done.13.refs_2_), channel_id=1, source_target_pairs={{0,2},{1,3},{2,0},{3,1},{4,6},{5,7},{6,4},{7,5},{8,10},{9,11},{10,... | collective-permute-start | bytes 331784 | tf_op jit(solution)/shard_map/ppermute | solution.py:321
  58.6 7.2 %collective-permute-start.16 = (bf16[9,16,384]{2,1,0:T(8,128)(2,1)S(1)}, bf16[9,16,384]{2,1,0:T(8,128)(2,1)S(1)}, u32[]{:S(2)}, u32[]{:S(2)}) collective-permute-start(bf16[9,16,384]{2,1,0:T(8,128)(2,1)S(1)} %collective-permute-done.12.refs_1_), channel_id=1, source_target_pairs={{0,2},{1,3},{2,0},{3,1},{4,6},{5,7},{6,4},{7,5},{8,10},{9,11},{10,... | collective-permute-start | bytes 331784 | tf_op jit(solution)/shard_map/ppermute | solution.py:321
  60.3 7.4 %collective-permute-start.21 = (bf16[9,16,384]{2,1,0:T(8,128)(2,1)S(1)}, bf16[9,16,384]{2,1,0:T(8,128)(2,1)S(1)}, u32[]{:S(2)}, u32[]{:S(2)}) collective-permute-start(bf16[9,16,384]{2,1,0:T(8,128)(2,1)S(1)} %collective-permute-done.13.refs_2_), channel_id=1, source_target_pairs={{0,1},{1,0},{2,3},{3,2},{4,5},{5,4},{6,7},{7,6},{8,9},{9,8},{10,11... | collective-permute-start | bytes 331784 | tf_op jit(solution)/shard_map/ppermute | solution.py:321
  60.3 7.4 %collective-permute-start.20 = (bf16[9,16,384]{2,1,0:T(8,128)(2,1)S(1)}, bf16[9,16,384]{2,1,0:T(8,128)(2,1)S(1)}, u32[]{:S(2)}, u32[]{:S(2)}) collective-permute-start(bf16[9,16,384]{2,1,0:T(8,128)(2,1)S(1)} %collective-permute-done.12.refs_1_), channel_id=1, source_target_pairs={{0,1},{1,0},{2,3},{3,2},{4,5},{5,4},{6,7},{7,6},{8,9},{9,8},{10,11... | collective-permute-start | bytes 331784 | tf_op jit(solution)/shard_map/ppermute | solution.py:321
  60.9 6.9 %collective-permute-start.26 = (bf16[9,16,384]{2,1,0:T(8,128)(2,1)S(1)}, bf16[9,16,384]{2,1,0:T(8,128)(2,1)S(1)}, u32[]{:S(2)}, u32[]{:S(2)}) collective-permute-start(bf16[9,16,384]{2,1,0:T(8,128)(2,1)S(1)} %collective-permute-done.18.refs_7_), channel_id=1, source_target_pairs={{0,1},{1,0},{2,3},{3,2},{4,5},{5,4},{6,7},{7,6},{8,9},{9,8},{10,11... | collective-permute-start | bytes 331784 | tf_op jit(solution)/shard_map/ppermute | solution.py:321
  64.2 3.6 %collective-permute-start.25 = (bf16[9,16,384]{2,1,0:T(8,128)(2,1)S(1)}, bf16[9,16,384]{2,1,0:T(8,128)(2,1)S(1)}, u32[]{:S(2)}, u32[]{:S(2)}) collective-permute-start(bf16[9,16,384]{2,1,0:T(8,128)(2,1)S(1)} %collective-permute-done.17.refs_6_), channel_id=1, source_target_pairs={{0,1},{1,0},{2,3},{3,2},{4,5},{5,4},{6,7},{7,6},{8,9},{9,8},{10,11... | collective-permute-start | bytes 331784 | tf_op jit(solution)/shard_map/ppermute | solution.py:321
  65.7 2.1 %collective-permute-start.24 = (bf16[9,16,384]{2,1,0:T(8,128)(2,1)S(1)}, bf16[9,16,384]{2,1,0:T(8,128)(2,1)S(1)}, u32[]{:S(2)}, u32[]{:S(2)}) collective-permute-start(bf16[9,16,384]{2,1,0:T(8,128)(2,1)S(1)} %collective-permute-done.16.refs_5_), channel_id=1, source_target_pairs={{0,1},{1,0},{2,3},{3,2},{4,5},{5,4},{6,7},{7,6},{8,9},{9,8},{10,11... | collective-permute-start | bytes 331784 | tf_op jit(solution)/shard_map/ppermute | solution.py:321

commit v2 on v1

--- a/solution.py
+++ b/solution.py
@@ -47,8 +47,38 @@
     )
 
 
+def edge_kernel(frames, cot, edge, sems):
+    core, _, _ = position()
+    rows, width = frames.shape[1:3]
+    short, half = cot.shape[1:3]
+    chans = frames.shape[-1]
+    first = pl.ds(core * (rows - 2), 2)
+    only = pl.ds(core * (short - 1), 1)
+    copies = [pltpu.make_async_copy(frames.at[:, first], edge.at[:, 0:2], sems.at[0])]
+    for k in range(2):
+        source = cot.at[:, only, :, k * chans : (k + 1) * chans]
+        target = edge.at[:, 2:3, k * half : (k + 1) * half]
+        copies.append(pltpu.make_async_copy(source, target, sems.at[1 + k]))
+    for copy in copies:
+        copy.start()
+    for copy in copies:
+        copy.wait()
+
+
+def stage_kernel(*refs):
+    sems = refs[-1]
+    count = (len(refs) - 1) // 2
+    copies = [
+        pltpu.make_async_copy(refs[k], refs[count + k], sems.at[k]) for k in range(count)
+    ]
+    for copy in copies:
+        copy.start()
+    for copy in copies:
+        copy.wait()
+
+
 def forward_kernel(
-    own_f, other_f, halo_1f, halo_2f, own_g, other_g, halo_1g, halo_2g, weight_a,
+    own_f, other_f, own_g, other_g, near, far, weight_a,
     keep_b, send_b, pre_ref, stacked_a, stacked_b, cot_ref, flat,
 ):
     core, side, plane = position()
@@ -58,16 +88,18 @@
     block = rows * width
     for t in range(frames):
         base = t * ext * width
-        top = jnp.where(core == 0, halo_1f[t].astype(F32), halo_2f[t].astype(F32))
-        low = jnp.where(core == 0, halo_2f[t].astype(F32), halo_1f[t].astype(F32))
-        flat[base : base + 2 * width] = top.reshape(2 * width, chans)
-        flat[base + (ext - 2) * width : base + ext * width] = low.reshape(2 * width, chans)
+        top = jnp.where(core == 0, near[t].astype(F32), far[t].astype(F32))
+        low = jnp.where(core == 0, far[t].astype(F32), near[t].astype(F32))
+        top_g = jnp.concatenate([top[2, 0:half], top[2, half:]], axis=-1).astype(BF16)
+        low_g = jnp.concatenate([low[2, 0:half], low[2, half:]], axis=-1).astype(BF16)
+        flat[base : base + 2 * width] = top[0:2].reshape(2 * width, chans)
+        flat[base + (ext - 2) * width : base + ext * width] = low[0:2].reshape(2 * width, chans)
         at = pl.multiple_of(base + 2 * width + core * block, 2 * width)
         flat[pl.ds(at, block)] = own_f[t].astype(F32).reshape(block, chans)
         at = pl.multiple_of(base + 2 * width + (1 - core) * block, 2 * width)
         flat[pl.ds(at, block)] = other_f[t].astype(F32).reshape(block, chans)
-        cot_ref[t, 0] = jnp.where(core == 0, halo_1g[t, 0], halo_2g[t, 0])
-        cot_ref[t, rows + 1] = jnp.where(core == 0, halo_2g[t, 0], halo_1g[t, 0])
+        cot_ref[t, 0] = top_g
+        cot_ref[t, rows + 1] = low_g
         cot_ref[t, pl.ds(1 + core * (rows // 2), rows // 2)] = own_g[t]
         cot_ref[t, pl.ds(1 + (1 - core) * (rows // 2), rows // 2)] = other_g[t]
     count = frames * ext
@@ -252,57 +284,74 @@
     frames_grad[...] = flat[...].reshape(frames_grad.shape).astype(BF16)
 
 
-def add_kernel(keep, recv, *outs):
+def add_kernel(keep_a, recv_a, keep_b, recv_b, *outs):
     _, _, plane = position()
     planes = len(outs)
-    rows = keep.shape[1] // planes
+    rows = keep_a.shape[1] // planes
+    chans = keep_a.shape[-1]
     for step in range(planes):
         at = pl.multiple_of(((plane + step) % planes) * rows, rows)
-        value = keep[:, pl.ds(at, rows)].astype(F32) + recv[:, pl.ds(at, rows)].astype(F32)
-        outs[step][...] = value.astype(BF16)
-
-
-def finish_kernel(scale, parts_a, parts_b, out):
-    chans = parts_a[0].shape[-1]
-
-    def total(parts):
-        value = parts[0][...].astype(F32)
-        for part in parts[1:]:
-            value = value + part[...].astype(F32)
-        return (value * scale).astype(BF16)
-
-    out[:, :, 0:chans] = total(parts_a)
-    out[:, :, chans:] = total(parts_b)
-
-
-def assemble_kernel(planes, *refs):
-    pieces, (out_a, out_b) = (refs[:-2], refs[-2:])
+        part = pl.ds(at, rows)
+        value = keep_a[:, part].astype(F32) + recv_a[:, part].astype(F32)
+        outs[step][:, :, 0:chans] = value.astype(BF16)
+        value = keep_b[:, part].astype(F32) + recv_b[:, part].astype(F32)
+        outs[step][:, :, chans:] = value.astype(BF16)
+
+
+def finish_kernel(scale, *refs):
+    value = refs[0][...].astype(F32)
+    for part in refs[1:-1]:
+        value = value + part[...].astype(F32)
+    refs[-1][...] = (value * scale).astype(BF16)
+
+
+def assemble_kernel(places, planes, *refs):
+    count = len(places)
+    pieces, (out_a, out_b), sems = (refs[:count], refs[count : count + 2], refs[-1])
     core, side, plane = position()
     chans = out_a.shape[-1]
     rows = pieces[0].shape[1]
-    at = 0
-    for flip_core in range(2):
-        for flip_side in range(2):
-            for step in range(planes):
-                piece = pieces[at]
-                at += 1
-                tap = core ^ flip_core
-                source = (plane - step + planes) % planes
-                start = pl.multiple_of((side ^ flip_side) * (chans // 2) + source * rows, rows)
-                for slot in (2 * tap, 1 + tap):
-                    out_a[slot, :, pl.ds(start, rows)] = piece[:, :, 0:chans]
-                    out_b[slot, :, pl.ds(start, rows)] = piece[:, :, chans:]
-
-
-def call(body, outs, args, scratch=(), flops=0):
+
+    def copies(piece, place, sem):
+        flip_core, flip_side, step = place
+        tap = core ^ flip_core
+        source = (plane - step + planes) % planes
+        at = pl.multiple_of((side ^ flip_side) * (chans // 2) + source * rows, rows)
+        for k, slot in enumerate((tap * 2, 1)):
+            for part, out in ((slice(0, chans), out_a), (slice(chans, None), out_b)):
+                lanes = piece.shape[-1] - chans if part.stop is None else chans
+                source_ref = piece.at[:, :, pl.ds(part.start, lanes)]
+                target_ref = out.at[slot, :, pl.ds(at, rows), :]
+                spot = sem.at[2 * k + (0 if part.stop else 1)]
+                yield k, tap, pltpu.make_async_copy(source_ref, target_ref, spot)
+
+    def each(act):
+        for index, (piece, place) in enumerate(zip(pieces, places, strict=True)):
+            for k, tap, copy in copies(piece, place, sems.at[index]):
+                if k == 0:
+                    act(copy)
+                else:
+                    pl.when(tap == 0)(lambda copy=copy: act(copy))
+
+    each(lambda copy: copy.start())
+    each(lambda copy: copy.wait())
+
+
+def call(body, outs, args, scratch=(), flops=0, whole=False):
     size = sum(a.size * a.dtype.itemsize for a in args)
     size += sum(o.size * o.dtype.itemsize for o in outs)
+    extra = {}
+    if whole:
+        extra["in_specs"] = [pl.BlockSpec(memory_space=pl.ANY)] * len(args)
+    if whole == "both":
+        extra["out_specs"] = (pl.BlockSpec(memory_space=pl.ANY),) * len(outs)
     return pl.pallas_call(
         body,
         out_shape=outs,
         scratch_shapes=scratch,
         compiler_params=pltpu.CompilerParams(vmem_limit_bytes=VMEM_LIMIT),
         cost_estimate=pl.CostEstimate(flops=flops, bytes_accessed=size, transcendentals=0),
+        **extra,
     )(*args)
 
 
@@ -324,20 +373,26 @@
     swap_side = [(i, i ^ 2) for i in range(n)]
     near = [(2 * k + 1, 2 * k + 2) for k in range(chips - 1)]
     near += [(2 * k + 2, 2 * k + 1) for k in range(chips - 1)]
-    far = [(2 * k + 1, 2 * k + 3) for k in range(chips - 1)]
-    far += [(2 * k + 2, 2 * k) for k in range(chips - 1)]
-
-    edge_f = lax.dynamic_slice_in_dim(frames, core * (rows - 2), 2, axis=1)
-    edge_g = lax.dynamic_slice_in_dim(cotangent, core * (rows // 2 - 1), 1, axis=1)
-    edge_g = jnp.concatenate([edge_g[..., :chans], edge_g[..., chans:]], axis=1)
-    edge = jnp.concatenate([edge_f, edge_g.reshape(count, 1, width, chans)], axis=1)
-    halos = [send(edge, near), send(edge, far)]
-    halo_f = [halo[:, 0:2] for halo in halos]
-    halo_g = [
-        jnp.concatenate([halo[:, 2:3, 0:half], halo[:, 2:3, half:]], axis=-1) for halo in halos
-    ]
+
+    (edge,) = call(
+        edge_kernel,
+        (shape((count, 3, width, chans), BF16),),
+        (frames, cotangent),
+        [pltpu.SemaphoreType.DMA((3,))],
+        whole=True,
+    )
+    near_edge = send(edge, near)
     other_f = send(frames, swap_core)
     other_g = send(cotangent, swap_core)
+    far_edge = send(near_edge, swap_core)
+    inputs = (frames, cotangent, weight_a, weight_b)
+    own_f, own_g, weight_a, weight_b = call(
+        stage_kernel,
+        tuple(shape(x.shape, x.dtype) for x in inputs),
+        inputs,
+        [pltpu.SemaphoreType.DMA((4,))],
+        whole=True,
+    )
 
     inner = 2 * rows + 2
     kernel_a = weight_a.reshape(3, 3, 3 * chans, chans)
@@ -353,7 +408,7 @@
             shape((count, inner // 2, 2, half, 3 * chans), BF16),
             shape((count, rows + 2, half, wide), BF16),
         ),
-        (frames, other_f, *halo_f, cotangent, other_g, *halo_g, kernel_a),
+        (own_f, other_f, own_g, other_g, near_edge, far_edge, kernel_a),
         [pltpu.VMEM((count * (inner + 2) * width, chans), F32)],
         flops=10**9,
     )
@@ -394,37 +449,40 @@
             both.append(jnp.concatenate([total[:1], total], axis=0))
         return (encoded, frames_grad, both[0], both[1])
 
-    parts = []
-    for keep, recv in ((keep_b, recv_b), (keep_a, recv_a)):
-        piece = shape((9, part // planes, keep.shape[-1]), BF16)
-        pieces = call(add_kernel, (piece,) * planes, (keep, recv))
-        got = [pieces[0]]
-        for step in range(1, planes):
-            to = [(i, (i + 4 * step) % n) for i in range(n)]
-            got.append(send(pieces[step], to))
-        parts.append(got)
+    held = (keep_a, keep_b, encoded, frames_grad)
+    keep_a, keep_b, encoded, frames_grad = lax.optimization_barrier(held)
+    piece = shape((9, part // planes, chans + wide), BF16)
+    pieces = call(add_kernel, (piece,) * planes, (keep_a, recv_a, keep_b, recv_b))
+    got = [pieces[0]]
+    for step in range(1, planes):
+        got.append(send(pieces[step], [(i, (i + 4 * step) % n) for i in range(n)]))
 
     def finish(*refs):
-        finish_kernel(scale, refs[:planes], refs[planes : 2 * planes], refs[-1])
-
-    (own,) = call(
-        finish,
-        (shape((9, part // planes, chans + wide), BF16),),
-        (*parts[1], *parts[0]),
-    )
-    pieces = [own]
+        finish_kernel(scale, *refs)
+
+    (own,) = call(finish, (piece,), got)
+    column = {(0, 0, 0): own}
     for step in range(1, planes):
-        pieces.append(send(own, [(i, (i + 4 * step) % n) for i in range(n)]))
-    pieces += [send(piece, swap_side) for piece in pieces]
-    pieces += [send(piece, swap_core) for piece in pieces]
+        to = [(i, (i + 4 * step) % n) for i in range(n)]
+        column[0, 0, step] = send(own, to)
+        if 2 * step == planes and planes > 2:
+            column[0, 1, step] = send(own, [(i, j ^ 2) for i, j in to])
+    for step in range(planes):
+        if (0, 1, step) not in column:
+            column[0, 1, step] = send(column[0, 0, step], swap_side)
+    for (_, flip, step), value in list(column.items()):
+        column[1, flip, step] = send(value, swap_core)
+    places = tuple(column)
 
     def assemble(*refs):
-        assemble_kernel(planes, *refs)
+        assemble_kernel(places, planes, *refs)
 
     grad_a, grad_b = call(
         assemble,
         (shape((3, 9, chans, chans), BF16), shape((3, 9, chans, wide), BF16)),
-        pieces,
+        tuple(column.values()),
+        [pltpu.SemaphoreType.DMA((len(places), 4))],
+        whole="both",
     )
     return (encoded, frames_grad, grad_a.reshape(weight_a.shape), grad_b.reshape(weight_b.shape))
 

time: 70.1 us -> 69.6 us (level)
  waiting for transfers between devices: 29.3 us -> 27.6 us
  Pallas kernels: 8.24 us -> 9.25 us
    ppermute x27 -> x24, waiting for transfers between devices: 29.3 us -> 27.6 us  [send(): return lax.ppermute(value, AXIS, pairs)]
    unnamed x10 -> x8, local copies, waits for them, and re-layouts: 2.92 us -> 4.39 us
    pallas_call x7 -> x8, Pallas kernels: 8.24 us -> 9.25 us  [call(): pl.pallas_call(body, out_shape=outs, scratch_shapes=scratch, compiler_par...]
    dynamic_slice x1 -> x0, local copies, waits for them, and re-layouts: 0.76 us -> none  [on_device(): edge_f = lax.dynamic_slice_in_dim(frames, core * (rows - 2), 2, axis=1)]
    slice x5 -> x0, local copies, waits for them, and re-layouts: 0.74 us -> none  [the longest x1 0.73 us: on_device(): edge_g = jnp.concatenate([edge_g[..., :chans], edge_g[..., chans:]], axis=1)]
    ppermute x27 -> x24, starting transfers between devices: 26.9 us -> 27.4 us  [send(): return lax.ppermute(value, AXIS, pairs)]
  transfers between devices with their start and end apart: 27 -> 24, of which waited for: 9 -> 8; matrix products, arithmetic and copies ran while one was open for 0% -> 0% of each run, Pallas kernels for 6% -> 7%
where the time goes in v2:
time: 69.6 us; the launch traced here: 69.4 us
  waiting for transfers between devices  27.6 us (40%)
  starting transfers between devices  27.4 us (39%)
  Pallas kernels  9.25 us (13%)
  local copies, waits for them, and re-layouts  4.39 us (6%)
  between operations  0.75 us (1%)
    ppermute x24, waiting for transfers between devices, send(): return lax.ppermute(value, AXIS, pairs)  27.6 us
    ppermute x24, starting transfers between devices, send(): return lax.ppermute(value, AXIS, pairs)  27.4 us
    pallas_call x8, Pallas kernels, call(): pl.pallas_call(body, out_shape=outs, scratch_shapes=scratch, compiler_par...  9.25 us
    unnamed x8, local copies, waits for them, and re-layouts  4.39 us
  transfers between devices with their start and end apart: 24, of which 8 were waited for; matrix products, arithmetic and copies ran while one was open for 0% of the time, Pallas kernels for 7%

profile of v2, /device:TPU:0, one launch (start us, length us, event | category | flops | bytes accessed | tf_op | source)
XLA Modules:
  0.0 69.4 jit_solution(11979554441673102159)
XLA Ops:
  0.6 0.5 collective-permute-start
  1.2 0.9 %copy-done.2 = bf16[2,8,32,128]{3,2,1,0:T(8,128)(2,1)S(1)} copy-done((bf16[2,8,32,128]{3,2,1,0:T(8,128)(2,1)S(1)}, bf16[2,8,32,128]{3,2,1,0:T(8,128)(2,1)}, u32[]{:S(2)}) %copy-start.2) | copy-done | bytes 131096
  2.1 0.8 %copy-done.3 = bf16[2,4,16,256]{3,2,1,0:T(8,128)(2,1)S(1)} copy-done((bf16[2,4,16,256]{3,2,1,0:T(8,128)(2,1)S(1)}, bf16[2,4,16,256]{3,2,1,0:T(8,128)(2,1)}, u32[]{:S(2)}) %copy-start.3) | copy-done | bytes 65560
  2.9 0.7 collective-permute-start.2
  3.6 4.0 %collective-permute-start.1 = (bf16[2,4,16,256]{3,2,1,0:T(8,128)(2,1)S(1)}, bf16[2,4,16,256]{3,2,1,0:T(8,128)(2,1)S(1)}, u32[]{:S(2)}, u32[]{:S(2)}) collective-permute-start(bf16[2,4,16,256]{3,2,1,0:T(8,128)(2,1)S(1)} %copy-done.3), channel_id=1, source_target_pairs={{0,1},{1,0},{2,3},{3,2},{4,5},{5,4},{6,7},{7,6},{8,9},{9,8},{10,11... | collective-permute-start | bytes 196616 | tf_op jit(solution)/shard_map/ppermute | solution.py:370
  7.6 1.7 %collective-permute-start.3 = (bf16[2,3,32,128]{3,2,1,0:T(8,128)(2,1)S(1)}, bf16[2,3,32,128]{3,2,1,0:T(8,128)(2,1)S(1)}, u32[]{:S(2)}, u32[]{:S(2)}) collective-permute-start(bf16[2,3,32,128]{3,2,1,0:T(8,128)(2,1)S(1)} %collective-permute-done.2.near), channel_id=1, source_target_pairs={{0,1},{1,0},{2,3},{3,2},{4,5},{5,4},{6,7},{7,6},{8,9},{9,8},{10,11... | collective-permute-start | bytes 147464 | tf_op jit(solution)/shard_map/ppermute | solution.py:370
  9.3 1.5 %copy-done = bf16[3,3,3,128,256]{4,3,2,1,0:T(8,128)(2,1)S(1)} copy-done((bf16[3,3,3,128,256]{4,3,2,1,0:T(8,128)(2,1)S(1)}, bf16[3,3,3,128,256]{4,3,2,1,0:T(8,128)(2,1)}, u32[]{:S(2)}) %copy-start) | copy-done | bytes 1769496
  10.7 1.2 %copy-done.1 = bf16[3,3,3,128,128]{4,3,2,1,0:T(8,128)(2,1)S(1)} copy-done((bf16[3,3,3,128,128]{4,3,2,1,0:T(8,128)(2,1)S(1)}, bf16[3,3,3,128,128]{4,3,2,1,0:T(8,128)(2,1)}, u32[]{:S(2)}) %copy-start.1) | copy-done | bytes 884760
  11.9 0.8 %shard_map.75 = (bf16[2,8,32,128]{3,2,1,0:T(8,128)(2,1)S(1)}, bf16[2,4,16,256]{3,2,1,0:T(8,128)(2,1)S(1)}, bf16[3,3,3,128,128]{4,3,2,1,0:T(8,128)(2,1)S(1)}, bf16[3,3,3,128,256]{4,3,2,1,0:T(8,128)(2,1)S(1)}) custom-call(bf16[2,8,32,128]{3,2,1,0:T(8,128)(2,1)S(1)} %copy-done.2, bf16[2,4,16,256]{3,2,1,0:T(8,128)(2,1)S(1)} %copy-done.3, ...), custom_call_target="tpu_custom_call" | custom-call | bytes 5701632 | tf_op jit(solution)/shard_map/pallas_call | solution.py:348
  12.7 0.0 collective-permute-done.1.other_g
  12.7 0.0 collective-permute-done.other_f
  12.7 2.1 %shard_map.77 = (bf16[9,64,256]{2,1,0:T(8,128)(2,1)S(1)}, bf16[9,64,256]{2,1,0:T(8,128)(2,1)S(1)}, f32[2,18,32,128]{3,2,1,0:T(8,128)S(1)}, bf16[2,20,32,384]{3,2...) custom-call(bf16[2,8,32,128]{3,2,1,0:T(8,128)(2,1)S(1)} %get-tuple-element.29.own_f, ...), custom_call_target="tpu_custom_call" | custom-call | flops 1000000000 | bytes 4145152 | tf_op jit(solution)/shard_map/pallas_call | solution.py:348
  14.8 3.1 %collective-permute-start.5 = (bf16[9,64,256]{2,1,0:T(8,128)(2,1)S(1)}, bf16[9,64,256]{2,1,0:T(8,128)(2,1)S(1)}, u32[]{:S(2)}, u32[]{:S(2)}) collective-permute-start(bf16[9,64,256]{2,1,0:T(8,128)(2,1)S(1)} %get-tuple-element.47), channel_id=1, source_target_pairs={{0,2},{1,3},{2,0},{3,1},{4,6},{5,7},{6,4},{7,5},{8,10},{9,11},{10,... | collective-permute-start | bytes 884744 | tf_op jit(solution)/shard_map/ppermute | solution.py:370
  17.9 2.1 %shard_map.78 = (bf16[9,64,128]{2,1,0:T(8,128)(2,1)S(1)}, bf16[9,64,128]{2,1,0:T(8,128)(2,1)S(1)}, bf16[2,18,32,128]{3,2,1,0:T(8,128)(2,1)S(1)}) custom-call(bf16[2,10,16,256]{3,2,1,0:T(8,128)(2,1)S(1)} %get-tuple-element.32.refs_0_, f32[2,18,32,128]{3,2,1,0:T(8,128)S(1)} %get-tuple-element.33.refs_1_, ...), custom_call_target="tpu_custom_call" | custom-call | flops 1000000000 | bytes 4096000 | tf_op jit(solution)/shard_map/pallas_call | solution.py:348
  20.0 0.1 collective-permute-start.4
  20.1 2.0 %shard_map.79 = (bf16[2,4,16,256]{3,2,1,0:T(8,128)(2,1)}, bf16[2,8,32,128]{3,2,1,0:T(8,128)(2,1)}) custom-call(bf16[2,9,2,16,384]{4,3,2,1,0:T(8,128)(2,1)S(1)} %get-tuple-element.38.stacked_b, bf16[2,18,32,128]{3,2,1,0:T(8,128)(2,1)S(1)} %get-tuple-element.39.pre_grad, bf16[3,3,3,128,128]{4,3,2,1,0:T(8,128)(2,1)S(1)} %get-tuple-element.31.weight_a, ...), custom_call_target="tpu_custom_call" | custom-call | flops 1000000000 | bytes 3588096 | tf_op jit(solution)/shard_map/pallas_call | solution.py:348
  22.1 6.1 %collective-permute-done.4.recv_a = bf16[9,64,128]{2,1,0:T(8,128)(2,1)S(1)} collective-permute-done((bf16[9,64,128]{2,1,0:T(8,128)(2,1)S(1)}, bf16[9,64,128]{2,1,0:T(8,128)(2,1)S(1)}, u32[]{:S(2)}, u32[]{:S(2)}) %collective-permute-start.4) | collective-permute-done | bytes 147488 | tf_op jit(solution)/shard_map/ppermute | solution.py:370
  28.3 0.0 collective-permute-done.5.recv_b
  28.3 0.1 shard_map.80
  28.4 2.0 %collective-permute-start.6 = (bf16[9,16,384]{2,1,0:T(8,128)(2,1)S(1)}, bf16[9,16,384]{2,1,0:T(8,128)(2,1)S(1)}, u32[]{:S(2)}, u32[]{:S(2)}) collective-permute-start(bf16[9,16,384]{2,1,0:T(8,128)(2,1)S(1)} %get-tuple-element.49), channel_id=1, source_target_pairs={{0,4},{1,5},{2,6},{3,7},{4,8},{5,9},{6,10},{7,11},{8,12},{9,13},{1... | collective-permute-start | bytes 331784 | tf_op jit(solution)/shard_map/ppermute | solution.py:370
  30.3 2.6 %collective-permute-start.7 = (bf16[9,16,384]{2,1,0:T(8,128)(2,1)S(1)}, bf16[9,16,384]{2,1,0:T(8,128)(2,1)S(1)}, u32[]{:S(2)}, u32[]{:S(2)}) collective-permute-start(bf16[9,16,384]{2,1,0:T(8,128)(2,1)S(1)} %get-tuple-element.50), channel_id=1, source_target_pairs={{0,8},{1,9},{2,10},{3,11},{4,12},{5,13},{6,14},{7,15},{8,0},{9,1},... | collective-permute-start | bytes 331784 | tf_op jit(solution)/shard_map/ppermute | solution.py:370
  32.9 1.3 %collective-permute-start.8 = (bf16[9,16,384]{2,1,0:T(8,128)(2,1)S(1)}, bf16[9,16,384]{2,1,0:T(8,128)(2,1)S(1)}, u32[]{:S(2)}, u32[]{:S(2)}) collective-permute-start(bf16[9,16,384]{2,1,0:T(8,128)(2,1)S(1)} %get-tuple-element.51), channel_id=1, source_target_pairs={{0,12},{1,13},{2,14},{3,15},{4,0},{5,1},{6,2},{7,3},{8,4},{9,5},{1... | collective-permute-start | bytes 331784 | tf_op jit(solution)/shard_map/ppermute | solution.py:370
  34.3 2.1 %collective-permute-done.6.refs_1_ = bf16[9,16,384]{2,1,0:T(8,128)(2,1)S(1)} collective-permute-done((bf16[9,16,384]{2,1,0:T(8,128)(2,1)S(1)}, bf16[9,16,384]{2,1,0:T(8,128)(2,1)S(1)}, u32[]{:S(2)}, u32[]{:S(2)}) %collective-permute-start.6) | collective-permute-done | bytes 110624 | tf_op jit(solution)/shard_map/ppermute | solution.py:370
  36.4 3.8 %collective-permute-done.7.refs_2_ = bf16[9,16,384]{2,1,0:T(8,128)(2,1)S(1)} collective-permute-done((bf16[9,16,384]{2,1,0:T(8,128)(2,1)S(1)}, bf16[9,16,384]{2,1,0:T(8,128)(2,1)S(1)}, u32[]{:S(2)}, u32[]{:S(2)}) %collective-permute-start.7) | collective-permute-done | bytes 110624 | tf_op jit(solution)/shard_map/ppermute | solution.py:370
  40.2 0.0 collective-permute-done.8.refs_3_
  40.2 0.1 shard_map.81.refs_0_
  40.3 0.1 collective-permute-start.16
  40.3 0.9 %collective-permute-start.13 = (bf16[9,16,384]{2,1,0:T(8,128)(2,1)S(1)}, bf16[9,16,384]{2,1,0:T(8,128)(2,1)S(1)}, u32[]{:S(2)}, u32[]{:S(2)}) collective-permute-start(bf16[9,16,384]{2,1,0:T(8,128)(2,1)S(1)} %shard_map.81.refs_0_), channel_id=1, source_target_pairs={{0,2},{1,3},{2,0},{3,1},{4,6},{5,7},{6,4},{7,5},{8,10},{9,11},{10,... | collective-permute-start | bytes 331784 | tf_op jit(solution)/shard_map/ppermute | solution.py:370
  41.3 3.8 %collective-permute-start.12 = (bf16[9,16,384]{2,1,0:T(8,128)(2,1)S(1)}, bf16[9,16,384]{2,1,0:T(8,128)(2,1)S(1)}, u32[]{:S(2)}, u32[]{:S(2)}) collective-permute-start(bf16[9,16,384]{2,1,0:T(8,128)(2,1)S(1)} %shard_map.81.refs_0_), channel_id=1, source_target_pairs={{0,12},{1,13},{2,14},{3,15},{4,0},{5,1},{6,2},{7,3},{8,4},{9,5},{1... | collective-permute-start | bytes 331784 | tf_op jit(solution)/shard_map/ppermute | solution.py:370
  45.1 1.1 %collective-permute-start.11 = (bf16[9,16,384]{2,1,0:T(8,128)(2,1)S(1)}, bf16[9,16,384]{2,1,0:T(8,128)(2,1)S(1)}, u32[]{:S(2)}, u32[]{:S(2)}) collective-permute-start(bf16[9,16,384]{2,1,0:T(8,128)(2,1)S(1)} %shard_map.81.refs_0_), channel_id=1, source_target_pairs={{0,10},{1,11},{2,8},{3,9},{4,14},{5,15},{6,12},{7,13},{8,2},{9,3},... | collective-permute-start | bytes 331784 | tf_op jit(solution)/shard_map/ppermute | solution.py:370
  46.2 0.1 collective-permute-start.9
  46.3 2.4 %collective-permute-start.10 = (bf16[9,16,384]{2,1,0:T(8,128)(2,1)S(1)}, bf16[9,16,384]{2,1,0:T(8,128)(2,1)S(1)}, u32[]{:S(2)}, u32[]{:S(2)}) collective-permute-start(bf16[9,16,384]{2,1,0:T(8,128)(2,1)S(1)} %shard_map.81.refs_0_), channel_id=1, source_target_pairs={{0,8},{1,9},{2,10},{3,11},{4,12},{5,13},{6,14},{7,15},{8,0},{9,1},... | collective-permute-start | bytes 331784 | tf_op jit(solution)/shard_map/ppermute | solution.py:370
  48.7 0.0 collective-permute-done.13.refs_5_
  48.7 0.0 collective-permute-start.21
  48.7 0.0 collective-permute-done.12.refs_4_
  48.7 0.5 collective-permute-start.20
  49.2 9.7 %collective-permute-done.11.refs_3_ = bf16[9,16,384]{2,1,0:T(8,128)(2,1)S(1)} collective-permute-done((bf16[9,16,384]{2,1,0:T(8,128)(2,1)S(1)}, bf16[9,16,384]{2,1,0:T(8,128)(2,1)S(1)}, u32[]{:S(2)}, u32[]{:S(2)}) %collective-permute-start.11) | collective-permute-done | bytes 110624 | tf_op jit(solution)/shard_map/ppermute | solution.py:370
  58.9 0.6 collective-permute-start.15
  59.5 1.4 %collective-permute-start.14 = (bf16[9,16,384]{2,1,0:T(8,128)(2,1)S(1)}, bf16[9,16,384]{2,1,0:T(8,128)(2,1)S(1)}, u32[]{:S(2)}, u32[]{:S(2)}) collective-permute-start(bf16[9,16,384]{2,1,0:T(8,128)(2,1)S(1)} %collective-permute-done.9.refs_1_), channel_id=1, source_target_pairs={{0,2},{1,3},{2,0},{3,1},{4,6},{5,7},{6,4},{7,5},{8,10},{9,11},{10,... | collective-permute-start | bytes 331784 | tf_op jit(solution)/shard_map/ppermute | solution.py:370
  61.0 0.0 collective-permute-done.10.refs_2_
  61.0 0.5 collective-permute-start.19
  61.5 0.0 collective-permute-done.20.refs_12_
  61.5 0.1 collective-permute-start.18
  61.6 3.3 %collective-permute-done.15.refs_7_ = bf16[9,16,384]{2,1,0:T(8,128)(2,1)S(1)} collective-permute-done((bf16[9,16,384]{2,1,0:T(8,128)(2,1)S(1)}, bf16[9,16,384]{2,1,0:T(8,128)(2,1)S(1)}, u32[]{:S(2)}, u32[]{:S(2)}) %collective-permute-start.15) | collective-permute-done | bytes 110624 | tf_op jit(solution)/shard_map/ppermute | solution.py:370
  64.8 1.2 %collective-permute-done.14.refs_6_ = bf16[9,16,384]{2,1,0:T(8,128)(2,1)S(1)} collective-permute-done((bf16[9,16,384]{2,1,0:T(8,128)(2,1)S(1)}, bf16[9,16,384]{2,1,0:T(8,128)(2,1)S(1)}, u32[]{:S(2)}, u32[]{:S(2)}) %collective-permute-start.14) | collective-permute-done | bytes 110624 | tf_op jit(solution)/shard_map/ppermute | solution.py:370
  66.0 0.1 collective-permute-done.23.refs_15_
  66.2 1.2 %collective-permute-done.22.refs_14_ = bf16[9,16,384]{2,1,0:T(8,128)(2,1)S(1)} collective-permute-done((bf16[9,16,384]{2,1,0:T(8,128)(2,1)S(1)}, bf16[9,16,384]{2,1,0:T(8,128)(2,1)S(1)}, u32[]{:S(2)}, u32[]{:S(2)}) %collective-permute-start.22) | collective-permute-done | bytes 110624 | tf_op jit(solution)/shard_map/ppermute | solution.py:370
  67.3 2.1 %shard_map.82 = (bf16[3,9,128,128]{3,2,1,0:T(8,128)(2,1)}, bf16[3,9,128,256]{3,2,1,0:T(8,128)(2,1)}) custom-call(bf16[9,16,384]{2,1,0:T(8,128)(2,1)S(1)} %shard_map.81.refs_0_, bf16[9,16,384]{2,1,0:T(8,128)(2,1)S(1)} %collective-permute-done.9.refs_1_, bf16[9,16,384]{2,1,0:T(8,128)(2,1)S(1)} %collective-permute-done.10.refs_2_, ...), custom_call_target="tpu_custom_call" | custom-call | bytes 4423680 | tf_op jit(solution)/shard_map/pallas_call | solution.py:348
  (16 shorter events, 0.1 us)
Async XLA Ops:
  0.6 12.1 %collective-permute-start = (bf16[2,8,32,128]{3,2,1,0:T(8,128)(2,1)}, bf16[2,8,32,128]{3,2,1,0:T(8,128)(2,1)S(1)}, u32[]{:S(2)}, u32[]{:S(2)}) collective-permute-start(bf16[2,8,32,128]{3,2,1,0:T(8,128)(2,1)} %frames.1), channel_id=1, source_target_pairs={{0,1},{1,0},{2,3},{3,2},{4,5},{5,4},{6,7},{7,6},{8,9},{9,8},{10,11... | collective-permute-start | bytes 393224 | tf_op jit(solution)/shard_map/ppermute | solution.py:370
  1.1 0.9 %copy-start.2 = (bf16[2,8,32,128]{3,2,1,0:T(8,128)(2,1)S(1)}, bf16[2,8,32,128]{3,2,1,0:T(8,128)(2,1)}, u32[]{:S(2)}) copy-start(bf16[2,8,32,128]{3,2,1,0:T(8,128)(2,1)} %frames.1) | copy-start | bytes 393220
  2.1 0.8 %copy-start.3 = (bf16[2,4,16,256]{3,2,1,0:T(8,128)(2,1)S(1)}, bf16[2,4,16,256]{3,2,1,0:T(8,128)(2,1)}, u32[]{:S(2)}) copy-start(bf16[2,4,16,256]{3,2,1,0:T(8,128)(2,1)} %cot.1) | copy-start | bytes 196612
  2.9 4.6 %collective-permute-start.2 = (bf16[2,3,32,128]{3,2,1,0:T(8,128)(2,1)S(1)}, bf16[2,3,32,128]{3,2,1,0:T(8,128)(2,1)S(1)}, u32[]{:S(2)}, u32[]{:S(2)}) collective-permute-start(bf16[2,3,32,128]{3,2,1,0:T(8,128)(2,1)S(1)} %shard_map.76), channel_id=1, source_target_pairs={{1,2},{3,4},{5,6},{7,8},{9,10},{11,12},{13,14},{2,1},{4,3},{6,5},{... | collective-permute-start | bytes 147464 | tf_op jit(solution)/shard_map/ppermute | solution.py:370
  3.6 9.1 %collective-permute-start.1 = (bf16[2,4,16,256]{3,2,1,0:T(8,128)(2,1)S(1)}, bf16[2,4,16,256]{3,2,1,0:T(8,128)(2,1)S(1)}, u32[]{:S(2)}, u32[]{:S(2)}) collective-permute-start(bf16[2,4,16,256]{3,2,1,0:T(8,128)(2,1)S(1)} %copy-done.3), channel_id=1, source_target_pairs={{0,1},{1,0},{2,3},{3,2},{4,5},{5,4},{6,7},{7,6},{8,9},{9,8},{10,11... | collective-permute-start | bytes 196616 | tf_op jit(solution)/shard_map/ppermute | solution.py:370
  7.6 5.2 %collective-permute-start.3 = (bf16[2,3,32,128]{3,2,1,0:T(8,128)(2,1)S(1)}, bf16[2,3,32,128]{3,2,1,0:T(8,128)(2,1)S(1)}, u32[]{:S(2)}, u32[]{:S(2)}) collective-permute-start(bf16[2,3,32,128]{3,2,1,0:T(8,128)(2,1)S(1)} %collective-permute-done.2.near), channel_id=1, source_target_pairs={{0,1},{1,0},{2,3},{3,2},{4,5},{5,4},{6,7},{7,6},{8,9},{9,8},{10,11... | collective-permute-start | bytes 147464 | tf_op jit(solution)/shard_map/ppermute | solution.py:370
  9.3 1.5 %copy-start = (bf16[3,3,3,128,256]{4,3,2,1,0:T(8,128)(2,1)S(1)}, bf16[3,3,3,128,256]{4,3,2,1,0:T(8,128)(2,1)}, u32[]{:S(2)}) copy-start(bf16[3,3,3,128,256]{4,3,2,1,0:T(8,128)(2,1)} %refs_3_.1) | copy-start | bytes 5308420
  10.7 1.2 %copy-start.1 = (bf16[3,3,3,128,128]{4,3,2,1,0:T(8,128)(2,1)S(1)}, bf16[3,3,3,128,128]{4,3,2,1,0:T(8,128)(2,1)}, u32[]{:S(2)}) copy-start(bf16[3,3,3,128,128]{4,3,2,1,0:T(8,128)(2,1)} %refs_2_.1) | copy-start | bytes 2654212
  14.8 13.4 %collective-permute-start.5 = (bf16[9,64,256]{2,1,0:T(8,128)(2,1)S(1)}, bf16[9,64,256]{2,1,0:T(8,128)(2,1)S(1)}, u32[]{:S(2)}, u32[]{:S(2)}) collective-permute-start(bf16[9,64,256]{2,1,0:T(8,128)(2,1)S(1)} %get-tuple-element.47), channel_id=1, source_target_pairs={{0,2},{1,3},{2,0},{3,1},{4,6},{5,7},{6,4},{7,5},{8,10},{9,11},{10,... | collective-permute-start | bytes 884744 | tf_op jit(solution)/shard_map/ppermute | solution.py:370
  20.0 8.3 %collective-permute-start.4 = (bf16[9,64,128]{2,1,0:T(8,128)(2,1)S(1)}, bf16[9,64,128]{2,1,0:T(8,128)(2,1)S(1)}, u32[]{:S(2)}, u32[]{:S(2)}) collective-permute-start(bf16[9,64,128]{2,1,0:T(8,128)(2,1)S(1)} %get-tuple-element.45), channel_id=1, source_target_pairs={{0,2},{1,3},{2,0},{3,1},{4,6},{5,7},{6,4},{7,5},{8,10},{9,11},{10,... | collective-permute-start | bytes 442376 | tf_op jit(solution)/shard_map/ppermute | solution.py:370
  28.4 8.0 %collective-permute-start.6 = (bf16[9,16,384]{2,1,0:T(8,128)(2,1)S(1)}, bf16[9,16,384]{2,1,0:T(8,128)(2,1)S(1)}, u32[]{:S(2)}, u32[]{:S(2)}) collective-permute-start(bf16[9,16,384]{2,1,0:T(8,128)(2,1)S(1)} %get-tuple-element.49), channel_id=1, source_target_pairs={{0,4},{1,5},{2,6},{3,7},{4,8},{5,9},{6,10},{7,11},{8,12},{9,13},{1... | collective-permute-start | bytes 331784 | tf_op jit(solution)/shard_map/ppermute | solution.py:370
  30.3 9.8 %collective-permute-start.7 = (bf16[9,16,384]{2,1,0:T(8,128)(2,1)S(1)}, bf16[9,16,384]{2,1,0:T(8,128)(2,1)S(1)}, u32[]{:S(2)}, u32[]{:S(2)}) collective-permute-start(bf16[9,16,384]{2,1,0:T(8,128)(2,1)S(1)} %get-tuple-element.50), channel_id=1, source_target_pairs={{0,8},{1,9},{2,10},{3,11},{4,12},{5,13},{6,14},{7,15},{8,0},{9,1},... | collective-permute-start | bytes 331784 | tf_op jit(solution)/shard_map/ppermute | solution.py:370
  32.9 7.3 %collective-permute-start.8 = (bf16[9,16,384]{2,1,0:T(8,128)(2,1)S(1)}, bf16[9,16,384]{2,1,0:T(8,128)(2,1)S(1)}, u32[]{:S(2)}, u32[]{:S(2)}) collective-permute-start(bf16[9,16,384]{2,1,0:T(8,128)(2,1)S(1)} %get-tuple-element.51), channel_id=1, source_target_pairs={{0,12},{1,13},{2,14},{3,15},{4,0},{5,1},{6,2},{7,3},{8,4},{9,5},{1... | collective-permute-start | bytes 331784 | tf_op jit(solution)/shard_map/ppermute | solution.py:370
  40.3 6.0 %collective-permute-start.16 = (bf16[9,16,384]{2,1,0:T(8,128)(2,1)S(1)}, bf16[9,16,384]{2,1,0:T(8,128)(2,1)S(1)}, u32[]{:S(2)}, u32[]{:S(2)}) collective-permute-start(bf16[9,16,384]{2,1,0:T(8,128)(2,1)S(1)} %shard_map.81.refs_0_), channel_id=1, source_target_pairs={{0,1},{1,0},{2,3},{3,2},{4,5},{5,4},{6,7},{7,6},{8,9},{9,8},{10,11... | collective-permute-start | bytes 331784 | tf_op jit(solution)/shard_map/ppermute | solution.py:370
  40.3 8.3 %collective-permute-start.13 = (bf16[9,16,384]{2,1,0:T(8,128)(2,1)S(1)}, bf16[9,16,384]{2,1,0:T(8,128)(2,1)S(1)}, u32[]{:S(2)}, u32[]{:S(2)}) collective-permute-start(bf16[9,16,384]{2,1,0:T(8,128)(2,1)S(1)} %shard_map.81.refs_0_), channel_id=1, source_target_pairs={{0,2},{1,3},{2,0},{3,1},{4,6},{5,7},{6,4},{7,5},{8,10},{9,11},{10,... | collective-permute-start | bytes 331784 | tf_op jit(solution)/shard_map/ppermute | solution.py:370
  41.3 7.4 %collective-permute-start.12 = (bf16[9,16,384]{2,1,0:T(8,128)(2,1)S(1)}, bf16[9,16,384]{2,1,0:T(8,128)(2,1)S(1)}, u32[]{:S(2)}, u32[]{:S(2)}) collective-permute-start(bf16[9,16,384]{2,1,0:T(8,128)(2,1)S(1)} %shard_map.81.refs_0_), channel_id=1, source_target_pairs={{0,12},{1,13},{2,14},{3,15},{4,0},{5,1},{6,2},{7,3},{8,4},{9,5},{1... | collective-permute-start | bytes 331784 | tf_op jit(solution)/shard_map/ppermute | solution.py:370
  45.1 13.8 %collective-permute-start.11 = (bf16[9,16,384]{2,1,0:T(8,128)(2,1)S(1)}, bf16[9,16,384]{2,1,0:T(8,128)(2,1)S(1)}, u32[]{:S(2)}, u32[]{:S(2)}) collective-permute-start(bf16[9,16,384]{2,1,0:T(8,128)(2,1)S(1)} %shard_map.81.refs_0_), channel_id=1, source_target_pairs={{0,10},{1,11},{2,8},{3,9},{4,14},{5,15},{6,12},{7,13},{8,2},{9,3},... | collective-permute-start | bytes 331784 | tf_op jit(solution)/shard_map/ppermute | solution.py:370
  46.2 13.4 %collective-permute-start.9 = (bf16[9,16,384]{2,1,0:T(8,128)(2,1)S(1)}, bf16[9,16,384]{2,1,0:T(8,128)(2,1)S(1)}, u32[]{:S(2)}, u32[]{:S(2)}) collective-permute-start(bf16[9,16,384]{2,1,0:T(8,128)(2,1)S(1)} %shard_map.81.refs_0_), channel_id=1, source_target_pairs={{0,4},{1,5},{2,6},{3,7},{4,8},{5,9},{6,10},{7,11},{8,12},{9,13},{1... | collective-permute-start | bytes 331784 | tf_op jit(solution)/shard_map/ppermute | solution.py:370
  46.3 14.7 %collective-permute-start.10 = (bf16[9,16,384]{2,1,0:T(8,128)(2,1)S(1)}, bf16[9,16,384]{2,1,0:T(8,128)(2,1)S(1)}, u32[]{:S(2)}, u32[]{:S(2)}) collective-permute-start(bf16[9,16,384]{2,1,0:T(8,128)(2,1)S(1)} %shard_map.81.refs_0_), channel_id=1, source_target_pairs={{0,8},{1,9},{2,10},{3,11},{4,12},{5,13},{6,14},{7,15},{8,0},{9,1},... | collective-permute-start | bytes 331784 | tf_op jit(solution)/shard_map/ppermute | solution.py:370
  48.7 12.3 %collective-permute-start.21 = (bf16[9,16,384]{2,1,0:T(8,128)(2,1)S(1)}, bf16[9,16,384]{2,1,0:T(8,128)(2,1)S(1)}, u32[]{:S(2)}, u32[]{:S(2)}) collective-permute-start(bf16[9,16,384]{2,1,0:T(8,128)(2,1)S(1)} %collective-permute-done.13.refs_5_), channel_id=1, source_target_pairs={{0,1},{1,0},{2,3},{3,2},{4,5},{5,4},{6,7},{7,6},{8,9},{9,8},{10,11... | collective-permute-start | bytes 331784 | tf_op jit(solution)/shard_map/ppermute | solution.py:370
  48.7 12.8 %collective-permute-start.20 = (bf16[9,16,384]{2,1,0:T(8,128)(2,1)S(1)}, bf16[9,16,384]{2,1,0:T(8,128)(2,1)S(1)}, u32[]{:S(2)}, u32[]{:S(2)}) collective-permute-start(bf16[9,16,384]{2,1,0:T(8,128)(2,1)S(1)} %collective-permute-done.12.refs_4_), channel_id=1, source_target_pairs={{0,1},{1,0},{2,3},{3,2},{4,5},{5,4},{6,7},{7,6},{8,9},{9,8},{10,11... | collective-permute-start | bytes 331784 | tf_op jit(solution)/shard_map/ppermute | solution.py:370
  58.9 5.9 %collective-permute-start.15 = (bf16[9,16,384]{2,1,0:T(8,128)(2,1)S(1)}, bf16[9,16,384]{2,1,0:T(8,128)(2,1)S(1)}, u32[]{:S(2)}, u32[]{:S(2)}) collective-permute-start(bf16[9,16,384]{2,1,0:T(8,128)(2,1)S(1)} %collective-permute-done.12.refs_4_), channel_id=1, source_target_pairs={{0,2},{1,3},{2,0},{3,1},{4,6},{5,7},{6,4},{7,5},{8,10},{9,11},{10,... | collective-permute-start | bytes 331784 | tf_op jit(solution)/shard_map/ppermute | solution.py:370
  59.5 6.5 %collective-permute-start.14 = (bf16[9,16,384]{2,1,0:T(8,128)(2,1)S(1)}, bf16[9,16,384]{2,1,0:T(8,128)(2,1)S(1)}, u32[]{:S(2)}, u32[]{:S(2)}) collective-permute-start(bf16[9,16,384]{2,1,0:T(8,128)(2,1)S(1)} %collective-permute-done.9.refs_1_), channel_id=1, source_target_pairs={{0,2},{1,3},{2,0},{3,1},{4,6},{5,7},{6,4},{7,5},{8,10},{9,11},{10,... | collective-permute-start | bytes 331784 | tf_op jit(solution)/shard_map/ppermute | solution.py:370
  61.0 5.1 %collective-permute-start.17 = (bf16[9,16,384]{2,1,0:T(8,128)(2,1)S(1)}, bf16[9,16,384]{2,1,0:T(8,128)(2,1)S(1)}, u32[]{:S(2)}, u32[]{:S(2)}) collective-permute-start(bf16[9,16,384]{2,1,0:T(8,128)(2,1)S(1)} %collective-permute-done.9.refs_1_), channel_id=1, source_target_pairs={{0,1},{1,0},{2,3},{3,2},{4,5},{5,4},{6,7},{7,6},{8,9},{9,8},{10,11... | collective-permute-start | bytes 331784 | tf_op jit(solution)/shard_map/ppermute | solution.py:370
  61.0 5.0 %collective-permute-start.19 = (bf16[9,16,384]{2,1,0:T(8,128)(2,1)S(1)}, bf16[9,16,384]{2,1,0:T(8,128)(2,1)S(1)}, u32[]{:S(2)}, u32[]{:S(2)}) collective-permute-start(bf16[9,16,384]{2,1,0:T(8,128)(2,1)S(1)} %collective-permute-done.11.refs_3_), channel_id=1, source_target_pairs={{0,1},{1,0},{2,3},{3,2},{4,5},{5,4},{6,7},{7,6},{8,9},{9,8},{10,11... | collective-permute-start | bytes 331784 | tf_op jit(solution)/shard_map/ppermute | solution.py:370
  61.5 4.5 %collective-permute-start.18 = (bf16[9,16,384]{2,1,0:T(8,128)(2,1)S(1)}, bf16[9,16,384]{2,1,0:T(8,128)(2,1)S(1)}, u32[]{:S(2)}, u32[]{:S(2)}) collective-permute-start(bf16[9,16,384]{2,1,0:T(8,128)(2,1)S(1)} %collective-permute-done.10.refs_2_), channel_id=1, source_target_pairs={{0,1},{1,0},{2,3},{3,2},{4,5},{5,4},{6,7},{7,6},{8,9},{9,8},{10,11... | collective-permute-start | bytes 331784 | tf_op jit(solution)/shard_map/ppermute | solution.py:370
  64.8 1.3 %collective-permute-start.23 = (bf16[9,16,384]{2,1,0:T(8,128)(2,1)S(1)}, bf16[9,16,384]{2,1,0:T(8,128)(2,1)S(1)}, u32[]{:S(2)}, u32[]{:S(2)}) collective-permute-start(bf16[9,16,384]{2,1,0:T(8,128)(2,1)S(1)} %collective-permute-done.15.refs_7_), channel_id=1, source_target_pairs={{0,1},{1,0},{2,3},{3,2},{4,5},{5,4},{6,7},{7,6},{8,9},{9,8},{10,11... | collective-permute-start | bytes 331784 | tf_op jit(solution)/shard_map/ppermute | solution.py:370
  66.0 1.3 %collective-permute-start.22 = (bf16[9,16,384]{2,1,0:T(8,128)(2,1)S(1)}, bf16[9,16,384]{2,1,0:T(8,128)(2,1)S(1)}, u32[]{:S(2)}, u32[]{:S(2)}) collective-permute-start(bf16[9,16,384]{2,1,0:T(8,128)(2,1)S(1)} %collective-permute-done.14.refs_6_), channel_id=1, source_target_pairs={{0,1},{1,0},{2,3},{3,2},{4,5},{5,4},{6,7},{7,6},{8,9},{9,8},{10,11... | collective-permute-start | bytes 331784 | tf_op jit(solution)/shard_map/ppermute | solution.py:370

commit v3 on v2

v3 whole, which is shorter than its diff:
```python
import jax
import jax.numpy as jnp
from jax import lax
from jax.experimental import pallas as pl
from jax.experimental.pallas import tpu as pltpu
from jax.sharding import PartitionSpec as P

F32 = jnp.float32
BF16 = jnp.bfloat16
AXIS = "height"
VMEM_LIMIT = 24 * 1024 * 1024


def position():
    index = lax.axis_index(AXIS)
    return (index % 2, (index // 2) % 2, index // 4)


def emit(total, outs):
    _, side, plane = position()
    part = total.shape[1] // 2
    count = len(outs)
    rows = part // count
    for step, out in enumerate(outs):
        owner = (plane + step) % count if count > 1 else 0
        at = pl.multiple_of(side * part + owner * rows, rows)
        out[...] = total[:, pl.ds(at, rows)].astype(out.dtype)


def mm(a, b):
    return lax.dot_general(a, b, (((1,), (0,)), ((), ())), preferred_element_type=F32)


def mm_nt(a, b):
    return lax.dot_general(a, b, (((1,), (1,)), ((), ())), preferred_element_type=F32)


def mm_tn(a, b):
    return lax.dot_general(a, b, (((0,), (0,)), ((), ())), preferred_element_type=F32)


def shifted(field, by, half):
    rows, _, chans = field.shape
    flat = field.reshape(rows * half, chans)
    column = lax.broadcasted_iota(jnp.int32, flat.shape, 0) % half
    moved = pltpu.roll(flat, by % (rows * half), axis=0)
    edge = 0 if by > 0 else half - 1
    return jnp.where(column == edge, 0.0, moved).reshape(field.shape)


def wide_pair(even, odd, half):
    before = shifted(odd, 1, half).astype(BF16)
    after = shifted(even, -1, half).astype(BF16)
    even, odd = (even.astype(BF16), odd.astype(BF16))
    return (
        jnp.concatenate([before, even, odd], axis=-1),
        jnp.concatenate([even, odd, after], axis=-1),
    )


def edge_kernel(frames, cot, pack, edge, sems):
    core, _, _ = position()
    rows, width = frames.shape[1:3]
    short, half = cot.shape[1:3]
    chans = frames.shape[-1]
    first = pl.ds(core * (rows - 2), 2)
    only = pl.ds(core * (short - 1), 1)
    moves = [(frames.at[:, first], edge.at[:, 0:2]), (frames, pack.at[:, 0:rows])]
    for k in range(2):
        lanes = slice(k * chans, (k + 1) * chans)
        columns = slice(k * half, (k + 1) * half)
        moves.append((cot.at[:, only, :, lanes], edge.at[:, 2:3, columns]))
        moves.append((cot.at[:, :, :, lanes], pack.at[:, rows:, columns]))
    copies = [pltpu.make_async_copy(*move, sems.at[k]) for k, move in enumerate(moves)]
    for copy in copies:
        copy.start()
    for copy in copies:
        copy.wait()


def stage_kernel(*refs):
    sems = refs[-1]
    count = (len(refs) - 1) // 2
    copies = [
        pltpu.make_async_copy(refs[k], refs[count + k], sems.at[k]) for k in range(count)
    ]
    for copy in copies:
        copy.start()
    for copy in copies:
        copy.wait()


def forward_kernel(split, *refs):
    packs, edges, weight_a = (refs[0:4], refs[4:8], refs[8])
    outs, flat, total_b = (refs[9:-2], refs[-2], refs[-1])
    pieces, (pre_ref, stacked_a, stacked_b, cot_ref) = (outs[:split], outs[split:])
    core, side, plane = position()
    place = 2 * side + core
    frames, packed, width, chans = packs[0].shape
    rows = packed // 3 * 2
    short = rows // 2
    half = width // 2
    ext = 4 * rows + 4
    block = rows * width

    def edge(t, index):
        chosen = edges[3][t].astype(F32)
        for k in range(3):
            chosen = jnp.where(index == k, edges[k][t].astype(F32), chosen)
        cot = jnp.concatenate([chosen[2, 0:half], chosen[2, half:]], axis=-1)
        return (chosen[0:2].reshape(2 * width, chans), cot.astype(BF16))

    for t in range(frames):
        base = t * ext * width
        flat[base : base + 2 * width], cot_ref[t, 0] = edge(t, place)
        low = base + (ext - 2) * width
        flat[low : low + 2 * width], cot_ref[t, 4 * short + 1] = edge(t, 3 - place)
        for k in range(4):
            at = pl.multiple_of(base + 2 * width + (place ^ k) * block, 2 * width)
            flat[pl.ds(at, block)] = packs[k][t, 0:rows].astype(F32).reshape(block, chans)
            cot = (packs[k][t, rows:, 0:half], packs[k][t, rows:, half:])
            spot = pl.ds(1 + (place ^ k) * short, short)
            cot_ref[t, spot] = jnp.concatenate(cot, axis=-1)
    count = frames * ext
    even = flat[pl.ds(0, count * half, stride=2), :].reshape(count, half, chans)
    odd = flat[pl.ds(1, count * half, stride=2), :].reshape(count, half, chans)
    taps_even, taps_odd = wide_pair(even, odd, half)
    stacked_a[:, :, 0:half] = taps_even.reshape(frames, ext, half, 3 * chans)
    stacked_a[:, :, half:width] = taps_odd.reshape(frames, ext, half, 3 * chans)

    inner = ext - 2
    shared = jnp.zeros((inner * width, chans), F32)
    latest = [jnp.zeros((inner * width, chans), F32) for _ in range(2)]
    for kh in range(3):
        first = stacked_a[0, kh : kh + inner].reshape(inner * width, 3 * chans)
        second = stacked_a[1, kh : kh + inner].reshape(inner * width, 3 * chans)
        shared += mm(first, weight_a[0, kh]) + mm(first, weight_a[1, kh])
        latest[0] += mm(first, weight_a[2, kh])
        latest[1] += mm(second, weight_a[2, kh])
    even = even.reshape(frames, ext, half, chans)
    odd = odd.reshape(frames, ext, half, chans)
    outside = plane == 0
    row = lax.broadcasted_iota(jnp.int32, (inner, half, chans), 0)
    hidden = outside & (row == 0)
    for t in range(frames):
        conv = (shared + latest[t]).reshape(inner, 2, half, chans)
        pre_even = even[t, 1 : ext - 1] + conv[:, 0]
        pre_odd = odd[t, 1 : ext - 1] + conv[:, 1]
        pre_ref[t, :, 0:half] = pre_even
        pre_ref[t, :, half:width] = pre_odd
        act_even = jnp.where(hidden, 0.0, pre_even * jax.nn.sigmoid(pre_even))
        act_odd = jnp.where(hidden, 0.0, pre_odd * jax.nn.sigmoid(pre_odd))
        stacked_b[t] = jnp.concatenate(
            [
                shifted(act_odd, 1, half).astype(BF16),
                act_even.astype(BF16),
                act_odd.astype(BF16),
            ],
            axis=-1,
        ).reshape(inner // 2, 2, half, 3 * chans)
    wide = cot_ref.shape[-1]
    tall = 4 * short
    grads = [cot_ref[t, 1 : tall + 1].reshape(tall * half, wide) for t in range(frames)]
    grad = jnp.concatenate(grads, axis=0)
    for kh in range(3):
        lo, parity = divmod(kh, 2)
        piece = [
            stacked_b[t, lo : lo + tall, parity].reshape(tall * half, 3 * chans)
            for t in (0, core)
        ]
        total = mm_tn(jnp.concatenate(piece, axis=0), grad)
        total_b[3 * kh : 3 * kh + 3] = total.reshape(3, chans, wide)
    emit(total_b, pieces)


def backward_kernel(last, cot_ref, pre_ref, stacked_a, weight_b, *refs):
    pieces, (pre_grad, total_a) = (refs[:-2], refs[-2:])
    core, side, plane = position()
    frames, ext_g, half, wide = cot_ref.shape
    chans = weight_b.shape[3]
    inner = pre_ref.shape[1]
    width = 2 * half
    mid = inner // 2
    cot = cot_ref[...].reshape(frames * ext_g, half, wide)
    ahead = shifted(cot.astype(F32), -1, half).astype(BF16)
    both = jnp.concatenate([cot, ahead], axis=-1).reshape(frames, ext_g, half, 2 * wide)
    later = both[:, 1:].reshape(frames * mid * half, 2 * wide)
    sooner = both[:, :-1].reshape(frames * mid * half, 2 * wide)
    zero = jnp.zeros((chans, wide), BF16)

    def taps(kt, kh):
        return jnp.concatenate(
            [
                jnp.concatenate([weight_b[kt, kh, 1], zero], axis=1),
                jnp.concatenate([weight_b[kt, kh, 2], weight_b[kt, kh, 0]], axis=1),
            ],
            axis=0,
        )

    def rows_of(kt):
        even = mm_nt(later, taps(kt, 1))
        odd = mm_nt(later, taps(kt, 0)) + mm_nt(sooner, taps(kt, 2))
        shape = (frames, mid, half, 2 * chans)
        return (even.reshape(shape), odd.reshape(shape))

    copies = [rows_of(kt) for kt in range(3)]
    row = lax.broadcasted_iota(jnp.int32, (inner, half, chans), 0)
    hidden = ((plane == 0) & (row == 0)) | ((plane == last) & (row == inner - 1))
    for t in range(frames):
        sums = []
        for parity in range(2):
            total = copies[2][parity][t]
            if t == 0:
                total = total + (copies[0][parity][0] + copies[1][parity][0])
                total = total + (copies[0][parity][1] + copies[1][parity][1])
            sums.append(total)
        grad = jnp.stack([sums[1], sums[0]], axis=1).reshape(inner, half, 2 * chans)
        for parity in range(2):
            act_grad = grad[:, :, parity * chans : (parity + 1) * chans]
            pre = pre_ref[t, :, parity * half : (parity + 1) * half]
            sig = jax.nn.sigmoid(pre)
            value = act_grad * sig * (1.0 + pre * (1.0 - sig))
            value = jnp.where(hidden, 0.0, value).astype(BF16)
            pre_grad[t, :, parity * half : (parity + 1) * half] = value
    rows = inner - 2
    grads = [pre_grad[t, 1 : rows + 1].reshape(rows * width, chans) for t in range(frames)]
    grad = jnp.concatenate(grads, axis=0)
    for kh in range(3):
        piece = [
            stacked_a[t, kh + 1 : kh + 1 + rows].reshape(rows * width, 3 * chans)
            for t in (0, core)
        ]
        total = mm_tn(jnp.concatenate(piece, axis=0), grad)
        total_a[3 * kh : 3 * kh + 3] = total.reshape(3, chans, chans)
    emit(total_a, pieces)


def output_kernel(stacked_b, pre_grad, weight_a, weight_b, encoded, frames_grad, flat):
    core, side, _ = position()
    place = 2 * side + core
    frames, _, _, half, _ = stacked_b.shape
    rows, width, chans = frames_grad.shape[1:]
    short = rows // 2
    wide = encoded.shape[-1]
    count = short * half
    shared = jnp.zeros((count, wide), F32)
    latest = jnp.zeros((frames * count, wide), F32)
    for kh in range(3):
        lo, parity = divmod(kh, 2)
        piece = [
            stacked_b[t, pl.ds(short * place + lo, short), parity].reshape(count, 3 * chans)
            for t in range(frames)
        ]
        shared += mm(piece[0], weight_b[0, kh]) + mm(piece[0], weight_b[1, kh])
        latest += mm(jnp.concatenate(piece, axis=0), weight_b[2, kh])
    for t in range(frames):
        value = shared + latest[t * count : (t + 1) * count]
        encoded[t] = value.astype(BF16).reshape(short, half, wide)

    ext = rows + 2
    own = pre_grad[:, pl.ds(rows * place, ext)].astype(F32)
    even = own[:, :, 0:half].reshape(frames * ext, half, chans)
    odd = own[:, :, half:width].reshape(frames * ext, half, chans)
    before = shifted(odd, 1, half).astype(BF16)
    after = shifted(even, -1, half).astype(BF16)
    even_16, odd_16 = (even.astype(BF16), odd.astype(BF16))
    stacked = jnp.stack(
        [
            jnp.concatenate([odd_16, even_16, before], axis=-1),
            jnp.concatenate([after, odd_16, even_16], axis=-1),
        ],
        axis=1,
    ).reshape(frames, ext, width, 3 * chans)
    early = jnp.zeros((frames * rows * width, chans), F32)
    late = jnp.zeros((frames * rows * width, chans), F32)
    for kh in range(3):
        piece = stacked[:, 2 - kh : 2 - kh + rows].reshape(frames * rows * width, 3 * chans)
        for kt in range(3):
            taps = jnp.concatenate([weight_a[kt, kh, kw] for kw in range(3)], axis=1)
            if kt == 2:
                late += mm_nt(piece, taps)
            else:
                early += mm_nt(piece, taps)
    early = early.reshape(frames, rows, 2, half, chans)
    late = late.reshape(frames, rows, 2, half, chans)
    even = even.reshape(frames, ext, half, chans)[:, 1 : rows + 1]
    odd = odd.reshape(frames, ext, half, chans)[:, 1 : rows + 1]
    size = rows * half
    for t in range(frames):
        total = late[t]
        if t == 0:
            total = total + (early[0] + early[1])
        for parity, value in ((0, even), (1, odd)):
            summed = value[t] + total[:, parity]
            flat[pl.ds(t * 2 * size + parity, size, stride=2), :] = summed.reshape(size, chans)
    frames_grad[...] = flat[...].reshape(frames_grad.shape).astype(BF16)


def finish_kernel(scale, *refs):
    half = len(refs) // 2
    chans = refs[0].shape[-1]

    def total(parts):
        value = parts[0][...].astype(F32)
        for part in parts[1:]:
            value = value + part[...].astype(F32)
        return (value * scale).astype(BF16)

    refs[-1][:, :, 0:chans] = total(refs[:half])
    refs[-1][:, :, chans:] = total(refs[half:-1])


def assemble_kernel(places, planes, *refs):
    pieces, (out_a, out_b) = (refs[:-2], refs[-2:])
    core, side, plane = position()
    chans = out_a.shape[-1]
    rows = pieces[0].shape[1]
    for piece, (flip_core, flip_side, step) in zip(pieces, places, strict=True):
        tap = core ^ flip_core
        source = (plane - step + planes) % planes
        at = pl.multiple_of((side ^ flip_side) * (chans // 2) + source * rows, rows)
        for slot in (2 * tap, 1 + tap):
            out_a[slot, :, pl.ds(at, rows)] = piece[:, :, 0:chans]
            out_b[slot, :, pl.ds(at, rows)] = piece[:, :, chans:]


def call(body, outs, args, scratch=(), flops=0, whole=False, limit=VMEM_LIMIT):
    extra = {}
    if whole:
        extra["in_specs"] = [pl.BlockSpec(memory_space=pl.ANY)] * len(args)
    return pl.pallas_call(
        body,
        out_shape=outs,
        scratch_shapes=scratch,
        compiler_params=pltpu.CompilerParams(vmem_limit_bytes=limit),
        cost_estimate=pl.CostEstimate(flops=flops, bytes_accessed=10**4, transcendentals=0),
        **extra,
    )(*args)


def on_device(frames, weight_a, weight_b, cotangent):
    count, rows, width, chans = frames.shape
    assert count == 2
    wide = weight_b.shape[-1]
    half = width // 2
    n = lax.axis_size(AXIS)
    planes = n // 4
    core, side, plane = position()
    shape = jax.ShapeDtypeStruct

    def send(value, pairs):
        return lax.ppermute(value, AXIS, pairs)

    swap_core = [(i, i ^ 1) for i in range(n)]
    swap_side = [(i, i ^ 2) for i in range(n)]
    near = [(4 * k + 3, 4 * k + 4) for k in range(planes - 1)]
    near += [(4 * k + 4, 4 * k + 3) for k in range(planes - 1)]

    pack, edge = call(
        edge_kernel,
        (
            shape((count, rows + rows // 2, width, chans), BF16),
            shape((count, 3, width, chans), BF16),
        ),
        (frames, cotangent),
        [pltpu.SemaphoreType.DMA((6,))],
        whole=True,
        limit=None,
    )
    packs = [pack, send(pack, swap_core), send(pack, swap_side), None]
    edges = [send(edge, near), None, None, None]
    edges[2] = send(edges[0], swap_side)
    edges[1] = send(edges[0], swap_core)
    packs[2], edges[2] = lax.optimization_barrier((packs[2], edges[2]))
    packs[3] = send(packs[2], swap_core)
    edges[3] = send(edges[2], swap_core)
    inputs = (pack, weight_a, weight_b)
    packs[0], staged_a, staged_b = call(
        stage_kernel,
        tuple(shape(x.shape, x.dtype) for x in inputs),
        inputs,
        [pltpu.SemaphoreType.DMA((3,))],
        whole=True,
    )

    inner = 4 * rows + 2
    kernel_a = staged_a.reshape(3, 3, 3 * chans, chans)
    kernel_b = staged_b.reshape(3, 3, 3 * chans, wide)
    part = chans // 2
    split = planes if part % (8 * planes) == 0 else 1

    def pieces_of(outputs):
        own = (9, part // split, outputs)
        return (shape(own, F32),) + (shape(own, BF16),) * (split - 1)

    def forward(*refs):
        forward_kernel(split, *refs)

    def backward(*refs):
        backward_kernel(planes - 1, *refs)

    *pieces_b, pre, stacked_a, stacked_b, cot = call(
        forward,
        pieces_of(wide)
        + (
            shape((count, inner, width, chans), F32),
            shape((count, inner + 2, width, 3 * chans), BF16),
            shape((count, inner // 2, 2, half, 3 * chans), BF16),
            shape((count, 2 * rows + 2, half, wide), BF16),
        ),
        (*packs, *edges, kernel_a),
        [
            pltpu.VMEM((count * (inner + 2) * width, chans), F32),
            pltpu.VMEM((9, chans, wide), F32),
        ],
        flops=10**7,
    )
    *pieces_a, pre_grad = call(
        backward,
        pieces_of(chans) + (shape((count, inner, width, chans), BF16),),
        (cot, pre, stacked_a, staged_b),
        [pltpu.VMEM((9, chans, chans), F32)],
        flops=10**7,
    )
    encoded, frames_grad = call(
        output_kernel,
        (shape(cotangent.shape, BF16), shape(frames.shape, BF16)),
        (stacked_b, pre_grad, staged_a, kernel_b),
        [pltpu.VMEM((count * rows * width, chans), F32)],
        flops=10**7,
    )

    scale = (count * rows * n * width) ** (-0.5)
    if split != planes:
        taps = jnp.arange(2)[:, None, None, None, None] == core
        sides = jnp.arange(2)[None, None, :, None, None] == side
        both = []
        for value in (pieces_a[0], pieces_b[0]):
            slots = jnp.where(taps & sides, value[None, :, None], 0.0)
            total = lax.psum(slots, AXIS) * scale
            total = total.astype(BF16).reshape(2, 3, 3, chans, -1)
            both.append(jnp.concatenate([total[:1], total], axis=0))
        return (encoded, frames_grad, both[0], both[1])

    rotations = [[(i, (i + 4 * step) % n) for i in range(n)] for step in range(planes)]
    got_b = [send(pieces_b[step], rotations[step]) for step in range(1, planes)]
    gate = lax.optimization_barrier((*got_b[:1], *pieces_a[1:]))
    got_b[:1] = gate[:1]
    pieces_a[1:] = gate[1:]
    got_a = [send(pieces_a[step], rotations[step]) for step in range(1, planes)]
    held = (pieces_a[0], encoded, frames_grad)
    own_a, encoded, frames_grad = lax.optimization_barrier(held)

    def finish(*refs):
        finish_kernel(scale, *refs)

    piece = shape((9, part // planes, chans + wide), BF16)
    (own,) = call(finish, (piece,), (own_a, *got_a, pieces_b[0], *got_b))
    column = {(0, 0, 0): own}
    for step in range(1, planes):
        column[0, 0, step] = send(own, rotations[step])
    for step in range(planes):
        column[0, 1, step] = send(column[0, 0, step], swap_side)
    for (_, flip, step), value in list(column.items()):
        column[1, flip, step] = send(value, swap_core)
    places = tuple(column)

    def assemble(*refs):
        assemble_kernel(places, planes, *refs)

    grad_a, grad_b = call(
        assemble,
        (shape((3, 9, chans, chans), BF16), shape((3, 9, chans, wide), BF16)),
        tuple(column.values()),
    )
    return (encoded, frames_grad, grad_a.reshape(weight_a.shape), grad_b.reshape(weight_b.shape))


def solution(mesh):
    in_specs = (P("groups", "height", None, None), P(), P(), P("groups", "height", None, None))
    out_specs = (
        P("groups", "height", None, None),
        P("groups", "height", None, None),
        P("groups", None, None, None, None),
        P("groups", None, None, None, None),
    )
    return jax.shard_map(
        on_device, mesh=mesh, in_specs=in_specs, out_specs=out_specs, check_vma=False
    )
```

time: 69.6 us -> 64.8 us (0.931)
  waiting for transfers between devices: 27.6 us -> 14.2 us
  starting transfers between devices: 27.4 us -> 32.1 us
  Pallas kernels: 9.25 us -> 13.9 us
  local copies, waits for them, and re-layouts: 4.39 us -> 3.57 us
    ppermute x24 -> x28, waiting for transfers between devices: 27.6 us -> 14.2 us  [send(): return lax.ppermute(value, AXIS, pairs)]
    ppermute x24 -> x28, starting transfers between devices: 27.4 us -> 32.1 us  [send(): return lax.ppermute(value, AXIS, pairs)]
    pallas_call x8 -> x7, Pallas kernels: 9.25 us -> 13.9 us  [call(): pl.pallas_call(body, out_shape=outs, scratch_shapes=scratch, compiler_par...]
    unnamed x8 -> x6, local copies, waits for them, and re-layouts: 4.39 us -> 3.57 us
  transfers between devices with their start and end apart: 24 -> 28, of which waited for: 8 -> 7; matrix products, arithmetic and copies ran while one was open for 0% -> 0% of each run, Pallas kernels for 7% -> 10%
where the time goes in v3:
time: 64.8 us; the launch traced here: 64.5 us
  starting transfers between devices  32.1 us (50%)
  waiting for transfers between devices  14.2 us (22%)
  Pallas kernels  13.9 us (21%)
  local copies, waits for them, and re-layouts  3.57 us (6%)
  between operations  0.77 us (1%)
    ppermute x28, starting transfers between devices, send(): return lax.ppermute(value, AXIS, pairs)  32.1 us
    ppermute x28, waiting for transfers between devices, send(): return lax.ppermute(value, AXIS, pairs)  14.2 us
    pallas_call x7, Pallas kernels, call(): pl.pallas_call(body, out_shape=outs, scratch_shapes=scratch, compiler_par...  13.9 us
    unnamed x6, local copies, waits for them, and re-layouts  3.57 us
  transfers between devices with their start and end apart: 28, of which 7 were waited for; matrix products, arithmetic and copies ran while one was open for 0% of the time, Pallas kernels for 10%

profile of v3, /device:TPU:0, one launch (start us, length us, event | category | flops | bytes accessed | tf_op | source)
XLA Modules:
  0.0 64.5 jit_solution(5652369803426448439)
XLA Ops:
  0.6 1.7 %shard_map.75 = (bf16[2,12,32,128]{3,2,1,0:T(8,128)(2,1)}, bf16[2,3,32,128]{3,2,1,0:T(8,128)(2,1)}) custom-call(bf16[2,8,32,128]{3,2,1,0:T(8,128)(2,1)} %frames.1, bf16[2,4,16,256]{3,2,1,0:T(8,128)(2,1)} %cot.1), custom_call_target="tpu_custom_call" | custom-call | bytes 10000 | tf_op jit(solution)/shard_map/pallas_call | solution.py:331
  2.4 3.0 %collective-permute-start.1 = (bf16[2,12,32,128]{3,2,1,0:T(8,128)(2,1)}, bf16[2,12,32,128]{3,2,1,0:T(8,128)(2,1)S(1)}, u32[]{:S(2)}, u32[]{:S(2)}) collective-permute-start(bf16[2,12,32,128]{3,2,1,0:T(8,128)(2,1)} %get-tuple-element.35.refs_0_), channel_id=1, source_target_pairs={{0,2},{1,3},{2,0},{3,1},{4,6},{5,7},{6,4},{7,5},{8,10},{9,11},{10,... | collective-permute-start | bytes 589832 | tf_op jit(solution)/shard_map/ppermute | solution.py:352
  5.4 0.7 %collective-permute-start.2 = (bf16[2,3,32,128]{3,2,1,0:T(8,128)(2,1)}, bf16[2,3,32,128]{3,2,1,0:T(8,128)(2,1)S(1)}, u32[]{:S(2)}, u32[]{:S(2)}) collective-permute-start(bf16[2,3,32,128]{3,2,1,0:T(8,128)(2,1)} %get-tuple-element.37), channel_id=1, source_target_pairs={{3,4},{7,8},{11,12},{4,3},{8,7},{12,11},{19,20},{23,24},{27,28},{2... | collective-permute-start | bytes 147464 | tf_op jit(solution)/shard_map/ppermute | solution.py:352
  6.1 0.0 collective-permute-done.2.refs_4_
  6.1 0.1 collective-permute-start.3
  6.2 6.1 %collective-permute-start = (bf16[2,12,32,128]{3,2,1,0:T(8,128)(2,1)}, bf16[2,12,32,128]{3,2,1,0:T(8,128)(2,1)S(1)}, u32[]{:S(2)}, u32[]{:S(2)}) collective-permute-start(bf16[2,12,32,128]{3,2,1,0:T(8,128)(2,1)} %get-tuple-element.35.refs_0_), channel_id=1, source_target_pairs={{0,1},{1,0},{2,3},{3,2},{4,5},{5,4},{6,7},{7,6},{8,9},{9,8},{10,11... | collective-permute-start | bytes 589832 | tf_op jit(solution)/shard_map/ppermute | solution.py:352
  12.3 1.5 %collective-permute-start.4 = (bf16[2,12,32,128]{3,2,1,0:T(8,128)(2,1)S(1)}, bf16[2,12,32,128]{3,2,1,0:T(8,128)(2,1)S(1)}, u32[]{:S(2)}, u32[]{:S(2)}) collective-permute-start(bf16[2,12,32,128]{3,2,1,0:T(8,128)(2,1)S(1)} %collective-permute-done.1.refs_2_), channel_id=1, source_target_pairs={{0,1},{1,0},{2,3},{3,2},{4,5},{5,4},{6,7},{7,6},{8,9},{9,8},{10,11... | collective-permute-start | bytes 589832 | tf_op jit(solution)/shard_map/ppermute | solution.py:352
  13.7 0.0 collective-permute-start.5
  13.7 0.5 collective-permute-start.6
  14.3 1.5 %copy-done = bf16[3,3,3,128,256]{4,3,2,1,0:T(8,128)(2,1)S(1)} copy-done((bf16[3,3,3,128,256]{4,3,2,1,0:T(8,128)(2,1)S(1)}, bf16[3,3,3,128,256]{4,3,2,1,0:T(8,128)(2,1)}, u32[]{:S(2)}) %copy-start) | copy-done | bytes 1769496
  15.7 1.2 %copy-done.1 = bf16[3,3,3,128,128]{4,3,2,1,0:T(8,128)(2,1)S(1)} copy-done((bf16[3,3,3,128,128]{4,3,2,1,0:T(8,128)(2,1)S(1)}, bf16[3,3,3,128,128]{4,3,2,1,0:T(8,128)(2,1)}, u32[]{:S(2)}) %copy-start.1) | copy-done | bytes 884760
  16.9 0.9 %copy-done.2 = bf16[2,12,32,128]{3,2,1,0:T(8,128)(2,1)S(1)} copy-done((bf16[2,12,32,128]{3,2,1,0:T(8,128)(2,1)S(1)}, bf16[2,12,32,128]{3,2,1,0:T(8,128)(2,1)}, u32[]{:S(2)}) %copy-start.2) | copy-done | bytes 196632
  17.8 0.8 %shard_map.76 = (bf16[2,12,32,128]{3,2,1,0:T(8,128)(2,1)S(1)}, bf16[3,3,3,128,128]{4,3,2,1,0:T(8,128)(2,1)S(1)}, bf16[3,3,3,128,256]{4,3,2,1,0:T(8,128)(2,1)S(1)}) custom-call(bf16[2,12,32,128]{3,2,1,0:T(8,128)(2,1)S(1)} %copy-done.2, bf16[3,3,3,128,128]{4,3,2,1,0:T(8,128)(2,1)S(1)} %copy-done.1, bf16[3,3,3,128,256]{4,3,2,1,0:T(8,128)(2,1)S(1)} %copy-done), custom_call_target="tpu_custom_call" | custom-call | bytes 10000 | tf_op jit(solution)/shard_map/pallas_call | solution.py:331
  18.6 0.0 collective-permute-done.5.refs_5_
  18.7 0.0 collective-permute-done.4.refs_3_
  18.7 3.7 %shard_map.77 = (f32[9,16,256]{2,1,0:T(8,128)S(1)}, bf16[9,16,256]{2,1,0:T(8,128)(2,1)S(1)}, bf16[9,16,256]{2,1,0:T(8,128)(2,1)S(1)}, bf16[9,16,256]{2,1,0:T(8,1...) custom-call(bf16[2,12,32,128]{3,2,1,0:T(8,128)(2,1)S(1)} %get-tuple-, ...), custom_call_target="tpu_custom_call" | custom-call | flops 10000000 | bytes 10000 | tf_op jit(solution)/shard_map/pallas_call | solution.py:331
  22.4 3.9 %collective-permute-start.7 = (bf16[9,16,256]{2,1,0:T(8,128)(2,1)S(1)}, bf16[9,16,256]{2,1,0:T(8,128)(2,1)S(1)}, u32[]{:S(2)}, u32[]{:S(2)}) collective-permute-start(bf16[9,16,256]{2,1,0:T(8,128)(2,1)S(1)} %get-tuple-element.53), channel_id=1, source_target_pairs={{0,4},{1,5},{2,6},{3,7},{4,8},{5,9},{6,10},{7,11},{8,12},{9,13},{1... | collective-permute-start | bytes 221192 | tf_op jit(solution)/shard_map/ppermute | solution.py:352
  26.3 2.6 %collective-permute-start.11 = (bf16[9,16,256]{2,1,0:T(8,128)(2,1)S(1)}, bf16[9,16,256]{2,1,0:T(8,128)(2,1)S(1)}, u32[]{:S(2)}, u32[]{:S(2)}) collective-permute-start(bf16[9,16,256]{2,1,0:T(8,128)(2,1)S(1)} %get-tuple-element.62), channel_id=1, source_target_pairs={{0,8},{1,9},{2,10},{3,11},{4,12},{5,13},{6,14},{7,15},{8,0},{9,1},... | collective-permute-start | bytes 221192 | tf_op jit(solution)/shard_map/ppermute | solution.py:352
  28.9 1.3 %collective-permute-start.12 = (bf16[9,16,256]{2,1,0:T(8,128)(2,1)S(1)}, bf16[9,16,256]{2,1,0:T(8,128)(2,1)S(1)}, u32[]{:S(2)}, u32[]{:S(2)}) collective-permute-start(bf16[9,16,256]{2,1,0:T(8,128)(2,1)S(1)} %get-tuple-element.63), channel_id=1, source_target_pairs={{0,12},{1,13},{2,14},{3,15},{4,0},{5,1},{6,2},{7,3},{8,4},{9,5},{1... | collective-permute-start | bytes 221192 | tf_op jit(solution)/shard_map/ppermute | solution.py:352
  30.2 3.7 %shard_map.78 = (f32[9,16,128]{2,1,0:T(8,128)S(1)}, bf16[9,16,128]{2,1,0:T(8,128)(2,1)S(1)}, bf16[9,16,128]{2,1,0:T(8,128)(2,1)S(1)}, bf16[9,16,128]{2,1,0:T(8,128)(2,1)S(1)}, bf16[2,34,32,128]{3,2,1,0:T(8,128)(2,1)S(1)}) custom-call(bf16[2,18,16,256]{3,2,1,0:T(8,128)(2,1)S(1)} %get-tuple-element.41.refs_0_, ...), custom_call_target="tpu_custom_call" | custom-call | flops 10000000 | bytes 10000 | tf_op jit(solution)/shard_map/pallas_call | solution.py:331
  33.9 0.0 collective-permute-done.7.refs_5_
  33.9 0.7 %collective-permute-start.8 = (bf16[9,16,128]{2,1,0:T(8,128)(2,1)S(1)}, bf16[9,16,128]{2,1,0:T(8,128)(2,1)S(1)}, u32[]{:S(2)}, u32[]{:S(2)}) collective-permute-start(bf16[9,16,128]{2,1,0:T(8,128)(2,1)S(1)} %get-tuple-element.57), channel_id=1, source_target_pairs={{0,4},{1,5},{2,6},{3,7},{4,8},{5,9},{6,10},{7,11},{8,12},{9,13},{1... | collective-permute-start | bytes 110600 | tf_op jit(solution)/shard_map/ppermute | solution.py:352
  34.6 0.3 collective-permute-start.9
  35.0 2.8 %collective-permute-start.10 = (bf16[9,16,128]{2,1,0:T(8,128)(2,1)S(1)}, bf16[9,16,128]{2,1,0:T(8,128)(2,1)S(1)}, u32[]{:S(2)}, u32[]{:S(2)}) collective-permute-start(bf16[9,16,128]{2,1,0:T(8,128)(2,1)S(1)} %get-tuple-element.59), channel_id=1, source_target_pairs={{0,12},{1,13},{2,14},{3,15},{4,0},{5,1},{6,2},{7,3},{8,4},{9,5},{1... | collective-permute-start | bytes 110600 | tf_op jit(solution)/shard_map/ppermute | solution.py:352
  37.8 2.1 %shard_map.79 = (bf16[2,4,16,256]{3,2,1,0:T(8,128)(2,1)}, bf16[2,8,32,128]{3,2,1,0:T(8,128)(2,1)}) custom-call(bf16[2,17,2,16,384]{4,3,2,1,0:T(8,128)(2,1)S(1)} %get-tuple-element.46.stacked_b, bf16[2,34,32,128]{3,2,1,0:T(8,128)(2,1)S(1)} %get-tuple-element.47.pre_grad, bf16[3,3,3,128,128]{4,3,2,1,0:T(8,128)(2,1)S(1)} %get-tuple-element.40.weight_a, ...), custom_call_target="tpu_custom_call" | custom-call | flops 10000000 | bytes 10000 | tf_op jit(solution)/shard_map/pallas_call | solution.py:331
  39.9 0.0 collective-permute-done.11.refs_6_
  39.9 0.0 collective-permute-done.12.refs_7_
  39.9 0.0 collective-permute-done.8.refs_1_
  39.9 0.5 collective-permute-done.9.refs_2_
  40.4 0.0 collective-permute-done.10.refs_3_
  40.4 0.1 shard_map.80.refs_0_
  40.4 0.2 collective-permute-start.16
  40.6 3.3 %collective-permute-start.15 = (bf16[9,16,384]{2,1,0:T(8,128)(2,1)S(1)}, bf16[9,16,384]{2,1,0:T(8,128)(2,1)S(1)}, u32[]{:S(2)}, u32[]{:S(2)}) collective-permute-start(bf16[9,16,384]{2,1,0:T(8,128)(2,1)S(1)} %shard_map.80.refs_0_), channel_id=1, source_target_pairs={{0,12},{1,13},{2,14},{3,15},{4,0},{5,1},{6,2},{7,3},{8,4},{9,5},{1... | collective-permute-start | bytes 331784 | tf_op jit(solution)/shard_map/ppermute | solution.py:352
  43.9 0.0 collective-permute-start.20
  43.9 0.2 collective-permute-start.14
  44.1 0.4 collective-permute-start.13
  44.5 0.8 %collective-permute-done.16.refs_4_ = bf16[9,16,384]{2,1,0:T(8,128)(2,1)S(1)} collective-permute-done((bf16[9,16,384]{2,1,0:T(8,128)(2,1)S(1)}, bf16[9,16,384]{2,1,0:T(8,128)(2,1)S(1)}, u32[]{:S(2)}, u32[]{:S(2)}) %collective-permute-start.16) | collective-permute-done | bytes 110624 | tf_op jit(solution)/shard_map/ppermute | solution.py:352
  45.3 2.1 %collective-permute-done.15.refs_3_ = bf16[9,16,384]{2,1,0:T(8,128)(2,1)S(1)} collective-permute-done((bf16[9,16,384]{2,1,0:T(8,128)(2,1)S(1)}, bf16[9,16,384]{2,1,0:T(8,128)(2,1)S(1)}, u32[]{:S(2)}, u32[]{:S(2)}) %collective-permute-start.15) | collective-permute-done | bytes 110624 | tf_op jit(solution)/shard_map/ppermute | solution.py:352
  47.4 1.8 %collective-permute-start.19 = (bf16[9,16,384]{2,1,0:T(8,128)(2,1)S(1)}, bf16[9,16,384]{2,1,0:T(8,128)(2,1)S(1)}, u32[]{:S(2)}, u32[]{:S(2)}) collective-permute-start(bf16[9,16,384]{2,1,0:T(8,128)(2,1)S(1)} %collective-permute-done.15.refs_3_), channel_id=1, source_target_pairs={{0,2},{1,3},{2,0},{3,1},{4,6},{5,7},{6,4},{7,5},{8,10},{9,11},{10,... | collective-permute-start | bytes 331784 | tf_op jit(solution)/shard_map/ppermute | solution.py:352
  49.2 4.7 %collective-permute-done.14.refs_2_ = bf16[9,16,384]{2,1,0:T(8,128)(2,1)S(1)} collective-permute-done((bf16[9,16,384]{2,1,0:T(8,128)(2,1)S(1)}, bf16[9,16,384]{2,1,0:T(8,128)(2,1)S(1)}, u32[]{:S(2)}, u32[]{:S(2)}) %collective-permute-start.14) | collective-permute-done | bytes 110624 | tf_op jit(solution)/shard_map/ppermute | solution.py:352
  53.9 1.8 %collective-permute-start.18 = (bf16[9,16,384]{2,1,0:T(8,128)(2,1)S(1)}, bf16[9,16,384]{2,1,0:T(8,128)(2,1)S(1)}, u32[]{:S(2)}, u32[]{:S(2)}) collective-permute-start(bf16[9,16,384]{2,1,0:T(8,128)(2,1)S(1)} %collective-permute-done.14.refs_2_), channel_id=1, source_target_pairs={{0,2},{1,3},{2,0},{3,1},{4,6},{5,7},{6,4},{7,5},{8,10},{9,11},{10,... | collective-permute-start | bytes 331784 | tf_op jit(solution)/shard_map/ppermute | solution.py:352
  55.8 0.2 collective-permute-start.17
  56.0 0.5 collective-permute-start.21
  56.5 0.1 collective-permute-start.27
  56.6 3.3 %collective-permute-done.18.refs_6_ = bf16[9,16,384]{2,1,0:T(8,128)(2,1)S(1)} collective-permute-done((bf16[9,16,384]{2,1,0:T(8,128)(2,1)S(1)}, bf16[9,16,384]{2,1,0:T(8,128)(2,1)S(1)}, u32[]{:S(2)}, u32[]{:S(2)}) %collective-permute-start.18) | collective-permute-done | bytes 110624 | tf_op jit(solution)/shard_map/ppermute | solution.py:352
  59.9 1.5 %collective-permute-done.17.refs_5_ = bf16[9,16,384]{2,1,0:T(8,128)(2,1)S(1)} collective-permute-done((bf16[9,16,384]{2,1,0:T(8,128)(2,1)S(1)}, bf16[9,16,384]{2,1,0:T(8,128)(2,1)S(1)}, u32[]{:S(2)}, u32[]{:S(2)}) %collective-permute-start.17) | collective-permute-done | bytes 110624 | tf_op jit(solution)/shard_map/ppermute | solution.py:352
  61.4 1.3 %collective-permute-done.25.refs_13_ = bf16[9,16,384]{2,1,0:T(8,128)(2,1)S(1)} collective-permute-done((bf16[9,16,384]{2,1,0:T(8,128)(2,1)S(1)}, bf16[9,16,384]{2,1,0:T(8,128)(2,1)S(1)}, u32[]{:S(2)}, u32[]{:S(2)}) %collective-permute-start.25) | collective-permute-done | bytes 110624 | tf_op jit(solution)/shard_map/ppermute | solution.py:352
  62.7 1.8 %shard_map.81 = (bf16[3,9,128,128]{3,2,1,0:T(8,128)(2,1)}, bf16[3,9,128,256]{3,2,1,0:T(8,128)(2,1)}) custom-call(bf16[9,16,384]{2,1,0:T(8,128)(2,1)S(1)} %shard_map.80.refs_0_, bf16[9,16,384]{2,1,0:T(8,128)(2,1)S(1)} %collective-permute-done.13.refs_1_, bf16[9,16,384]{2,1,0:T(8,128)(2,1)S(1)} %collective-permute-done.14.refs_2_, ...), custom_call_target="tpu_custom_call" | custom-call | bytes 10000 | tf_op jit(solution)/shard_map/pallas_call | solution.py:331
  (21 shorter events, 0.1 us)
Async XLA Ops:
  2.4 9.9 %collective-permute-start.1 = (bf16[2,12,32,128]{3,2,1,0:T(8,128)(2,1)}, bf16[2,12,32,128]{3,2,1,0:T(8,128)(2,1)S(1)}, u32[]{:S(2)}, u32[]{:S(2)}) collective-permute-start(bf16[2,12,32,128]{3,2,1,0:T(8,128)(2,1)} %get-tuple-element.35.refs_0_), channel_id=1, source_target_pairs={{0,2},{1,3},{2,0},{3,1},{4,6},{5,7},{6,4},{7,5},{8,10},{9,11},{10,... | collective-permute-start | bytes 589832 | tf_op jit(solution)/shard_map/ppermute | solution.py:352
  5.4 0.7 %collective-permute-start.2 = (bf16[2,3,32,128]{3,2,1,0:T(8,128)(2,1)}, bf16[2,3,32,128]{3,2,1,0:T(8,128)(2,1)S(1)}, u32[]{:S(2)}, u32[]{:S(2)}) collective-permute-start(bf16[2,3,32,128]{3,2,1,0:T(8,128)(2,1)} %get-tuple-element.37), channel_id=1, source_target_pairs={{3,4},{7,8},{11,12},{4,3},{8,7},{12,11},{19,20},{23,24},{27,28},{2... | collective-permute-start | bytes 147464 | tf_op jit(solution)/shard_map/ppermute | solution.py:352
  6.1 6.2 %collective-permute-start.3 = (bf16[2,3,32,128]{3,2,1,0:T(8,128)(2,1)S(1)}, bf16[2,3,32,128]{3,2,1,0:T(8,128)(2,1)S(1)}, u32[]{:S(2)}, u32[]{:S(2)}) collective-permute-start(bf16[2,3,32,128]{3,2,1,0:T(8,128)(2,1)S(1)} %collective-permute-done.2.refs_4_), channel_id=1, source_target_pairs={{0,2},{1,3},{2,0},{3,1},{4,6},{5,7},{6,4},{7,5},{8,10},{9,11},{10,... | collective-permute-start | bytes 147464 | tf_op jit(solution)/shard_map/ppermute | solution.py:352
  6.2 12.5 %collective-permute-start = (bf16[2,12,32,128]{3,2,1,0:T(8,128)(2,1)}, bf16[2,12,32,128]{3,2,1,0:T(8,128)(2,1)S(1)}, u32[]{:S(2)}, u32[]{:S(2)}) collective-permute-start(bf16[2,12,32,128]{3,2,1,0:T(8,128)(2,1)} %get-tuple-element.35.refs_0_), channel_id=1, source_target_pairs={{0,1},{1,0},{2,3},{3,2},{4,5},{5,4},{6,7},{7,6},{8,9},{9,8},{10,11... | collective-permute-start | bytes 589832 | tf_op jit(solution)/shard_map/ppermute | solution.py:352
  12.3 6.4 %collective-permute-start.4 = (bf16[2,12,32,128]{3,2,1,0:T(8,128)(2,1)S(1)}, bf16[2,12,32,128]{3,2,1,0:T(8,128)(2,1)S(1)}, u32[]{:S(2)}, u32[]{:S(2)}) collective-permute-start(bf16[2,12,32,128]{3,2,1,0:T(8,128)(2,1)S(1)} %collective-permute-done.1.refs_2_), channel_id=1, source_target_pairs={{0,1},{1,0},{2,3},{3,2},{4,5},{5,4},{6,7},{7,6},{8,9},{9,8},{10,11... | collective-permute-start | bytes 589832 | tf_op jit(solution)/shard_map/ppermute | solution.py:352
  13.7 4.9 %collective-permute-start.5 = (bf16[2,3,32,128]{3,2,1,0:T(8,128)(2,1)S(1)}, bf16[2,3,32,128]{3,2,1,0:T(8,128)(2,1)S(1)}, u32[]{:S(2)}, u32[]{:S(2)}) collective-permute-start(bf16[2,3,32,128]{3,2,1,0:T(8,128)(2,1)S(1)} %collective-permute-done.2.refs_4_), channel_id=1, source_target_pairs={{0,1},{1,0},{2,3},{3,2},{4,5},{5,4},{6,7},{7,6},{8,9},{9,8},{10,11... | collective-permute-start | bytes 147464 | tf_op jit(solution)/shard_map/ppermute | solution.py:352
  13.7 4.9 %collective-permute-start.6 = (bf16[2,3,32,128]{3,2,1,0:T(8,128)(2,1)S(1)}, bf16[2,3,32,128]{3,2,1,0:T(8,128)(2,1)S(1)}, u32[]{:S(2)}, u32[]{:S(2)}) collective-permute-start(bf16[2,3,32,128]{3,2,1,0:T(8,128)(2,1)S(1)} %collective-permute-done.3.refs_6_), channel_id=1, source_target_pairs={{0,1},{1,0},{2,3},{3,2},{4,5},{5,4},{6,7},{7,6},{8,9},{9,8},{10,11... | collective-permute-start | bytes 147464 | tf_op jit(solution)/shard_map/ppermute | solution.py:352
  14.3 1.5 %copy-start = (bf16[3,3,3,128,256]{4,3,2,1,0:T(8,128)(2,1)S(1)}, bf16[3,3,3,128,256]{4,3,2,1,0:T(8,128)(2,1)}, u32[]{:S(2)}) copy-start(bf16[3,3,3,128,256]{4,3,2,1,0:T(8,128)(2,1)} %refs_2_.1) | copy-start | bytes 5308420
  15.7 1.2 %copy-start.1 = (bf16[3,3,3,128,128]{4,3,2,1,0:T(8,128)(2,1)S(1)}, bf16[3,3,3,128,128]{4,3,2,1,0:T(8,128)(2,1)}, u32[]{:S(2)}) copy-start(bf16[3,3,3,128,128]{4,3,2,1,0:T(8,128)(2,1)} %refs_1_.1) | copy-start | bytes 2654212
  16.9 0.9 %copy-start.2 = (bf16[2,12,32,128]{3,2,1,0:T(8,128)(2,1)S(1)}, bf16[2,12,32,128]{3,2,1,0:T(8,128)(2,1)}, u32[]{:S(2)}) copy-start(bf16[2,12,32,128]{3,2,1,0:T(8,128)(2,1)} %get-tuple-element.35.refs_0_) | copy-start | bytes 589828
  22.4 11.5 %collective-permute-start.7 = (bf16[9,16,256]{2,1,0:T(8,128)(2,1)S(1)}, bf16[9,16,256]{2,1,0:T(8,128)(2,1)S(1)}, u32[]{:S(2)}, u32[]{:S(2)}) collective-permute-start(bf16[9,16,256]{2,1,0:T(8,128)(2,1)S(1)} %get-tuple-element.53), channel_id=1, source_target_pairs={{0,4},{1,5},{2,6},{3,7},{4,8},{5,9},{6,10},{7,11},{8,12},{9,13},{1... | collective-permute-start | bytes 221192 | tf_op jit(solution)/shard_map/ppermute | solution.py:352
  26.3 13.6 %collective-permute-start.11 = (bf16[9,16,256]{2,1,0:T(8,128)(2,1)S(1)}, bf16[9,16,256]{2,1,0:T(8,128)(2,1)S(1)}, u32[]{:S(2)}, u32[]{:S(2)}) collective-permute-start(bf16[9,16,256]{2,1,0:T(8,128)(2,1)S(1)} %get-tuple-element.62), channel_id=1, source_target_pairs={{0,8},{1,9},{2,10},{3,11},{4,12},{5,13},{6,14},{7,15},{8,0},{9,1},... | collective-permute-start | bytes 221192 | tf_op jit(solution)/shard_map/ppermute | solution.py:352
  28.9 11.0 %collective-permute-start.12 = (bf16[9,16,256]{2,1,0:T(8,128)(2,1)S(1)}, bf16[9,16,256]{2,1,0:T(8,128)(2,1)S(1)}, u32[]{:S(2)}, u32[]{:S(2)}) collective-permute-start(bf16[9,16,256]{2,1,0:T(8,128)(2,1)S(1)} %get-tuple-element.63), channel_id=1, source_target_pairs={{0,12},{1,13},{2,14},{3,15},{4,0},{5,1},{6,2},{7,3},{8,4},{9,5},{1... | collective-permute-start | bytes 221192 | tf_op jit(solution)/shard_map/ppermute | solution.py:352
  33.9 6.0 %collective-permute-start.8 = (bf16[9,16,128]{2,1,0:T(8,128)(2,1)S(1)}, bf16[9,16,128]{2,1,0:T(8,128)(2,1)S(1)}, u32[]{:S(2)}, u32[]{:S(2)}) collective-permute-start(bf16[9,16,128]{2,1,0:T(8,128)(2,1)S(1)} %get-tuple-element.57), channel_id=1, source_target_pairs={{0,4},{1,5},{2,6},{3,7},{4,8},{5,9},{6,10},{7,11},{8,12},{9,13},{1... | collective-permute-start | bytes 110600 | tf_op jit(solution)/shard_map/ppermute | solution.py:352
  34.6 5.7 %collective-permute-start.9 = (bf16[9,16,128]{2,1,0:T(8,128)(2,1)S(1)}, bf16[9,16,128]{2,1,0:T(8,128)(2,1)S(1)}, u32[]{:S(2)}, u32[]{:S(2)}) collective-permute-start(bf16[9,16,128]{2,1,0:T(8,128)(2,1)S(1)} %get-tuple-element.58), channel_id=1, source_target_pairs={{0,8},{1,9},{2,10},{3,11},{4,12},{5,13},{6,14},{7,15},{8,0},{9,1},... | collective-permute-start | bytes 110600 | tf_op jit(solution)/shard_map/ppermute | solution.py:352
  35.0 5.4 %collective-permute-start.10 = (bf16[9,16,128]{2,1,0:T(8,128)(2,1)S(1)}, bf16[9,16,128]{2,1,0:T(8,128)(2,1)S(1)}, u32[]{:S(2)}, u32[]{:S(2)}) collective-permute-start(bf16[9,16,128]{2,1,0:T(8,128)(2,1)S(1)} %get-tuple-element.59), channel_id=1, source_target_pairs={{0,12},{1,13},{2,14},{3,15},{4,0},{5,1},{6,2},{7,3},{8,4},{9,5},{1... | collective-permute-start | bytes 110600 | tf_op jit(solution)/shard_map/ppermute | solution.py:352
  40.4 4.8 %collective-permute-start.16 = (bf16[9,16,384]{2,1,0:T(8,128)(2,1)S(1)}, bf16[9,16,384]{2,1,0:T(8,128)(2,1)S(1)}, u32[]{:S(2)}, u32[]{:S(2)}) collective-permute-start(bf16[9,16,384]{2,1,0:T(8,128)(2,1)S(1)} %shard_map.80.refs_0_), channel_id=1, source_target_pairs={{0,2},{1,3},{2,0},{3,1},{4,6},{5,7},{6,4},{7,5},{8,10},{9,11},{10,... | collective-permute-start | bytes 331784 | tf_op jit(solution)/shard_map/ppermute | solution.py:352
  40.6 6.8 %collective-permute-start.15 = (bf16[9,16,384]{2,1,0:T(8,128)(2,1)S(1)}, bf16[9,16,384]{2,1,0:T(8,128)(2,1)S(1)}, u32[]{:S(2)}, u32[]{:S(2)}) collective-permute-start(bf16[9,16,384]{2,1,0:T(8,128)(2,1)S(1)} %shard_map.80.refs_0_), channel_id=1, source_target_pairs={{0,12},{1,13},{2,14},{3,15},{4,0},{5,1},{6,2},{7,3},{8,4},{9,5},{1... | collective-permute-start | bytes 331784 | tf_op jit(solution)/shard_map/ppermute | solution.py:352
  43.9 3.5 %collective-permute-start.20 = (bf16[9,16,384]{2,1,0:T(8,128)(2,1)S(1)}, bf16[9,16,384]{2,1,0:T(8,128)(2,1)S(1)}, u32[]{:S(2)}, u32[]{:S(2)}) collective-permute-start(bf16[9,16,384]{2,1,0:T(8,128)(2,1)S(1)} %shard_map.80.refs_0_), channel_id=1, source_target_pairs={{0,1},{1,0},{2,3},{3,2},{4,5},{5,4},{6,7},{7,6},{8,9},{9,8},{10,11... | collective-permute-start | bytes 331784 | tf_op jit(solution)/shard_map/ppermute | solution.py:352
  43.9 10.1 %collective-permute-start.14 = (bf16[9,16,384]{2,1,0:T(8,128)(2,1)S(1)}, bf16[9,16,384]{2,1,0:T(8,128)(2,1)S(1)}, u32[]{:S(2)}, u32[]{:S(2)}) collective-permute-start(bf16[9,16,384]{2,1,0:T(8,128)(2,1)S(1)} %shard_map.80.refs_0_), channel_id=1, source_target_pairs={{0,8},{1,9},{2,10},{3,11},{4,12},{5,13},{6,14},{7,15},{8,0},{9,1},... | collective-permute-start | bytes 331784 | tf_op jit(solution)/shard_map/ppermute | solution.py:352
  44.1 11.7 %collective-permute-start.13 = (bf16[9,16,384]{2,1,0:T(8,128)(2,1)S(1)}, bf16[9,16,384]{2,1,0:T(8,128)(2,1)S(1)}, u32[]{:S(2)}, u32[]{:S(2)}) collective-permute-start(bf16[9,16,384]{2,1,0:T(8,128)(2,1)S(1)} %shard_map.80.refs_0_), channel_id=1, source_target_pairs={{0,4},{1,5},{2,6},{3,7},{4,8},{5,9},{6,10},{7,11},{8,12},{9,13},{1... | collective-permute-start | bytes 331784 | tf_op jit(solution)/shard_map/ppermute | solution.py:352
  45.3 10.7 %collective-permute-start.24 = (bf16[9,16,384]{2,1,0:T(8,128)(2,1)S(1)}, bf16[9,16,384]{2,1,0:T(8,128)(2,1)S(1)}, u32[]{:S(2)}, u32[]{:S(2)}) collective-permute-start(bf16[9,16,384]{2,1,0:T(8,128)(2,1)S(1)} %collective-permute-done.16.refs_4_), channel_id=1, source_target_pairs={{0,1},{1,0},{2,3},{3,2},{4,5},{5,4},{6,7},{7,6},{8,9},{9,8},{10,11... | collective-permute-start | bytes 331784 | tf_op jit(solution)/shard_map/ppermute | solution.py:352
  47.4 8.6 %collective-permute-start.23 = (bf16[9,16,384]{2,1,0:T(8,128)(2,1)S(1)}, bf16[9,16,384]{2,1,0:T(8,128)(2,1)S(1)}, u32[]{:S(2)}, u32[]{:S(2)}) collective-permute-start(bf16[9,16,384]{2,1,0:T(8,128)(2,1)S(1)} %collective-permute-done.15.refs_3_), channel_id=1, source_target_pairs={{0,1},{1,0},{2,3},{3,2},{4,5},{5,4},{6,7},{7,6},{8,9},{9,8},{10,11... | collective-permute-start | bytes 331784 | tf_op jit(solution)/shard_map/ppermute | solution.py:352
  47.4 9.1 %collective-permute-start.19 = (bf16[9,16,384]{2,1,0:T(8,128)(2,1)S(1)}, bf16[9,16,384]{2,1,0:T(8,128)(2,1)S(1)}, u32[]{:S(2)}, u32[]{:S(2)}) collective-permute-start(bf16[9,16,384]{2,1,0:T(8,128)(2,1)S(1)} %collective-permute-done.15.refs_3_), channel_id=1, source_target_pairs={{0,2},{1,3},{2,0},{3,1},{4,6},{5,7},{6,4},{7,5},{8,10},{9,11},{10,... | collective-permute-start | bytes 331784 | tf_op jit(solution)/shard_map/ppermute | solution.py:352
  53.9 5.9 %collective-permute-start.18 = (bf16[9,16,384]{2,1,0:T(8,128)(2,1)S(1)}, bf16[9,16,384]{2,1,0:T(8,128)(2,1)S(1)}, u32[]{:S(2)}, u32[]{:S(2)}) collective-permute-start(bf16[9,16,384]{2,1,0:T(8,128)(2,1)S(1)} %collective-permute-done.14.refs_2_), channel_id=1, source_target_pairs={{0,2},{1,3},{2,0},{3,1},{4,6},{5,7},{6,4},{7,5},{8,10},{9,11},{10,... | collective-permute-start | bytes 331784 | tf_op jit(solution)/shard_map/ppermute | solution.py:352
  55.8 5.6 %collective-permute-start.17 = (bf16[9,16,384]{2,1,0:T(8,128)(2,1)S(1)}, bf16[9,16,384]{2,1,0:T(8,128)(2,1)S(1)}, u32[]{:S(2)}, u32[]{:S(2)}) collective-permute-start(bf16[9,16,384]{2,1,0:T(8,128)(2,1)S(1)} %collective-permute-done.13.refs_1_), channel_id=1, source_target_pairs={{0,2},{1,3},{2,0},{3,1},{4,6},{5,7},{6,4},{7,5},{8,10},{9,11},{10,... | collective-permute-start | bytes 331784 | tf_op jit(solution)/shard_map/ppermute | solution.py:352
  56.0 5.4 %collective-permute-start.22 = (bf16[9,16,384]{2,1,0:T(8,128)(2,1)S(1)}, bf16[9,16,384]{2,1,0:T(8,128)(2,1)S(1)}, u32[]{:S(2)}, u32[]{:S(2)}) collective-permute-start(bf16[9,16,384]{2,1,0:T(8,128)(2,1)S(1)} %collective-permute-done.14.refs_2_), channel_id=1, source_target_pairs={{0,1},{1,0},{2,3},{3,2},{4,5},{5,4},{6,7},{7,6},{8,9},{9,8},{10,11... | collective-permute-start | bytes 331784 | tf_op jit(solution)/shard_map/ppermute | solution.py:352
  56.0 5.4 %collective-permute-start.21 = (bf16[9,16,384]{2,1,0:T(8,128)(2,1)S(1)}, bf16[9,16,384]{2,1,0:T(8,128)(2,1)S(1)}, u32[]{:S(2)}, u32[]{:S(2)}) collective-permute-start(bf16[9,16,384]{2,1,0:T(8,128)(2,1)S(1)} %collective-permute-done.13.refs_1_), channel_id=1, source_target_pairs={{0,1},{1,0},{2,3},{3,2},{4,5},{5,4},{6,7},{7,6},{8,9},{9,8},{10,11... | collective-permute-start | bytes 331784 | tf_op jit(solution)/shard_map/ppermute | solution.py:352
  56.5 4.9 %collective-permute-start.27 = (bf16[9,16,384]{2,1,0:T(8,128)(2,1)S(1)}, bf16[9,16,384]{2,1,0:T(8,128)(2,1)S(1)}, u32[]{:S(2)}, u32[]{:S(2)}) collective-permute-start(bf16[9,16,384]{2,1,0:T(8,128)(2,1)S(1)} %collective-permute-done.19.refs_7_), channel_id=1, source_target_pairs={{0,1},{1,0},{2,3},{3,2},{4,5},{5,4},{6,7},{7,6},{8,9},{9,8},{10,11... | collective-permute-start | bytes 331784 | tf_op jit(solution)/shard_map/ppermute | solution.py:352
  59.8 1.6 %collective-permute-start.26 = (bf16[9,16,384]{2,1,0:T(8,128)(2,1)S(1)}, bf16[9,16,384]{2,1,0:T(8,128)(2,1)S(1)}, u32[]{:S(2)}, u32[]{:S(2)}) collective-permute-start(bf16[9,16,384]{2,1,0:T(8,128)(2,1)S(1)} %collective-permute-done.18.refs_6_), channel_id=1, source_target_pairs={{0,1},{1,0},{2,3},{3,2},{4,5},{5,4},{6,7},{7,6},{8,9},{9,8},{10,11... | collective-permute-start | bytes 331784 | tf_op jit(solution)/shard_map/ppermute | solution.py:352
  61.4 1.3 %collective-permute-start.25 = (bf16[9,16,384]{2,1,0:T(8,128)(2,1)S(1)}, bf16[9,16,384]{2,1,0:T(8,128)(2,1)S(1)}, u32[]{:S(2)}, u32[]{:S(2)}) collective-permute-start(bf16[9,16,384]{2,1,0:T(8,128)(2,1)S(1)} %collective-permute-done.17.refs_5_), channel_id=1, source_target_pairs={{0,1},{1,0},{2,3},{3,2},{4,5},{5,4},{6,7},{7,6},{8,9},{9,8},{10,11... | collective-permute-start | bytes 331784 | tf_op jit(solution)/shard_map/ppermute | solution.py:352

commit v4 on v3

--- a/solution.py
+++ b/solution.py
@@ -78,49 +78,39 @@
         copy.wait()
 
 
-def stage_kernel(*refs):
-    sems = refs[-1]
-    count = (len(refs) - 1) // 2
-    copies = [
-        pltpu.make_async_copy(refs[k], refs[count + k], sems.at[k]) for k in range(count)
-    ]
-    for copy in copies:
-        copy.start()
-    for copy in copies:
-        copy.wait()
-
-
 def forward_kernel(split, *refs):
-    packs, edges, weight_a = (refs[0:4], refs[4:8], refs[8])
-    outs, flat, total_b = (refs[9:-2], refs[-2], refs[-1])
+    own_f, own_g, packs, edges, weight_a = (*refs[0:2], refs[2:5], refs[5:7], refs[7])
+    outs, flat, total_b = (refs[8:-2], refs[-2], refs[-1])
     pieces, (pre_ref, stacked_a, stacked_b, cot_ref) = (outs[:split], outs[split:])
     core, side, plane = position()
     place = 2 * side + core
-    frames, packed, width, chans = packs[0].shape
-    rows = packed // 3 * 2
+    frames, rows, width, chans = own_f.shape
     short = rows // 2
     half = width // 2
     ext = 4 * rows + 4
     block = rows * width
 
-    def edge(t, index):
-        chosen = edges[3][t].astype(F32)
-        for k in range(3):
-            chosen = jnp.where(index == k, edges[k][t].astype(F32), chosen)
+    def edge(t, own):
+        chosen = jnp.where(core == own, edges[0][t].astype(F32), edges[1][t].astype(F32))
         cot = jnp.concatenate([chosen[2, 0:half], chosen[2, half:]], axis=-1)
         return (chosen[0:2].reshape(2 * width, chans), cot.astype(BF16))
 
     for t in range(frames):
         base = t * ext * width
-        flat[base : base + 2 * width], cot_ref[t, 0] = edge(t, place)
+        flat[base : base + 2 * width], cot_ref[t, 0] = edge(t, 0)
         low = base + (ext - 2) * width
-        flat[low : low + 2 * width], cot_ref[t, 4 * short + 1] = edge(t, 3 - place)
+        flat[low : low + 2 * width], cot_ref[t, 4 * short + 1] = edge(t, 1)
         for k in range(4):
             at = pl.multiple_of(base + 2 * width + (place ^ k) * block, 2 * width)
-            flat[pl.ds(at, block)] = packs[k][t, 0:rows].astype(F32).reshape(block, chans)
-            cot = (packs[k][t, rows:, 0:half], packs[k][t, rows:, half:])
             spot = pl.ds(1 + (place ^ k) * short, short)
-            cot_ref[t, spot] = jnp.concatenate(cot, axis=-1)
+            if k == 0:
+                field, cot = (own_f[t], own_g[t])
+            else:
+                pack = packs[k - 1]
+                cot = (pack[t, rows:, 0:half], pack[t, rows:, half:])
+                field, cot = (pack[t, 0:rows], jnp.concatenate(cot, axis=-1))
+            flat[pl.ds(at, block)] = field.astype(F32).reshape(block, chans)
+            cot_ref[t, spot] = cot
     count = frames * ext
     even = flat[pl.ds(0, count * half, stride=2), :].reshape(count, half, chans)
     odd = flat[pl.ds(1, count * half, stride=2), :].reshape(count, half, chans)
@@ -129,14 +119,22 @@
     stacked_a[:, :, half:width] = taps_odd.reshape(frames, ext, half, 3 * chans)
 
     inner = ext - 2
-    shared = jnp.zeros((inner * width, chans), F32)
-    latest = [jnp.zeros((inner * width, chans), F32) for _ in range(2)]
-    for kh in range(3):
-        first = stacked_a[0, kh : kh + inner].reshape(inner * width, 3 * chans)
-        second = stacked_a[1, kh : kh + inner].reshape(inner * width, 3 * chans)
-        shared += mm(first, weight_a[0, kh]) + mm(first, weight_a[1, kh])
-        latest[0] += mm(first, weight_a[2, kh])
-        latest[1] += mm(second, weight_a[2, kh])
+    taps = [
+        jnp.concatenate([weight_a[kt, kh] for kh in range(3)], axis=0) for kt in range(3)
+    ]
+    fields = [
+        jnp.concatenate(
+            [
+                stacked_a[t, kh : kh + inner].reshape(inner * width, 3 * chans)
+                for kh in range(3)
+            ],
+            axis=1,
+        )
+        for t in range(2)
+    ]
+    early = mm(fields[0], jnp.concatenate(taps[:2], axis=1))
+    shared = early[:, :chans] + early[:, chans:]
+    latest = [mm(field, taps[2]) for field in fields]
     even = even.reshape(frames, ext, half, chans)
     odd = odd.reshape(frames, ext, half, chans)
     outside = plane == 0
@@ -225,13 +223,22 @@
     rows = inner - 2
     grads = [pre_grad[t, 1 : rows + 1].reshape(rows * width, chans) for t in range(frames)]
     grad = jnp.concatenate(grads, axis=0)
-    for kh in range(3):
-        piece = [
-            stacked_a[t, kh + 1 : kh + 1 + rows].reshape(rows * width, 3 * chans)
-            for t in (0, core)
-        ]
-        total = mm_tn(jnp.concatenate(piece, axis=0), grad)
-        total_a[3 * kh : 3 * kh + 3] = total.reshape(3, chans, chans)
+    field = jnp.concatenate(
+        [
+            jnp.concatenate(
+                [
+                    stacked_a[t, kh + 1 : kh + 1 + rows].reshape(rows * width, 3 * chans)
+                    for t in (0, core)
+                ],
+                axis=0,
+            )
+            for kh in range(3)
+        ],
+        axis=1,
+    )
+    total = mm(grad.T, field)
+    for k in range(9):
+        total_a[k] = total[:, k * chans : (k + 1) * chans].T
     emit(total_a, pieces)
 
 
@@ -353,8 +360,9 @@
 
     swap_core = [(i, i ^ 1) for i in range(n)]
     swap_side = [(i, i ^ 2) for i in range(n)]
-    near = [(4 * k + 3, 4 * k + 4) for k in range(planes - 1)]
-    near += [(4 * k + 4, 4 * k + 3) for k in range(planes - 1)]
+    along = []
+    for k in range(0, n - 4, 4):
+        along += [(k + 2, k + 6), (k + 3, k + 4), (k + 4, k + 3), (k + 5, k + 1)]
 
     pack, edge = call(
         edge_kernel,
@@ -366,22 +374,15 @@
         [pltpu.SemaphoreType.DMA((6,))],
         whole=True,
         limit=None,
-    )
-    packs = [pack, send(pack, swap_core), send(pack, swap_side), None]
-    edges = [send(edge, near), None, None, None]
-    edges[2] = send(edges[0], swap_side)
+        flops=4 * 10**9,
+    )
+    outer = jnp.where(core == side, edge, send(edge, swap_core))
+    packs = [send(pack, swap_core), send(pack, swap_side), None]
+    edges = [send(outer, along), None]
     edges[1] = send(edges[0], swap_core)
-    packs[2], edges[2] = lax.optimization_barrier((packs[2], edges[2]))
-    packs[3] = send(packs[2], swap_core)
-    edges[3] = send(edges[2], swap_core)
-    inputs = (pack, weight_a, weight_b)
-    packs[0], staged_a, staged_b = call(
-        stage_kernel,
-        tuple(shape(x.shape, x.dtype) for x in inputs),
-        inputs,
-        [pltpu.SemaphoreType.DMA((3,))],
-        whole=True,
-    )
+    packs[1], edges[0] = lax.optimization_barrier((packs[1], edges[0]))
+    packs[2] = send(packs[1], swap_core)
+    staged_a, staged_b = (weight_a, weight_b)
 
     inner = 4 * rows + 2
     kernel_a = staged_a.reshape(3, 3, 3 * chans, chans)
@@ -408,7 +409,7 @@
             shape((count, inner // 2, 2, half, 3 * chans), BF16),
             shape((count, 2 * rows + 2, half, wide), BF16),
         ),
-        (*packs, *edges, kernel_a),
+        (frames, cotangent, *packs, *edges, kernel_a),
         [
             pltpu.VMEM((count * (inner + 2) * width, chans), F32),
             pltpu.VMEM((9, chans, wide), F32),
@@ -422,16 +423,18 @@
         [pltpu.VMEM((9, chans, chans), F32)],
         flops=10**7,
     )
-    encoded, frames_grad = call(
-        output_kernel,
-        (shape(cotangent.shape, BF16), shape(frames.shape, BF16)),
-        (stacked_b, pre_grad, staged_a, kernel_b),
-        [pltpu.VMEM((count * rows * width, chans), F32)],
-        flops=10**7,
-    )
+    def outputs(stacked_b):
+        return call(
+            output_kernel,
+            (shape(cotangent.shape, BF16), shape(frames.shape, BF16)),
+            (stacked_b, pre_grad, staged_a, kernel_b),
+            [pltpu.VMEM((count * rows * width, chans), F32)],
+            flops=10**7,
+        )
 
     scale = (count * rows * n * width) ** (-0.5)
     if split != planes:
+        encoded, frames_grad = outputs(stacked_b)
         taps = jnp.arange(2)[:, None, None, None, None] == core
         sides = jnp.arange(2)[None, None, :, None, None] == side
         both = []
@@ -448,18 +451,22 @@
     got_b[:1] = gate[:1]
     pieces_a[1:] = gate[1:]
     got_a = [send(pieces_a[step], rotations[step]) for step in range(1, planes)]
-    held = (pieces_a[0], encoded, frames_grad)
-    own_a, encoded, frames_grad = lax.optimization_barrier(held)
 
     def finish(*refs):
         finish_kernel(scale, *refs)
 
     piece = shape((9, part // planes, chans + wide), BF16)
-    (own,) = call(finish, (piece,), (own_a, *got_a, pieces_b[0], *got_b))
+    (own,) = call(finish, (piece,), (pieces_a[0], *got_a, pieces_b[0], *got_b))
+    own, stacked_b = lax.optimization_barrier((own, stacked_b))
     column = {(0, 0, 0): own}
-    for step in range(1, planes):
+    order = sorted(range(1, planes), key=lambda step: -min(step, planes - step))
+    for step in order:
         column[0, 0, step] = send(own, rotations[step])
-    for step in range(planes):
+    first = (0, 0, order[-1] if order else 0)
+    encoded, frames_grad = outputs(stacked_b)
+    held = lax.optimization_barrier((column[first], encoded, frames_grad))
+    column[first], encoded, frames_grad = held
+    for step in (*order, 0):
         column[0, 1, step] = send(column[0, 0, step], swap_side)
     for (_, flip, step), value in list(column.items()):
         column[1, flip, step] = send(value, swap_core)

time: 64.8 us -> 58.8 us (0.907)
  starting transfers between devices: 32.1 us -> 24.3 us
  waiting for transfers between devices: 14.2 us -> 20.4 us
  local copies, waits for them, and re-layouts: 3.57 us -> 0.02 us
  Pallas kernels: 13.9 us -> 12.4 us
  other arithmetic: 0 us -> 0.81 us
    ppermute x28 -> x27, starting transfers between devices: 32.1 us -> 24.3 us  [send(): return lax.ppermute(value, AXIS, pairs)]
    ppermute x28 -> x27, waiting for transfers between devices: 14.2 us -> 20.4 us  [send(): return lax.ppermute(value, AXIS, pairs)]
    unnamed x6 -> x8, local copies, waits for them, and re-layouts: 3.57 us -> 0.02 us
    pallas_call x7 -> x6, Pallas kernels: 13.9 us -> 12.4 us  [call(): pl.pallas_call(body, out_shape=outs, scratch_shapes=scratch, compiler_par...]
    select_n x0 -> x1, other arithmetic: none -> 0.81 us  [on_device(): outer = jnp.where(core == side, edge, send(edge, swap_core))]
  transfers between devices with their start and end apart: 28 -> 27, of which waited for: 7 -> 10; matrix products, arithmetic and copies ran while one was open for 0% -> 1% of each run, Pallas kernels for 10% -> 9%
where the time goes in v4:
time: 58.8 us; the launch traced here: 58.6 us
  starting transfers between devices  24.3 us (41%)
  waiting for transfers between devices  20.4 us (35%)
  Pallas kernels  12.4 us (21%)
  other arithmetic  0.81 us (1%)
  between operations  0.78 us (1%)
    ppermute x27, starting transfers between devices, send(): return lax.ppermute(value, AXIS, pairs)  24.3 us
    ppermute x27, waiting for transfers between devices, send(): return lax.ppermute(value, AXIS, pairs)  20.4 us
    pallas_call x6, Pallas kernels, call(): pl.pallas_call(body, out_shape=outs, scratch_shapes=scratch, compiler_par...  12.4 us
  transfers between devices with their start and end apart: 27, of which 10 were waited for; matrix products, arithmetic and copies ran while one was open for 1% of the time, Pallas kernels for 9%

profile of v4, /device:TPU:0, one launch (start us, length us, event | category | flops | bytes accessed | tf_op | source)
XLA Modules:
  0.0 58.6 jit_solution(1657843662151849317)
XLA Ops:
  0.7 1.8 %shard_map.75 = (bf16[2,12,32,128]{3,2,1,0:T(8,128)(2,1)}, bf16[2,3,32,128]{3,2,1,0:T(8,128)(2,1)}) custom-call(bf16[2,8,32,128]{3,2,1,0:T(8,128)(2,1)} %refs_0_.1, bf16[2,4,16,256]{3,2,1,0:T(8,128)(2,1)} %refs_1_.1), custom_call_target="tpu_custom_call" | custom-call | flops 4000000000 | bytes 10000 | tf_op jit(solution)/shard_map/pallas_call | solution.py:338
  2.4 0.0 copy-start
  2.5 0.5 collective-permute-start.2
  3.0 2.6 %collective-permute-start.1 = (bf16[2,12,32,128]{3,2,1,0:T(8,128)(2,1)}, bf16[2,12,32,128]{3,2,1,0:T(8,128)(2,1)S(1)}, u32[]{:S(2)}, u32[]{:S(2)}) collective-permute-start(bf16[2,12,32,128]{3,2,1,0:T(8,128)(2,1)} %get-tuple-element.34), channel_id=1, source_target_pairs={{0,2},{1,3},{2,0},{3,1},{4,6},{5,7},{6,4},{7,5},{8,10},{9,11},{10,... | collective-permute-start | bytes 589832 | tf_op jit(solution)/shard_map/ppermute | solution.py:359
  5.6 0.0 collective-permute-done.2
  5.6 0.8 %broadcast_select_fusion = bf16[2,3,32,128]{3,2,1,0:T(8,128)(2,1)S(1)} fusion(bf16[2,3,32,128]{3,2,1,0:T(8,128)(2,1)} %get-tuple-element.35, bf16[2,3,32,128]{3,2,1,0:T(8,128)(2,1)S(1)} %collective-permute-done.2, pred[]{:T(512)S(6)} %eq.6), kind=kLoop, calls=%fused_computation | loop fusion | flops 24576 | bytes 147457 | tf_op jit(solution)/shard_map/jit(_where)/select_n | solution.py:379
  6.4 0.7 %collective-permute-start.3 = (bf16[2,3,32,128]{3,2,1,0:T(8,128)(2,1)S(1)}, bf16[2,3,32,128]{3,2,1,0:T(8,128)(2,1)S(1)}, u32[]{:S(2)}, u32[]{:S(2)}) collective-permute-start(bf16[2,3,32,128]{3,2,1,0:T(8,128)(2,1)S(1)} %broadcast_select_fusion), channel_id=1, source_target_pairs={{2,6},{3,4},{4,3},{5,1},{6,10},{7,8},{8,7},{9,5},{10,14},{11,12},{... | collective-permute-start | bytes 147464 | tf_op jit(solution)/shard_map/ppermute | solution.py:359
  7.0 0.1 collective-permute-start
  7.1 4.1 %collective-permute-done.1.refs_3_ = bf16[2,12,32,128]{3,2,1,0:T(8,128)(2,1)S(1)} collective-permute-done((bf16[2,12,32,128]{3,2,1,0:T(8,128)(2,1)}, bf16[2,12,32,128]{3,2,1,0:T(8,128)(2,1)S(1)}, u32[]{:S(2)}, u32[]{:S(2)}) %collective-permute-start.1) | collective-permute-done | bytes 196640 | tf_op jit(solution)/shard_map/ppermute | solution.py:359
  11.3 0.5 collective-permute-start.5
  11.8 1.0 %collective-permute-done.5.refs_6_ = bf16[2,3,32,128]{3,2,1,0:T(8,128)(2,1)S(1)} collective-permute-done((bf16[2,3,32,128]{3,2,1,0:T(8,128)(2,1)S(1)}, bf16[2,3,32,128]{3,2,1,0:T(8,128)(2,1)S(1)}, u32[]{:S(2)}, u32[]{:S(2)}) %collective-permute-start.5) | collective-permute-done | bytes 49184 | tf_op jit(solution)/shard_map/ppermute | solution.py:359
  12.8 0.0 collective-permute-done.refs_2_
  12.8 0.0 collective-permute-done.4.refs_4_
  12.8 3.4 %shard_map.76 = (f32[9,16,256]{2,1,0:T(8,128)S(1)}, bf16[9,16,256]{2,1,0:T(8,128)(2,1)S(1)}, bf16[9,16,256]{2,1,0:T(8,128)(2,1)S(1)}, bf16[9,16,256]{2,1,0:T(8,1...) custom-call(bf16[2,8,32,128]{3,2,1,0:T(8,128)(2,1)S(1)} %copy-done.2, ...), custom_call_target="tpu_custom_call" | custom-call | flops 10000000 | bytes 10000 | tf_op jit(solution)/shard_map/pallas_call | solution.py:338
  16.2 3.3 %collective-permute-start.6 = (bf16[9,16,256]{2,1,0:T(8,128)(2,1)S(1)}, bf16[9,16,256]{2,1,0:T(8,128)(2,1)S(1)}, u32[]{:S(2)}, u32[]{:S(2)}) collective-permute-start(bf16[9,16,256]{2,1,0:T(8,128)(2,1)S(1)} %get-tuple-element.42), channel_id=1, source_target_pairs={{0,4},{1,5},{2,6},{3,7},{4,8},{5,9},{6,10},{7,11},{8,12},{9,13},{1... | collective-permute-start | bytes 221192 | tf_op jit(solution)/shard_map/ppermute | solution.py:359
  19.5 2.6 %collective-permute-start.10 = (bf16[9,16,256]{2,1,0:T(8,128)(2,1)S(1)}, bf16[9,16,256]{2,1,0:T(8,128)(2,1)S(1)}, u32[]{:S(2)}, u32[]{:S(2)}) collective-permute-start(bf16[9,16,256]{2,1,0:T(8,128)(2,1)S(1)} %get-tuple-element.51), channel_id=1, source_target_pairs={{0,8},{1,9},{2,10},{3,11},{4,12},{5,13},{6,14},{7,15},{8,0},{9,1},... | collective-permute-start | bytes 221192 | tf_op jit(solution)/shard_map/ppermute | solution.py:359
  22.1 1.4 %collective-permute-start.11 = (bf16[9,16,256]{2,1,0:T(8,128)(2,1)S(1)}, bf16[9,16,256]{2,1,0:T(8,128)(2,1)S(1)}, u32[]{:S(2)}, u32[]{:S(2)}) collective-permute-start(bf16[9,16,256]{2,1,0:T(8,128)(2,1)S(1)} %get-tuple-element.52), channel_id=1, source_target_pairs={{0,12},{1,13},{2,14},{3,15},{4,0},{5,1},{6,2},{7,3},{8,4},{9,5},{1... | collective-permute-start | bytes 221192 | tf_op jit(solution)/shard_map/ppermute | solution.py:359
  23.4 3.2 %shard_map.77 = (f32[9,16,128]{2,1,0:T(8,128)S(1)}, bf16[9,16,128]{2,1,0:T(8,128)(2,1)S(1)}, bf16[9,16,128]{2,1,0:T(8,128)(2,1)S(1)}, bf16[9,16,128]{2,1,0:T(8,128)(2,1)S(1)}, bf16[2,34,32,128]{3,2,1,0:T(8,128)(2,1)S(1)}) custom-call(bf16[2,18,16,256]{3,2,1,0:T(8,128)(2,1)S(1)} %get-tuple-element.38.refs_0_, ...), custom_call_target="tpu_custom_call" | custom-call | flops 10000000 | bytes 10000 | tf_op jit(solution)/shard_map/pallas_call | solution.py:338
  26.7 0.7 %collective-permute-start.7 = (bf16[9,16,128]{2,1,0:T(8,128)(2,1)S(1)}, bf16[9,16,128]{2,1,0:T(8,128)(2,1)S(1)}, u32[]{:S(2)}, u32[]{:S(2)}) collective-permute-start(bf16[9,16,128]{2,1,0:T(8,128)(2,1)S(1)} %get-tuple-element.46), channel_id=1, source_target_pairs={{0,4},{1,5},{2,6},{3,7},{4,8},{5,9},{6,10},{7,11},{8,12},{9,13},{1... | collective-permute-start | bytes 110600 | tf_op jit(solution)/shard_map/ppermute | solution.py:359
  27.4 0.3 collective-permute-start.8
  27.8 2.8 %collective-permute-start.9 = (bf16[9,16,128]{2,1,0:T(8,128)(2,1)S(1)}, bf16[9,16,128]{2,1,0:T(8,128)(2,1)S(1)}, u32[]{:S(2)}, u32[]{:S(2)}) collective-permute-start(bf16[9,16,128]{2,1,0:T(8,128)(2,1)S(1)} %get-tuple-element.48), channel_id=1, source_target_pairs={{0,12},{1,13},{2,14},{3,15},{4,0},{5,1},{6,2},{7,3},{8,4},{9,5},{1... | collective-permute-start | bytes 110600 | tf_op jit(solution)/shard_map/ppermute | solution.py:359
  30.6 0.0 collective-permute-done.10.refs_6_
  30.6 0.0 collective-permute-done.11.refs_7_
  30.6 2.0 %collective-permute-done.7.refs_1_ = bf16[9,16,128]{2,1,0:T(8,128)(2,1)S(1)} collective-permute-done((bf16[9,16,128]{2,1,0:T(8,128)(2,1)S(1)}, bf16[9,16,128]{2,1,0:T(8,128)(2,1)S(1)}, u32[]{:S(2)}, u32[]{:S(2)}) %collective-permute-start.7) | collective-permute-done | bytes 36896 | tf_op jit(solution)/shard_map/ppermute | solution.py:359
  32.6 0.7 %collective-permute-done.8.refs_2_ = bf16[9,16,128]{2,1,0:T(8,128)(2,1)S(1)} collective-permute-done((bf16[9,16,128]{2,1,0:T(8,128)(2,1)S(1)}, bf16[9,16,128]{2,1,0:T(8,128)(2,1)S(1)}, u32[]{:S(2)}, u32[]{:S(2)}) %collective-permute-start.8) | collective-permute-done | bytes 36896 | tf_op jit(solution)/shard_map/ppermute | solution.py:359
  33.3 0.1 shard_map.78.refs_0_
  33.4 3.0 %collective-permute-start.12 = (bf16[9,16,384]{2,1,0:T(8,128)(2,1)S(1)}, bf16[9,16,384]{2,1,0:T(8,128)(2,1)S(1)}, u32[]{:S(2)}, u32[]{:S(2)}) collective-permute-start(bf16[9,16,384]{2,1,0:T(8,128)(2,1)S(1)} %shard_map.78.refs_0_), channel_id=1, source_target_pairs={{0,12},{1,13},{2,14},{3,15},{4,0},{5,1},{6,2},{7,3},{8,4},{9,5},{1... | collective-permute-start | bytes 331784 | tf_op jit(solution)/shard_map/ppermute | solution.py:359
  36.5 2.1 %collective-permute-start.18 = (bf16[9,16,384]{2,1,0:T(8,128)(2,1)S(1)}, bf16[9,16,384]{2,1,0:T(8,128)(2,1)S(1)}, u32[]{:S(2)}, u32[]{:S(2)}) collective-permute-start(bf16[9,16,384]{2,1,0:T(8,128)(2,1)S(1)} %shard_map.78.refs_0_), channel_id=1, source_target_pairs={{0,2},{1,3},{2,0},{3,1},{4,6},{5,7},{6,4},{7,5},{8,10},{9,11},{10,... | collective-permute-start | bytes 331784 | tf_op jit(solution)/shard_map/ppermute | solution.py:359
  38.6 0.6 %collective-permute-start.13 = (bf16[9,16,384]{2,1,0:T(8,128)(2,1)S(1)}, bf16[9,16,384]{2,1,0:T(8,128)(2,1)S(1)}, u32[]{:S(2)}, u32[]{:S(2)}) collective-permute-start(bf16[9,16,384]{2,1,0:T(8,128)(2,1)S(1)} %shard_map.78.refs_0_), channel_id=1, source_target_pairs={{0,8},{1,9},{2,10},{3,11},{4,12},{5,13},{6,14},{7,15},{8,0},{9,1},... | collective-permute-start | bytes 331784 | tf_op jit(solution)/shard_map/ppermute | solution.py:359
  39.2 2.0 %shard_map.79 = (bf16[2,4,16,256]{3,2,1,0:T(8,128)(2,1)}, bf16[2,8,32,128]{3,2,1,0:T(8,128)(2,1)}) custom-call(bf16[2,17,2,16,384]{4,3,2,1,0:T(8,128)(2,1)S(1)} %get-tuple-element.55.stacked_b, bf16[2,34,32,128]{3,2,1,0:T(8,128)(2,1)S(1)} %get-tuple-element.56.pre_grad, bf16[3,3,3,128,128]{4,3,2,1,0:T(8,128)(2,1)S(1)} %copy-done.1, ...), custom_call_target="tpu_custom_call" | custom-call | flops 10000000 | bytes 10000 | tf_op jit(solution)/shard_map/pallas_call | solution.py:338
  41.3 0.0 collective-permute-done.12.refs_3_
  41.3 0.0 collective-permute-done.18.refs_7_
  41.3 0.5 collective-permute-start.26
  41.8 3.4 %collective-permute-done.14.refs_2_ = bf16[9,16,384]{2,1,0:T(8,128)(2,1)S(1)} collective-permute-done((bf16[9,16,384]{2,1,0:T(8,128)(2,1)S(1)}, bf16[9,16,384]{2,1,0:T(8,128)(2,1)S(1)}, u32[]{:S(2)}, u32[]{:S(2)}) %collective-permute-start.14) | collective-permute-done | bytes 110624 | tf_op jit(solution)/shard_map/ppermute | solution.py:359
  45.2 0.0 collective-permute-start.16
  45.2 1.4 %collective-permute-done.13.refs_1_ = bf16[9,16,384]{2,1,0:T(8,128)(2,1)S(1)} collective-permute-done((bf16[9,16,384]{2,1,0:T(8,128)(2,1)S(1)}, bf16[9,16,384]{2,1,0:T(8,128)(2,1)S(1)}, u32[]{:S(2)}, u32[]{:S(2)}) %collective-permute-start.13) | collective-permute-done | bytes 110624 | tf_op jit(solution)/shard_map/ppermute | solution.py:359
  46.6 0.9 %collective-permute-start.15 = (bf16[9,16,384]{2,1,0:T(8,128)(2,1)S(1)}, bf16[9,16,384]{2,1,0:T(8,128)(2,1)S(1)}, u32[]{:S(2)}, u32[]{:S(2)}) collective-permute-start(bf16[9,16,384]{2,1,0:T(8,128)(2,1)S(1)} %collective-permute-done.13.refs_1_), channel_id=1, source_target_pairs={{0,2},{1,3},{2,0},{3,1},{4,6},{5,7},{6,4},{7,5},{8,10},{9,11},{10,... | collective-permute-start | bytes 331784 | tf_op jit(solution)/shard_map/ppermute | solution.py:359
  47.5 0.0 collective-permute-done.19.refs_8_
  47.5 1.1 %collective-permute-start.17 = (bf16[9,16,384]{2,1,0:T(8,128)(2,1)S(1)}, bf16[9,16,384]{2,1,0:T(8,128)(2,1)S(1)}, u32[]{:S(2)}, u32[]{:S(2)}) collective-permute-start(bf16[9,16,384]{2,1,0:T(8,128)(2,1)S(1)} %collective-permute-done.12.refs_3_), channel_id=1, source_target_pairs={{0,2},{1,3},{2,0},{3,1},{4,6},{5,7},{6,4},{7,5},{8,10},{9,11},{10,... | collective-permute-start | bytes 331784 | tf_op jit(solution)/shard_map/ppermute | solution.py:359
  48.6 0.5 collective-permute-start.20
  49.1 1.9 %collective-permute-done.16.refs_5_ = bf16[9,16,384]{2,1,0:T(8,128)(2,1)S(1)} collective-permute-done((bf16[9,16,384]{2,1,0:T(8,128)(2,1)S(1)}, bf16[9,16,384]{2,1,0:T(8,128)(2,1)S(1)}, u32[]{:S(2)}, u32[]{:S(2)}) %collective-permute-start.16) | collective-permute-done | bytes 110624 | tf_op jit(solution)/shard_map/ppermute | solution.py:359
  51.1 2.4 %collective-permute-done.15.refs_4_ = bf16[9,16,384]{2,1,0:T(8,128)(2,1)S(1)} collective-permute-done((bf16[9,16,384]{2,1,0:T(8,128)(2,1)S(1)}, bf16[9,16,384]{2,1,0:T(8,128)(2,1)S(1)}, u32[]{:S(2)}, u32[]{:S(2)}) %collective-permute-start.15) | collective-permute-done | bytes 110624 | tf_op jit(solution)/shard_map/ppermute | solution.py:359
  53.5 2.0 %collective-permute-done.17.refs_6_ = bf16[9,16,384]{2,1,0:T(8,128)(2,1)S(1)} collective-permute-done((bf16[9,16,384]{2,1,0:T(8,128)(2,1)S(1)}, bf16[9,16,384]{2,1,0:T(8,128)(2,1)S(1)}, u32[]{:S(2)}, u32[]{:S(2)}) %collective-permute-start.17) | collective-permute-done | bytes 110624 | tf_op jit(solution)/shard_map/ppermute | solution.py:359
  55.4 0.0 collective-permute-start.25
  55.4 0.0 collective-permute-done.20.refs_9_
  55.5 0.0 collective-permute-done.23.refs_12_
  55.5 1.3 %collective-permute-done.25.refs_14_ = bf16[9,16,384]{2,1,0:T(8,128)(2,1)S(1)} collective-permute-done((bf16[9,16,384]{2,1,0:T(8,128)(2,1)S(1)}, bf16[9,16,384]{2,1,0:T(8,128)(2,1)S(1)}, u32[]{:S(2)}, u32[]{:S(2)}) %collective-permute-start.25) | collective-permute-done | bytes 110624 | tf_op jit(solution)/shard_map/ppermute | solution.py:359
  56.8 1.8 %shard_map.80 = (bf16[3,9,128,128]{3,2,1,0:T(8,128)(2,1)}, bf16[3,9,128,256]{3,2,1,0:T(8,128)(2,1)}) custom-call(bf16[9,16,384]{2,1,0:T(8,128)(2,1)S(1)} %shard_map.78.refs_0_, bf16[9,16,384]{2,1,0:T(8,128)(2,1)S(1)} %collective-permute-done.13.refs_1_, bf16[9,16,384]{2,1,0:T(8,128)(2,1)S(1)} %collective-permute-done.14.refs_2_, ...), custom_call_target="tpu_custom_call" | custom-call | bytes 10000 | tf_op jit(solution)/shard_map/pallas_call | solution.py:338
  (21 shorter events, 0.1 us)
Async XLA Ops:
  0.6 12.2 %copy-start.3 = (bf16[2,4,16,256]{3,2,1,0:T(8,128)(2,1)S(1)}, bf16[2,4,16,256]{3,2,1,0:T(8,128)(2,1)}, u32[]{:S(2)}) copy-start(bf16[2,4,16,256]{3,2,1,0:T(8,128)(2,1)} %refs_1_.1) | copy-start | bytes 196612
  0.6 12.2 %copy-start.2 = (bf16[2,8,32,128]{3,2,1,0:T(8,128)(2,1)S(1)}, bf16[2,8,32,128]{3,2,1,0:T(8,128)(2,1)}, u32[]{:S(2)}) copy-start(bf16[2,8,32,128]{3,2,1,0:T(8,128)(2,1)} %refs_0_.1) | copy-start | bytes 393220
  0.7 12.2 %copy-start.1 = (bf16[3,3,3,128,128]{4,3,2,1,0:T(8,128)(2,1)S(1)}, bf16[3,3,3,128,128]{4,3,2,1,0:T(8,128)(2,1)}, u32[]{:S(2)}) copy-start(bf16[3,3,3,128,128]{4,3,2,1,0:T(8,128)(2,1)} %weight_a.1) | copy-start | bytes 2654212
  2.4 21.0 %copy-start = (bf16[3,3,3,128,256]{4,3,2,1,0:T(8,128)(2,1)S(1)}, bf16[3,3,3,128,256]{4,3,2,1,0:T(8,128)(2,1)}, u32[]{:S(2)}) copy-start(bf16[3,3,3,128,256]{4,3,2,1,0:T(8,128)(2,1)} %refs_3_.1) | copy-start | bytes 5308420
  2.5 3.1 %collective-permute-start.2 = (bf16[2,3,32,128]{3,2,1,0:T(8,128)(2,1)}, bf16[2,3,32,128]{3,2,1,0:T(8,128)(2,1)S(1)}, u32[]{:S(2)}, u32[]{:S(2)}) collective-permute-start(bf16[2,3,32,128]{3,2,1,0:T(8,128)(2,1)} %get-tuple-element.35), channel_id=1, source_target_pairs={{0,1},{1,0},{2,3},{3,2},{4,5},{5,4},{6,7},{7,6},{8,9},{9,8},{10,11... | collective-permute-start | bytes 147464 | tf_op jit(solution)/shard_map/ppermute | solution.py:359
  3.0 8.3 %collective-permute-start.1 = (bf16[2,12,32,128]{3,2,1,0:T(8,128)(2,1)}, bf16[2,12,32,128]{3,2,1,0:T(8,128)(2,1)S(1)}, u32[]{:S(2)}, u32[]{:S(2)}) collective-permute-start(bf16[2,12,32,128]{3,2,1,0:T(8,128)(2,1)} %get-tuple-element.34), channel_id=1, source_target_pairs={{0,2},{1,3},{2,0},{3,1},{4,6},{5,7},{6,4},{7,5},{8,10},{9,11},{10,... | collective-permute-start | bytes 589832 | tf_op jit(solution)/shard_map/ppermute | solution.py:359
  6.4 0.7 %collective-permute-start.3 = (bf16[2,3,32,128]{3,2,1,0:T(8,128)(2,1)S(1)}, bf16[2,3,32,128]{3,2,1,0:T(8,128)(2,1)S(1)}, u32[]{:S(2)}, u32[]{:S(2)}) collective-permute-start(bf16[2,3,32,128]{3,2,1,0:T(8,128)(2,1)S(1)} %broadcast_select_fusion), channel_id=1, source_target_pairs={{2,6},{3,4},{4,3},{5,1},{6,10},{7,8},{8,7},{9,5},{10,14},{11,12},{... | collective-permute-start | bytes 147464 | tf_op jit(solution)/shard_map/ppermute | solution.py:359
  7.0 5.8 %collective-permute-start = (bf16[2,12,32,128]{3,2,1,0:T(8,128)(2,1)}, bf16[2,12,32,128]{3,2,1,0:T(8,128)(2,1)S(1)}, u32[]{:S(2)}, u32[]{:S(2)}) collective-permute-start(bf16[2,12,32,128]{3,2,1,0:T(8,128)(2,1)} %get-tuple-element.34), channel_id=1, source_target_pairs={{0,1},{1,0},{2,3},{3,2},{4,5},{5,4},{6,7},{7,6},{8,9},{9,8},{10,11... | collective-permute-start | bytes 589832 | tf_op jit(solution)/shard_map/ppermute | solution.py:359
  11.3 1.5 %collective-permute-start.4 = (bf16[2,12,32,128]{3,2,1,0:T(8,128)(2,1)S(1)}, bf16[2,12,32,128]{3,2,1,0:T(8,128)(2,1)S(1)}, u32[]{:S(2)}, u32[]{:S(2)}) collective-permute-start(bf16[2,12,32,128]{3,2,1,0:T(8,128)(2,1)S(1)} %collective-permute-done.1.refs_3_), channel_id=1, source_target_pairs={{0,1},{1,0},{2,3},{3,2},{4,5},{5,4},{6,7},{7,6},{8,9},{9,8},{10,11... | collective-permute-start | bytes 589832 | tf_op jit(solution)/shard_map/ppermute | solution.py:359
  11.3 1.5 %collective-permute-start.5 = (bf16[2,3,32,128]{3,2,1,0:T(8,128)(2,1)S(1)}, bf16[2,3,32,128]{3,2,1,0:T(8,128)(2,1)S(1)}, u32[]{:S(2)}, u32[]{:S(2)}) collective-permute-start(bf16[2,3,32,128]{3,2,1,0:T(8,128)(2,1)S(1)} %collective-permute-done.3.refs_5_), channel_id=1, source_target_pairs={{0,1},{1,0},{2,3},{3,2},{4,5},{5,4},{6,7},{7,6},{8,9},{9,8},{10,11... | collective-permute-start | bytes 147464 | tf_op jit(solution)/shard_map/ppermute | solution.py:359
  16.2 10.4 %collective-permute-start.6 = (bf16[9,16,256]{2,1,0:T(8,128)(2,1)S(1)}, bf16[9,16,256]{2,1,0:T(8,128)(2,1)S(1)}, u32[]{:S(2)}, u32[]{:S(2)}) collective-permute-start(bf16[9,16,256]{2,1,0:T(8,128)(2,1)S(1)} %get-tuple-element.42), channel_id=1, source_target_pairs={{0,4},{1,5},{2,6},{3,7},{4,8},{5,9},{6,10},{7,11},{8,12},{9,13},{1... | collective-permute-start | bytes 221192 | tf_op jit(solution)/shard_map/ppermute | solution.py:359
  19.5 11.1 %collective-permute-start.10 = (bf16[9,16,256]{2,1,0:T(8,128)(2,1)S(1)}, bf16[9,16,256]{2,1,0:T(8,128)(2,1)S(1)}, u32[]{:S(2)}, u32[]{:S(2)}) collective-permute-start(bf16[9,16,256]{2,1,0:T(8,128)(2,1)S(1)} %get-tuple-element.51), channel_id=1, source_target_pairs={{0,8},{1,9},{2,10},{3,11},{4,12},{5,13},{6,14},{7,15},{8,0},{9,1},... | collective-permute-start | bytes 221192 | tf_op jit(solution)/shard_map/ppermute | solution.py:359
  22.1 8.5 %collective-permute-start.11 = (bf16[9,16,256]{2,1,0:T(8,128)(2,1)S(1)}, bf16[9,16,256]{2,1,0:T(8,128)(2,1)S(1)}, u32[]{:S(2)}, u32[]{:S(2)}) collective-permute-start(bf16[9,16,256]{2,1,0:T(8,128)(2,1)S(1)} %get-tuple-element.52), channel_id=1, source_target_pairs={{0,12},{1,13},{2,14},{3,15},{4,0},{5,1},{6,2},{7,3},{8,4},{9,5},{1... | collective-permute-start | bytes 221192 | tf_op jit(solution)/shard_map/ppermute | solution.py:359
  26.7 5.9 %collective-permute-start.7 = (bf16[9,16,128]{2,1,0:T(8,128)(2,1)S(1)}, bf16[9,16,128]{2,1,0:T(8,128)(2,1)S(1)}, u32[]{:S(2)}, u32[]{:S(2)}) collective-permute-start(bf16[9,16,128]{2,1,0:T(8,128)(2,1)S(1)} %get-tuple-element.46), channel_id=1, source_target_pairs={{0,4},{1,5},{2,6},{3,7},{4,8},{5,9},{6,10},{7,11},{8,12},{9,13},{1... | collective-permute-start | bytes 110600 | tf_op jit(solution)/shard_map/ppermute | solution.py:359
  27.4 5.9 %collective-permute-start.8 = (bf16[9,16,128]{2,1,0:T(8,128)(2,1)S(1)}, bf16[9,16,128]{2,1,0:T(8,128)(2,1)S(1)}, u32[]{:S(2)}, u32[]{:S(2)}) collective-permute-start(bf16[9,16,128]{2,1,0:T(8,128)(2,1)S(1)} %get-tuple-element.47), channel_id=1, source_target_pairs={{0,8},{1,9},{2,10},{3,11},{4,12},{5,13},{6,14},{7,15},{8,0},{9,1},... | collective-permute-start | bytes 110600 | tf_op jit(solution)/shard_map/ppermute | solution.py:359
  27.8 5.6 %collective-permute-start.9 = (bf16[9,16,128]{2,1,0:T(8,128)(2,1)S(1)}, bf16[9,16,128]{2,1,0:T(8,128)(2,1)S(1)}, u32[]{:S(2)}, u32[]{:S(2)}) collective-permute-start(bf16[9,16,128]{2,1,0:T(8,128)(2,1)S(1)} %get-tuple-element.48), channel_id=1, source_target_pairs={{0,12},{1,13},{2,14},{3,15},{4,0},{5,1},{6,2},{7,3},{8,4},{9,5},{1... | collective-permute-start | bytes 110600 | tf_op jit(solution)/shard_map/ppermute | solution.py:359
  33.4 7.9 %collective-permute-start.12 = (bf16[9,16,384]{2,1,0:T(8,128)(2,1)S(1)}, bf16[9,16,384]{2,1,0:T(8,128)(2,1)S(1)}, u32[]{:S(2)}, u32[]{:S(2)}) collective-permute-start(bf16[9,16,384]{2,1,0:T(8,128)(2,1)S(1)} %shard_map.78.refs_0_), channel_id=1, source_target_pairs={{0,12},{1,13},{2,14},{3,15},{4,0},{5,1},{6,2},{7,3},{8,4},{9,5},{1... | collective-permute-start | bytes 331784 | tf_op jit(solution)/shard_map/ppermute | solution.py:359
  36.5 4.9 %collective-permute-start.18 = (bf16[9,16,384]{2,1,0:T(8,128)(2,1)S(1)}, bf16[9,16,384]{2,1,0:T(8,128)(2,1)S(1)}, u32[]{:S(2)}, u32[]{:S(2)}) collective-permute-start(bf16[9,16,384]{2,1,0:T(8,128)(2,1)S(1)} %shard_map.78.refs_0_), channel_id=1, source_target_pairs={{0,2},{1,3},{2,0},{3,1},{4,6},{5,7},{6,4},{7,5},{8,10},{9,11},{10,... | collective-permute-start | bytes 331784 | tf_op jit(solution)/shard_map/ppermute | solution.py:359
  38.6 6.6 %collective-permute-start.14 = (bf16[9,16,384]{2,1,0:T(8,128)(2,1)S(1)}, bf16[9,16,384]{2,1,0:T(8,128)(2,1)S(1)}, u32[]{:S(2)}, u32[]{:S(2)}) collective-permute-start(bf16[9,16,384]{2,1,0:T(8,128)(2,1)S(1)} %shard_map.78.refs_0_), channel_id=1, source_target_pairs={{0,4},{1,5},{2,6},{3,7},{4,8},{5,9},{6,10},{7,11},{8,12},{9,13},{1... | collective-permute-start | bytes 331784 | tf_op jit(solution)/shard_map/ppermute | solution.py:359
  38.6 8.0 %collective-permute-start.13 = (bf16[9,16,384]{2,1,0:T(8,128)(2,1)S(1)}, bf16[9,16,384]{2,1,0:T(8,128)(2,1)S(1)}, u32[]{:S(2)}, u32[]{:S(2)}) collective-permute-start(bf16[9,16,384]{2,1,0:T(8,128)(2,1)S(1)} %shard_map.78.refs_0_), channel_id=1, source_target_pairs={{0,8},{1,9},{2,10},{3,11},{4,12},{5,13},{6,14},{7,15},{8,0},{9,1},... | collective-permute-start | bytes 331784 | tf_op jit(solution)/shard_map/ppermute | solution.py:359
  39.2 8.3 %collective-permute-start.19 = (bf16[9,16,384]{2,1,0:T(8,128)(2,1)S(1)}, bf16[9,16,384]{2,1,0:T(8,128)(2,1)S(1)}, u32[]{:S(2)}, u32[]{:S(2)}) collective-permute-start(bf16[9,16,384]{2,1,0:T(8,128)(2,1)S(1)} %shard_map.78.refs_0_), channel_id=1, source_target_pairs={{0,1},{1,0},{2,3},{3,2},{4,5},{5,4},{6,7},{7,6},{8,9},{9,8},{10,11... | collective-permute-start | bytes 331784 | tf_op jit(solution)/shard_map/ppermute | solution.py:359
  41.3 7.3 %collective-permute-start.26 = (bf16[9,16,384]{2,1,0:T(8,128)(2,1)S(1)}, bf16[9,16,384]{2,1,0:T(8,128)(2,1)S(1)}, u32[]{:S(2)}, u32[]{:S(2)}) collective-permute-start(bf16[9,16,384]{2,1,0:T(8,128)(2,1)S(1)} %collective-permute-done.18.refs_7_), channel_id=1, source_target_pairs={{0,1},{1,0},{2,3},{3,2},{4,5},{5,4},{6,7},{7,6},{8,9},{9,8},{10,11... | collective-permute-start | bytes 331784 | tf_op jit(solution)/shard_map/ppermute | solution.py:359
  45.2 3.4 %collective-permute-start.21 = (bf16[9,16,384]{2,1,0:T(8,128)(2,1)S(1)}, bf16[9,16,384]{2,1,0:T(8,128)(2,1)S(1)}, u32[]{:S(2)}, u32[]{:S(2)}) collective-permute-start(bf16[9,16,384]{2,1,0:T(8,128)(2,1)S(1)} %collective-permute-done.14.refs_2_), channel_id=1, source_target_pairs={{0,1},{1,0},{2,3},{3,2},{4,5},{5,4},{6,7},{7,6},{8,9},{9,8},{10,11... | collective-permute-start | bytes 331784 | tf_op jit(solution)/shard_map/ppermute | solution.py:359
  45.2 5.9 %collective-permute-start.16 = (bf16[9,16,384]{2,1,0:T(8,128)(2,1)S(1)}, bf16[9,16,384]{2,1,0:T(8,128)(2,1)S(1)}, u32[]{:S(2)}, u32[]{:S(2)}) collective-permute-start(bf16[9,16,384]{2,1,0:T(8,128)(2,1)S(1)} %collective-permute-done.14.refs_2_), channel_id=1, source_target_pairs={{0,2},{1,3},{2,0},{3,1},{4,6},{5,7},{6,4},{7,5},{8,10},{9,11},{10,... | collective-permute-start | bytes 331784 | tf_op jit(solution)/shard_map/ppermute | solution.py:359
  46.6 6.9 %collective-permute-start.15 = (bf16[9,16,384]{2,1,0:T(8,128)(2,1)S(1)}, bf16[9,16,384]{2,1,0:T(8,128)(2,1)S(1)}, u32[]{:S(2)}, u32[]{:S(2)}) collective-permute-start(bf16[9,16,384]{2,1,0:T(8,128)(2,1)S(1)} %collective-permute-done.13.refs_1_), channel_id=1, source_target_pairs={{0,2},{1,3},{2,0},{3,1},{4,6},{5,7},{6,4},{7,5},{8,10},{9,11},{10,... | collective-permute-start | bytes 331784 | tf_op jit(solution)/shard_map/ppermute | solution.py:359
  47.5 7.9 %collective-permute-start.17 = (bf16[9,16,384]{2,1,0:T(8,128)(2,1)S(1)}, bf16[9,16,384]{2,1,0:T(8,128)(2,1)S(1)}, u32[]{:S(2)}, u32[]{:S(2)}) collective-permute-start(bf16[9,16,384]{2,1,0:T(8,128)(2,1)S(1)} %collective-permute-done.12.refs_3_), channel_id=1, source_target_pairs={{0,2},{1,3},{2,0},{3,1},{4,6},{5,7},{6,4},{7,5},{8,10},{9,11},{10,... | collective-permute-start | bytes 331784 | tf_op jit(solution)/shard_map/ppermute | solution.py:359
  48.6 6.8 %collective-permute-start.22 = (bf16[9,16,384]{2,1,0:T(8,128)(2,1)S(1)}, bf16[9,16,384]{2,1,0:T(8,128)(2,1)S(1)}, u32[]{:S(2)}, u32[]{:S(2)}) collective-permute-start(bf16[9,16,384]{2,1,0:T(8,128)(2,1)S(1)} %collective-permute-done.12.refs_3_), channel_id=1, source_target_pairs={{0,1},{1,0},{2,3},{3,2},{4,5},{5,4},{6,7},{7,6},{8,9},{9,8},{10,11... | collective-permute-start | bytes 331784 | tf_op jit(solution)/shard_map/ppermute | solution.py:359
  48.6 6.8 %collective-permute-start.20 = (bf16[9,16,384]{2,1,0:T(8,128)(2,1)S(1)}, bf16[9,16,384]{2,1,0:T(8,128)(2,1)S(1)}, u32[]{:S(2)}, u32[]{:S(2)}) collective-permute-start(bf16[9,16,384]{2,1,0:T(8,128)(2,1)S(1)} %collective-permute-done.13.refs_1_), channel_id=1, source_target_pairs={{0,1},{1,0},{2,3},{3,2},{4,5},{5,4},{6,7},{7,6},{8,9},{9,8},{10,11... | collective-permute-start | bytes 331784 | tf_op jit(solution)/shard_map/ppermute | solution.py:359
  51.1 4.4 %collective-permute-start.24 = (bf16[9,16,384]{2,1,0:T(8,128)(2,1)S(1)}, bf16[9,16,384]{2,1,0:T(8,128)(2,1)S(1)}, u32[]{:S(2)}, u32[]{:S(2)}) collective-permute-start(bf16[9,16,384]{2,1,0:T(8,128)(2,1)S(1)} %collective-permute-done.16.refs_5_), channel_id=1, source_target_pairs={{0,1},{1,0},{2,3},{3,2},{4,5},{5,4},{6,7},{7,6},{8,9},{9,8},{10,11... | collective-permute-start | bytes 331784 | tf_op jit(solution)/shard_map/ppermute | solution.py:359
  53.5 2.0 %collective-permute-start.23 = (bf16[9,16,384]{2,1,0:T(8,128)(2,1)S(1)}, bf16[9,16,384]{2,1,0:T(8,128)(2,1)S(1)}, u32[]{:S(2)}, u32[]{:S(2)}) collective-permute-start(bf16[9,16,384]{2,1,0:T(8,128)(2,1)S(1)} %collective-permute-done.15.refs_4_), channel_id=1, source_target_pairs={{0,1},{1,0},{2,3},{3,2},{4,5},{5,4},{6,7},{7,6},{8,9},{9,8},{10,11... | collective-permute-start | bytes 331784 | tf_op jit(solution)/shard_map/ppermute | solution.py:359
  55.4 1.3 %collective-permute-start.25 = (bf16[9,16,384]{2,1,0:T(8,128)(2,1)S(1)}, bf16[9,16,384]{2,1,0:T(8,128)(2,1)S(1)}, u32[]{:S(2)}, u32[]{:S(2)}) collective-permute-start(bf16[9,16,384]{2,1,0:T(8,128)(2,1)S(1)} %collective-permute-done.17.refs_6_), channel_id=1, source_target_pairs={{0,1},{1,0},{2,3},{3,2},{4,5},{5,4},{6,7},{7,6},{8,9},{9,8},{10,11... | collective-permute-start | bytes 331784 | tf_op jit(solution)/shard_map/ppermute | solution.py:359

commit v5 on v4

--- a/solution.py
+++ b/solution.py
@@ -24,7 +24,8 @@
     for step, out in enumerate(outs):
         owner = (plane + step) % count if count > 1 else 0
         at = pl.multiple_of(side * part + owner * rows, rows)
-        out[...] = total[:, pl.ds(at, rows)].astype(out.dtype)
+        value = total[:, pl.ds(at, rows)].astype(out.dtype)
+        out[:, :, 0 : value.shape[-1]] = value
 
 
 def mm(a, b):
@@ -171,7 +172,10 @@
     emit(total_b, pieces)
 
 
-def backward_kernel(last, cot_ref, pre_ref, stacked_a, weight_b, *refs):
+def backward_kernel(last, join, cot_ref, pre_ref, stacked_a, weight_b, *refs):
+    if join:
+        refs[1 + join][:, :, weight_b.shape[3] :] = refs[0][...]
+        refs = refs[1:]
     pieces, (pre_grad, total_a) = (refs[:-2], refs[-2:])
     core, side, plane = position()
     frames, ext_g, half, wide = cot_ref.shape
@@ -303,18 +307,20 @@
     frames_grad[...] = flat[...].reshape(frames_grad.shape).astype(BF16)
 
 
-def finish_kernel(scale, *refs):
-    half = len(refs) // 2
+def finish_kernel(scale, count, *refs):
     chans = refs[0].shape[-1]
-
-    def total(parts):
+    shared, out = (refs[2 * count : -1], refs[-1])
+
+    def total(parts, lanes):
         value = parts[0][...].astype(F32)
         for part in parts[1:]:
             value = value + part[...].astype(F32)
+        for part in shared:
+            value = value + part[:, :, lanes].astype(F32)
         return (value * scale).astype(BF16)
 
-    refs[-1][:, :, 0:chans] = total(refs[:half])
-    refs[-1][:, :, chans:] = total(refs[half:-1])
+    out[:, :, 0:chans] = total(refs[:count], slice(0, chans))
+    out[:, :, chans:] = total(refs[count : 2 * count], slice(chans, None))
 
 
 def assemble_kernel(places, planes, *refs):
@@ -331,16 +337,52 @@
             out_b[slot, :, pl.ds(at, rows)] = piece[:, :, chans:]
 
 
-def call(body, outs, args, scratch=(), flops=0, whole=False, limit=VMEM_LIMIT):
+def append_kernel(places, planes, old_a, old_b, *refs):
+    del old_a, old_b
+    count = len(places)
+    pieces, (out_a, out_b, sems) = (refs[:count], refs[count:])
+    core, side, plane = position()
+    chans = out_a.shape[-1]
+    rows = pieces[0].shape[1]
+
+    def each(act):
+        for index, (flip_core, flip_side, step) in enumerate(places):
+            tap = core ^ flip_core
+            source = (plane - step + planes) % planes
+            at = pl.multiple_of((side ^ flip_side) * (chans // 2) + source * rows, rows)
+            for k, out in enumerate((out_a, out_b)):
+                lanes = slice(0, chans) if k == 0 else slice(chans, None)
+                piece = pieces[index].at[:, :, lanes]
+                move = pltpu.make_async_copy(
+                    piece, out.at[tap * 2, :, pl.ds(at, rows)], sems.at[index, k]
+                )
+                twin = pltpu.make_async_copy(
+                    piece, out.at[1, :, pl.ds(at, rows)], sems.at[index, 2 + k]
+                )
+                act(move)
+                pl.when(tap == 0)(lambda twin=twin: act(twin))
+
+    each(lambda copy: copy.start())
+    each(lambda copy: copy.wait())
+
+
+def call(
+    body, outs, args, scratch=(), flops=0, whole=0, limit=VMEM_LIMIT, aliases=None, size=10**4
+):
     extra = {}
     if whole:
-        extra["in_specs"] = [pl.BlockSpec(memory_space=pl.ANY)] * len(args)
+        held = pl.BlockSpec(memory_space=pl.ANY)
+        inside = pl.BlockSpec(memory_space=pltpu.VMEM)
+        extra["in_specs"] = [held] * whole + [inside] * (len(args) - whole)
+    if aliases:
+        extra["out_specs"] = (held,) * len(outs)
+        extra["input_output_aliases"] = aliases
     return pl.pallas_call(
         body,
         out_shape=outs,
         scratch_shapes=scratch,
         compiler_params=pltpu.CompilerParams(vmem_limit_bytes=limit),
-        cost_estimate=pl.CostEstimate(flops=flops, bytes_accessed=10**4, transcendentals=0),
+        cost_estimate=pl.CostEstimate(flops=flops, bytes_accessed=size, transcendentals=0),
         **extra,
     )(*args)
 
@@ -372,7 +414,7 @@
         ),
         (frames, cotangent),
         [pltpu.SemaphoreType.DMA((6,))],
-        whole=True,
+        whole=2,
         limit=None,
         flops=4 * 10**9,
     )
@@ -397,8 +439,10 @@
     def forward(*refs):
         forward_kernel(split, *refs)
 
+    join = split // 2 if split > 2 else 0
+
     def backward(*refs):
-        backward_kernel(planes - 1, *refs)
+        backward_kernel(planes - 1, join, *refs)
 
     *pieces_b, pre, stacked_a, stacked_b, cot = call(
         forward,
@@ -416,10 +460,15 @@
         ],
         flops=10**7,
     )
+    shapes_a = list(pieces_of(chans))
+    joined = ()
+    if join:
+        shapes_a[join] = shape((9, part // split, chans + wide), BF16)
+        joined = (pieces_b[join],)
     *pieces_a, pre_grad = call(
         backward,
-        pieces_of(chans) + (shape((count, inner, width, chans), BF16),),
-        (cot, pre, stacked_a, staged_b),
+        (*shapes_a, shape((count, inner, width, chans), BF16)),
+        (cot, pre, stacked_a, staged_b, *joined),
         [pltpu.VMEM((9, chans, chans), F32)],
         flops=10**7,
     )
@@ -446,39 +495,68 @@
         return (encoded, frames_grad, both[0], both[1])
 
     rotations = [[(i, (i + 4 * step) % n) for i in range(n)] for step in range(planes)]
-    got_b = [send(pieces_b[step], rotations[step]) for step in range(1, planes)]
-    gate = lax.optimization_barrier((*got_b[:1], *pieces_a[1:]))
-    got_b[:1] = gate[:1]
-    pieces_a[1:] = gate[1:]
-    got_a = [send(pieces_a[step], rotations[step]) for step in range(1, planes)]
+    close = [step for step in range(1, planes) if step != join]
+    got_b = [send(pieces_b[step], rotations[step]) for step in close]
+    if join:
+        gate = lax.optimization_barrier((*got_b, pieces_a[close[-1]]))
+        *got_b, pieces_a[close[-1]] = gate
+    got_a = [send(pieces_a[step], rotations[step]) for step in close]
+    both = [send(pieces_a[join], rotations[join])] if join else []
 
     def finish(*refs):
-        finish_kernel(scale, *refs)
-
+        finish_kernel(scale, 1 + len(close), *refs)
+
+    encoded, frames_grad = outputs(stacked_b)
+    held = lax.optimization_barrier((pieces_a[0], encoded, frames_grad))
+    pieces_a[0], encoded, frames_grad = held
     piece = shape((9, part // planes, chans + wide), BF16)
-    (own,) = call(finish, (piece,), (pieces_a[0], *got_a, pieces_b[0], *got_b))
-    own, stacked_b = lax.optimization_barrier((own, stacked_b))
+    (own,) = call(finish, (piece,), (pieces_a[0], *got_a, pieces_b[0], *got_b, *both))
     column = {(0, 0, 0): own}
-    order = sorted(range(1, planes), key=lambda step: -min(step, planes - step))
-    for step in order:
+    order = sorted(range(1, planes), key=lambda step: min(step, planes - step))
+    for step in order[:-1]:
         column[0, 0, step] = send(own, rotations[step])
-    first = (0, 0, order[-1] if order else 0)
-    encoded, frames_grad = outputs(stacked_b)
-    held = lax.optimization_barrier((column[first], encoded, frames_grad))
-    column[first], encoded, frames_grad = held
-    for step in (*order, 0):
-        column[0, 1, step] = send(column[0, 0, step], swap_side)
+    if planes == 1:
+        column[0, 1, 0] = send(own, swap_side)
+    else:
+        far = (0, 0, order[-1])
+        column[far] = send(own, rotations[order[-1]])
+        for step in (0, *order[:-1]):
+            column[0, 1, step] = send(column[0, 0, step], swap_side)
+        if len(order) > 1:
+            key = (0, 1, order[0])
+            column[far], column[key] = lax.optimization_barrier((column[far], column[key]))
+        column[0, 1, far[2]] = send(column[far], swap_side)
+    last = (0, 1, order[-1] if order else 0)
     for (_, flip, step), value in list(column.items()):
-        column[1, flip, step] = send(value, swap_core)
+        if (0, flip, step) != last:
+            column[1, flip, step] = send(value, swap_core)
+    slow = column.pop(last)
+    tail = {key: column.pop(key) for key in list(column) if key[1] and key[2]}
     places = tuple(column)
 
     def assemble(*refs):
         assemble_kernel(places, planes, *refs)
 
-    grad_a, grad_b = call(
+    grads = call(
         assemble,
         (shape((3, 9, chans, chans), BF16), shape((3, 9, chans, wide), BF16)),
         tuple(column.values()),
+    )
+    slow, *grads = lax.optimization_barrier((slow, *grads))
+    tail[last] = slow
+    tail[1, *last[1:]] = send(slow, swap_core)
+    ends = tuple(tail)
+
+    def append(*refs):
+        append_kernel(ends, planes, *refs)
+
+    grad_a, grad_b = call(
+        append,
+        tuple(shape(x.shape, x.dtype) for x in grads),
+        (*grads, *tail.values()),
+        [pltpu.SemaphoreType.DMA((len(ends), 4))],
+        whole=2,
+        aliases={0: 0, 1: 1},
     )
     return (encoded, frames_grad, grad_a.reshape(weight_a.shape), grad_b.reshape(weight_b.shape))
 

time: 58.8 us -> 55.7 us (0.947)
  waiting for transfers between devices: 20.4 us -> 16.4 us
  Pallas kernels: 12.4 us -> 13.4 us
    ppermute x27 -> x26, waiting for transfers between devices: 20.4 us -> 16.4 us  [send(): return lax.ppermute(value, AXIS, pairs)]
    pallas_call x6 -> x7, Pallas kernels: 12.4 us -> 13.4 us  [call(): pl.pallas_call(body, out_shape=outs, scratch_shapes=scratch, compiler_par...]
    ppermute x27 -> x26, starting transfers between devices: 24.3 us -> 24.2 us  [send(): return lax.ppermute(value, AXIS, pairs)]
  transfers between devices with their start and end apart: 27 -> 26, of which waited for: 10 -> 9; matrix products, arithmetic and copies ran while one was open for 1% -> 1% of each run, Pallas kernels for 9% -> 13%
where the time goes in v5:
time: 55.7 us; the launch traced here: 55.5 us
  starting transfers between devices  24.2 us (43%)
  waiting for transfers between devices  16.4 us (29%)
  Pallas kernels  13.4 us (24%)
  other arithmetic  0.81 us (1%)
  between operations  0.75 us (1%)
    ppermute x26, starting transfers between devices, send(): return lax.ppermute(value, AXIS, pairs)  24.2 us
    ppermute x26, waiting for transfers between devices, send(): return lax.ppermute(value, AXIS, pairs)  16.4 us
    pallas_call x7, Pallas kernels, call(): pl.pallas_call(body, out_shape=outs, scratch_shapes=scratch, compiler_par...  13.4 us
  transfers between devices with their start and end apart: 26, of which 9 were waited for; matrix products, arithmetic and copies ran while one was open for 1% of the time, Pallas kernels for 13%

profile of v5, /device:TPU:0, one launch (start us, length us, event | category | flops | bytes accessed | tf_op | source)
XLA Modules:
  0.0 55.5 jit_solution(10142931109402251408)
XLA Ops:
  0.7 1.8 %shard_map.75 = (bf16[2,12,32,128]{3,2,1,0:T(8,128)(2,1)}, bf16[2,3,32,128]{3,2,1,0:T(8,128)(2,1)}) custom-call(bf16[2,8,32,128]{3,2,1,0:T(8,128)(2,1)} %refs_0_.1, bf16[2,4,16,256]{3,2,1,0:T(8,128)(2,1)} %refs_1_.1), custom_call_target="tpu_custom_call" | custom-call | flops 4000000000 | bytes 10000 | tf_op jit(solution)/shard_map/pallas_call | solution.py:380
  2.4 0.0 copy-start
  2.5 0.5 collective-permute-start.2
  3.0 2.6 %collective-permute-start.1 = (bf16[2,12,32,128]{3,2,1,0:T(8,128)(2,1)}, bf16[2,12,32,128]{3,2,1,0:T(8,128)(2,1)S(1)}, u32[]{:S(2)}, u32[]{:S(2)}) collective-permute-start(bf16[2,12,32,128]{3,2,1,0:T(8,128)(2,1)} %get-tuple-element.38), channel_id=1, source_target_pairs={{0,2},{1,3},{2,0},{3,1},{4,6},{5,7},{6,4},{7,5},{8,10},{9,11},{10,... | collective-permute-start | bytes 589832 | tf_op jit(solution)/shard_map/ppermute | solution.py:401
  5.6 0.0 collective-permute-done.2
  5.6 0.8 %broadcast_select_fusion = bf16[2,3,32,128]{3,2,1,0:T(8,128)(2,1)S(1)} fusion(bf16[2,3,32,128]{3,2,1,0:T(8,128)(2,1)} %get-tuple-element.39, bf16[2,3,32,128]{3,2,1,0:T(8,128)(2,1)S(1)} %collective-permute-done.2, pred[]{:T(512)S(6)} %eq.6), kind=kLoop, calls=%fused_computation | loop fusion | flops 24576 | bytes 147457 | tf_op jit(solution)/shard_map/jit(_where)/select_n | solution.py:421
  6.4 0.7 %collective-permute-start.3 = (bf16[2,3,32,128]{3,2,1,0:T(8,128)(2,1)S(1)}, bf16[2,3,32,128]{3,2,1,0:T(8,128)(2,1)S(1)}, u32[]{:S(2)}, u32[]{:S(2)}) collective-permute-start(bf16[2,3,32,128]{3,2,1,0:T(8,128)(2,1)S(1)} %broadcast_select_fusion), channel_id=1, source_target_pairs={{2,6},{3,4},{4,3},{5,1},{6,10},{7,8},{8,7},{9,5},{10,14},{11,12},{... | collective-permute-start | bytes 147464 | tf_op jit(solution)/shard_map/ppermute | solution.py:401
  7.0 0.1 collective-permute-start
  7.1 0.0 collective-permute-done.3.refs_5_
  7.1 4.1 %collective-permute-done.1.refs_3_ = bf16[2,12,32,128]{3,2,1,0:T(8,128)(2,1)S(1)} collective-permute-done((bf16[2,12,32,128]{3,2,1,0:T(8,128)(2,1)}, bf16[2,12,32,128]{3,2,1,0:T(8,128)(2,1)S(1)}, u32[]{:S(2)}, u32[]{:S(2)}) %collective-permute-start.1) | collective-permute-done | bytes 196640 | tf_op jit(solution)/shard_map/ppermute | solution.py:401
  11.3 0.0 collective-permute-start.4
  11.3 0.5 collective-permute-start.5
  11.8 1.0 %collective-permute-done.5.refs_6_ = bf16[2,3,32,128]{3,2,1,0:T(8,128)(2,1)S(1)} collective-permute-done((bf16[2,3,32,128]{3,2,1,0:T(8,128)(2,1)S(1)}, bf16[2,3,32,128]{3,2,1,0:T(8,128)(2,1)S(1)}, u32[]{:S(2)}, u32[]{:S(2)}) %collective-permute-start.5) | collective-permute-done | bytes 49184 | tf_op jit(solution)/shard_map/ppermute | solution.py:401
  12.8 3.4 %shard_map.76 = (f32[9,16,256]{2,1,0:T(8,128)S(1)}, bf16[9,16,256]{2,1,0:T(8,128)(2,1)S(1)}, bf16[9,16,256]{2,1,0:T(8,128)(2,1)S(1)}, bf16[9,16,256]{2,1,0:T(8,1...) custom-call(bf16[2,8,32,128]{3,2,1,0:T(8,128)(2,1)S(1)} %copy-done.2, ...), custom_call_target="tpu_custom_call" | custom-call | flops 10000000 | bytes 10000 | tf_op jit(solution)/shard_map/pallas_call | solution.py:380
  16.2 3.3 %collective-permute-start.7 = (bf16[9,16,256]{2,1,0:T(8,128)(2,1)S(1)}, bf16[9,16,256]{2,1,0:T(8,128)(2,1)S(1)}, u32[]{:S(2)}, u32[]{:S(2)}) collective-permute-start(bf16[9,16,256]{2,1,0:T(8,128)(2,1)S(1)} %get-tuple-element.55), channel_id=1, source_target_pairs={{0,4},{1,5},{2,6},{3,7},{4,8},{5,9},{6,10},{7,11},{8,12},{9,13},{1... | collective-permute-start | bytes 221192 | tf_op jit(solution)/shard_map/ppermute | solution.py:401
  19.5 2.1 %collective-permute-start.8 = (bf16[9,16,256]{2,1,0:T(8,128)(2,1)S(1)}, bf16[9,16,256]{2,1,0:T(8,128)(2,1)S(1)}, u32[]{:S(2)}, u32[]{:S(2)}) collective-permute-start(bf16[9,16,256]{2,1,0:T(8,128)(2,1)S(1)} %get-tuple-element.56), channel_id=1, source_target_pairs={{0,12},{1,13},{2,14},{3,15},{4,0},{5,1},{6,2},{7,3},{8,4},{9,5},{1... | collective-permute-start | bytes 221192 | tf_op jit(solution)/shard_map/ppermute | solution.py:401
  21.6 3.2 %shard_map.77 = (f32[9,16,128]{2,1,0:T(8,128)S(1)}, bf16[9,16,128]{2,1,0:T(8,128)(2,1)S(1)}, bf16[9,16,384]{2,1,0:T(8,128)(2,1)S(1)}, bf16[9,16,128]{2,1,0:T(8,128)(2,1)S(1)}, bf16[2,34,32,128]{3,2,1,0:T(8,128)(2,1)S(1)}) custom-call(bf16[2,18,16,256]{3,2,1,0:T(8,128)(2,1)S(1)} %get-tuple-element.42.refs_0_, ...), custom_call_target="tpu_custom_call" | custom-call | flops 10000000 | bytes 10000 | tf_op jit(solution)/shard_map/pallas_call | solution.py:380
  24.8 1.0 %collective-permute-start.10 = (bf16[9,16,384]{2,1,0:T(8,128)(2,1)S(1)}, bf16[9,16,384]{2,1,0:T(8,128)(2,1)S(1)}, u32[]{:S(2)}, u32[]{:S(2)}) collective-permute-start(bf16[9,16,384]{2,1,0:T(8,128)(2,1)S(1)} %get-tuple-element.62), channel_id=1, source_target_pairs={{0,8},{1,9},{2,10},{3,11},{4,12},{5,13},{6,14},{7,15},{8,0},{9,1},... | collective-permute-start | bytes 331784 | tf_op jit(solution)/shard_map/ppermute | solution.py:401
  25.8 1.6 %collective-permute-start.6 = (bf16[9,16,128]{2,1,0:T(8,128)(2,1)S(1)}, bf16[9,16,128]{2,1,0:T(8,128)(2,1)S(1)}, u32[]{:S(2)}, u32[]{:S(2)}) collective-permute-start(bf16[9,16,128]{2,1,0:T(8,128)(2,1)S(1)} %get-tuple-element.54), channel_id=1, source_target_pairs={{0,4},{1,5},{2,6},{3,7},{4,8},{5,9},{6,10},{7,11},{8,12},{9,13},{1... | collective-permute-start | bytes 110600 | tf_op jit(solution)/shard_map/ppermute | solution.py:401
  27.4 0.0 collective-permute-done.7.refs_4_
  27.4 0.0 collective-permute-done.8.refs_5_
  27.4 2.2 %collective-permute-start.9 = (bf16[9,16,128]{2,1,0:T(8,128)(2,1)S(1)}, bf16[9,16,128]{2,1,0:T(8,128)(2,1)S(1)}, u32[]{:S(2)}, u32[]{:S(2)}) collective-permute-start(bf16[9,16,128]{2,1,0:T(8,128)(2,1)S(1)} %get-tuple-element.58), channel_id=1, source_target_pairs={{0,12},{1,13},{2,14},{3,15},{4,0},{5,1},{6,2},{7,3},{8,4},{9,5},{1... | collective-permute-start | bytes 110600 | tf_op jit(solution)/shard_map/ppermute | solution.py:401
  29.7 2.0 %shard_map.78 = (bf16[2,4,16,256]{3,2,1,0:T(8,128)(2,1)}, bf16[2,8,32,128]{3,2,1,0:T(8,128)(2,1)}) custom-call(bf16[2,17,2,16,384]{4,3,2,1,0:T(8,128)(2,1)S(1)} %get-tuple-element.47.stacked_b, bf16[2,34,32,128]{3,2,1,0:T(8,128)(2,1)S(1)} %get-tuple-element.48.pre_grad, bf16[3,3,3,128,128]{4,3,2,1,0:T(8,128)(2,1)S(1)} %copy-done.1, ...), custom_call_target="tpu_custom_call" | custom-call | flops 10000000 | bytes 10000 | tf_op jit(solution)/shard_map/pallas_call | solution.py:380
  31.7 0.1 collective-permute-done.6.refs_1_
  31.8 1.3 %collective-permute-done.10.refs_6_ = bf16[9,16,384]{2,1,0:T(8,128)(2,1)S(1)} collective-permute-done((bf16[9,16,384]{2,1,0:T(8,128)(2,1)S(1)}, bf16[9,16,384]{2,1,0:T(8,128)(2,1)S(1)}, u32[]{:S(2)}, u32[]{:S(2)}) %collective-permute-start.10) | collective-permute-done | bytes 110624 | tf_op jit(solution)/shard_map/ppermute | solution.py:401
  33.1 0.3 collective-permute-done.9.refs_2_
  33.4 0.1 shard_map.79.refs_0_
  33.4 1.1 %collective-permute-start.12 = (bf16[9,16,384]{2,1,0:T(8,128)(2,1)S(1)}, bf16[9,16,384]{2,1,0:T(8,128)(2,1)S(1)}, u32[]{:S(2)}, u32[]{:S(2)}) collective-permute-start(bf16[9,16,384]{2,1,0:T(8,128)(2,1)S(1)} %shard_map.79.refs_0_), channel_id=1, source_target_pairs={{0,4},{1,5},{2,6},{3,7},{4,8},{5,9},{6,10},{7,11},{8,12},{9,13},{1... | collective-permute-start | bytes 331784 | tf_op jit(solution)/shard_map/ppermute | solution.py:401
  34.5 1.1 %collective-permute-start.16 = (bf16[9,16,384]{2,1,0:T(8,128)(2,1)S(1)}, bf16[9,16,384]{2,1,0:T(8,128)(2,1)S(1)}, u32[]{:S(2)}, u32[]{:S(2)}) collective-permute-start(bf16[9,16,384]{2,1,0:T(8,128)(2,1)S(1)} %shard_map.79.refs_0_), channel_id=1, source_target_pairs={{0,2},{1,3},{2,0},{3,1},{4,6},{5,7},{6,4},{7,5},{8,10},{9,11},{10,... | collective-permute-start | bytes 331784 | tf_op jit(solution)/shard_map/ppermute | solution.py:401
  35.6 2.8 %collective-permute-start.15 = (bf16[9,16,384]{2,1,0:T(8,128)(2,1)S(1)}, bf16[9,16,384]{2,1,0:T(8,128)(2,1)S(1)}, u32[]{:S(2)}, u32[]{:S(2)}) collective-permute-start(bf16[9,16,384]{2,1,0:T(8,128)(2,1)S(1)} %shard_map.79.refs_0_), channel_id=1, source_target_pairs={{0,12},{1,13},{2,14},{3,15},{4,0},{5,1},{6,2},{7,3},{8,4},{9,5},{1... | collective-permute-start | bytes 331784 | tf_op jit(solution)/shard_map/ppermute | solution.py:401
  38.4 2.9 %collective-permute-done.12.refs_1_ = bf16[9,16,384]{2,1,0:T(8,128)(2,1)S(1)} collective-permute-done((bf16[9,16,384]{2,1,0:T(8,128)(2,1)S(1)}, bf16[9,16,384]{2,1,0:T(8,128)(2,1)S(1)}, u32[]{:S(2)}, u32[]{:S(2)}) %collective-permute-start.12) | collective-permute-done | bytes 110624 | tf_op jit(solution)/shard_map/ppermute | solution.py:401
  41.3 1.1 %collective-permute-start.13 = (bf16[9,16,384]{2,1,0:T(8,128)(2,1)S(1)}, bf16[9,16,384]{2,1,0:T(8,128)(2,1)S(1)}, u32[]{:S(2)}, u32[]{:S(2)}) collective-permute-start(bf16[9,16,384]{2,1,0:T(8,128)(2,1)S(1)} %collective-permute-done.12.refs_1_), channel_id=1, source_target_pairs={{0,2},{1,3},{2,0},{3,1},{4,6},{5,7},{6,4},{7,5},{8,10},{9,11},{10,... | collective-permute-start | bytes 331784 | tf_op jit(solution)/shard_map/ppermute | solution.py:401
  42.4 0.5 collective-permute-start.21
  42.9 1.0 %collective-permute-start.22 = (bf16[9,16,384]{2,1,0:T(8,128)(2,1)S(1)}, bf16[9,16,384]{2,1,0:T(8,128)(2,1)S(1)}, u32[]{:S(2)}, u32[]{:S(2)}) collective-permute-start(bf16[9,16,384]{2,1,0:T(8,128)(2,1)S(1)} %collective-permute-done.15.refs_2_), channel_id=1, source_target_pairs={{0,2},{1,3},{2,0},{3,1},{4,6},{5,7},{6,4},{7,5},{8,10},{9,11},{10,... | collective-permute-start | bytes 331784 | tf_op jit(solution)/shard_map/ppermute | solution.py:401
  43.8 3.2 %collective-permute-done.11.refs_3_ = bf16[9,16,384]{2,1,0:T(8,128)(2,1)S(1)} collective-permute-done((bf16[9,16,384]{2,1,0:T(8,128)(2,1)S(1)}, bf16[9,16,384]{2,1,0:T(8,128)(2,1)S(1)}, u32[]{:S(2)}, u32[]{:S(2)}) %collective-permute-start.11) | collective-permute-done | bytes 110624 | tf_op jit(solution)/shard_map/ppermute | solution.py:401
  47.0 0.0 collective-permute-start.19
  47.0 0.0 collective-permute-done.13.refs_2_
  47.0 0.5 collective-permute-start.18
  47.6 0.0 collective-permute-done.17.refs_5_
  47.6 0.1 collective-permute-start.20
  47.6 0.0 collective-permute-done.21.refs_9_
  47.6 1.1 %collective-permute-start.14 = (bf16[9,16,384]{2,1,0:T(8,128)(2,1)S(1)}, bf16[9,16,384]{2,1,0:T(8,128)(2,1)S(1)}, u32[]{:S(2)}, u32[]{:S(2)}) collective-permute-start(bf16[9,16,384]{2,1,0:T(8,128)(2,1)S(1)} %collective-permute-done.11.refs_3_), channel_id=1, source_target_pairs={{0,2},{1,3},{2,0},{3,1},{4,6},{5,7},{6,4},{7,5},{8,10},{9,11},{10,... | collective-permute-start | bytes 331784 | tf_op jit(solution)/shard_map/ppermute | solution.py:401
  48.7 0.2 collective-permute-start.23
  48.9 0.3 collective-permute-start.24
  49.2 1.7 %shard_map.80 = (bf16[3,9,128,128]{3,2,1,0:T(8,128)(2,1)}, bf16[3,9,128,256]{3,2,1,0:T(8,128)(2,1)}) custom-call(bf16[9,16,384]{2,1,0:T(8,128)(2,1)S(1)} %shard_map.79.refs_0_, bf16[9,16,384]{2,1,0:T(8,128)(2,1)S(1)} %collective-permute-done.12.refs_1_, bf16[9,16,384]{2,1,0:T(8,128)(2,1)S(1)} %collective-permute-done.15.refs_2_, ...), custom_call_target="tpu_custom_call" | custom-call | bytes 10000 | tf_op jit(solution)/shard_map/pallas_call | solution.py:380
  50.9 2.1 %collective-permute-done.14.refs_6_ = bf16[9,16,384]{2,1,0:T(8,128)(2,1)S(1)} collective-permute-done((bf16[9,16,384]{2,1,0:T(8,128)(2,1)S(1)}, bf16[9,16,384]{2,1,0:T(8,128)(2,1)S(1)}, u32[]{:S(2)}, u32[]{:S(2)}) %collective-permute-start.14) | collective-permute-done | bytes 110624 | tf_op jit(solution)/shard_map/ppermute | solution.py:401
  53.0 1.3 %collective-permute-done.25.refs_7_ = bf16[9,16,384]{2,1,0:T(8,128)(2,1)S(1)} collective-permute-done((bf16[9,16,384]{2,1,0:T(8,128)(2,1)S(1)}, bf16[9,16,384]{2,1,0:T(8,128)(2,1)S(1)}, u32[]{:S(2)}, u32[]{:S(2)}) %collective-permute-start.25) | collective-permute-done | bytes 110624 | tf_op jit(solution)/shard_map/ppermute | solution.py:401
  54.4 1.1 %shard_map.81 = (bf16[3,9,128,128]{3,2,1,0:T(8,128)(2,1)}, bf16[3,9,128,256]{3,2,1,0:T(8,128)(2,1)}) custom-call(bf16[3,9,128,128]{3,2,1,0:T(8,128)(2,1)} %get-tuple-element.66.refs_0_, bf16[3,9,128,256]{3,2,1,0:T(8,128)(2,1)} %get-tuple-element.67.refs_1_, ...), custom_call_target="tpu_custom_call", output_to_operand_aliasing={{0}: (0, {}), {1}: (1, {})} | custom-call | bytes 10000 | tf_op jit(solution)/shard_map/pallas_call | solution.py:380
  (20 shorter events, 0.0 us)
Async XLA Ops:
  0.6 12.2 %copy-start.3 = (bf16[2,4,16,256]{3,2,1,0:T(8,128)(2,1)S(1)}, bf16[2,4,16,256]{3,2,1,0:T(8,128)(2,1)}, u32[]{:S(2)}) copy-start(bf16[2,4,16,256]{3,2,1,0:T(8,128)(2,1)} %refs_1_.1) | copy-start | bytes 196612
  0.6 12.2 %copy-start.2 = (bf16[2,8,32,128]{3,2,1,0:T(8,128)(2,1)S(1)}, bf16[2,8,32,128]{3,2,1,0:T(8,128)(2,1)}, u32[]{:S(2)}) copy-start(bf16[2,8,32,128]{3,2,1,0:T(8,128)(2,1)} %refs_0_.1) | copy-start | bytes 393220
  0.7 12.2 %copy-start.1 = (bf16[3,3,3,128,128]{4,3,2,1,0:T(8,128)(2,1)S(1)}, bf16[3,3,3,128,128]{4,3,2,1,0:T(8,128)(2,1)}, u32[]{:S(2)}) copy-start(bf16[3,3,3,128,128]{4,3,2,1,0:T(8,128)(2,1)} %weight_a.1) | copy-start | bytes 2654212
  2.4 19.1 %copy-start = (bf16[3,3,3,128,256]{4,3,2,1,0:T(8,128)(2,1)S(1)}, bf16[3,3,3,128,256]{4,3,2,1,0:T(8,128)(2,1)}, u32[]{:S(2)}) copy-start(bf16[3,3,3,128,256]{4,3,2,1,0:T(8,128)(2,1)} %refs_3_.1) | copy-start | bytes 5308420
  2.5 3.1 %collective-permute-start.2 = (bf16[2,3,32,128]{3,2,1,0:T(8,128)(2,1)}, bf16[2,3,32,128]{3,2,1,0:T(8,128)(2,1)S(1)}, u32[]{:S(2)}, u32[]{:S(2)}) collective-permute-start(bf16[2,3,32,128]{3,2,1,0:T(8,128)(2,1)} %get-tuple-element.39), channel_id=1, source_target_pairs={{0,1},{1,0},{2,3},{3,2},{4,5},{5,4},{6,7},{7,6},{8,9},{9,8},{10,11... | collective-permute-start | bytes 147464 | tf_op jit(solution)/shard_map/ppermute | solution.py:401
  3.0 8.3 %collective-permute-start.1 = (bf16[2,12,32,128]{3,2,1,0:T(8,128)(2,1)}, bf16[2,12,32,128]{3,2,1,0:T(8,128)(2,1)S(1)}, u32[]{:S(2)}, u32[]{:S(2)}) collective-permute-start(bf16[2,12,32,128]{3,2,1,0:T(8,128)(2,1)} %get-tuple-element.38), channel_id=1, source_target_pairs={{0,2},{1,3},{2,0},{3,1},{4,6},{5,7},{6,4},{7,5},{8,10},{9,11},{10,... | collective-permute-start | bytes 589832 | tf_op jit(solution)/shard_map/ppermute | solution.py:401
  6.4 0.7 %collective-permute-start.3 = (bf16[2,3,32,128]{3,2,1,0:T(8,128)(2,1)S(1)}, bf16[2,3,32,128]{3,2,1,0:T(8,128)(2,1)S(1)}, u32[]{:S(2)}, u32[]{:S(2)}) collective-permute-start(bf16[2,3,32,128]{3,2,1,0:T(8,128)(2,1)S(1)} %broadcast_select_fusion), channel_id=1, source_target_pairs={{2,6},{3,4},{4,3},{5,1},{6,10},{7,8},{8,7},{9,5},{10,14},{11,12},{... | collective-permute-start | bytes 147464 | tf_op jit(solution)/shard_map/ppermute | solution.py:401
  7.0 5.8 %collective-permute-start = (bf16[2,12,32,128]{3,2,1,0:T(8,128)(2,1)}, bf16[2,12,32,128]{3,2,1,0:T(8,128)(2,1)S(1)}, u32[]{:S(2)}, u32[]{:S(2)}) collective-permute-start(bf16[2,12,32,128]{3,2,1,0:T(8,128)(2,1)} %get-tuple-element.38), channel_id=1, source_target_pairs={{0,1},{1,0},{2,3},{3,2},{4,5},{5,4},{6,7},{7,6},{8,9},{9,8},{10,11... | collective-permute-start | bytes 589832 | tf_op jit(solution)/shard_map/ppermute | solution.py:401
  11.3 1.5 %collective-permute-start.4 = (bf16[2,12,32,128]{3,2,1,0:T(8,128)(2,1)S(1)}, bf16[2,12,32,128]{3,2,1,0:T(8,128)(2,1)S(1)}, u32[]{:S(2)}, u32[]{:S(2)}) collective-permute-start(bf16[2,12,32,128]{3,2,1,0:T(8,128)(2,1)S(1)} %collective-permute-done.1.refs_3_), channel_id=1, source_target_pairs={{0,1},{1,0},{2,3},{3,2},{4,5},{5,4},{6,7},{7,6},{8,9},{9,8},{10,11... | collective-permute-start | bytes 589832 | tf_op jit(solution)/shard_map/ppermute | solution.py:401
  11.3 1.5 %collective-permute-start.5 = (bf16[2,3,32,128]{3,2,1,0:T(8,128)(2,1)S(1)}, bf16[2,3,32,128]{3,2,1,0:T(8,128)(2,1)S(1)}, u32[]{:S(2)}, u32[]{:S(2)}) collective-permute-start(bf16[2,3,32,128]{3,2,1,0:T(8,128)(2,1)S(1)} %collective-permute-done.3.refs_5_), channel_id=1, source_target_pairs={{0,1},{1,0},{2,3},{3,2},{4,5},{5,4},{6,7},{7,6},{8,9},{9,8},{10,11... | collective-permute-start | bytes 147464 | tf_op jit(solution)/shard_map/ppermute | solution.py:401
  16.2 11.2 %collective-permute-start.7 = (bf16[9,16,256]{2,1,0:T(8,128)(2,1)S(1)}, bf16[9,16,256]{2,1,0:T(8,128)(2,1)S(1)}, u32[]{:S(2)}, u32[]{:S(2)}) collective-permute-start(bf16[9,16,256]{2,1,0:T(8,128)(2,1)S(1)} %get-tuple-element.55), channel_id=1, source_target_pairs={{0,4},{1,5},{2,6},{3,7},{4,8},{5,9},{6,10},{7,11},{8,12},{9,13},{1... | collective-permute-start | bytes 221192 | tf_op jit(solution)/shard_map/ppermute | solution.py:401
  19.5 7.9 %collective-permute-start.8 = (bf16[9,16,256]{2,1,0:T(8,128)(2,1)S(1)}, bf16[9,16,256]{2,1,0:T(8,128)(2,1)S(1)}, u32[]{:S(2)}, u32[]{:S(2)}) collective-permute-start(bf16[9,16,256]{2,1,0:T(8,128)(2,1)S(1)} %get-tuple-element.56), channel_id=1, source_target_pairs={{0,12},{1,13},{2,14},{3,15},{4,0},{5,1},{6,2},{7,3},{8,4},{9,5},{1... | collective-permute-start | bytes 221192 | tf_op jit(solution)/shard_map/ppermute | solution.py:401
  24.8 8.3 %collective-permute-start.10 = (bf16[9,16,384]{2,1,0:T(8,128)(2,1)S(1)}, bf16[9,16,384]{2,1,0:T(8,128)(2,1)S(1)}, u32[]{:S(2)}, u32[]{:S(2)}) collective-permute-start(bf16[9,16,384]{2,1,0:T(8,128)(2,1)S(1)} %get-tuple-element.62), channel_id=1, source_target_pairs={{0,8},{1,9},{2,10},{3,11},{4,12},{5,13},{6,14},{7,15},{8,0},{9,1},... | collective-permute-start | bytes 331784 | tf_op jit(solution)/shard_map/ppermute | solution.py:401
  25.8 5.9 %collective-permute-start.6 = (bf16[9,16,128]{2,1,0:T(8,128)(2,1)S(1)}, bf16[9,16,128]{2,1,0:T(8,128)(2,1)S(1)}, u32[]{:S(2)}, u32[]{:S(2)}) collective-permute-start(bf16[9,16,128]{2,1,0:T(8,128)(2,1)S(1)} %get-tuple-element.54), channel_id=1, source_target_pairs={{0,4},{1,5},{2,6},{3,7},{4,8},{5,9},{6,10},{7,11},{8,12},{9,13},{1... | collective-permute-start | bytes 110600 | tf_op jit(solution)/shard_map/ppermute | solution.py:401
  27.4 5.9 %collective-permute-start.9 = (bf16[9,16,128]{2,1,0:T(8,128)(2,1)S(1)}, bf16[9,16,128]{2,1,0:T(8,128)(2,1)S(1)}, u32[]{:S(2)}, u32[]{:S(2)}) collective-permute-start(bf16[9,16,128]{2,1,0:T(8,128)(2,1)S(1)} %get-tuple-element.58), channel_id=1, source_target_pairs={{0,12},{1,13},{2,14},{3,15},{4,0},{5,1},{6,2},{7,3},{8,4},{9,5},{1... | collective-permute-start | bytes 110600 | tf_op jit(solution)/shard_map/ppermute | solution.py:401
  33.4 7.9 %collective-permute-start.12 = (bf16[9,16,384]{2,1,0:T(8,128)(2,1)S(1)}, bf16[9,16,384]{2,1,0:T(8,128)(2,1)S(1)}, u32[]{:S(2)}, u32[]{:S(2)}) collective-permute-start(bf16[9,16,384]{2,1,0:T(8,128)(2,1)S(1)} %shard_map.79.refs_0_), channel_id=1, source_target_pairs={{0,4},{1,5},{2,6},{3,7},{4,8},{5,9},{6,10},{7,11},{8,12},{9,13},{1... | collective-permute-start | bytes 331784 | tf_op jit(solution)/shard_map/ppermute | solution.py:401
  34.5 7.9 %collective-permute-start.16 = (bf16[9,16,384]{2,1,0:T(8,128)(2,1)S(1)}, bf16[9,16,384]{2,1,0:T(8,128)(2,1)S(1)}, u32[]{:S(2)}, u32[]{:S(2)}) collective-permute-start(bf16[9,16,384]{2,1,0:T(8,128)(2,1)S(1)} %shard_map.79.refs_0_), channel_id=1, source_target_pairs={{0,2},{1,3},{2,0},{3,1},{4,6},{5,7},{6,4},{7,5},{8,10},{9,11},{10,... | collective-permute-start | bytes 331784 | tf_op jit(solution)/shard_map/ppermute | solution.py:401
  35.6 7.3 %collective-permute-start.15 = (bf16[9,16,384]{2,1,0:T(8,128)(2,1)S(1)}, bf16[9,16,384]{2,1,0:T(8,128)(2,1)S(1)}, u32[]{:S(2)}, u32[]{:S(2)}) collective-permute-start(bf16[9,16,384]{2,1,0:T(8,128)(2,1)S(1)} %shard_map.79.refs_0_), channel_id=1, source_target_pairs={{0,12},{1,13},{2,14},{3,15},{4,0},{5,1},{6,2},{7,3},{8,4},{9,5},{1... | collective-permute-start | bytes 331784 | tf_op jit(solution)/shard_map/ppermute | solution.py:401
  38.4 8.6 %collective-permute-start.11 = (bf16[9,16,384]{2,1,0:T(8,128)(2,1)S(1)}, bf16[9,16,384]{2,1,0:T(8,128)(2,1)S(1)}, u32[]{:S(2)}, u32[]{:S(2)}) collective-permute-start(bf16[9,16,384]{2,1,0:T(8,128)(2,1)S(1)} %shard_map.79.refs_0_), channel_id=1, source_target_pairs={{0,8},{1,9},{2,10},{3,11},{4,12},{5,13},{6,14},{7,15},{8,0},{9,1},... | collective-permute-start | bytes 331784 | tf_op jit(solution)/shard_map/ppermute | solution.py:401
  41.3 5.7 %collective-permute-start.13 = (bf16[9,16,384]{2,1,0:T(8,128)(2,1)S(1)}, bf16[9,16,384]{2,1,0:T(8,128)(2,1)S(1)}, u32[]{:S(2)}, u32[]{:S(2)}) collective-permute-start(bf16[9,16,384]{2,1,0:T(8,128)(2,1)S(1)} %collective-permute-done.12.refs_1_), channel_id=1, source_target_pairs={{0,2},{1,3},{2,0},{3,1},{4,6},{5,7},{6,4},{7,5},{8,10},{9,11},{10,... | collective-permute-start | bytes 331784 | tf_op jit(solution)/shard_map/ppermute | solution.py:401
  42.4 5.2 %collective-permute-start.17 = (bf16[9,16,384]{2,1,0:T(8,128)(2,1)S(1)}, bf16[9,16,384]{2,1,0:T(8,128)(2,1)S(1)}, u32[]{:S(2)}, u32[]{:S(2)}) collective-permute-start(bf16[9,16,384]{2,1,0:T(8,128)(2,1)S(1)} %shard_map.79.refs_0_), channel_id=1, source_target_pairs={{0,1},{1,0},{2,3},{3,2},{4,5},{5,4},{6,7},{7,6},{8,9},{9,8},{10,11... | collective-permute-start | bytes 331784 | tf_op jit(solution)/shard_map/ppermute | solution.py:401
  42.4 5.2 %collective-permute-start.21 = (bf16[9,16,384]{2,1,0:T(8,128)(2,1)S(1)}, bf16[9,16,384]{2,1,0:T(8,128)(2,1)S(1)}, u32[]{:S(2)}, u32[]{:S(2)}) collective-permute-start(bf16[9,16,384]{2,1,0:T(8,128)(2,1)S(1)} %collective-permute-done.16.refs_4_), channel_id=1, source_target_pairs={{0,1},{1,0},{2,3},{3,2},{4,5},{5,4},{6,7},{7,6},{8,9},{9,8},{10,11... | collective-permute-start | bytes 331784 | tf_op jit(solution)/shard_map/ppermute | solution.py:401
  42.9 5.8 %collective-permute-start.22 = (bf16[9,16,384]{2,1,0:T(8,128)(2,1)S(1)}, bf16[9,16,384]{2,1,0:T(8,128)(2,1)S(1)}, u32[]{:S(2)}, u32[]{:S(2)}) collective-permute-start(bf16[9,16,384]{2,1,0:T(8,128)(2,1)S(1)} %collective-permute-done.15.refs_2_), channel_id=1, source_target_pairs={{0,2},{1,3},{2,0},{3,1},{4,6},{5,7},{6,4},{7,5},{8,10},{9,11},{10,... | collective-permute-start | bytes 331784 | tf_op jit(solution)/shard_map/ppermute | solution.py:401
  47.0 1.8 %collective-permute-start.19 = (bf16[9,16,384]{2,1,0:T(8,128)(2,1)S(1)}, bf16[9,16,384]{2,1,0:T(8,128)(2,1)S(1)}, u32[]{:S(2)}, u32[]{:S(2)}) collective-permute-start(bf16[9,16,384]{2,1,0:T(8,128)(2,1)S(1)} %collective-permute-done.15.refs_2_), channel_id=1, source_target_pairs={{0,1},{1,0},{2,3},{3,2},{4,5},{5,4},{6,7},{7,6},{8,9},{9,8},{10,11... | collective-permute-start | bytes 331784 | tf_op jit(solution)/shard_map/ppermute | solution.py:401
  47.0 2.2 %collective-permute-start.18 = (bf16[9,16,384]{2,1,0:T(8,128)(2,1)S(1)}, bf16[9,16,384]{2,1,0:T(8,128)(2,1)S(1)}, u32[]{:S(2)}, u32[]{:S(2)}) collective-permute-start(bf16[9,16,384]{2,1,0:T(8,128)(2,1)S(1)} %collective-permute-done.12.refs_1_), channel_id=1, source_target_pairs={{0,1},{1,0},{2,3},{3,2},{4,5},{5,4},{6,7},{7,6},{8,9},{9,8},{10,11... | collective-permute-start | bytes 331784 | tf_op jit(solution)/shard_map/ppermute | solution.py:401
  47.6 1.7 %collective-permute-start.20 = (bf16[9,16,384]{2,1,0:T(8,128)(2,1)S(1)}, bf16[9,16,384]{2,1,0:T(8,128)(2,1)S(1)}, u32[]{:S(2)}, u32[]{:S(2)}) collective-permute-start(bf16[9,16,384]{2,1,0:T(8,128)(2,1)S(1)} %collective-permute-done.11.refs_3_), channel_id=1, source_target_pairs={{0,1},{1,0},{2,3},{3,2},{4,5},{5,4},{6,7},{7,6},{8,9},{9,8},{10,11... | collective-permute-start | bytes 331784 | tf_op jit(solution)/shard_map/ppermute | solution.py:401
  47.6 5.4 %collective-permute-start.14 = (bf16[9,16,384]{2,1,0:T(8,128)(2,1)S(1)}, bf16[9,16,384]{2,1,0:T(8,128)(2,1)S(1)}, u32[]{:S(2)}, u32[]{:S(2)}) collective-permute-start(bf16[9,16,384]{2,1,0:T(8,128)(2,1)S(1)} %collective-permute-done.11.refs_3_), channel_id=1, source_target_pairs={{0,2},{1,3},{2,0},{3,1},{4,6},{5,7},{6,4},{7,5},{8,10},{9,11},{10,... | collective-permute-start | bytes 331784 | tf_op jit(solution)/shard_map/ppermute | solution.py:401
  48.7 4.3 %collective-permute-start.23 = (bf16[9,16,384]{2,1,0:T(8,128)(2,1)S(1)}, bf16[9,16,384]{2,1,0:T(8,128)(2,1)S(1)}, u32[]{:S(2)}, u32[]{:S(2)}) collective-permute-start(bf16[9,16,384]{2,1,0:T(8,128)(2,1)S(1)} %collective-permute-done.13.refs_2_), channel_id=1, source_target_pairs={{0,1},{1,0},{2,3},{3,2},{4,5},{5,4},{6,7},{7,6},{8,9},{9,8},{10,11... | collective-permute-start | bytes 331784 | tf_op jit(solution)/shard_map/ppermute | solution.py:401
  48.9 4.2 %collective-permute-start.24 = (bf16[9,16,384]{2,1,0:T(8,128)(2,1)S(1)}, bf16[9,16,384]{2,1,0:T(8,128)(2,1)S(1)}, u32[]{:S(2)}, u32[]{:S(2)}) collective-permute-start(bf16[9,16,384]{2,1,0:T(8,128)(2,1)S(1)} %collective-permute-done.22.refs_3_), channel_id=1, source_target_pairs={{0,1},{1,0},{2,3},{3,2},{4,5},{5,4},{6,7},{7,6},{8,9},{9,8},{10,11... | collective-permute-start | bytes 331784 | tf_op jit(solution)/shard_map/ppermute | solution.py:401
  53.0 1.3 %collective-permute-start.25 = (bf16[9,16,384]{2,1,0:T(8,128)(2,1)S(1)}, bf16[9,16,384]{2,1,0:T(8,128)(2,1)S(1)}, u32[]{:S(2)}, u32[]{:S(2)}) collective-permute-start(bf16[9,16,384]{2,1,0:T(8,128)(2,1)S(1)} %collective-permute-done.14.refs_6_), channel_id=1, source_target_pairs={{0,1},{1,0},{2,3},{3,2},{4,5},{5,4},{6,7},{7,6},{8,9},{9,8},{10,11... | collective-permute-start | bytes 331784 | tf_op jit(solution)/shard_map/ppermute | solution.py:401

commit v6 on v5

--- a/solution.py
+++ b/solution.py
@@ -14,6 +14,12 @@
 def position():
     index = lax.axis_index(AXIS)
     return (index % 2, (index // 2) % 2, index // 4)
+
+
+def folded(weight, kt, *taps):
+    if kt:
+        return weight[(2, *taps)]
+    return (weight[(0, *taps)].astype(F32) + weight[(1, *taps)].astype(F32)).astype(BF16)
 
 
 def emit(total, outs):
@@ -121,7 +127,7 @@
 
     inner = ext - 2
     taps = [
-        jnp.concatenate([weight_a[kt, kh] for kh in range(3)], axis=0) for kt in range(3)
+        jnp.concatenate([folded(weight_a, kt, kh) for kh in range(3)], axis=0) for kt in range(2)
     ]
     fields = [
         jnp.concatenate(
@@ -133,9 +139,9 @@
         )
         for t in range(2)
     ]
-    early = mm(fields[0], jnp.concatenate(taps[:2], axis=1))
-    shared = early[:, :chans] + early[:, chans:]
-    latest = [mm(field, taps[2]) for field in fields]
+    early = mm(fields[0], jnp.concatenate(taps, axis=1))
+    shared = early[:, :chans]
+    latest = [early[:, chans:], mm(fields[1], taps[1])]
     even = even.reshape(frames, ext, half, chans)
     odd = odd.reshape(frames, ext, half, chans)
     outside = plane == 0
@@ -191,10 +197,11 @@
     zero = jnp.zeros((chans, wide), BF16)
 
     def taps(kt, kh):
+        left, mid, right = (folded(weight_b, kt, kh, kw) for kw in range(3))
         return jnp.concatenate(
             [
-                jnp.concatenate([weight_b[kt, kh, 1], zero], axis=1),
-                jnp.concatenate([weight_b[kt, kh, 2], weight_b[kt, kh, 0]], axis=1),
+                jnp.concatenate([mid, zero], axis=1),
+                jnp.concatenate([right, left], axis=1),
             ],
             axis=0,
         )
@@ -205,16 +212,15 @@
         shape = (frames, mid, half, 2 * chans)
         return (even.reshape(shape), odd.reshape(shape))
 
-    copies = [rows_of(kt) for kt in range(3)]
+    copies = [rows_of(kt) for kt in range(2)]
     row = lax.broadcasted_iota(jnp.int32, (inner, half, chans), 0)
     hidden = ((plane == 0) & (row == 0)) | ((plane == last) & (row == inner - 1))
     for t in range(frames):
         sums = []
         for parity in range(2):
-            total = copies[2][parity][t]
+            total = copies[1][parity][t]
             if t == 0:
-                total = total + (copies[0][parity][0] + copies[1][parity][0])
-                total = total + (copies[0][parity][1] + copies[1][parity][1])
+                total = total + (copies[0][parity][0] + copies[0][parity][1])
             sums.append(total)
         grad = jnp.stack([sums[1], sums[0]], axis=1).reshape(inner, half, 2 * chans)
         for parity in range(2):

time: 55.7 us -> 53.9 us (0.968)
  Pallas kernels: 13.4 us -> 11.6 us
    pallas_call x7, Pallas kernels: 13.4 us -> 11.6 us  [call(): pl.pallas_call(body, out_shape=outs, scratch_shapes=scratch, compiler_par...]
  transfers between devices with their start and end apart: 26 -> 26, of which waited for: 9 -> 9; matrix products, arithmetic and copies ran while one was open for 1% -> 2% of each run, Pallas kernels for 13% -> 12%
where the time goes in v6:
time: 53.9 us; the launch traced here: 53.7 us
  starting transfers between devices  24.2 us (45%)
  waiting for transfers between devices  16.3 us (30%)
  Pallas kernels  11.6 us (22%)
  other arithmetic  0.81 us (2%)
  between operations  0.75 us (1%)
    ppermute x26, starting transfers between devices, send(): return lax.ppermute(value, AXIS, pairs)  24.2 us
    ppermute x26, waiting for transfers between devices, send(): return lax.ppermute(value, AXIS, pairs)  16.3 us
    pallas_call x7, Pallas kernels, call(): pl.pallas_call(body, out_shape=outs, scratch_shapes=scratch, compiler_par...  11.6 us
  transfers between devices with their start and end apart: 26, of which 9 were waited for; matrix products, arithmetic and copies ran while one was open for 2% of the time, Pallas kernels for 12%

profile of v6, /device:TPU:0, one launch (start us, length us, event | category | flops | bytes accessed | tf_op | source)
XLA Modules:
  0.0 53.7 jit_solution(7423560927351498637)
XLA Ops:
  0.7 1.8 %shard_map.75 = (bf16[2,12,32,128]{3,2,1,0:T(8,128)(2,1)}, bf16[2,3,32,128]{3,2,1,0:T(8,128)(2,1)}) custom-call(bf16[2,8,32,128]{3,2,1,0:T(8,128)(2,1)} %refs_0_.1, bf16[2,4,16,256]{3,2,1,0:T(8,128)(2,1)} %refs_1_.1), custom_call_target="tpu_custom_call" | custom-call | flops 4000000000 | bytes 10000 | tf_op jit(solution)/shard_map/pallas_call | solution.py:386
  2.4 0.0 copy-start
  2.5 0.5 collective-permute-start.2
  3.0 2.6 %collective-permute-start.1 = (bf16[2,12,32,128]{3,2,1,0:T(8,128)(2,1)}, bf16[2,12,32,128]{3,2,1,0:T(8,128)(2,1)S(1)}, u32[]{:S(2)}, u32[]{:S(2)}) collective-permute-start(bf16[2,12,32,128]{3,2,1,0:T(8,128)(2,1)} %get-tuple-element.38), channel_id=1, source_target_pairs={{0,2},{1,3},{2,0},{3,1},{4,6},{5,7},{6,4},{7,5},{8,10},{9,11},{10,... | collective-permute-start | bytes 589832 | tf_op jit(solution)/shard_map/ppermute | solution.py:407
  5.6 0.0 collective-permute-done.2
  5.6 0.8 %broadcast_select_fusion = bf16[2,3,32,128]{3,2,1,0:T(8,128)(2,1)S(1)} fusion(bf16[2,3,32,128]{3,2,1,0:T(8,128)(2,1)} %get-tuple-element.39, bf16[2,3,32,128]{3,2,1,0:T(8,128)(2,1)S(1)} %collective-permute-done.2, pred[]{:T(512)S(6)} %eq.6), kind=kLoop, calls=%fused_computation | loop fusion | flops 24576 | bytes 147457 | tf_op jit(solution)/shard_map/jit(_where)/select_n | solution.py:427
  6.4 0.7 %collective-permute-start.3 = (bf16[2,3,32,128]{3,2,1,0:T(8,128)(2,1)S(1)}, bf16[2,3,32,128]{3,2,1,0:T(8,128)(2,1)S(1)}, u32[]{:S(2)}, u32[]{:S(2)}) collective-permute-start(bf16[2,3,32,128]{3,2,1,0:T(8,128)(2,1)S(1)} %broadcast_select_fusion), channel_id=1, source_target_pairs={{2,6},{3,4},{4,3},{5,1},{6,10},{7,8},{8,7},{9,5},{10,14},{11,12},{... | collective-permute-start | bytes 147464 | tf_op jit(solution)/shard_map/ppermute | solution.py:407
  7.0 0.1 collective-permute-start
  7.1 4.1 %collective-permute-done.1.refs_3_ = bf16[2,12,32,128]{3,2,1,0:T(8,128)(2,1)S(1)} collective-permute-done((bf16[2,12,32,128]{3,2,1,0:T(8,128)(2,1)}, bf16[2,12,32,128]{3,2,1,0:T(8,128)(2,1)S(1)}, u32[]{:S(2)}, u32[]{:S(2)}) %collective-permute-start.1) | collective-permute-done | bytes 196640 | tf_op jit(solution)/shard_map/ppermute | solution.py:407
  11.3 0.5 collective-permute-start.5
  11.8 1.0 %collective-permute-done.5.refs_6_ = bf16[2,3,32,128]{3,2,1,0:T(8,128)(2,1)S(1)} collective-permute-done((bf16[2,3,32,128]{3,2,1,0:T(8,128)(2,1)S(1)}, bf16[2,3,32,128]{3,2,1,0:T(8,128)(2,1)S(1)}, u32[]{:S(2)}, u32[]{:S(2)}) %collective-permute-start.5) | collective-permute-done | bytes 49184 | tf_op jit(solution)/shard_map/ppermute | solution.py:407
  12.8 0.0 collective-permute-done.refs_2_
  12.8 0.0 collective-permute-done.4.refs_4_
  12.8 2.4 %shard_map.76 = (f32[9,16,256]{2,1,0:T(8,128)S(1)}, bf16[9,16,256]{2,1,0:T(8,128)(2,1)S(1)}, bf16[9,16,256]{2,1,0:T(8,128)(2,1)S(1)}, bf16[9,16,256]{2,1,0:T(8,1...) custom-call(bf16[2,8,32,128]{3,2,1,0:T(8,128)(2,1)S(1)} %copy-done.2, ...), custom_call_target="tpu_custom_call" | custom-call | flops 10000000 | bytes 10000 | tf_op jit(solution)/shard_map/pallas_call | solution.py:386
  15.2 3.2 %collective-permute-start.7 = (bf16[9,16,256]{2,1,0:T(8,128)(2,1)S(1)}, bf16[9,16,256]{2,1,0:T(8,128)(2,1)S(1)}, u32[]{:S(2)}, u32[]{:S(2)}) collective-permute-start(bf16[9,16,256]{2,1,0:T(8,128)(2,1)S(1)} %get-tuple-element.55), channel_id=1, source_target_pairs={{0,4},{1,5},{2,6},{3,7},{4,8},{5,9},{6,10},{7,11},{8,12},{9,13},{1... | collective-permute-start | bytes 221192 | tf_op jit(solution)/shard_map/ppermute | solution.py:407
  18.4 2.1 %collective-permute-start.8 = (bf16[9,16,256]{2,1,0:T(8,128)(2,1)S(1)}, bf16[9,16,256]{2,1,0:T(8,128)(2,1)S(1)}, u32[]{:S(2)}, u32[]{:S(2)}) collective-permute-start(bf16[9,16,256]{2,1,0:T(8,128)(2,1)S(1)} %get-tuple-element.56), channel_id=1, source_target_pairs={{0,12},{1,13},{2,14},{3,15},{4,0},{5,1},{6,2},{7,3},{8,4},{9,5},{1... | collective-permute-start | bytes 221192 | tf_op jit(solution)/shard_map/ppermute | solution.py:407
  20.5 2.5 %shard_map.77 = (f32[9,16,128]{2,1,0:T(8,128)S(1)}, bf16[9,16,128]{2,1,0:T(8,128)(2,1)S(1)}, bf16[9,16,384]{2,1,0:T(8,128)(2,1)S(1)}, bf16[9,16,128]{2,1,0:T(8,128)(2,1)S(1)}, bf16[2,34,32,128]{3,2,1,0:T(8,128)(2,1)S(1)}) custom-call(bf16[2,18,16,256]{3,2,1,0:T(8,128)(2,1)S(1)} %get-tuple-element.42.refs_0_, ...), custom_call_target="tpu_custom_call" | custom-call | flops 10000000 | bytes 10000 | tf_op jit(solution)/shard_map/pallas_call | solution.py:386
  23.1 1.0 %collective-permute-start.10 = (bf16[9,16,384]{2,1,0:T(8,128)(2,1)S(1)}, bf16[9,16,384]{2,1,0:T(8,128)(2,1)S(1)}, u32[]{:S(2)}, u32[]{:S(2)}) collective-permute-start(bf16[9,16,384]{2,1,0:T(8,128)(2,1)S(1)} %get-tuple-element.62), channel_id=1, source_target_pairs={{0,8},{1,9},{2,10},{3,11},{4,12},{5,13},{6,14},{7,15},{8,0},{9,1},... | collective-permute-start | bytes 331784 | tf_op jit(solution)/shard_map/ppermute | solution.py:407
  24.1 1.6 %collective-permute-start.6 = (bf16[9,16,128]{2,1,0:T(8,128)(2,1)S(1)}, bf16[9,16,128]{2,1,0:T(8,128)(2,1)S(1)}, u32[]{:S(2)}, u32[]{:S(2)}) collective-permute-start(bf16[9,16,128]{2,1,0:T(8,128)(2,1)S(1)} %get-tuple-element.54), channel_id=1, source_target_pairs={{0,4},{1,5},{2,6},{3,7},{4,8},{5,9},{6,10},{7,11},{8,12},{9,13},{1... | collective-permute-start | bytes 110600 | tf_op jit(solution)/shard_map/ppermute | solution.py:407
  25.6 0.0 collective-permute-done.7.refs_4_
  25.6 0.0 collective-permute-done.8.refs_5_
  25.6 2.2 %collective-permute-start.9 = (bf16[9,16,128]{2,1,0:T(8,128)(2,1)S(1)}, bf16[9,16,128]{2,1,0:T(8,128)(2,1)S(1)}, u32[]{:S(2)}, u32[]{:S(2)}) collective-permute-start(bf16[9,16,128]{2,1,0:T(8,128)(2,1)S(1)} %get-tuple-element.58), channel_id=1, source_target_pairs={{0,12},{1,13},{2,14},{3,15},{4,0},{5,1},{6,2},{7,3},{8,4},{9,5},{1... | collective-permute-start | bytes 110600 | tf_op jit(solution)/shard_map/ppermute | solution.py:407
  27.9 2.0 %shard_map.78 = (bf16[2,4,16,256]{3,2,1,0:T(8,128)(2,1)}, bf16[2,8,32,128]{3,2,1,0:T(8,128)(2,1)}) custom-call(bf16[2,17,2,16,384]{4,3,2,1,0:T(8,128)(2,1)S(1)} %get-tuple-element.47.stacked_b, bf16[2,34,32,128]{3,2,1,0:T(8,128)(2,1)S(1)} %get-tuple-element.48.pre_grad, bf16[3,3,3,128,128]{4,3,2,1,0:T(8,128)(2,1)S(1)} %copy-done.1, ...), custom_call_target="tpu_custom_call" | custom-call | flops 10000000 | bytes 10000 | tf_op jit(solution)/shard_map/pallas_call | solution.py:386
  29.9 0.1 collective-permute-done.6.refs_1_
  30.0 1.3 %collective-permute-done.10.refs_6_ = bf16[9,16,384]{2,1,0:T(8,128)(2,1)S(1)} collective-permute-done((bf16[9,16,384]{2,1,0:T(8,128)(2,1)S(1)}, bf16[9,16,384]{2,1,0:T(8,128)(2,1)S(1)}, u32[]{:S(2)}, u32[]{:S(2)}) %collective-permute-start.10) | collective-permute-done | bytes 110624 | tf_op jit(solution)/shard_map/ppermute | solution.py:407
  31.3 0.2 collective-permute-done.9.refs_2_
  31.6 0.1 shard_map.79.refs_0_
  31.6 1.1 %collective-permute-start.12 = (bf16[9,16,384]{2,1,0:T(8,128)(2,1)S(1)}, bf16[9,16,384]{2,1,0:T(8,128)(2,1)S(1)}, u32[]{:S(2)}, u32[]{:S(2)}) collective-permute-start(bf16[9,16,384]{2,1,0:T(8,128)(2,1)S(1)} %shard_map.79.refs_0_), channel_id=1, source_target_pairs={{0,4},{1,5},{2,6},{3,7},{4,8},{5,9},{6,10},{7,11},{8,12},{9,13},{1... | collective-permute-start | bytes 331784 | tf_op jit(solution)/shard_map/ppermute | solution.py:407
  32.7 1.1 %collective-permute-start.16 = (bf16[9,16,384]{2,1,0:T(8,128)(2,1)S(1)}, bf16[9,16,384]{2,1,0:T(8,128)(2,1)S(1)}, u32[]{:S(2)}, u32[]{:S(2)}) collective-permute-start(bf16[9,16,384]{2,1,0:T(8,128)(2,1)S(1)} %shard_map.79.refs_0_), channel_id=1, source_target_pairs={{0,2},{1,3},{2,0},{3,1},{4,6},{5,7},{6,4},{7,5},{8,10},{9,11},{10,... | collective-permute-start | bytes 331784 | tf_op jit(solution)/shard_map/ppermute | solution.py:407
  33.8 2.8 %collective-permute-start.15 = (bf16[9,16,384]{2,1,0:T(8,128)(2,1)S(1)}, bf16[9,16,384]{2,1,0:T(8,128)(2,1)S(1)}, u32[]{:S(2)}, u32[]{:S(2)}) collective-permute-start(bf16[9,16,384]{2,1,0:T(8,128)(2,1)S(1)} %shard_map.79.refs_0_), channel_id=1, source_target_pairs={{0,12},{1,13},{2,14},{3,15},{4,0},{5,1},{6,2},{7,3},{8,4},{9,5},{1... | collective-permute-start | bytes 331784 | tf_op jit(solution)/shard_map/ppermute | solution.py:407
  36.6 0.0 collective-permute-start.11
  36.6 2.9 %collective-permute-done.12.refs_1_ = bf16[9,16,384]{2,1,0:T(8,128)(2,1)S(1)} collective-permute-done((bf16[9,16,384]{2,1,0:T(8,128)(2,1)S(1)}, bf16[9,16,384]{2,1,0:T(8,128)(2,1)S(1)}, u32[]{:S(2)}, u32[]{:S(2)}) %collective-permute-start.12) | collective-permute-done | bytes 110624 | tf_op jit(solution)/shard_map/ppermute | solution.py:407
  39.5 1.1 %collective-permute-start.13 = (bf16[9,16,384]{2,1,0:T(8,128)(2,1)S(1)}, bf16[9,16,384]{2,1,0:T(8,128)(2,1)S(1)}, u32[]{:S(2)}, u32[]{:S(2)}) collective-permute-start(bf16[9,16,384]{2,1,0:T(8,128)(2,1)S(1)} %collective-permute-done.12.refs_1_), channel_id=1, source_target_pairs={{0,2},{1,3},{2,0},{3,1},{4,6},{5,7},{6,4},{7,5},{8,10},{9,11},{10,... | collective-permute-start | bytes 331784 | tf_op jit(solution)/shard_map/ppermute | solution.py:407
  40.6 0.0 collective-permute-start.17
  40.6 0.0 collective-permute-done.16.refs_4_
  40.6 0.5 collective-permute-start.21
  41.1 0.0 collective-permute-done.15.refs_2_
  41.1 1.0 %collective-permute-start.22 = (bf16[9,16,384]{2,1,0:T(8,128)(2,1)S(1)}, bf16[9,16,384]{2,1,0:T(8,128)(2,1)S(1)}, u32[]{:S(2)}, u32[]{:S(2)}) collective-permute-start(bf16[9,16,384]{2,1,0:T(8,128)(2,1)S(1)} %collective-permute-done.15.refs_2_), channel_id=1, source_target_pairs={{0,2},{1,3},{2,0},{3,1},{4,6},{5,7},{6,4},{7,5},{8,10},{9,11},{10,... | collective-permute-start | bytes 331784 | tf_op jit(solution)/shard_map/ppermute | solution.py:407
  42.1 3.2 %collective-permute-done.11.refs_3_ = bf16[9,16,384]{2,1,0:T(8,128)(2,1)S(1)} collective-permute-done((bf16[9,16,384]{2,1,0:T(8,128)(2,1)S(1)}, bf16[9,16,384]{2,1,0:T(8,128)(2,1)S(1)}, u32[]{:S(2)}, u32[]{:S(2)}) %collective-permute-start.11) | collective-permute-done | bytes 110624 | tf_op jit(solution)/shard_map/ppermute | solution.py:407
  45.2 0.5 collective-permute-start.18
  45.7 0.1 collective-permute-start.20
  45.8 1.1 %collective-permute-start.14 = (bf16[9,16,384]{2,1,0:T(8,128)(2,1)S(1)}, bf16[9,16,384]{2,1,0:T(8,128)(2,1)S(1)}, u32[]{:S(2)}, u32[]{:S(2)}) collective-permute-start(bf16[9,16,384]{2,1,0:T(8,128)(2,1)S(1)} %collective-permute-done.11.refs_3_), channel_id=1, source_target_pairs={{0,2},{1,3},{2,0},{3,1},{4,6},{5,7},{6,4},{7,5},{8,10},{9,11},{10,... | collective-permute-start | bytes 331784 | tf_op jit(solution)/shard_map/ppermute | solution.py:407
  46.9 0.2 collective-permute-start.23
  47.1 0.3 collective-permute-start.24
  47.4 1.7 %shard_map.80 = (bf16[3,9,128,128]{3,2,1,0:T(8,128)(2,1)}, bf16[3,9,128,256]{3,2,1,0:T(8,128)(2,1)}) custom-call(bf16[9,16,384]{2,1,0:T(8,128)(2,1)S(1)} %shard_map.79.refs_0_, bf16[9,16,384]{2,1,0:T(8,128)(2,1)S(1)} %collective-permute-done.12.refs_1_, bf16[9,16,384]{2,1,0:T(8,128)(2,1)S(1)} %collective-permute-done.15.refs_2_, ...), custom_call_target="tpu_custom_call" | custom-call | bytes 10000 | tf_op jit(solution)/shard_map/pallas_call | solution.py:386
  49.1 2.1 %collective-permute-done.14.refs_6_ = bf16[9,16,384]{2,1,0:T(8,128)(2,1)S(1)} collective-permute-done((bf16[9,16,384]{2,1,0:T(8,128)(2,1)S(1)}, bf16[9,16,384]{2,1,0:T(8,128)(2,1)S(1)}, u32[]{:S(2)}, u32[]{:S(2)}) %collective-permute-start.14) | collective-permute-done | bytes 110624 | tf_op jit(solution)/shard_map/ppermute | solution.py:407
  51.2 1.3 %collective-permute-done.25.refs_7_ = bf16[9,16,384]{2,1,0:T(8,128)(2,1)S(1)} collective-permute-done((bf16[9,16,384]{2,1,0:T(8,128)(2,1)S(1)}, bf16[9,16,384]{2,1,0:T(8,128)(2,1)S(1)}, u32[]{:S(2)}, u32[]{:S(2)}) %collective-permute-start.25) | collective-permute-done | bytes 110624 | tf_op jit(solution)/shard_map/ppermute | solution.py:407
  52.5 1.1 %shard_map.81 = (bf16[3,9,128,128]{3,2,1,0:T(8,128)(2,1)}, bf16[3,9,128,256]{3,2,1,0:T(8,128)(2,1)}) custom-call(bf16[3,9,128,128]{3,2,1,0:T(8,128)(2,1)} %get-tuple-element.66.refs_0_, bf16[3,9,128,256]{3,2,1,0:T(8,128)(2,1)} %get-tuple-element.67.refs_1_, ...), custom_call_target="tpu_custom_call", output_to_operand_aliasing={{0}: (0, {}), {1}: (1, {})} | custom-call | bytes 10000 | tf_op jit(solution)/shard_map/pallas_call | solution.py:386
  (20 shorter events, 0.0 us)
Async XLA Ops:
  0.6 12.2 %copy-start.3 = (bf16[2,4,16,256]{3,2,1,0:T(8,128)(2,1)S(1)}, bf16[2,4,16,256]{3,2,1,0:T(8,128)(2,1)}, u32[]{:S(2)}) copy-start(bf16[2,4,16,256]{3,2,1,0:T(8,128)(2,1)} %refs_1_.1) | copy-start | bytes 196612
  0.6 12.2 %copy-start.2 = (bf16[2,8,32,128]{3,2,1,0:T(8,128)(2,1)S(1)}, bf16[2,8,32,128]{3,2,1,0:T(8,128)(2,1)}, u32[]{:S(2)}) copy-start(bf16[2,8,32,128]{3,2,1,0:T(8,128)(2,1)} %refs_0_.1) | copy-start | bytes 393220
  0.7 12.2 %copy-start.1 = (bf16[3,3,3,128,128]{4,3,2,1,0:T(8,128)(2,1)S(1)}, bf16[3,3,3,128,128]{4,3,2,1,0:T(8,128)(2,1)}, u32[]{:S(2)}) copy-start(bf16[3,3,3,128,128]{4,3,2,1,0:T(8,128)(2,1)} %weight_a.1) | copy-start | bytes 2654212
  2.4 18.1 %copy-start = (bf16[3,3,3,128,256]{4,3,2,1,0:T(8,128)(2,1)S(1)}, bf16[3,3,3,128,256]{4,3,2,1,0:T(8,128)(2,1)}, u32[]{:S(2)}) copy-start(bf16[3,3,3,128,256]{4,3,2,1,0:T(8,128)(2,1)} %refs_3_.1) | copy-start | bytes 5308420
  2.5 3.1 %collective-permute-start.2 = (bf16[2,3,32,128]{3,2,1,0:T(8,128)(2,1)}, bf16[2,3,32,128]{3,2,1,0:T(8,128)(2,1)S(1)}, u32[]{:S(2)}, u32[]{:S(2)}) collective-permute-start(bf16[2,3,32,128]{3,2,1,0:T(8,128)(2,1)} %get-tuple-element.39), channel_id=1, source_target_pairs={{0,1},{1,0},{2,3},{3,2},{4,5},{5,4},{6,7},{7,6},{8,9},{9,8},{10,11... | collective-permute-start | bytes 147464 | tf_op jit(solution)/shard_map/ppermute | solution.py:407
  3.0 8.3 %collective-permute-start.1 = (bf16[2,12,32,128]{3,2,1,0:T(8,128)(2,1)}, bf16[2,12,32,128]{3,2,1,0:T(8,128)(2,1)S(1)}, u32[]{:S(2)}, u32[]{:S(2)}) collective-permute-start(bf16[2,12,32,128]{3,2,1,0:T(8,128)(2,1)} %get-tuple-element.38), channel_id=1, source_target_pairs={{0,2},{1,3},{2,0},{3,1},{4,6},{5,7},{6,4},{7,5},{8,10},{9,11},{10,... | collective-permute-start | bytes 589832 | tf_op jit(solution)/shard_map/ppermute | solution.py:407
  6.4 0.7 %collective-permute-start.3 = (bf16[2,3,32,128]{3,2,1,0:T(8,128)(2,1)S(1)}, bf16[2,3,32,128]{3,2,1,0:T(8,128)(2,1)S(1)}, u32[]{:S(2)}, u32[]{:S(2)}) collective-permute-start(bf16[2,3,32,128]{3,2,1,0:T(8,128)(2,1)S(1)} %broadcast_select_fusion), channel_id=1, source_target_pairs={{2,6},{3,4},{4,3},{5,1},{6,10},{7,8},{8,7},{9,5},{10,14},{11,12},{... | collective-permute-start | bytes 147464 | tf_op jit(solution)/shard_map/ppermute | solution.py:407
  7.0 5.8 %collective-permute-start = (bf16[2,12,32,128]{3,2,1,0:T(8,128)(2,1)}, bf16[2,12,32,128]{3,2,1,0:T(8,128)(2,1)S(1)}, u32[]{:S(2)}, u32[]{:S(2)}) collective-permute-start(bf16[2,12,32,128]{3,2,1,0:T(8,128)(2,1)} %get-tuple-element.38), channel_id=1, source_target_pairs={{0,1},{1,0},{2,3},{3,2},{4,5},{5,4},{6,7},{7,6},{8,9},{9,8},{10,11... | collective-permute-start | bytes 589832 | tf_op jit(solution)/shard_map/ppermute | solution.py:407
  11.3 1.5 %collective-permute-start.4 = (bf16[2,12,32,128]{3,2,1,0:T(8,128)(2,1)S(1)}, bf16[2,12,32,128]{3,2,1,0:T(8,128)(2,1)S(1)}, u32[]{:S(2)}, u32[]{:S(2)}) collective-permute-start(bf16[2,12,32,128]{3,2,1,0:T(8,128)(2,1)S(1)} %collective-permute-done.1.refs_3_), channel_id=1, source_target_pairs={{0,1},{1,0},{2,3},{3,2},{4,5},{5,4},{6,7},{7,6},{8,9},{9,8},{10,11... | collective-permute-start | bytes 589832 | tf_op jit(solution)/shard_map/ppermute | solution.py:407
  11.3 1.5 %collective-permute-start.5 = (bf16[2,3,32,128]{3,2,1,0:T(8,128)(2,1)S(1)}, bf16[2,3,32,128]{3,2,1,0:T(8,128)(2,1)S(1)}, u32[]{:S(2)}, u32[]{:S(2)}) collective-permute-start(bf16[2,3,32,128]{3,2,1,0:T(8,128)(2,1)S(1)} %collective-permute-done.3.refs_5_), channel_id=1, source_target_pairs={{0,1},{1,0},{2,3},{3,2},{4,5},{5,4},{6,7},{7,6},{8,9},{9,8},{10,11... | collective-permute-start | bytes 147464 | tf_op jit(solution)/shard_map/ppermute | solution.py:407
  15.2 10.5 %collective-permute-start.7 = (bf16[9,16,256]{2,1,0:T(8,128)(2,1)S(1)}, bf16[9,16,256]{2,1,0:T(8,128)(2,1)S(1)}, u32[]{:S(2)}, u32[]{:S(2)}) collective-permute-start(bf16[9,16,256]{2,1,0:T(8,128)(2,1)S(1)} %get-tuple-element.55), channel_id=1, source_target_pairs={{0,4},{1,5},{2,6},{3,7},{4,8},{5,9},{6,10},{7,11},{8,12},{9,13},{1... | collective-permute-start | bytes 221192 | tf_op jit(solution)/shard_map/ppermute | solution.py:407
  18.4 7.2 %collective-permute-start.8 = (bf16[9,16,256]{2,1,0:T(8,128)(2,1)S(1)}, bf16[9,16,256]{2,1,0:T(8,128)(2,1)S(1)}, u32[]{:S(2)}, u32[]{:S(2)}) collective-permute-start(bf16[9,16,256]{2,1,0:T(8,128)(2,1)S(1)} %get-tuple-element.56), channel_id=1, source_target_pairs={{0,12},{1,13},{2,14},{3,15},{4,0},{5,1},{6,2},{7,3},{8,4},{9,5},{1... | collective-permute-start | bytes 221192 | tf_op jit(solution)/shard_map/ppermute | solution.py:407
  23.1 8.3 %collective-permute-start.10 = (bf16[9,16,384]{2,1,0:T(8,128)(2,1)S(1)}, bf16[9,16,384]{2,1,0:T(8,128)(2,1)S(1)}, u32[]{:S(2)}, u32[]{:S(2)}) collective-permute-start(bf16[9,16,384]{2,1,0:T(8,128)(2,1)S(1)} %get-tuple-element.62), channel_id=1, source_target_pairs={{0,8},{1,9},{2,10},{3,11},{4,12},{5,13},{6,14},{7,15},{8,0},{9,1},... | collective-permute-start | bytes 331784 | tf_op jit(solution)/shard_map/ppermute | solution.py:407
  24.1 5.9 %collective-permute-start.6 = (bf16[9,16,128]{2,1,0:T(8,128)(2,1)S(1)}, bf16[9,16,128]{2,1,0:T(8,128)(2,1)S(1)}, u32[]{:S(2)}, u32[]{:S(2)}) collective-permute-start(bf16[9,16,128]{2,1,0:T(8,128)(2,1)S(1)} %get-tuple-element.54), channel_id=1, source_target_pairs={{0,4},{1,5},{2,6},{3,7},{4,8},{5,9},{6,10},{7,11},{8,12},{9,13},{1... | collective-permute-start | bytes 110600 | tf_op jit(solution)/shard_map/ppermute | solution.py:407
  25.6 5.9 %collective-permute-start.9 = (bf16[9,16,128]{2,1,0:T(8,128)(2,1)S(1)}, bf16[9,16,128]{2,1,0:T(8,128)(2,1)S(1)}, u32[]{:S(2)}, u32[]{:S(2)}) collective-permute-start(bf16[9,16,128]{2,1,0:T(8,128)(2,1)S(1)} %get-tuple-element.58), channel_id=1, source_target_pairs={{0,12},{1,13},{2,14},{3,15},{4,0},{5,1},{6,2},{7,3},{8,4},{9,5},{1... | collective-permute-start | bytes 110600 | tf_op jit(solution)/shard_map/ppermute | solution.py:407
  31.6 7.9 %collective-permute-start.12 = (bf16[9,16,384]{2,1,0:T(8,128)(2,1)S(1)}, bf16[9,16,384]{2,1,0:T(8,128)(2,1)S(1)}, u32[]{:S(2)}, u32[]{:S(2)}) collective-permute-start(bf16[9,16,384]{2,1,0:T(8,128)(2,1)S(1)} %shard_map.79.refs_0_), channel_id=1, source_target_pairs={{0,4},{1,5},{2,6},{3,7},{4,8},{5,9},{6,10},{7,11},{8,12},{9,13},{1... | collective-permute-start | bytes 331784 | tf_op jit(solution)/shard_map/ppermute | solution.py:407
  32.7 7.9 %collective-permute-start.16 = (bf16[9,16,384]{2,1,0:T(8,128)(2,1)S(1)}, bf16[9,16,384]{2,1,0:T(8,128)(2,1)S(1)}, u32[]{:S(2)}, u32[]{:S(2)}) collective-permute-start(bf16[9,16,384]{2,1,0:T(8,128)(2,1)S(1)} %shard_map.79.refs_0_), channel_id=1, source_target_pairs={{0,2},{1,3},{2,0},{3,1},{4,6},{5,7},{6,4},{7,5},{8,10},{9,11},{10,... | collective-permute-start | bytes 331784 | tf_op jit(solution)/shard_map/ppermute | solution.py:407
  33.8 7.3 %collective-permute-start.15 = (bf16[9,16,384]{2,1,0:T(8,128)(2,1)S(1)}, bf16[9,16,384]{2,1,0:T(8,128)(2,1)S(1)}, u32[]{:S(2)}, u32[]{:S(2)}) collective-permute-start(bf16[9,16,384]{2,1,0:T(8,128)(2,1)S(1)} %shard_map.79.refs_0_), channel_id=1, source_target_pairs={{0,12},{1,13},{2,14},{3,15},{4,0},{5,1},{6,2},{7,3},{8,4},{9,5},{1... | collective-permute-start | bytes 331784 | tf_op jit(solution)/shard_map/ppermute | solution.py:407
  36.6 8.6 %collective-permute-start.11 = (bf16[9,16,384]{2,1,0:T(8,128)(2,1)S(1)}, bf16[9,16,384]{2,1,0:T(8,128)(2,1)S(1)}, u32[]{:S(2)}, u32[]{:S(2)}) collective-permute-start(bf16[9,16,384]{2,1,0:T(8,128)(2,1)S(1)} %shard_map.79.refs_0_), channel_id=1, source_target_pairs={{0,8},{1,9},{2,10},{3,11},{4,12},{5,13},{6,14},{7,15},{8,0},{9,1},... | collective-permute-start | bytes 331784 | tf_op jit(solution)/shard_map/ppermute | solution.py:407
  39.5 5.7 %collective-permute-start.13 = (bf16[9,16,384]{2,1,0:T(8,128)(2,1)S(1)}, bf16[9,16,384]{2,1,0:T(8,128)(2,1)S(1)}, u32[]{:S(2)}, u32[]{:S(2)}) collective-permute-start(bf16[9,16,384]{2,1,0:T(8,128)(2,1)S(1)} %collective-permute-done.12.refs_1_), channel_id=1, source_target_pairs={{0,2},{1,3},{2,0},{3,1},{4,6},{5,7},{6,4},{7,5},{8,10},{9,11},{10,... | collective-permute-start | bytes 331784 | tf_op jit(solution)/shard_map/ppermute | solution.py:407
  40.6 5.2 %collective-permute-start.17 = (bf16[9,16,384]{2,1,0:T(8,128)(2,1)S(1)}, bf16[9,16,384]{2,1,0:T(8,128)(2,1)S(1)}, u32[]{:S(2)}, u32[]{:S(2)}) collective-permute-start(bf16[9,16,384]{2,1,0:T(8,128)(2,1)S(1)} %shard_map.79.refs_0_), channel_id=1, source_target_pairs={{0,1},{1,0},{2,3},{3,2},{4,5},{5,4},{6,7},{7,6},{8,9},{9,8},{10,11... | collective-permute-start | bytes 331784 | tf_op jit(solution)/shard_map/ppermute | solution.py:407
  40.6 5.2 %collective-permute-start.21 = (bf16[9,16,384]{2,1,0:T(8,128)(2,1)S(1)}, bf16[9,16,384]{2,1,0:T(8,128)(2,1)S(1)}, u32[]{:S(2)}, u32[]{:S(2)}) collective-permute-start(bf16[9,16,384]{2,1,0:T(8,128)(2,1)S(1)} %collective-permute-done.16.refs_4_), channel_id=1, source_target_pairs={{0,1},{1,0},{2,3},{3,2},{4,5},{5,4},{6,7},{7,6},{8,9},{9,8},{10,11... | collective-permute-start | bytes 331784 | tf_op jit(solution)/shard_map/ppermute | solution.py:407
  41.1 5.8 %collective-permute-start.22 = (bf16[9,16,384]{2,1,0:T(8,128)(2,1)S(1)}, bf16[9,16,384]{2,1,0:T(8,128)(2,1)S(1)}, u32[]{:S(2)}, u32[]{:S(2)}) collective-permute-start(bf16[9,16,384]{2,1,0:T(8,128)(2,1)S(1)} %collective-permute-done.15.refs_2_), channel_id=1, source_target_pairs={{0,2},{1,3},{2,0},{3,1},{4,6},{5,7},{6,4},{7,5},{8,10},{9,11},{10,... | collective-permute-start | bytes 331784 | tf_op jit(solution)/shard_map/ppermute | solution.py:407
  45.2 1.9 %collective-permute-start.19 = (bf16[9,16,384]{2,1,0:T(8,128)(2,1)S(1)}, bf16[9,16,384]{2,1,0:T(8,128)(2,1)S(1)}, u32[]{:S(2)}, u32[]{:S(2)}) collective-permute-start(bf16[9,16,384]{2,1,0:T(8,128)(2,1)S(1)} %collective-permute-done.15.refs_2_), channel_id=1, source_target_pairs={{0,1},{1,0},{2,3},{3,2},{4,5},{5,4},{6,7},{7,6},{8,9},{9,8},{10,11... | collective-permute-start | bytes 331784 | tf_op jit(solution)/shard_map/ppermute | solution.py:407
  45.2 2.2 %collective-permute-start.18 = (bf16[9,16,384]{2,1,0:T(8,128)(2,1)S(1)}, bf16[9,16,384]{2,1,0:T(8,128)(2,1)S(1)}, u32[]{:S(2)}, u32[]{:S(2)}) collective-permute-start(bf16[9,16,384]{2,1,0:T(8,128)(2,1)S(1)} %collective-permute-done.12.refs_1_), channel_id=1, source_target_pairs={{0,1},{1,0},{2,3},{3,2},{4,5},{5,4},{6,7},{7,6},{8,9},{9,8},{10,11... | collective-permute-start | bytes 331784 | tf_op jit(solution)/shard_map/ppermute | solution.py:407
  45.7 1.7 %collective-permute-start.20 = (bf16[9,16,384]{2,1,0:T(8,128)(2,1)S(1)}, bf16[9,16,384]{2,1,0:T(8,128)(2,1)S(1)}, u32[]{:S(2)}, u32[]{:S(2)}) collective-permute-start(bf16[9,16,384]{2,1,0:T(8,128)(2,1)S(1)} %collective-permute-done.11.refs_3_), channel_id=1, source_target_pairs={{0,1},{1,0},{2,3},{3,2},{4,5},{5,4},{6,7},{7,6},{8,9},{9,8},{10,11... | collective-permute-start | bytes 331784 | tf_op jit(solution)/shard_map/ppermute | solution.py:407
  45.8 5.4 %collective-permute-start.14 = (bf16[9,16,384]{2,1,0:T(8,128)(2,1)S(1)}, bf16[9,16,384]{2,1,0:T(8,128)(2,1)S(1)}, u32[]{:S(2)}, u32[]{:S(2)}) collective-permute-start(bf16[9,16,384]{2,1,0:T(8,128)(2,1)S(1)} %collective-permute-done.11.refs_3_), channel_id=1, source_target_pairs={{0,2},{1,3},{2,0},{3,1},{4,6},{5,7},{6,4},{7,5},{8,10},{9,11},{10,... | collective-permute-start | bytes 331784 | tf_op jit(solution)/shard_map/ppermute | solution.py:407
  46.9 4.3 %collective-permute-start.23 = (bf16[9,16,384]{2,1,0:T(8,128)(2,1)S(1)}, bf16[9,16,384]{2,1,0:T(8,128)(2,1)S(1)}, u32[]{:S(2)}, u32[]{:S(2)}) collective-permute-start(bf16[9,16,384]{2,1,0:T(8,128)(2,1)S(1)} %collective-permute-done.13.refs_2_), channel_id=1, source_target_pairs={{0,1},{1,0},{2,3},{3,2},{4,5},{5,4},{6,7},{7,6},{8,9},{9,8},{10,11... | collective-permute-start | bytes 331784 | tf_op jit(solution)/shard_map/ppermute | solution.py:407
  47.1 4.1 %collective-permute-start.24 = (bf16[9,16,384]{2,1,0:T(8,128)(2,1)S(1)}, bf16[9,16,384]{2,1,0:T(8,128)(2,1)S(1)}, u32[]{:S(2)}, u32[]{:S(2)}) collective-permute-start(bf16[9,16,384]{2,1,0:T(8,128)(2,1)S(1)} %collective-permute-done.22.refs_3_), channel_id=1, source_target_pairs={{0,1},{1,0},{2,3},{3,2},{4,5},{5,4},{6,7},{7,6},{8,9},{9,8},{10,11... | collective-permute-start | bytes 331784 | tf_op jit(solution)/shard_map/ppermute | solution.py:407
  51.2 1.3 %collective-permute-start.25 = (bf16[9,16,384]{2,1,0:T(8,128)(2,1)S(1)}, bf16[9,16,384]{2,1,0:T(8,128)(2,1)S(1)}, u32[]{:S(2)}, u32[]{:S(2)}) collective-permute-start(bf16[9,16,384]{2,1,0:T(8,128)(2,1)S(1)} %collective-permute-done.14.refs_6_), channel_id=1, source_target_pairs={{0,1},{1,0},{2,3},{3,2},{4,5},{5,4},{6,7},{7,6},{8,9},{9,8},{10,11... | collective-permute-start | bytes 331784 | tf_op jit(solution)/shard_map/ppermute | solution.py:407

commit v7 on v6

--- a/solution.py
+++ b/solution.py
@@ -178,10 +178,10 @@
     emit(total_b, pieces)
 
 
-def backward_kernel(last, join, cot_ref, pre_ref, stacked_a, weight_b, *refs):
-    if join:
-        refs[1 + join][:, :, weight_b.shape[3] :] = refs[0][...]
-        refs = refs[1:]
+def backward_kernel(last, joins, cot_ref, pre_ref, stacked_a, weight_b, *refs):
+    given, refs = (refs[: len(joins)], refs[len(joins) :])
+    for step, piece in zip(joins, given, strict=True):
+        refs[step][:, :, weight_b.shape[3] :] = piece[...]
     pieces, (pre_grad, total_a) = (refs[:-2], refs[-2:])
     core, side, plane = position()
     frames, ext_g, half, wide = cot_ref.shape
@@ -445,10 +445,11 @@
     def forward(*refs):
         forward_kernel(split, *refs)
 
-    join = split // 2 if split > 2 else 0
+    far = split // 2
+    joins = tuple(step for step in range(1, split) if step != far)
 
     def backward(*refs):
-        backward_kernel(planes - 1, join, *refs)
+        backward_kernel(planes - 1, joins, *refs)
 
     *pieces_b, pre, stacked_a, stacked_b, cot = call(
         forward,
@@ -467,10 +468,9 @@
         flops=10**7,
     )
     shapes_a = list(pieces_of(chans))
-    joined = ()
-    if join:
-        shapes_a[join] = shape((9, part // split, chans + wide), BF16)
-        joined = (pieces_b[join],)
+    for step in joins:
+        shapes_a[step] = shape((9, part // split, chans + wide), BF16)
+    joined = tuple(pieces_b[step] for step in joins)
     *pieces_a, pre_grad = call(
         backward,
         (*shapes_a, shape((count, inner, width, chans), BF16)),
@@ -501,22 +501,22 @@
         return (encoded, frames_grad, both[0], both[1])
 
     rotations = [[(i, (i + 4 * step) % n) for i in range(n)] for step in range(planes)]
-    close = [step for step in range(1, planes) if step != join]
-    got_b = [send(pieces_b[step], rotations[step]) for step in close]
-    if join:
-        gate = lax.optimization_barrier((*got_b, pieces_a[close[-1]]))
-        *got_b, pieces_a[close[-1]] = gate
-    got_a = [send(pieces_a[step], rotations[step]) for step in close]
-    both = [send(pieces_a[join], rotations[join])] if join else []
+    alone_a, alone_b = (pieces_a[:1], pieces_b[:1])
+    if far:
+        alone_b.append(send(pieces_b[far], rotations[far]))
+        gate = lax.optimization_barrier((alone_b[1], pieces_a[far]))
+        alone_b[1], pieces_a[far] = gate
+        alone_a.append(send(pieces_a[far], rotations[far]))
+    both = [send(pieces_a[step], rotations[step]) for step in joins]
 
     def finish(*refs):
-        finish_kernel(scale, 1 + len(close), *refs)
+        finish_kernel(scale, len(alone_a), *refs)
 
     encoded, frames_grad = outputs(stacked_b)
-    held = lax.optimization_barrier((pieces_a[0], encoded, frames_grad))
-    pieces_a[0], encoded, frames_grad = held
+    held = lax.optimization_barrier((alone_a[0], encoded, frames_grad))
+    alone_a[0], encoded, frames_grad = held
     piece = shape((9, part // planes, chans + wide), BF16)
-    (own,) = call(finish, (piece,), (pieces_a[0], *got_a, pieces_b[0], *got_b, *both))
+    (own,) = call(finish, (piece,), (*alone_a, *alone_b, *both))
     column = {(0, 0, 0): own}
     order = sorted(range(1, planes), key=lambda step: min(step, planes - step))
     for step in order[:-1]:
@@ -524,14 +524,14 @@
     if planes == 1:
         column[0, 1, 0] = send(own, swap_side)
     else:
-        far = (0, 0, order[-1])
-        column[far] = send(own, rotations[order[-1]])
+        distant = (0, 0, order[-1])
+        column[distant] = send(own, rotations[order[-1]])
         for step in (0, *order[:-1]):
             column[0, 1, step] = send(column[0, 0, step], swap_side)
         if len(order) > 1:
             key = (0, 1, order[0])
-            column[far], column[key] = lax.optimization_barrier((column[far], column[key]))
-        column[0, 1, far[2]] = send(column[far], swap_side)
+            column[distant], column[key] = lax.optimization_barrier((column[distant], column[key]))
+        column[0, 1, distant[2]] = send(column[distant], swap_side)
     last = (0, 1, order[-1] if order else 0)
     for (_, flip, step), value in list(column.items()):
         if (0, flip, step) != last:

time: 53.9 us -> 53.5 us (level)
  starting transfers between devices: 24.2 us -> 20.9 us
  waiting for transfers between devices: 16.3 us -> 19.2 us
    ppermute x26 -> x25, starting transfers between devices: 24.2 us -> 20.9 us  [send(): return lax.ppermute(value, AXIS, pairs)]
    ppermute x26 -> x25, waiting for transfers between devices: 16.3 us -> 19.2 us  [send(): return lax.ppermute(value, AXIS, pairs)]
  transfers between devices with their start and end apart: 26 -> 25, of which waited for: 9 -> 11; matrix products, arithmetic and copies ran while one was open for 2% -> 2% of each run, Pallas kernels for 12% -> 12%
where the time goes in v7:
time: 53.5 us; the launch traced here: 53.3 us
  starting transfers between devices  20.9 us (39%)
  waiting for transfers between devices  19.2 us (36%)
  Pallas kernels  11.6 us (22%)
  other arithmetic  0.81 us (2%)
  between operations  0.76 us (1%)
    ppermute x25, starting transfers between devices, send(): return lax.ppermute(value, AXIS, pairs)  20.9 us
    ppermute x25, waiting for transfers between devices, send(): return lax.ppermute(value, AXIS, pairs)  19.2 us
    pallas_call x7, Pallas kernels, call(): pl.pallas_call(body, out_shape=outs, scratch_shapes=scratch, compiler_par...  11.6 us
  transfers between devices with their start and end apart: 25, of which 11 were waited for; matrix products, arithmetic and copies ran while one was open for 2% of the time, Pallas kernels for 12%

profile of v7, /device:TPU:0, one launch (start us, length us, event | category | flops | bytes accessed | tf_op | source)
XLA Modules:
  0.0 53.3 jit_solution(259869702568023728)
XLA Ops:
  0.7 1.8 %shard_map.75 = (bf16[2,12,32,128]{3,2,1,0:T(8,128)(2,1)}, bf16[2,3,32,128]{3,2,1,0:T(8,128)(2,1)}) custom-call(bf16[2,8,32,128]{3,2,1,0:T(8,128)(2,1)} %refs_0_.1, bf16[2,4,16,256]{3,2,1,0:T(8,128)(2,1)} %refs_1_.1), custom_call_target="tpu_custom_call" | custom-call | flops 4000000000 | bytes 10000 | tf_op jit(solution)/shard_map/pallas_call | solution.py:386
  2.4 0.0 copy-start
  2.5 0.5 collective-permute-start.2
  3.0 2.6 %collective-permute-start.1 = (bf16[2,12,32,128]{3,2,1,0:T(8,128)(2,1)}, bf16[2,12,32,128]{3,2,1,0:T(8,128)(2,1)S(1)}, u32[]{:S(2)}, u32[]{:S(2)}) collective-permute-start(bf16[2,12,32,128]{3,2,1,0:T(8,128)(2,1)} %get-tuple-element.37), channel_id=1, source_target_pairs={{0,2},{1,3},{2,0},{3,1},{4,6},{5,7},{6,4},{7,5},{8,10},{9,11},{10,... | collective-permute-start | bytes 589832 | tf_op jit(solution)/shard_map/ppermute | solution.py:407
  5.6 0.0 collective-permute-done.2
  5.6 0.8 %broadcast_select_fusion = bf16[2,3,32,128]{3,2,1,0:T(8,128)(2,1)S(1)} fusion(bf16[2,3,32,128]{3,2,1,0:T(8,128)(2,1)} %get-tuple-element.38, bf16[2,3,32,128]{3,2,1,0:T(8,128)(2,1)S(1)} %collective-permute-done.2, pred[]{:T(512)S(6)} %eq.6), kind=kLoop, calls=%fused_computation | loop fusion | flops 24576 | bytes 147457 | tf_op jit(solution)/shard_map/jit(_where)/select_n | solution.py:427
  6.4 0.7 %collective-permute-start.3 = (bf16[2,3,32,128]{3,2,1,0:T(8,128)(2,1)S(1)}, bf16[2,3,32,128]{3,2,1,0:T(8,128)(2,1)S(1)}, u32[]{:S(2)}, u32[]{:S(2)}) collective-permute-start(bf16[2,3,32,128]{3,2,1,0:T(8,128)(2,1)S(1)} %broadcast_select_fusion), channel_id=1, source_target_pairs={{2,6},{3,4},{4,3},{5,1},{6,10},{7,8},{8,7},{9,5},{10,14},{11,12},{... | collective-permute-start | bytes 147464 | tf_op jit(solution)/shard_map/ppermute | solution.py:407
  7.0 0.1 collective-permute-start
  7.1 0.0 collective-permute-done.3.refs_5_
  7.1 4.1 %collective-permute-done.1.refs_3_ = bf16[2,12,32,128]{3,2,1,0:T(8,128)(2,1)S(1)} collective-permute-done((bf16[2,12,32,128]{3,2,1,0:T(8,128)(2,1)}, bf16[2,12,32,128]{3,2,1,0:T(8,128)(2,1)S(1)}, u32[]{:S(2)}, u32[]{:S(2)}) %collective-permute-start.1) | collective-permute-done | bytes 196640 | tf_op jit(solution)/shard_map/ppermute | solution.py:407
  11.3 0.0 collective-permute-start.4
  11.3 0.5 collective-permute-start.5
  11.8 1.0 %collective-permute-done.5.refs_6_ = bf16[2,3,32,128]{3,2,1,0:T(8,128)(2,1)S(1)} collective-permute-done((bf16[2,3,32,128]{3,2,1,0:T(8,128)(2,1)S(1)}, bf16[2,3,32,128]{3,2,1,0:T(8,128)(2,1)S(1)}, u32[]{:S(2)}, u32[]{:S(2)}) %collective-permute-start.5) | collective-permute-done | bytes 49184 | tf_op jit(solution)/shard_map/ppermute | solution.py:407
  12.8 0.0 collective-permute-done.refs_2_
  12.8 0.0 collective-permute-done.4.refs_4_
  12.8 2.4 %shard_map.76 = (f32[9,16,256]{2,1,0:T(8,128)S(1)}, bf16[9,16,256]{2,1,0:T(8,128)(2,1)S(1)}, bf16[9,16,256]{2,1,0:T(8,128)(2,1)S(1)}, bf16[9,16,256]{2,1,0:T(8,1...) custom-call(bf16[2,8,32,128]{3,2,1,0:T(8,128)(2,1)S(1)} %copy-done.2, ...), custom_call_target="tpu_custom_call" | custom-call | flops 10000000 | bytes 10000 | tf_op jit(solution)/shard_map/pallas_call | solution.py:386
  15.2 4.3 %collective-permute-start.6 = (bf16[9,16,256]{2,1,0:T(8,128)(2,1)S(1)}, bf16[9,16,256]{2,1,0:T(8,128)(2,1)S(1)}, u32[]{:S(2)}, u32[]{:S(2)}) collective-permute-start(bf16[9,16,256]{2,1,0:T(8,128)(2,1)S(1)} %get-tuple-element.54), channel_id=1, source_target_pairs={{0,8},{1,9},{2,10},{3,11},{4,12},{5,13},{6,14},{7,15},{8,0},{9,1},... | collective-permute-start | bytes 221192 | tf_op jit(solution)/shard_map/ppermute | solution.py:407
  19.5 2.5 %shard_map.77 = (f32[9,16,128]{2,1,0:T(8,128)S(1)}, bf16[9,16,384]{2,1,0:T(8,128)(2,1)S(1)}, bf16[9,16,128]{2,1,0:T(8,128)(2,1)S(1)}, bf16[9,16,384]{2,1,0:T(8,128)(2,1)S(1)}, bf16[2,34,32,128]{3,2,1,0:T(8,128)(2,1)S(1)}) custom-call(bf16[2,18,16,256]{3,2,1,0:T(8,128)(2,1)S(1)} %get-tuple-element.41.refs_0_, ...), custom_call_target="tpu_custom_call" | custom-call | flops 10000000 | bytes 10000 | tf_op jit(solution)/shard_map/pallas_call | solution.py:386
  22.0 1.6 %collective-permute-start.8 = (bf16[9,16,384]{2,1,0:T(8,128)(2,1)S(1)}, bf16[9,16,384]{2,1,0:T(8,128)(2,1)S(1)}, u32[]{:S(2)}, u32[]{:S(2)}) collective-permute-start(bf16[9,16,384]{2,1,0:T(8,128)(2,1)S(1)} %get-tuple-element.59), channel_id=1, source_target_pairs={{0,4},{1,5},{2,6},{3,7},{4,8},{5,9},{6,10},{7,11},{8,12},{9,13},{1... | collective-permute-start | bytes 331784 | tf_op jit(solution)/shard_map/ppermute | solution.py:407
  23.6 2.2 %collective-permute-start.9 = (bf16[9,16,384]{2,1,0:T(8,128)(2,1)S(1)}, bf16[9,16,384]{2,1,0:T(8,128)(2,1)S(1)}, u32[]{:S(2)}, u32[]{:S(2)}) collective-permute-start(bf16[9,16,384]{2,1,0:T(8,128)(2,1)S(1)} %get-tuple-element.60), channel_id=1, source_target_pairs={{0,12},{1,13},{2,14},{3,15},{4,0},{5,1},{6,2},{7,3},{8,4},{9,5},{1... | collective-permute-start | bytes 331784 | tf_op jit(solution)/shard_map/ppermute | solution.py:407
  25.9 0.0 collective-permute-done.6.refs_3_
  25.9 0.0 collective-permute-start.7
  25.9 2.0 %shard_map.78 = (bf16[2,4,16,256]{3,2,1,0:T(8,128)(2,1)}, bf16[2,8,32,128]{3,2,1,0:T(8,128)(2,1)}) custom-call(bf16[2,17,2,16,384]{4,3,2,1,0:T(8,128)(2,1)S(1)} %get-tuple-element.47.stacked_b, bf16[2,34,32,128]{3,2,1,0:T(8,128)(2,1)S(1)} %get-tuple-element.48.pre_grad, bf16[3,3,3,128,128]{4,3,2,1,0:T(8,128)(2,1)S(1)} %copy-done.1, ...), custom_call_target="tpu_custom_call" | custom-call | flops 10000000 | bytes 10000 | tf_op jit(solution)/shard_map/pallas_call | solution.py:386
  27.9 1.9 %collective-permute-done.8.refs_4_ = bf16[9,16,384]{2,1,0:T(8,128)(2,1)S(1)} collective-permute-done((bf16[9,16,384]{2,1,0:T(8,128)(2,1)S(1)}, bf16[9,16,384]{2,1,0:T(8,128)(2,1)S(1)}, u32[]{:S(2)}, u32[]{:S(2)}) %collective-permute-start.8) | collective-permute-done | bytes 110624 | tf_op jit(solution)/shard_map/ppermute | solution.py:407
  29.8 1.2 %collective-permute-done.9.refs_5_ = bf16[9,16,384]{2,1,0:T(8,128)(2,1)S(1)} collective-permute-done((bf16[9,16,384]{2,1,0:T(8,128)(2,1)S(1)}, bf16[9,16,384]{2,1,0:T(8,128)(2,1)S(1)}, u32[]{:S(2)}, u32[]{:S(2)}) %collective-permute-start.9) | collective-permute-done | bytes 110624 | tf_op jit(solution)/shard_map/ppermute | solution.py:407
  31.0 0.6 %collective-permute-done.7.refs_1_ = bf16[9,16,128]{2,1,0:T(8,128)(2,1)S(1)} collective-permute-done((bf16[9,16,128]{2,1,0:T(8,128)(2,1)S(1)}, bf16[9,16,128]{2,1,0:T(8,128)(2,1)S(1)}, u32[]{:S(2)}, u32[]{:S(2)}) %collective-permute-start.7) | collective-permute-done | bytes 36896 | tf_op jit(solution)/shard_map/ppermute | solution.py:407
  31.6 0.1 shard_map.79.refs_0_
  31.7 1.0 %collective-permute-start.11 = (bf16[9,16,384]{2,1,0:T(8,128)(2,1)S(1)}, bf16[9,16,384]{2,1,0:T(8,128)(2,1)S(1)}, u32[]{:S(2)}, u32[]{:S(2)}) collective-permute-start(bf16[9,16,384]{2,1,0:T(8,128)(2,1)S(1)} %shard_map.79.refs_0_), channel_id=1, source_target_pairs={{0,4},{1,5},{2,6},{3,7},{4,8},{5,9},{6,10},{7,11},{8,12},{9,13},{1... | collective-permute-start | bytes 331784 | tf_op jit(solution)/shard_map/ppermute | solution.py:407
  32.7 1.0 %collective-permute-start.15 = (bf16[9,16,384]{2,1,0:T(8,128)(2,1)S(1)}, bf16[9,16,384]{2,1,0:T(8,128)(2,1)S(1)}, u32[]{:S(2)}, u32[]{:S(2)}) collective-permute-start(bf16[9,16,384]{2,1,0:T(8,128)(2,1)S(1)} %shard_map.79.refs_0_), channel_id=1, source_target_pairs={{0,2},{1,3},{2,0},{3,1},{4,6},{5,7},{6,4},{7,5},{8,10},{9,11},{10,... | collective-permute-start | bytes 331784 | tf_op jit(solution)/shard_map/ppermute | solution.py:407
  33.7 2.3 %collective-permute-start.14 = (bf16[9,16,384]{2,1,0:T(8,128)(2,1)S(1)}, bf16[9,16,384]{2,1,0:T(8,128)(2,1)S(1)}, u32[]{:S(2)}, u32[]{:S(2)}) collective-permute-start(bf16[9,16,384]{2,1,0:T(8,128)(2,1)S(1)} %shard_map.79.refs_0_), channel_id=1, source_target_pairs={{0,12},{1,13},{2,14},{3,15},{4,0},{5,1},{6,2},{7,3},{8,4},{9,5},{1... | collective-permute-start | bytes 331784 | tf_op jit(solution)/shard_map/ppermute | solution.py:407
  36.0 0.0 collective-permute-start.10
  36.1 3.3 %collective-permute-done.11.refs_1_ = bf16[9,16,384]{2,1,0:T(8,128)(2,1)S(1)} collective-permute-done((bf16[9,16,384]{2,1,0:T(8,128)(2,1)S(1)}, bf16[9,16,384]{2,1,0:T(8,128)(2,1)S(1)}, u32[]{:S(2)}, u32[]{:S(2)}) %collective-permute-start.11) | collective-permute-done | bytes 110624 | tf_op jit(solution)/shard_map/ppermute | solution.py:407
  39.4 0.0 collective-permute-start.12
  39.4 0.5 collective-permute-start.20
  39.9 0.0 collective-permute-done.14.refs_2_
  39.9 2.0 %collective-permute-start.21 = (bf16[9,16,384]{2,1,0:T(8,128)(2,1)S(1)}, bf16[9,16,384]{2,1,0:T(8,128)(2,1)S(1)}, u32[]{:S(2)}, u32[]{:S(2)}) collective-permute-start(bf16[9,16,384]{2,1,0:T(8,128)(2,1)S(1)} %collective-permute-done.14.refs_2_), channel_id=1, source_target_pairs={{0,2},{1,3},{2,0},{3,1},{4,6},{5,7},{6,4},{7,5},{8,10},{9,11},{10,... | collective-permute-start | bytes 331784 | tf_op jit(solution)/shard_map/ppermute | solution.py:407
  41.9 2.8 %collective-permute-done.10.refs_3_ = bf16[9,16,384]{2,1,0:T(8,128)(2,1)S(1)} collective-permute-done((bf16[9,16,384]{2,1,0:T(8,128)(2,1)S(1)}, bf16[9,16,384]{2,1,0:T(8,128)(2,1)S(1)}, u32[]{:S(2)}, u32[]{:S(2)}) %collective-permute-start.10) | collective-permute-done | bytes 110624 | tf_op jit(solution)/shard_map/ppermute | solution.py:407
  44.7 0.5 collective-permute-done.12.refs_2_
  45.2 0.0 collective-permute-start.17
  45.3 0.5 collective-permute-start.19
  45.8 0.4 collective-permute-start.13
  46.2 0.2 collective-permute-done.21.refs_3_
  46.4 0.5 collective-permute-start.23
  46.9 1.7 %shard_map.80 = (bf16[3,9,128,128]{3,2,1,0:T(8,128)(2,1)}, bf16[3,9,128,256]{3,2,1,0:T(8,128)(2,1)}) custom-call(bf16[9,16,384]{2,1,0:T(8,128)(2,1)S(1)} %shard_map.79.refs_0_, bf16[9,16,384]{2,1,0:T(8,128)(2,1)S(1)} %collective-permute-done.11.refs_1_, bf16[9,16,384]{2,1,0:T(8,128)(2,1)S(1)} %collective-permute-done.14.refs_2_, ...), custom_call_target="tpu_custom_call" | custom-call | bytes 10000 | tf_op jit(solution)/shard_map/pallas_call | solution.py:386
  48.6 2.2 %collective-permute-done.13.refs_6_ = bf16[9,16,384]{2,1,0:T(8,128)(2,1)S(1)} collective-permute-done((bf16[9,16,384]{2,1,0:T(8,128)(2,1)S(1)}, bf16[9,16,384]{2,1,0:T(8,128)(2,1)S(1)}, u32[]{:S(2)}, u32[]{:S(2)}) %collective-permute-start.13) | collective-permute-done | bytes 110624 | tf_op jit(solution)/shard_map/ppermute | solution.py:407
  50.8 0.0 collective-permute-done.22.refs_4_
  50.8 1.3 %collective-permute-done.24.refs_7_ = bf16[9,16,384]{2,1,0:T(8,128)(2,1)S(1)} collective-permute-done((bf16[9,16,384]{2,1,0:T(8,128)(2,1)S(1)}, bf16[9,16,384]{2,1,0:T(8,128)(2,1)S(1)}, u32[]{:S(2)}, u32[]{:S(2)}) %collective-permute-start.24) | collective-permute-done | bytes 110624 | tf_op jit(solution)/shard_map/ppermute | solution.py:407
  52.1 1.1 %shard_map.81 = (bf16[3,9,128,128]{3,2,1,0:T(8,128)(2,1)}, bf16[3,9,128,256]{3,2,1,0:T(8,128)(2,1)}) custom-call(bf16[3,9,128,128]{3,2,1,0:T(8,128)(2,1)} %get-tuple-element.64.refs_0_, bf16[3,9,128,256]{3,2,1,0:T(8,128)(2,1)} %get-tuple-element.65.refs_1_, ...), custom_call_target="tpu_custom_call", output_to_operand_aliasing={{0}: (0, {}), {1}: (1, {})} | custom-call | bytes 10000 | tf_op jit(solution)/shard_map/pallas_call | solution.py:386
  (18 shorter events, 0.0 us)
Async XLA Ops:
  0.6 12.2 %copy-start.3 = (bf16[2,4,16,256]{3,2,1,0:T(8,128)(2,1)S(1)}, bf16[2,4,16,256]{3,2,1,0:T(8,128)(2,1)}, u32[]{:S(2)}) copy-start(bf16[2,4,16,256]{3,2,1,0:T(8,128)(2,1)} %refs_1_.1) | copy-start | bytes 196612
  0.6 12.2 %copy-start.2 = (bf16[2,8,32,128]{3,2,1,0:T(8,128)(2,1)S(1)}, bf16[2,8,32,128]{3,2,1,0:T(8,128)(2,1)}, u32[]{:S(2)}) copy-start(bf16[2,8,32,128]{3,2,1,0:T(8,128)(2,1)} %refs_0_.1) | copy-start | bytes 393220
  0.7 12.2 %copy-start.1 = (bf16[3,3,3,128,128]{4,3,2,1,0:T(8,128)(2,1)S(1)}, bf16[3,3,3,128,128]{4,3,2,1,0:T(8,128)(2,1)}, u32[]{:S(2)}) copy-start(bf16[3,3,3,128,128]{4,3,2,1,0:T(8,128)(2,1)} %weight_a.1) | copy-start | bytes 2654212
  2.4 17.0 %copy-start = (bf16[3,3,3,128,256]{4,3,2,1,0:T(8,128)(2,1)S(1)}, bf16[3,3,3,128,256]{4,3,2,1,0:T(8,128)(2,1)}, u32[]{:S(2)}) copy-start(bf16[3,3,3,128,256]{4,3,2,1,0:T(8,128)(2,1)} %refs_3_.1) | copy-start | bytes 5308420
  2.5 3.1 %collective-permute-start.2 = (bf16[2,3,32,128]{3,2,1,0:T(8,128)(2,1)}, bf16[2,3,32,128]{3,2,1,0:T(8,128)(2,1)S(1)}, u32[]{:S(2)}, u32[]{:S(2)}) collective-permute-start(bf16[2,3,32,128]{3,2,1,0:T(8,128)(2,1)} %get-tuple-element.38), channel_id=1, source_target_pairs={{0,1},{1,0},{2,3},{3,2},{4,5},{5,4},{6,7},{7,6},{8,9},{9,8},{10,11... | collective-permute-start | bytes 147464 | tf_op jit(solution)/shard_map/ppermute | solution.py:407
  3.0 8.3 %collective-permute-start.1 = (bf16[2,12,32,128]{3,2,1,0:T(8,128)(2,1)}, bf16[2,12,32,128]{3,2,1,0:T(8,128)(2,1)S(1)}, u32[]{:S(2)}, u32[]{:S(2)}) collective-permute-start(bf16[2,12,32,128]{3,2,1,0:T(8,128)(2,1)} %get-tuple-element.37), channel_id=1, source_target_pairs={{0,2},{1,3},{2,0},{3,1},{4,6},{5,7},{6,4},{7,5},{8,10},{9,11},{10,... | collective-permute-start | bytes 589832 | tf_op jit(solution)/shard_map/ppermute | solution.py:407
  6.4 0.7 %collective-permute-start.3 = (bf16[2,3,32,128]{3,2,1,0:T(8,128)(2,1)S(1)}, bf16[2,3,32,128]{3,2,1,0:T(8,128)(2,1)S(1)}, u32[]{:S(2)}, u32[]{:S(2)}) collective-permute-start(bf16[2,3,32,128]{3,2,1,0:T(8,128)(2,1)S(1)} %broadcast_select_fusion), channel_id=1, source_target_pairs={{2,6},{3,4},{4,3},{5,1},{6,10},{7,8},{8,7},{9,5},{10,14},{11,12},{... | collective-permute-start | bytes 147464 | tf_op jit(solution)/shard_map/ppermute | solution.py:407
  7.0 5.8 %collective-permute-start = (bf16[2,12,32,128]{3,2,1,0:T(8,128)(2,1)}, bf16[2,12,32,128]{3,2,1,0:T(8,128)(2,1)S(1)}, u32[]{:S(2)}, u32[]{:S(2)}) collective-permute-start(bf16[2,12,32,128]{3,2,1,0:T(8,128)(2,1)} %get-tuple-element.37), channel_id=1, source_target_pairs={{0,1},{1,0},{2,3},{3,2},{4,5},{5,4},{6,7},{7,6},{8,9},{9,8},{10,11... | collective-permute-start | bytes 589832 | tf_op jit(solution)/shard_map/ppermute | solution.py:407
  11.3 1.5 %collective-permute-start.4 = (bf16[2,12,32,128]{3,2,1,0:T(8,128)(2,1)S(1)}, bf16[2,12,32,128]{3,2,1,0:T(8,128)(2,1)S(1)}, u32[]{:S(2)}, u32[]{:S(2)}) collective-permute-start(bf16[2,12,32,128]{3,2,1,0:T(8,128)(2,1)S(1)} %collective-permute-done.1.refs_3_), channel_id=1, source_target_pairs={{0,1},{1,0},{2,3},{3,2},{4,5},{5,4},{6,7},{7,6},{8,9},{9,8},{10,11... | collective-permute-start | bytes 589832 | tf_op jit(solution)/shard_map/ppermute | solution.py:407
  11.3 1.5 %collective-permute-start.5 = (bf16[2,3,32,128]{3,2,1,0:T(8,128)(2,1)S(1)}, bf16[2,3,32,128]{3,2,1,0:T(8,128)(2,1)S(1)}, u32[]{:S(2)}, u32[]{:S(2)}) collective-permute-start(bf16[2,3,32,128]{3,2,1,0:T(8,128)(2,1)S(1)} %collective-permute-done.3.refs_5_), channel_id=1, source_target_pairs={{0,1},{1,0},{2,3},{3,2},{4,5},{5,4},{6,7},{7,6},{8,9},{9,8},{10,11... | collective-permute-start | bytes 147464 | tf_op jit(solution)/shard_map/ppermute | solution.py:407
  15.2 10.7 %collective-permute-start.6 = (bf16[9,16,256]{2,1,0:T(8,128)(2,1)S(1)}, bf16[9,16,256]{2,1,0:T(8,128)(2,1)S(1)}, u32[]{:S(2)}, u32[]{:S(2)}) collective-permute-start(bf16[9,16,256]{2,1,0:T(8,128)(2,1)S(1)} %get-tuple-element.54), channel_id=1, source_target_pairs={{0,8},{1,9},{2,10},{3,11},{4,12},{5,13},{6,14},{7,15},{8,0},{9,1},... | collective-permute-start | bytes 221192 | tf_op jit(solution)/shard_map/ppermute | solution.py:407
  22.0 7.8 %collective-permute-start.8 = (bf16[9,16,384]{2,1,0:T(8,128)(2,1)S(1)}, bf16[9,16,384]{2,1,0:T(8,128)(2,1)S(1)}, u32[]{:S(2)}, u32[]{:S(2)}) collective-permute-start(bf16[9,16,384]{2,1,0:T(8,128)(2,1)S(1)} %get-tuple-element.59), channel_id=1, source_target_pairs={{0,4},{1,5},{2,6},{3,7},{4,8},{5,9},{6,10},{7,11},{8,12},{9,13},{1... | collective-permute-start | bytes 331784 | tf_op jit(solution)/shard_map/ppermute | solution.py:407
  23.6 7.4 %collective-permute-start.9 = (bf16[9,16,384]{2,1,0:T(8,128)(2,1)S(1)}, bf16[9,16,384]{2,1,0:T(8,128)(2,1)S(1)}, u32[]{:S(2)}, u32[]{:S(2)}) collective-permute-start(bf16[9,16,384]{2,1,0:T(8,128)(2,1)S(1)} %get-tuple-element.60), channel_id=1, source_target_pairs={{0,12},{1,13},{2,14},{3,15},{4,0},{5,1},{6,2},{7,3},{8,4},{9,5},{1... | collective-permute-start | bytes 331784 | tf_op jit(solution)/shard_map/ppermute | solution.py:407
  25.9 5.7 %collective-permute-start.7 = (bf16[9,16,128]{2,1,0:T(8,128)(2,1)S(1)}, bf16[9,16,128]{2,1,0:T(8,128)(2,1)S(1)}, u32[]{:S(2)}, u32[]{:S(2)}) collective-permute-start(bf16[9,16,128]{2,1,0:T(8,128)(2,1)S(1)} %get-tuple-element.56), channel_id=1, source_target_pairs={{0,8},{1,9},{2,10},{3,11},{4,12},{5,13},{6,14},{7,15},{8,0},{9,1},... | collective-permute-start | bytes 110600 | tf_op jit(solution)/shard_map/ppermute | solution.py:407
  31.7 7.7 %collective-permute-start.11 = (bf16[9,16,384]{2,1,0:T(8,128)(2,1)S(1)}, bf16[9,16,384]{2,1,0:T(8,128)(2,1)S(1)}, u32[]{:S(2)}, u32[]{:S(2)}) collective-permute-start(bf16[9,16,384]{2,1,0:T(8,128)(2,1)S(1)} %shard_map.79.refs_0_), channel_id=1, source_target_pairs={{0,4},{1,5},{2,6},{3,7},{4,8},{5,9},{6,10},{7,11},{8,12},{9,13},{1... | collective-permute-start | bytes 331784 | tf_op jit(solution)/shard_map/ppermute | solution.py:407
  32.7 6.7 %collective-permute-start.15 = (bf16[9,16,384]{2,1,0:T(8,128)(2,1)S(1)}, bf16[9,16,384]{2,1,0:T(8,128)(2,1)S(1)}, u32[]{:S(2)}, u32[]{:S(2)}) collective-permute-start(bf16[9,16,384]{2,1,0:T(8,128)(2,1)S(1)} %shard_map.79.refs_0_), channel_id=1, source_target_pairs={{0,2},{1,3},{2,0},{3,1},{4,6},{5,7},{6,4},{7,5},{8,10},{9,11},{10,... | collective-permute-start | bytes 331784 | tf_op jit(solution)/shard_map/ppermute | solution.py:407
  33.7 6.2 %collective-permute-start.14 = (bf16[9,16,384]{2,1,0:T(8,128)(2,1)S(1)}, bf16[9,16,384]{2,1,0:T(8,128)(2,1)S(1)}, u32[]{:S(2)}, u32[]{:S(2)}) collective-permute-start(bf16[9,16,384]{2,1,0:T(8,128)(2,1)S(1)} %shard_map.79.refs_0_), channel_id=1, source_target_pairs={{0,12},{1,13},{2,14},{3,15},{4,0},{5,1},{6,2},{7,3},{8,4},{9,5},{1... | collective-permute-start | bytes 331784 | tf_op jit(solution)/shard_map/ppermute | solution.py:407
  36.0 8.7 %collective-permute-start.10 = (bf16[9,16,384]{2,1,0:T(8,128)(2,1)S(1)}, bf16[9,16,384]{2,1,0:T(8,128)(2,1)S(1)}, u32[]{:S(2)}, u32[]{:S(2)}) collective-permute-start(bf16[9,16,384]{2,1,0:T(8,128)(2,1)S(1)} %shard_map.79.refs_0_), channel_id=1, source_target_pairs={{0,8},{1,9},{2,10},{3,11},{4,12},{5,13},{6,14},{7,15},{8,0},{9,1},... | collective-permute-start | bytes 331784 | tf_op jit(solution)/shard_map/ppermute | solution.py:407
  39.4 5.8 %collective-permute-start.12 = (bf16[9,16,384]{2,1,0:T(8,128)(2,1)S(1)}, bf16[9,16,384]{2,1,0:T(8,128)(2,1)S(1)}, u32[]{:S(2)}, u32[]{:S(2)}) collective-permute-start(bf16[9,16,384]{2,1,0:T(8,128)(2,1)S(1)} %collective-permute-done.11.refs_1_), channel_id=1, source_target_pairs={{0,2},{1,3},{2,0},{3,1},{4,6},{5,7},{6,4},{7,5},{8,10},{9,11},{10,... | collective-permute-start | bytes 331784 | tf_op jit(solution)/shard_map/ppermute | solution.py:407
  39.4 5.9 %collective-permute-start.16 = (bf16[9,16,384]{2,1,0:T(8,128)(2,1)S(1)}, bf16[9,16,384]{2,1,0:T(8,128)(2,1)S(1)}, u32[]{:S(2)}, u32[]{:S(2)}) collective-permute-start(bf16[9,16,384]{2,1,0:T(8,128)(2,1)S(1)} %shard_map.79.refs_0_), channel_id=1, source_target_pairs={{0,1},{1,0},{2,3},{3,2},{4,5},{5,4},{6,7},{7,6},{8,9},{9,8},{10,11... | collective-permute-start | bytes 331784 | tf_op jit(solution)/shard_map/ppermute | solution.py:407
  39.4 6.3 %collective-permute-start.20 = (bf16[9,16,384]{2,1,0:T(8,128)(2,1)S(1)}, bf16[9,16,384]{2,1,0:T(8,128)(2,1)S(1)}, u32[]{:S(2)}, u32[]{:S(2)}) collective-permute-start(bf16[9,16,384]{2,1,0:T(8,128)(2,1)S(1)} %collective-permute-done.15.refs_4_), channel_id=1, source_target_pairs={{0,1},{1,0},{2,3},{3,2},{4,5},{5,4},{6,7},{7,6},{8,9},{9,8},{10,11... | collective-permute-start | bytes 331784 | tf_op jit(solution)/shard_map/ppermute | solution.py:407
  39.9 6.5 %collective-permute-start.21 = (bf16[9,16,384]{2,1,0:T(8,128)(2,1)S(1)}, bf16[9,16,384]{2,1,0:T(8,128)(2,1)S(1)}, u32[]{:S(2)}, u32[]{:S(2)}) collective-permute-start(bf16[9,16,384]{2,1,0:T(8,128)(2,1)S(1)} %collective-permute-done.14.refs_2_), channel_id=1, source_target_pairs={{0,2},{1,3},{2,0},{3,1},{4,6},{5,7},{6,4},{7,5},{8,10},{9,11},{10,... | collective-permute-start | bytes 331784 | tf_op jit(solution)/shard_map/ppermute | solution.py:407
  44.7 1.7 %collective-permute-start.18 = (bf16[9,16,384]{2,1,0:T(8,128)(2,1)S(1)}, bf16[9,16,384]{2,1,0:T(8,128)(2,1)S(1)}, u32[]{:S(2)}, u32[]{:S(2)}) collective-permute-start(bf16[9,16,384]{2,1,0:T(8,128)(2,1)S(1)} %collective-permute-done.14.refs_2_), channel_id=1, source_target_pairs={{0,1},{1,0},{2,3},{3,2},{4,5},{5,4},{6,7},{7,6},{8,9},{9,8},{10,11... | collective-permute-start | bytes 331784 | tf_op jit(solution)/shard_map/ppermute | solution.py:407
  45.2 1.7 %collective-permute-start.17 = (bf16[9,16,384]{2,1,0:T(8,128)(2,1)S(1)}, bf16[9,16,384]{2,1,0:T(8,128)(2,1)S(1)}, u32[]{:S(2)}, u32[]{:S(2)}) collective-permute-start(bf16[9,16,384]{2,1,0:T(8,128)(2,1)S(1)} %collective-permute-done.11.refs_1_), channel_id=1, source_target_pairs={{0,1},{1,0},{2,3},{3,2},{4,5},{5,4},{6,7},{7,6},{8,9},{9,8},{10,11... | collective-permute-start | bytes 331784 | tf_op jit(solution)/shard_map/ppermute | solution.py:407
  45.3 1.7 %collective-permute-start.19 = (bf16[9,16,384]{2,1,0:T(8,128)(2,1)S(1)}, bf16[9,16,384]{2,1,0:T(8,128)(2,1)S(1)}, u32[]{:S(2)}, u32[]{:S(2)}) collective-permute-start(bf16[9,16,384]{2,1,0:T(8,128)(2,1)S(1)} %collective-permute-done.10.refs_3_), channel_id=1, source_target_pairs={{0,1},{1,0},{2,3},{3,2},{4,5},{5,4},{6,7},{7,6},{8,9},{9,8},{10,11... | collective-permute-start | bytes 331784 | tf_op jit(solution)/shard_map/ppermute | solution.py:407
  45.8 5.0 %collective-permute-start.13 = (bf16[9,16,384]{2,1,0:T(8,128)(2,1)S(1)}, bf16[9,16,384]{2,1,0:T(8,128)(2,1)S(1)}, u32[]{:S(2)}, u32[]{:S(2)}) collective-permute-start(bf16[9,16,384]{2,1,0:T(8,128)(2,1)S(1)} %collective-permute-done.10.refs_3_), channel_id=1, source_target_pairs={{0,2},{1,3},{2,0},{3,1},{4,6},{5,7},{6,4},{7,5},{8,10},{9,11},{10,... | collective-permute-start | bytes 331784 | tf_op jit(solution)/shard_map/ppermute | solution.py:407
  46.4 4.4 %collective-permute-start.22 = (bf16[9,16,384]{2,1,0:T(8,128)(2,1)S(1)}, bf16[9,16,384]{2,1,0:T(8,128)(2,1)S(1)}, u32[]{:S(2)}, u32[]{:S(2)}) collective-permute-start(bf16[9,16,384]{2,1,0:T(8,128)(2,1)S(1)} %collective-permute-done.12.refs_2_), channel_id=1, source_target_pairs={{0,1},{1,0},{2,3},{3,2},{4,5},{5,4},{6,7},{7,6},{8,9},{9,8},{10,11... | collective-permute-start | bytes 331784 | tf_op jit(solution)/shard_map/ppermute | solution.py:407
  46.4 4.4 %collective-permute-start.23 = (bf16[9,16,384]{2,1,0:T(8,128)(2,1)S(1)}, bf16[9,16,384]{2,1,0:T(8,128)(2,1)S(1)}, u32[]{:S(2)}, u32[]{:S(2)}) collective-permute-start(bf16[9,16,384]{2,1,0:T(8,128)(2,1)S(1)} %collective-permute-done.21.refs_3_), channel_id=1, source_target_pairs={{0,1},{1,0},{2,3},{3,2},{4,5},{5,4},{6,7},{7,6},{8,9},{9,8},{10,11... | collective-permute-start | bytes 331784 | tf_op jit(solution)/shard_map/ppermute | solution.py:407
  50.8 1.3 %collective-permute-start.24 = (bf16[9,16,384]{2,1,0:T(8,128)(2,1)S(1)}, bf16[9,16,384]{2,1,0:T(8,128)(2,1)S(1)}, u32[]{:S(2)}, u32[]{:S(2)}) collective-permute-start(bf16[9,16,384]{2,1,0:T(8,128)(2,1)S(1)} %collective-permute-done.13.refs_6_), channel_id=1, source_target_pairs={{0,1},{1,0},{2,3},{3,2},{4,5},{5,4},{6,7},{7,6},{8,9},{9,8},{10,11... | collective-permute-start | bytes 331784 | tf_op jit(solution)/shard_map/ppermute | solution.py:407

commit v8 on v7

--- a/solution.py
+++ b/solution.py
@@ -547,23 +547,28 @@
         assemble,
         (shape((3, 9, chans, chans), BF16), shape((3, 9, chans, wide), BF16)),
         tuple(column.values()),
-    )
+        flops=4 * 10**9,
+    )
+
+    def append(grads, pieces):
+        ends = tuple(pieces)
+
+        def body(*refs):
+            append_kernel(ends, planes, *refs)
+
+        return call(
+            body,
+            tuple(shape(x.shape, x.dtype) for x in grads),
+            (*grads, *pieces.values()),
+            [pltpu.SemaphoreType.DMA((len(ends), 4))],
+            whole=2,
+            aliases={0: 0, 1: 1},
+        )
+
+    if tail:
+        grads = append(grads, tail)
     slow, *grads = lax.optimization_barrier((slow, *grads))
-    tail[last] = slow
-    tail[1, *last[1:]] = send(slow, swap_core)
-    ends = tuple(tail)
-
-    def append(*refs):
-        append_kernel(ends, planes, *refs)
-
-    grad_a, grad_b = call(
-        append,
-        tuple(shape(x.shape, x.dtype) for x in grads),
-        (*grads, *tail.values()),
-        [pltpu.SemaphoreType.DMA((len(ends), 4))],
-        whole=2,
-        aliases={0: 0, 1: 1},
-    )
+    grad_a, grad_b = append(grads, {last: slow, (1, *last[1:]): send(slow, swap_core)})
     return (encoded, frames_grad, grad_a.reshape(weight_a.shape), grad_b.reshape(weight_b.shape))
 
 

time: 53.5 us -> 53.1 us (level)
  waiting for transfers between devices: 19.2 us -> 18.2 us
  Pallas kernels: 11.6 us -> 12.2 us
    ppermute x25, waiting for transfers between devices: 19.2 us -> 18.2 us  [send(): return lax.ppermute(value, AXIS, pairs)]
    pallas_call x7 -> x8, Pallas kernels: 11.6 us -> 12.2 us  [call(): pl.pallas_call(body, out_shape=outs, scratch_shapes=scratch, compiler_par...]
  transfers between devices with their start and end apart: 25 -> 25, of which waited for: 11 -> 11; matrix products, arithmetic and copies ran while one was open for 2% -> 2% of each run, Pallas kernels for 12% -> 14%
where the time goes in v8:
time: 53.1 us; the launch traced here: 52.9 us
  starting transfers between devices  20.9 us (39%)
  waiting for transfers between devices  18.2 us (34%)
  Pallas kernels  12.2 us (23%)
  other arithmetic  0.81 us (2%)
  between operations  0.76 us (1%)
    ppermute x25, starting transfers between devices, send(): return lax.ppermute(value, AXIS, pairs)  20.9 us
    ppermute x25, waiting for transfers between devices, send(): return lax.ppermute(value, AXIS, pairs)  18.2 us
    pallas_call x8, Pallas kernels, call(): pl.pallas_call(body, out_shape=outs, scratch_shapes=scratch, compiler_par...  12.2 us
  transfers between devices with their start and end apart: 25, of which 11 were waited for; matrix products, arithmetic and copies ran while one was open for 2% of the time, Pallas kernels for 14%

profile of v8, /device:TPU:0, one launch (start us, length us, event | category | flops | bytes accessed | tf_op | source)
XLA Modules:
  0.0 52.9 jit_solution(2271242028572906989)
XLA Ops:
  0.7 1.8 %shard_map.75 = (bf16[2,12,32,128]{3,2,1,0:T(8,128)(2,1)}, bf16[2,3,32,128]{3,2,1,0:T(8,128)(2,1)}) custom-call(bf16[2,8,32,128]{3,2,1,0:T(8,128)(2,1)} %refs_0_.1, bf16[2,4,16,256]{3,2,1,0:T(8,128)(2,1)} %refs_1_.1), custom_call_target="tpu_custom_call" | custom-call | flops 4000000000 | bytes 10000 | tf_op jit(solution)/shard_map/pallas_call | solution.py:386
  2.4 0.0 copy-start
  2.5 0.5 collective-permute-start.2
  3.0 2.6 %collective-permute-start.1 = (bf16[2,12,32,128]{3,2,1,0:T(8,128)(2,1)}, bf16[2,12,32,128]{3,2,1,0:T(8,128)(2,1)S(1)}, u32[]{:S(2)}, u32[]{:S(2)}) collective-permute-start(bf16[2,12,32,128]{3,2,1,0:T(8,128)(2,1)} %get-tuple-element.39), channel_id=1, source_target_pairs={{0,2},{1,3},{2,0},{3,1},{4,6},{5,7},{6,4},{7,5},{8,10},{9,11},{10,... | collective-permute-start | bytes 589832 | tf_op jit(solution)/shard_map/ppermute | solution.py:407
  5.6 0.0 collective-permute-done.2
  5.6 0.8 %broadcast_select_fusion = bf16[2,3,32,128]{3,2,1,0:T(8,128)(2,1)S(1)} fusion(bf16[2,3,32,128]{3,2,1,0:T(8,128)(2,1)} %get-tuple-element.40, bf16[2,3,32,128]{3,2,1,0:T(8,128)(2,1)S(1)} %collective-permute-done.2, pred[]{:T(512)S(6)} %eq.6), kind=kLoop, calls=%fused_computation | loop fusion | flops 24576 | bytes 147457 | tf_op jit(solution)/shard_map/jit(_where)/select_n | solution.py:427
  6.4 0.7 %collective-permute-start.3 = (bf16[2,3,32,128]{3,2,1,0:T(8,128)(2,1)S(1)}, bf16[2,3,32,128]{3,2,1,0:T(8,128)(2,1)S(1)}, u32[]{:S(2)}, u32[]{:S(2)}) collective-permute-start(bf16[2,3,32,128]{3,2,1,0:T(8,128)(2,1)S(1)} %broadcast_select_fusion), channel_id=1, source_target_pairs={{2,6},{3,4},{4,3},{5,1},{6,10},{7,8},{8,7},{9,5},{10,14},{11,12},{... | collective-permute-start | bytes 147464 | tf_op jit(solution)/shard_map/ppermute | solution.py:407
  7.0 0.1 collective-permute-start
  7.1 0.0 collective-permute-done.3.refs_5_
  7.1 4.1 %collective-permute-done.1.refs_3_ = bf16[2,12,32,128]{3,2,1,0:T(8,128)(2,1)S(1)} collective-permute-done((bf16[2,12,32,128]{3,2,1,0:T(8,128)(2,1)}, bf16[2,12,32,128]{3,2,1,0:T(8,128)(2,1)S(1)}, u32[]{:S(2)}, u32[]{:S(2)}) %collective-permute-start.1) | collective-permute-done | bytes 196640 | tf_op jit(solution)/shard_map/ppermute | solution.py:407
  11.3 0.0 collective-permute-start.4
  11.3 0.5 collective-permute-start.5
  11.8 1.0 %collective-permute-done.5.refs_6_ = bf16[2,3,32,128]{3,2,1,0:T(8,128)(2,1)S(1)} collective-permute-done((bf16[2,3,32,128]{3,2,1,0:T(8,128)(2,1)S(1)}, bf16[2,3,32,128]{3,2,1,0:T(8,128)(2,1)S(1)}, u32[]{:S(2)}, u32[]{:S(2)}) %collective-permute-start.5) | collective-permute-done | bytes 49184 | tf_op jit(solution)/shard_map/ppermute | solution.py:407
  12.8 0.0 collective-permute-done.refs_2_
  12.8 0.0 collective-permute-done.4.refs_4_
  12.8 2.4 %shard_map.76 = (f32[9,16,256]{2,1,0:T(8,128)S(1)}, bf16[9,16,256]{2,1,0:T(8,128)(2,1)S(1)}, bf16[9,16,256]{2,1,0:T(8,128)(2,1)S(1)}, bf16[9,16,256]{2,1,0:T(8,1...) custom-call(bf16[2,8,32,128]{3,2,1,0:T(8,128)(2,1)S(1)} %copy-done.2, ...), custom_call_target="tpu_custom_call" | custom-call | flops 10000000 | bytes 10000 | tf_op jit(solution)/shard_map/pallas_call | solution.py:386
  15.2 4.3 %collective-permute-start.6 = (bf16[9,16,256]{2,1,0:T(8,128)(2,1)S(1)}, bf16[9,16,256]{2,1,0:T(8,128)(2,1)S(1)}, u32[]{:S(2)}, u32[]{:S(2)}) collective-permute-start(bf16[9,16,256]{2,1,0:T(8,128)(2,1)S(1)} %get-tuple-element.56), channel_id=1, source_target_pairs={{0,8},{1,9},{2,10},{3,11},{4,12},{5,13},{6,14},{7,15},{8,0},{9,1},... | collective-permute-start | bytes 221192 | tf_op jit(solution)/shard_map/ppermute | solution.py:407
  19.5 2.5 %shard_map.77 = (f32[9,16,128]{2,1,0:T(8,128)S(1)}, bf16[9,16,384]{2,1,0:T(8,128)(2,1)S(1)}, bf16[9,16,128]{2,1,0:T(8,128)(2,1)S(1)}, bf16[9,16,384]{2,1,0:T(8,128)(2,1)S(1)}, bf16[2,34,32,128]{3,2,1,0:T(8,128)(2,1)S(1)}) custom-call(bf16[2,18,16,256]{3,2,1,0:T(8,128)(2,1)S(1)} %get-tuple-element.43.refs_0_, ...), custom_call_target="tpu_custom_call" | custom-call | flops 10000000 | bytes 10000 | tf_op jit(solution)/shard_map/pallas_call | solution.py:386
  22.0 1.6 %collective-permute-start.8 = (bf16[9,16,384]{2,1,0:T(8,128)(2,1)S(1)}, bf16[9,16,384]{2,1,0:T(8,128)(2,1)S(1)}, u32[]{:S(2)}, u32[]{:S(2)}) collective-permute-start(bf16[9,16,384]{2,1,0:T(8,128)(2,1)S(1)} %get-tuple-element.61), channel_id=1, source_target_pairs={{0,4},{1,5},{2,6},{3,7},{4,8},{5,9},{6,10},{7,11},{8,12},{9,13},{1... | collective-permute-start | bytes 331784 | tf_op jit(solution)/shard_map/ppermute | solution.py:407
  23.6 2.2 %collective-permute-start.9 = (bf16[9,16,384]{2,1,0:T(8,128)(2,1)S(1)}, bf16[9,16,384]{2,1,0:T(8,128)(2,1)S(1)}, u32[]{:S(2)}, u32[]{:S(2)}) collective-permute-start(bf16[9,16,384]{2,1,0:T(8,128)(2,1)S(1)} %get-tuple-element.62), channel_id=1, source_target_pairs={{0,12},{1,13},{2,14},{3,15},{4,0},{5,1},{6,2},{7,3},{8,4},{9,5},{1... | collective-permute-start | bytes 331784 | tf_op jit(solution)/shard_map/ppermute | solution.py:407
  25.9 0.0 collective-permute-done.6.refs_3_
  25.9 2.0 %shard_map.78 = (bf16[2,4,16,256]{3,2,1,0:T(8,128)(2,1)}, bf16[2,8,32,128]{3,2,1,0:T(8,128)(2,1)}) custom-call(bf16[2,17,2,16,384]{4,3,2,1,0:T(8,128)(2,1)S(1)} %get-tuple-element.49.stacked_b, bf16[2,34,32,128]{3,2,1,0:T(8,128)(2,1)S(1)} %get-tuple-element.50.pre_grad, bf16[3,3,3,128,128]{4,3,2,1,0:T(8,128)(2,1)S(1)} %copy-done.1, ...), custom_call_target="tpu_custom_call" | custom-call | flops 10000000 | bytes 10000 | tf_op jit(solution)/shard_map/pallas_call | solution.py:386
  27.9 1.9 %collective-permute-done.8.refs_4_ = bf16[9,16,384]{2,1,0:T(8,128)(2,1)S(1)} collective-permute-done((bf16[9,16,384]{2,1,0:T(8,128)(2,1)S(1)}, bf16[9,16,384]{2,1,0:T(8,128)(2,1)S(1)}, u32[]{:S(2)}, u32[]{:S(2)}) %collective-permute-start.8) | collective-permute-done | bytes 110624 | tf_op jit(solution)/shard_map/ppermute | solution.py:407
  29.8 1.2 %collective-permute-done.9.refs_5_ = bf16[9,16,384]{2,1,0:T(8,128)(2,1)S(1)} collective-permute-done((bf16[9,16,384]{2,1,0:T(8,128)(2,1)S(1)}, bf16[9,16,384]{2,1,0:T(8,128)(2,1)S(1)}, u32[]{:S(2)}, u32[]{:S(2)}) %collective-permute-start.9) | collective-permute-done | bytes 110624 | tf_op jit(solution)/shard_map/ppermute | solution.py:407
  31.0 0.6 %collective-permute-done.7.refs_1_ = bf16[9,16,128]{2,1,0:T(8,128)(2,1)S(1)} collective-permute-done((bf16[9,16,128]{2,1,0:T(8,128)(2,1)S(1)}, bf16[9,16,128]{2,1,0:T(8,128)(2,1)S(1)}, u32[]{:S(2)}, u32[]{:S(2)}) %collective-permute-start.7) | collective-permute-done | bytes 36896 | tf_op jit(solution)/shard_map/ppermute | solution.py:407
  31.6 0.1 shard_map.79.refs_0_
  31.7 1.0 %collective-permute-start.11 = (bf16[9,16,384]{2,1,0:T(8,128)(2,1)S(1)}, bf16[9,16,384]{2,1,0:T(8,128)(2,1)S(1)}, u32[]{:S(2)}, u32[]{:S(2)}) collective-permute-start(bf16[9,16,384]{2,1,0:T(8,128)(2,1)S(1)} %shard_map.79.refs_0_), channel_id=1, source_target_pairs={{0,4},{1,5},{2,6},{3,7},{4,8},{5,9},{6,10},{7,11},{8,12},{9,13},{1... | collective-permute-start | bytes 331784 | tf_op jit(solution)/shard_map/ppermute | solution.py:407
  32.7 1.1 %collective-permute-start.15 = (bf16[9,16,384]{2,1,0:T(8,128)(2,1)S(1)}, bf16[9,16,384]{2,1,0:T(8,128)(2,1)S(1)}, u32[]{:S(2)}, u32[]{:S(2)}) collective-permute-start(bf16[9,16,384]{2,1,0:T(8,128)(2,1)S(1)} %shard_map.79.refs_0_), channel_id=1, source_target_pairs={{0,2},{1,3},{2,0},{3,1},{4,6},{5,7},{6,4},{7,5},{8,10},{9,11},{10,... | collective-permute-start | bytes 331784 | tf_op jit(solution)/shard_map/ppermute | solution.py:407
  33.7 2.3 %collective-permute-start.14 = (bf16[9,16,384]{2,1,0:T(8,128)(2,1)S(1)}, bf16[9,16,384]{2,1,0:T(8,128)(2,1)S(1)}, u32[]{:S(2)}, u32[]{:S(2)}) collective-permute-start(bf16[9,16,384]{2,1,0:T(8,128)(2,1)S(1)} %shard_map.79.refs_0_), channel_id=1, source_target_pairs={{0,12},{1,13},{2,14},{3,15},{4,0},{5,1},{6,2},{7,3},{8,4},{9,5},{1... | collective-permute-start | bytes 331784 | tf_op jit(solution)/shard_map/ppermute | solution.py:407
  36.1 3.3 %collective-permute-done.11.refs_1_ = bf16[9,16,384]{2,1,0:T(8,128)(2,1)S(1)} collective-permute-done((bf16[9,16,384]{2,1,0:T(8,128)(2,1)S(1)}, bf16[9,16,384]{2,1,0:T(8,128)(2,1)S(1)}, u32[]{:S(2)}, u32[]{:S(2)}) %collective-permute-start.11) | collective-permute-done | bytes 110624 | tf_op jit(solution)/shard_map/ppermute | solution.py:407
  39.4 0.5 collective-permute-start.20
  39.9 0.0 collective-permute-done.14.refs_2_
  39.9 2.0 %collective-permute-start.21 = (bf16[9,16,384]{2,1,0:T(8,128)(2,1)S(1)}, bf16[9,16,384]{2,1,0:T(8,128)(2,1)S(1)}, u32[]{:S(2)}, u32[]{:S(2)}) collective-permute-start(bf16[9,16,384]{2,1,0:T(8,128)(2,1)S(1)} %collective-permute-done.14.refs_2_), channel_id=1, source_target_pairs={{0,2},{1,3},{2,0},{3,1},{4,6},{5,7},{6,4},{7,5},{8,10},{9,11},{10,... | collective-permute-start | bytes 331784 | tf_op jit(solution)/shard_map/ppermute | solution.py:407
  41.9 2.8 %collective-permute-done.10.refs_3_ = bf16[9,16,384]{2,1,0:T(8,128)(2,1)S(1)} collective-permute-done((bf16[9,16,384]{2,1,0:T(8,128)(2,1)S(1)}, bf16[9,16,384]{2,1,0:T(8,128)(2,1)S(1)}, u32[]{:S(2)}, u32[]{:S(2)}) %collective-permute-start.10) | collective-permute-done | bytes 110624 | tf_op jit(solution)/shard_map/ppermute | solution.py:407
  44.7 0.5 collective-permute-done.12.refs_2_
  45.2 0.0 collective-permute-start.17
  45.3 0.5 collective-permute-start.19
  45.8 0.0 collective-permute-done.20.refs_9_
  45.8 0.4 collective-permute-start.13
  46.2 0.2 collective-permute-done.21.refs_3_
  46.4 0.5 collective-permute-start.23
  46.9 1.7 %shard_map.80 = (bf16[3,9,128,128]{3,2,1,0:T(8,128)(2,1)}, bf16[3,9,128,256]{3,2,1,0:T(8,128)(2,1)}) custom-call(bf16[9,16,384]{2,1,0:T(8,128)(2,1)S(1)} %shard_map.79.refs_0_, bf16[9,16,384]{2,1,0:T(8,128)(2,1)S(1)} %collective-permute-done.11.refs_1_, bf16[9,16,384]{2,1,0:T(8,128)(2,1)S(1)} %collective-permute-done.14.refs_2_, ...), custom_call_target="tpu_custom_call" | custom-call | flops 4000000000 | bytes 10000 | tf_op jit(solution)/shard_map/pallas_call | solution.py:386
  48.6 0.0 collective-permute-done.23.refs_5_
  48.6 0.0 collective-permute-done.22.refs_4_
  48.6 1.0 %shard_map.81 = (bf16[3,9,128,128]{3,2,1,0:T(8,128)(2,1)}, bf16[3,9,128,256]{3,2,1,0:T(8,128)(2,1)}) custom-call(bf16[3,9,128,128]{3,2,1,0:T(8,128)(2,1)} %get-tuple-element.64.refs_0_, bf16[3,9,128,256]{3,2,1,0:T(8,128)(2,1)} %get-tuple-element.65.refs_1_, ...), custom_call_target="tpu_custom_call", output_to_operand_aliasing={{0}: (0, {}), {1}: (1, {})} | custom-call | bytes 10000 | tf_op jit(solution)/shard_map/pallas_call | solution.py:386
  49.6 1.2 %collective-permute-done.13.refs_2_ = bf16[9,16,384]{2,1,0:T(8,128)(2,1)S(1)} collective-permute-done((bf16[9,16,384]{2,1,0:T(8,128)(2,1)S(1)}, bf16[9,16,384]{2,1,0:T(8,128)(2,1)S(1)}, u32[]{:S(2)}, u32[]{:S(2)}) %collective-permute-start.13) | collective-permute-done | bytes 110624 | tf_op jit(solution)/shard_map/ppermute | solution.py:407
  50.8 1.3 %collective-permute-done.24.refs_3_ = bf16[9,16,384]{2,1,0:T(8,128)(2,1)S(1)} collective-permute-done((bf16[9,16,384]{2,1,0:T(8,128)(2,1)S(1)}, bf16[9,16,384]{2,1,0:T(8,128)(2,1)S(1)}, u32[]{:S(2)}, u32[]{:S(2)}) %collective-permute-start.24) | collective-permute-done | bytes 110624 | tf_op jit(solution)/shard_map/ppermute | solution.py:407
  52.1 0.8 %shard_map.82 = (bf16[3,9,128,128]{3,2,1,0:T(8,128)(2,1)}, bf16[3,9,128,256]{3,2,1,0:T(8,128)(2,1)}) custom-call(bf16[3,9,128,128]{3,2,1,0:T(8,128)(2,1)} %get-tuple-element.69.refs_0_, bf16[3,9,128,256]{3,2,1,0:T(8,128)(2,1)} %get-tuple-element.70.refs_1_, ...), custom_call_target="tpu_custom_call", output_to_operand_aliasing={{0}: (0, {}), {1}: (1, {})} | custom-call | bytes 10000 | tf_op jit(solution)/shard_map/pallas_call | solution.py:386
  (19 shorter events, 0.0 us)
Async XLA Ops:
  0.6 12.2 %copy-start.3 = (bf16[2,4,16,256]{3,2,1,0:T(8,128)(2,1)S(1)}, bf16[2,4,16,256]{3,2,1,0:T(8,128)(2,1)}, u32[]{:S(2)}) copy-start(bf16[2,4,16,256]{3,2,1,0:T(8,128)(2,1)} %refs_1_.1) | copy-start | bytes 196612
  0.6 12.2 %copy-start.2 = (bf16[2,8,32,128]{3,2,1,0:T(8,128)(2,1)S(1)}, bf16[2,8,32,128]{3,2,1,0:T(8,128)(2,1)}, u32[]{:S(2)}) copy-start(bf16[2,8,32,128]{3,2,1,0:T(8,128)(2,1)} %refs_0_.1) | copy-start | bytes 393220
  0.7 12.2 %copy-start.1 = (bf16[3,3,3,128,128]{4,3,2,1,0:T(8,128)(2,1)S(1)}, bf16[3,3,3,128,128]{4,3,2,1,0:T(8,128)(2,1)}, u32[]{:S(2)}) copy-start(bf16[3,3,3,128,128]{4,3,2,1,0:T(8,128)(2,1)} %weight_a.1) | copy-start | bytes 2654212
  2.4 17.0 %copy-start = (bf16[3,3,3,128,256]{4,3,2,1,0:T(8,128)(2,1)S(1)}, bf16[3,3,3,128,256]{4,3,2,1,0:T(8,128)(2,1)}, u32[]{:S(2)}) copy-start(bf16[3,3,3,128,256]{4,3,2,1,0:T(8,128)(2,1)} %refs_3_.1) | copy-start | bytes 5308420
  2.5 3.1 %collective-permute-start.2 = (bf16[2,3,32,128]{3,2,1,0:T(8,128)(2,1)}, bf16[2,3,32,128]{3,2,1,0:T(8,128)(2,1)S(1)}, u32[]{:S(2)}, u32[]{:S(2)}) collective-permute-start(bf16[2,3,32,128]{3,2,1,0:T(8,128)(2,1)} %get-tuple-element.40), channel_id=1, source_target_pairs={{0,1},{1,0},{2,3},{3,2},{4,5},{5,4},{6,7},{7,6},{8,9},{9,8},{10,11... | collective-permute-start | bytes 147464 | tf_op jit(solution)/shard_map/ppermute | solution.py:407
  3.0 8.3 %collective-permute-start.1 = (bf16[2,12,32,128]{3,2,1,0:T(8,128)(2,1)}, bf16[2,12,32,128]{3,2,1,0:T(8,128)(2,1)S(1)}, u32[]{:S(2)}, u32[]{:S(2)}) collective-permute-start(bf16[2,12,32,128]{3,2,1,0:T(8,128)(2,1)} %get-tuple-element.39), channel_id=1, source_target_pairs={{0,2},{1,3},{2,0},{3,1},{4,6},{5,7},{6,4},{7,5},{8,10},{9,11},{10,... | collective-permute-start | bytes 589832 | tf_op jit(solution)/shard_map/ppermute | solution.py:407
  6.4 0.7 %collective-permute-start.3 = (bf16[2,3,32,128]{3,2,1,0:T(8,128)(2,1)S(1)}, bf16[2,3,32,128]{3,2,1,0:T(8,128)(2,1)S(1)}, u32[]{:S(2)}, u32[]{:S(2)}) collective-permute-start(bf16[2,3,32,128]{3,2,1,0:T(8,128)(2,1)S(1)} %broadcast_select_fusion), channel_id=1, source_target_pairs={{2,6},{3,4},{4,3},{5,1},{6,10},{7,8},{8,7},{9,5},{10,14},{11,12},{... | collective-permute-start | bytes 147464 | tf_op jit(solution)/shard_map/ppermute | solution.py:407
  7.0 5.8 %collective-permute-start = (bf16[2,12,32,128]{3,2,1,0:T(8,128)(2,1)}, bf16[2,12,32,128]{3,2,1,0:T(8,128)(2,1)S(1)}, u32[]{:S(2)}, u32[]{:S(2)}) collective-permute-start(bf16[2,12,32,128]{3,2,1,0:T(8,128)(2,1)} %get-tuple-element.39), channel_id=1, source_target_pairs={{0,1},{1,0},{2,3},{3,2},{4,5},{5,4},{6,7},{7,6},{8,9},{9,8},{10,11... | collective-permute-start | bytes 589832 | tf_op jit(solution)/shard_map/ppermute | solution.py:407
  11.3 1.5 %collective-permute-start.4 = (bf16[2,12,32,128]{3,2,1,0:T(8,128)(2,1)S(1)}, bf16[2,12,32,128]{3,2,1,0:T(8,128)(2,1)S(1)}, u32[]{:S(2)}, u32[]{:S(2)}) collective-permute-start(bf16[2,12,32,128]{3,2,1,0:T(8,128)(2,1)S(1)} %collective-permute-done.1.refs_3_), channel_id=1, source_target_pairs={{0,1},{1,0},{2,3},{3,2},{4,5},{5,4},{6,7},{7,6},{8,9},{9,8},{10,11... | collective-permute-start | bytes 589832 | tf_op jit(solution)/shard_map/ppermute | solution.py:407
  11.3 1.5 %collective-permute-start.5 = (bf16[2,3,32,128]{3,2,1,0:T(8,128)(2,1)S(1)}, bf16[2,3,32,128]{3,2,1,0:T(8,128)(2,1)S(1)}, u32[]{:S(2)}, u32[]{:S(2)}) collective-permute-start(bf16[2,3,32,128]{3,2,1,0:T(8,128)(2,1)S(1)} %collective-permute-done.3.refs_5_), channel_id=1, source_target_pairs={{0,1},{1,0},{2,3},{3,2},{4,5},{5,4},{6,7},{7,6},{8,9},{9,8},{10,11... | collective-permute-start | bytes 147464 | tf_op jit(solution)/shard_map/ppermute | solution.py:407
  15.2 10.7 %collective-permute-start.6 = (bf16[9,16,256]{2,1,0:T(8,128)(2,1)S(1)}, bf16[9,16,256]{2,1,0:T(8,128)(2,1)S(1)}, u32[]{:S(2)}, u32[]{:S(2)}) collective-permute-start(bf16[9,16,256]{2,1,0:T(8,128)(2,1)S(1)} %get-tuple-element.56), channel_id=1, source_target_pairs={{0,8},{1,9},{2,10},{3,11},{4,12},{5,13},{6,14},{7,15},{8,0},{9,1},... | collective-permute-start | bytes 221192 | tf_op jit(solution)/shard_map/ppermute | solution.py:407
  22.0 7.8 %collective-permute-start.8 = (bf16[9,16,384]{2,1,0:T(8,128)(2,1)S(1)}, bf16[9,16,384]{2,1,0:T(8,128)(2,1)S(1)}, u32[]{:S(2)}, u32[]{:S(2)}) collective-permute-start(bf16[9,16,384]{2,1,0:T(8,128)(2,1)S(1)} %get-tuple-element.61), channel_id=1, source_target_pairs={{0,4},{1,5},{2,6},{3,7},{4,8},{5,9},{6,10},{7,11},{8,12},{9,13},{1... | collective-permute-start | bytes 331784 | tf_op jit(solution)/shard_map/ppermute | solution.py:407
  23.6 7.4 %collective-permute-start.9 = (bf16[9,16,384]{2,1,0:T(8,128)(2,1)S(1)}, bf16[9,16,384]{2,1,0:T(8,128)(2,1)S(1)}, u32[]{:S(2)}, u32[]{:S(2)}) collective-permute-start(bf16[9,16,384]{2,1,0:T(8,128)(2,1)S(1)} %get-tuple-element.62), channel_id=1, source_target_pairs={{0,12},{1,13},{2,14},{3,15},{4,0},{5,1},{6,2},{7,3},{8,4},{9,5},{1... | collective-permute-start | bytes 331784 | tf_op jit(solution)/shard_map/ppermute | solution.py:407
  25.9 5.7 %collective-permute-start.7 = (bf16[9,16,128]{2,1,0:T(8,128)(2,1)S(1)}, bf16[9,16,128]{2,1,0:T(8,128)(2,1)S(1)}, u32[]{:S(2)}, u32[]{:S(2)}) collective-permute-start(bf16[9,16,128]{2,1,0:T(8,128)(2,1)S(1)} %get-tuple-element.58), channel_id=1, source_target_pairs={{0,8},{1,9},{2,10},{3,11},{4,12},{5,13},{6,14},{7,15},{8,0},{9,1},... | collective-permute-start | bytes 110600 | tf_op jit(solution)/shard_map/ppermute | solution.py:407
  31.7 7.7 %collective-permute-start.11 = (bf16[9,16,384]{2,1,0:T(8,128)(2,1)S(1)}, bf16[9,16,384]{2,1,0:T(8,128)(2,1)S(1)}, u32[]{:S(2)}, u32[]{:S(2)}) collective-permute-start(bf16[9,16,384]{2,1,0:T(8,128)(2,1)S(1)} %shard_map.79.refs_0_), channel_id=1, source_target_pairs={{0,4},{1,5},{2,6},{3,7},{4,8},{5,9},{6,10},{7,11},{8,12},{9,13},{1... | collective-permute-start | bytes 331784 | tf_op jit(solution)/shard_map/ppermute | solution.py:407
  32.7 6.7 %collective-permute-start.15 = (bf16[9,16,384]{2,1,0:T(8,128)(2,1)S(1)}, bf16[9,16,384]{2,1,0:T(8,128)(2,1)S(1)}, u32[]{:S(2)}, u32[]{:S(2)}) collective-permute-start(bf16[9,16,384]{2,1,0:T(8,128)(2,1)S(1)} %shard_map.79.refs_0_), channel_id=1, source_target_pairs={{0,2},{1,3},{2,0},{3,1},{4,6},{5,7},{6,4},{7,5},{8,10},{9,11},{10,... | collective-permute-start | bytes 331784 | tf_op jit(solution)/shard_map/ppermute | solution.py:407
  33.7 6.2 %collective-permute-start.14 = (bf16[9,16,384]{2,1,0:T(8,128)(2,1)S(1)}, bf16[9,16,384]{2,1,0:T(8,128)(2,1)S(1)}, u32[]{:S(2)}, u32[]{:S(2)}) collective-permute-start(bf16[9,16,384]{2,1,0:T(8,128)(2,1)S(1)} %shard_map.79.refs_0_), channel_id=1, source_target_pairs={{0,12},{1,13},{2,14},{3,15},{4,0},{5,1},{6,2},{7,3},{8,4},{9,5},{1... | collective-permute-start | bytes 331784 | tf_op jit(solution)/shard_map/ppermute | solution.py:407
  36.1 8.7 %collective-permute-start.10 = (bf16[9,16,384]{2,1,0:T(8,128)(2,1)S(1)}, bf16[9,16,384]{2,1,0:T(8,128)(2,1)S(1)}, u32[]{:S(2)}, u32[]{:S(2)}) collective-permute-start(bf16[9,16,384]{2,1,0:T(8,128)(2,1)S(1)} %shard_map.79.refs_0_), channel_id=1, source_target_pairs={{0,8},{1,9},{2,10},{3,11},{4,12},{5,13},{6,14},{7,15},{8,0},{9,1},... | collective-permute-start | bytes 331784 | tf_op jit(solution)/shard_map/ppermute | solution.py:407
  39.4 5.8 %collective-permute-start.12 = (bf16[9,16,384]{2,1,0:T(8,128)(2,1)S(1)}, bf16[9,16,384]{2,1,0:T(8,128)(2,1)S(1)}, u32[]{:S(2)}, u32[]{:S(2)}) collective-permute-start(bf16[9,16,384]{2,1,0:T(8,128)(2,1)S(1)} %collective-permute-done.11.refs_1_), channel_id=1, source_target_pairs={{0,2},{1,3},{2,0},{3,1},{4,6},{5,7},{6,4},{7,5},{8,10},{9,11},{10,... | collective-permute-start | bytes 331784 | tf_op jit(solution)/shard_map/ppermute | solution.py:407
  39.4 5.9 %collective-permute-start.16 = (bf16[9,16,384]{2,1,0:T(8,128)(2,1)S(1)}, bf16[9,16,384]{2,1,0:T(8,128)(2,1)S(1)}, u32[]{:S(2)}, u32[]{:S(2)}) collective-permute-start(bf16[9,16,384]{2,1,0:T(8,128)(2,1)S(1)} %shard_map.79.refs_0_), channel_id=1, source_target_pairs={{0,1},{1,0},{2,3},{3,2},{4,5},{5,4},{6,7},{7,6},{8,9},{9,8},{10,11... | collective-permute-start | bytes 331784 | tf_op jit(solution)/shard_map/ppermute | solution.py:407
  39.4 6.3 %collective-permute-start.20 = (bf16[9,16,384]{2,1,0:T(8,128)(2,1)S(1)}, bf16[9,16,384]{2,1,0:T(8,128)(2,1)S(1)}, u32[]{:S(2)}, u32[]{:S(2)}) collective-permute-start(bf16[9,16,384]{2,1,0:T(8,128)(2,1)S(1)} %collective-permute-done.15.refs_4_), channel_id=1, source_target_pairs={{0,1},{1,0},{2,3},{3,2},{4,5},{5,4},{6,7},{7,6},{8,9},{9,8},{10,11... | collective-permute-start | bytes 331784 | tf_op jit(solution)/shard_map/ppermute | solution.py:407
  39.9 6.5 %collective-permute-start.21 = (bf16[9,16,384]{2,1,0:T(8,128)(2,1)S(1)}, bf16[9,16,384]{2,1,0:T(8,128)(2,1)S(1)}, u32[]{:S(2)}, u32[]{:S(2)}) collective-permute-start(bf16[9,16,384]{2,1,0:T(8,128)(2,1)S(1)} %collective-permute-done.14.refs_2_), channel_id=1, source_target_pairs={{0,2},{1,3},{2,0},{3,1},{4,6},{5,7},{6,4},{7,5},{8,10},{9,11},{10,... | collective-permute-start | bytes 331784 | tf_op jit(solution)/shard_map/ppermute | solution.py:407
  44.7 1.7 %collective-permute-start.18 = (bf16[9,16,384]{2,1,0:T(8,128)(2,1)S(1)}, bf16[9,16,384]{2,1,0:T(8,128)(2,1)S(1)}, u32[]{:S(2)}, u32[]{:S(2)}) collective-permute-start(bf16[9,16,384]{2,1,0:T(8,128)(2,1)S(1)} %collective-permute-done.14.refs_2_), channel_id=1, source_target_pairs={{0,1},{1,0},{2,3},{3,2},{4,5},{5,4},{6,7},{7,6},{8,9},{9,8},{10,11... | collective-permute-start | bytes 331784 | tf_op jit(solution)/shard_map/ppermute | solution.py:407
  45.2 1.7 %collective-permute-start.17 = (bf16[9,16,384]{2,1,0:T(8,128)(2,1)S(1)}, bf16[9,16,384]{2,1,0:T(8,128)(2,1)S(1)}, u32[]{:S(2)}, u32[]{:S(2)}) collective-permute-start(bf16[9,16,384]{2,1,0:T(8,128)(2,1)S(1)} %collective-permute-done.11.refs_1_), channel_id=1, source_target_pairs={{0,1},{1,0},{2,3},{3,2},{4,5},{5,4},{6,7},{7,6},{8,9},{9,8},{10,11... | collective-permute-start | bytes 331784 | tf_op jit(solution)/shard_map/ppermute | solution.py:407
  45.3 1.7 %collective-permute-start.19 = (bf16[9,16,384]{2,1,0:T(8,128)(2,1)S(1)}, bf16[9,16,384]{2,1,0:T(8,128)(2,1)S(1)}, u32[]{:S(2)}, u32[]{:S(2)}) collective-permute-start(bf16[9,16,384]{2,1,0:T(8,128)(2,1)S(1)} %collective-permute-done.10.refs_3_), channel_id=1, source_target_pairs={{0,1},{1,0},{2,3},{3,2},{4,5},{5,4},{6,7},{7,6},{8,9},{9,8},{10,11... | collective-permute-start | bytes 331784 | tf_op jit(solution)/shard_map/ppermute | solution.py:407
  45.8 5.0 %collective-permute-start.13 = (bf16[9,16,384]{2,1,0:T(8,128)(2,1)S(1)}, bf16[9,16,384]{2,1,0:T(8,128)(2,1)S(1)}, u32[]{:S(2)}, u32[]{:S(2)}) collective-permute-start(bf16[9,16,384]{2,1,0:T(8,128)(2,1)S(1)} %collective-permute-done.10.refs_3_), channel_id=1, source_target_pairs={{0,2},{1,3},{2,0},{3,1},{4,6},{5,7},{6,4},{7,5},{8,10},{9,11},{10,... | collective-permute-start | bytes 331784 | tf_op jit(solution)/shard_map/ppermute | solution.py:407
  46.4 2.2 %collective-permute-start.22 = (bf16[9,16,384]{2,1,0:T(8,128)(2,1)S(1)}, bf16[9,16,384]{2,1,0:T(8,128)(2,1)S(1)}, u32[]{:S(2)}, u32[]{:S(2)}) collective-permute-start(bf16[9,16,384]{2,1,0:T(8,128)(2,1)S(1)} %collective-permute-done.12.refs_2_), channel_id=1, source_target_pairs={{0,1},{1,0},{2,3},{3,2},{4,5},{5,4},{6,7},{7,6},{8,9},{9,8},{10,11... | collective-permute-start | bytes 331784 | tf_op jit(solution)/shard_map/ppermute | solution.py:407
  46.4 2.2 %collective-permute-start.23 = (bf16[9,16,384]{2,1,0:T(8,128)(2,1)S(1)}, bf16[9,16,384]{2,1,0:T(8,128)(2,1)S(1)}, u32[]{:S(2)}, u32[]{:S(2)}) collective-permute-start(bf16[9,16,384]{2,1,0:T(8,128)(2,1)S(1)} %collective-permute-done.21.refs_3_), channel_id=1, source_target_pairs={{0,1},{1,0},{2,3},{3,2},{4,5},{5,4},{6,7},{7,6},{8,9},{9,8},{10,11... | collective-permute-start | bytes 331784 | tf_op jit(solution)/shard_map/ppermute | solution.py:407
  50.8 1.3 %collective-permute-start.24 = (bf16[9,16,384]{2,1,0:T(8,128)(2,1)S(1)}, bf16[9,16,384]{2,1,0:T(8,128)(2,1)S(1)}, u32[]{:S(2)}, u32[]{:S(2)}) collective-permute-start(bf16[9,16,384]{2,1,0:T(8,128)(2,1)S(1)} %collective-permute-done.13.refs_2_), channel_id=1, source_target_pairs={{0,1},{1,0},{2,3},{3,2},{4,5},{5,4},{6,7},{7,6},{8,9},{9,8},{10,11... | collective-permute-start | bytes 331784 | tf_op jit(solution)/shard_map/ppermute | solution.py:407

commit v9 on v8

--- a/solution.py
+++ b/solution.py
@@ -518,7 +518,7 @@
     piece = shape((9, part // planes, chans + wide), BF16)
     (own,) = call(finish, (piece,), (*alone_a, *alone_b, *both))
     column = {(0, 0, 0): own}
-    order = sorted(range(1, planes), key=lambda step: min(step, planes - step))
+    order = sorted(range(planes - 1, 0, -1), key=lambda step: min(step, planes - step))
     for step in order[:-1]:
         column[0, 0, step] = send(own, rotations[step])
     if planes == 1:

time: 53.1 us -> 53 us (level)
  no operation moved by 1% of the time
where the time goes in v9:
time: 53 us; the launch traced here: 52.8 us
  starting transfers between devices  20.9 us (39%)
  waiting for transfers between devices  18.1 us (34%)
  Pallas kernels  12.2 us (23%)
  other arithmetic  0.81 us (2%)
  between operations  0.76 us (1%)
    ppermute x25, starting transfers between devices, send(): return lax.ppermute(value, AXIS, pairs)  20.9 us
    ppermute x25, waiting for transfers between devices, send(): return lax.ppermute(value, AXIS, pairs)  18.1 us
    pallas_call x8, Pallas kernels, call(): pl.pallas_call(body, out_shape=outs, scratch_shapes=scratch, compiler_par...  12.2 us
  transfers between devices with their start and end apart: 25, of which 11 were waited for; matrix products, arithmetic and copies ran while one was open for 2% of the time, Pallas kernels for 14%

profile of v9, /device:TPU:0, one launch (start us, length us, event | category | flops | bytes accessed | tf_op | source)
XLA Modules:
  0.0 52.8 jit_solution(17105752253434470769)
XLA Ops:
  0.7 1.8 %shard_map.75 = (bf16[2,12,32,128]{3,2,1,0:T(8,128)(2,1)}, bf16[2,3,32,128]{3,2,1,0:T(8,128)(2,1)}) custom-call(bf16[2,8,32,128]{3,2,1,0:T(8,128)(2,1)} %refs_0_.1, bf16[2,4,16,256]{3,2,1,0:T(8,128)(2,1)} %refs_1_.1), custom_call_target="tpu_custom_call" | custom-call | flops 4000000000 | bytes 10000 | tf_op jit(solution)/shard_map/pallas_call | solution.py:386
  2.4 0.0 copy-start
  2.5 0.5 collective-permute-start.2
  3.0 2.6 %collective-permute-start.1 = (bf16[2,12,32,128]{3,2,1,0:T(8,128)(2,1)}, bf16[2,12,32,128]{3,2,1,0:T(8,128)(2,1)S(1)}, u32[]{:S(2)}, u32[]{:S(2)}) collective-permute-start(bf16[2,12,32,128]{3,2,1,0:T(8,128)(2,1)} %get-tuple-element.39), channel_id=1, source_target_pairs={{0,2},{1,3},{2,0},{3,1},{4,6},{5,7},{6,4},{7,5},{8,10},{9,11},{10,... | collective-permute-start | bytes 589832 | tf_op jit(solution)/shard_map/ppermute | solution.py:407
  5.6 0.8 %broadcast_select_fusion = bf16[2,3,32,128]{3,2,1,0:T(8,128)(2,1)S(1)} fusion(bf16[2,3,32,128]{3,2,1,0:T(8,128)(2,1)} %get-tuple-element.40, bf16[2,3,32,128]{3,2,1,0:T(8,128)(2,1)S(1)} %collective-permute-done.2, pred[]{:T(512)S(6)} %eq.6), kind=kLoop, calls=%fused_computation | loop fusion | flops 24576 | bytes 147457 | tf_op jit(solution)/shard_map/jit(_where)/select_n | solution.py:427
  6.4 0.7 %collective-permute-start.3 = (bf16[2,3,32,128]{3,2,1,0:T(8,128)(2,1)S(1)}, bf16[2,3,32,128]{3,2,1,0:T(8,128)(2,1)S(1)}, u32[]{:S(2)}, u32[]{:S(2)}) collective-permute-start(bf16[2,3,32,128]{3,2,1,0:T(8,128)(2,1)S(1)} %broadcast_select_fusion), channel_id=1, source_target_pairs={{2,6},{3,4},{4,3},{5,1},{6,10},{7,8},{8,7},{9,5},{10,14},{11,12},{... | collective-permute-start | bytes 147464 | tf_op jit(solution)/shard_map/ppermute | solution.py:407
  7.0 0.1 collective-permute-start
  7.1 0.0 collective-permute-done.3.refs_5_
  7.1 4.1 %collective-permute-done.1.refs_3_ = bf16[2,12,32,128]{3,2,1,0:T(8,128)(2,1)S(1)} collective-permute-done((bf16[2,12,32,128]{3,2,1,0:T(8,128)(2,1)}, bf16[2,12,32,128]{3,2,1,0:T(8,128)(2,1)S(1)}, u32[]{:S(2)}, u32[]{:S(2)}) %collective-permute-start.1) | collective-permute-done | bytes 196640 | tf_op jit(solution)/shard_map/ppermute | solution.py:407
  11.3 0.5 collective-permute-start.5
  11.8 1.0 %collective-permute-done.5.refs_6_ = bf16[2,3,32,128]{3,2,1,0:T(8,128)(2,1)S(1)} collective-permute-done((bf16[2,3,32,128]{3,2,1,0:T(8,128)(2,1)S(1)}, bf16[2,3,32,128]{3,2,1,0:T(8,128)(2,1)S(1)}, u32[]{:S(2)}, u32[]{:S(2)}) %collective-permute-start.5) | collective-permute-done | bytes 49184 | tf_op jit(solution)/shard_map/ppermute | solution.py:407
  12.8 0.0 collective-permute-done.refs_2_
  12.8 0.0 collective-permute-done.4.refs_4_
  12.8 2.4 %shard_map.76 = (f32[9,16,256]{2,1,0:T(8,128)S(1)}, bf16[9,16,256]{2,1,0:T(8,128)(2,1)S(1)}, bf16[9,16,256]{2,1,0:T(8,128)(2,1)S(1)}, bf16[9,16,256]{2,1,0:T(8,1...) custom-call(bf16[2,8,32,128]{3,2,1,0:T(8,128)(2,1)S(1)} %copy-done.2, ...), custom_call_target="tpu_custom_call" | custom-call | flops 10000000 | bytes 10000 | tf_op jit(solution)/shard_map/pallas_call | solution.py:386
  15.2 4.3 %collective-permute-start.6 = (bf16[9,16,256]{2,1,0:T(8,128)(2,1)S(1)}, bf16[9,16,256]{2,1,0:T(8,128)(2,1)S(1)}, u32[]{:S(2)}, u32[]{:S(2)}) collective-permute-start(bf16[9,16,256]{2,1,0:T(8,128)(2,1)S(1)} %get-tuple-element.56), channel_id=1, source_target_pairs={{0,8},{1,9},{2,10},{3,11},{4,12},{5,13},{6,14},{7,15},{8,0},{9,1},... | collective-permute-start | bytes 221192 | tf_op jit(solution)/shard_map/ppermute | solution.py:407
  19.5 2.5 %shard_map.77 = (f32[9,16,128]{2,1,0:T(8,128)S(1)}, bf16[9,16,384]{2,1,0:T(8,128)(2,1)S(1)}, bf16[9,16,128]{2,1,0:T(8,128)(2,1)S(1)}, bf16[9,16,384]{2,1,0:T(8,128)(2,1)S(1)}, bf16[2,34,32,128]{3,2,1,0:T(8,128)(2,1)S(1)}) custom-call(bf16[2,18,16,256]{3,2,1,0:T(8,128)(2,1)S(1)} %get-tuple-element.43.refs_0_, ...), custom_call_target="tpu_custom_call" | custom-call | flops 10000000 | bytes 10000 | tf_op jit(solution)/shard_map/pallas_call | solution.py:386
  22.0 1.6 %collective-permute-start.8 = (bf16[9,16,384]{2,1,0:T(8,128)(2,1)S(1)}, bf16[9,16,384]{2,1,0:T(8,128)(2,1)S(1)}, u32[]{:S(2)}, u32[]{:S(2)}) collective-permute-start(bf16[9,16,384]{2,1,0:T(8,128)(2,1)S(1)} %get-tuple-element.61), channel_id=1, source_target_pairs={{0,4},{1,5},{2,6},{3,7},{4,8},{5,9},{6,10},{7,11},{8,12},{9,13},{1... | collective-permute-start | bytes 331784 | tf_op jit(solution)/shard_map/ppermute | solution.py:407
  23.6 2.2 %collective-permute-start.9 = (bf16[9,16,384]{2,1,0:T(8,128)(2,1)S(1)}, bf16[9,16,384]{2,1,0:T(8,128)(2,1)S(1)}, u32[]{:S(2)}, u32[]{:S(2)}) collective-permute-start(bf16[9,16,384]{2,1,0:T(8,128)(2,1)S(1)} %get-tuple-element.62), channel_id=1, source_target_pairs={{0,12},{1,13},{2,14},{3,15},{4,0},{5,1},{6,2},{7,3},{8,4},{9,5},{1... | collective-permute-start | bytes 331784 | tf_op jit(solution)/shard_map/ppermute | solution.py:407
  25.9 0.0 collective-permute-done.6.refs_3_
  25.9 0.0 collective-permute-start.7
  25.9 2.0 %shard_map.78 = (bf16[2,4,16,256]{3,2,1,0:T(8,128)(2,1)}, bf16[2,8,32,128]{3,2,1,0:T(8,128)(2,1)}) custom-call(bf16[2,17,2,16,384]{4,3,2,1,0:T(8,128)(2,1)S(1)} %get-tuple-element.49.stacked_b, bf16[2,34,32,128]{3,2,1,0:T(8,128)(2,1)S(1)} %get-tuple-element.50.pre_grad, bf16[3,3,3,128,128]{4,3,2,1,0:T(8,128)(2,1)S(1)} %copy-done.1, ...), custom_call_target="tpu_custom_call" | custom-call | flops 10000000 | bytes 10000 | tf_op jit(solution)/shard_map/pallas_call | solution.py:386
  27.9 1.9 %collective-permute-done.8.refs_4_ = bf16[9,16,384]{2,1,0:T(8,128)(2,1)S(1)} collective-permute-done((bf16[9,16,384]{2,1,0:T(8,128)(2,1)S(1)}, bf16[9,16,384]{2,1,0:T(8,128)(2,1)S(1)}, u32[]{:S(2)}, u32[]{:S(2)}) %collective-permute-start.8) | collective-permute-done | bytes 110624 | tf_op jit(solution)/shard_map/ppermute | solution.py:407
  29.8 1.2 %collective-permute-done.9.refs_5_ = bf16[9,16,384]{2,1,0:T(8,128)(2,1)S(1)} collective-permute-done((bf16[9,16,384]{2,1,0:T(8,128)(2,1)S(1)}, bf16[9,16,384]{2,1,0:T(8,128)(2,1)S(1)}, u32[]{:S(2)}, u32[]{:S(2)}) %collective-permute-start.9) | collective-permute-done | bytes 110624 | tf_op jit(solution)/shard_map/ppermute | solution.py:407
  31.0 0.6 %collective-permute-done.7.refs_1_ = bf16[9,16,128]{2,1,0:T(8,128)(2,1)S(1)} collective-permute-done((bf16[9,16,128]{2,1,0:T(8,128)(2,1)S(1)}, bf16[9,16,128]{2,1,0:T(8,128)(2,1)S(1)}, u32[]{:S(2)}, u32[]{:S(2)}) %collective-permute-start.7) | collective-permute-done | bytes 36896 | tf_op jit(solution)/shard_map/ppermute | solution.py:407
  31.6 0.1 shard_map.79.refs_0_
  31.7 2.7 %collective-permute-start.11 = (bf16[9,16,384]{2,1,0:T(8,128)(2,1)S(1)}, bf16[9,16,384]{2,1,0:T(8,128)(2,1)S(1)}, u32[]{:S(2)}, u32[]{:S(2)}) collective-permute-start(bf16[9,16,384]{2,1,0:T(8,128)(2,1)S(1)} %shard_map.79.refs_0_), channel_id=1, source_target_pairs={{0,12},{1,13},{2,14},{3,15},{4,0},{5,1},{6,2},{7,3},{8,4},{9,5},{1... | collective-permute-start | bytes 331784 | tf_op jit(solution)/shard_map/ppermute | solution.py:407
  34.4 0.3 collective-permute-start.15
  34.7 0.8 %collective-permute-start.10 = (bf16[9,16,384]{2,1,0:T(8,128)(2,1)S(1)}, bf16[9,16,384]{2,1,0:T(8,128)(2,1)S(1)}, u32[]{:S(2)}, u32[]{:S(2)}) collective-permute-start(bf16[9,16,384]{2,1,0:T(8,128)(2,1)S(1)} %shard_map.79.refs_0_), channel_id=1, source_target_pairs={{0,8},{1,9},{2,10},{3,11},{4,12},{5,13},{6,14},{7,15},{8,0},{9,1},... | collective-permute-start | bytes 331784 | tf_op jit(solution)/shard_map/ppermute | solution.py:407
  35.5 2.3 %collective-permute-done.11.refs_1_ = bf16[9,16,384]{2,1,0:T(8,128)(2,1)S(1)} collective-permute-done((bf16[9,16,384]{2,1,0:T(8,128)(2,1)S(1)}, bf16[9,16,384]{2,1,0:T(8,128)(2,1)S(1)}, u32[]{:S(2)}, u32[]{:S(2)}) %collective-permute-start.11) | collective-permute-done | bytes 110624 | tf_op jit(solution)/shard_map/ppermute | solution.py:407
  37.8 1.8 %collective-permute-done.15.refs_4_ = bf16[9,16,384]{2,1,0:T(8,128)(2,1)S(1)} collective-permute-done((bf16[9,16,384]{2,1,0:T(8,128)(2,1)S(1)}, bf16[9,16,384]{2,1,0:T(8,128)(2,1)S(1)}, u32[]{:S(2)}, u32[]{:S(2)}) %collective-permute-start.15) | collective-permute-done | bytes 110624 | tf_op jit(solution)/shard_map/ppermute | solution.py:407
  39.7 2.5 %collective-permute-done.14.refs_2_ = bf16[9,16,384]{2,1,0:T(8,128)(2,1)S(1)} collective-permute-done((bf16[9,16,384]{2,1,0:T(8,128)(2,1)S(1)}, bf16[9,16,384]{2,1,0:T(8,128)(2,1)S(1)}, u32[]{:S(2)}, u32[]{:S(2)}) %collective-permute-start.14) | collective-permute-done | bytes 110624 | tf_op jit(solution)/shard_map/ppermute | solution.py:407
  42.2 1.7 %collective-permute-start.21 = (bf16[9,16,384]{2,1,0:T(8,128)(2,1)S(1)}, bf16[9,16,384]{2,1,0:T(8,128)(2,1)S(1)}, u32[]{:S(2)}, u32[]{:S(2)}) collective-permute-start(bf16[9,16,384]{2,1,0:T(8,128)(2,1)S(1)} %collective-permute-done.14.refs_2_), channel_id=1, source_target_pairs={{0,2},{1,3},{2,0},{3,1},{4,6},{5,7},{6,4},{7,5},{8,10},{9,11},{10,... | collective-permute-start | bytes 331784 | tf_op jit(solution)/shard_map/ppermute | solution.py:407
  43.9 0.8 %collective-permute-done.10.refs_3_ = bf16[9,16,384]{2,1,0:T(8,128)(2,1)S(1)} collective-permute-done((bf16[9,16,384]{2,1,0:T(8,128)(2,1)S(1)}, bf16[9,16,384]{2,1,0:T(8,128)(2,1)S(1)}, u32[]{:S(2)}, u32[]{:S(2)}) %collective-permute-start.10) | collective-permute-done | bytes 110624 | tf_op jit(solution)/shard_map/ppermute | solution.py:407
  44.7 0.0 collective-permute-start.18
  44.7 0.5 collective-permute-start.17
  45.3 0.1 collective-permute-start.19
  45.3 0.0 collective-permute-done.20.refs_9_
  45.3 1.7 %collective-permute-start.13 = (bf16[9,16,384]{2,1,0:T(8,128)(2,1)S(1)}, bf16[9,16,384]{2,1,0:T(8,128)(2,1)S(1)}, u32[]{:S(2)}, u32[]{:S(2)}) collective-permute-start(bf16[9,16,384]{2,1,0:T(8,128)(2,1)S(1)} %collective-permute-done.10.refs_3_), channel_id=1, source_target_pairs={{0,2},{1,3},{2,0},{3,1},{4,6},{5,7},{6,4},{7,5},{8,10},{9,11},{10,... | collective-permute-start | bytes 331784 | tf_op jit(solution)/shard_map/ppermute | solution.py:407
  47.1 0.0 collective-permute-done.21.refs_3_
  47.1 0.2 collective-permute-start.22
  47.2 0.0 collective-permute-done.18.refs_7_
  47.2 0.3 collective-permute-start.23
  47.6 0.0 collective-permute-done.17.refs_6_
  47.6 1.7 %shard_map.80 = (bf16[3,9,128,128]{3,2,1,0:T(8,128)(2,1)}, bf16[3,9,128,256]{3,2,1,0:T(8,128)(2,1)}) custom-call(bf16[9,16,384]{2,1,0:T(8,128)(2,1)S(1)} %shard_map.79.refs_0_, bf16[9,16,384]{2,1,0:T(8,128)(2,1)S(1)} %collective-permute-done.11.refs_1_, bf16[9,16,384]{2,1,0:T(8,128)(2,1)S(1)} %collective-permute-done.14.refs_2_, ...), custom_call_target="tpu_custom_call" | custom-call | flops 4000000000 | bytes 10000 | tf_op jit(solution)/shard_map/pallas_call | solution.py:386
  49.3 1.0 %shard_map.81 = (bf16[3,9,128,128]{3,2,1,0:T(8,128)(2,1)}, bf16[3,9,128,256]{3,2,1,0:T(8,128)(2,1)}) custom-call(bf16[3,9,128,128]{3,2,1,0:T(8,128)(2,1)} %get-tuple-element.64.refs_0_, bf16[3,9,128,256]{3,2,1,0:T(8,128)(2,1)} %get-tuple-element.65.refs_1_, ...), custom_call_target="tpu_custom_call", output_to_operand_aliasing={{0}: (0, {}), {1}: (1, {})} | custom-call | bytes 10000 | tf_op jit(solution)/shard_map/pallas_call | solution.py:386
  50.3 0.5 collective-permute-done.13.refs_2_
  50.7 1.3 %collective-permute-done.24.refs_3_ = bf16[9,16,384]{2,1,0:T(8,128)(2,1)S(1)} collective-permute-done((bf16[9,16,384]{2,1,0:T(8,128)(2,1)S(1)}, bf16[9,16,384]{2,1,0:T(8,128)(2,1)S(1)}, u32[]{:S(2)}, u32[]{:S(2)}) %collective-permute-start.24) | collective-permute-done | bytes 110624 | tf_op jit(solution)/shard_map/ppermute | solution.py:407
  52.1 0.8 %shard_map.82 = (bf16[3,9,128,128]{3,2,1,0:T(8,128)(2,1)}, bf16[3,9,128,256]{3,2,1,0:T(8,128)(2,1)}) custom-call(bf16[3,9,128,128]{3,2,1,0:T(8,128)(2,1)} %get-tuple-element.69.refs_0_, bf16[3,9,128,256]{3,2,1,0:T(8,128)(2,1)} %get-tuple-element.70.refs_1_, ...), custom_call_target="tpu_custom_call", output_to_operand_aliasing={{0}: (0, {}), {1}: (1, {})} | custom-call | bytes 10000 | tf_op jit(solution)/shard_map/pallas_call | solution.py:386
  (19 shorter events, 0.0 us)
Async XLA Ops:
  0.6 12.2 %copy-start.3 = (bf16[2,4,16,256]{3,2,1,0:T(8,128)(2,1)S(1)}, bf16[2,4,16,256]{3,2,1,0:T(8,128)(2,1)}, u32[]{:S(2)}) copy-start(bf16[2,4,16,256]{3,2,1,0:T(8,128)(2,1)} %refs_1_.1) | copy-start | bytes 196612
  0.6 12.2 %copy-start.2 = (bf16[2,8,32,128]{3,2,1,0:T(8,128)(2,1)S(1)}, bf16[2,8,32,128]{3,2,1,0:T(8,128)(2,1)}, u32[]{:S(2)}) copy-start(bf16[2,8,32,128]{3,2,1,0:T(8,128)(2,1)} %refs_0_.1) | copy-start | bytes 393220
  0.7 12.2 %copy-start.1 = (bf16[3,3,3,128,128]{4,3,2,1,0:T(8,128)(2,1)S(1)}, bf16[3,3,3,128,128]{4,3,2,1,0:T(8,128)(2,1)}, u32[]{:S(2)}) copy-start(bf16[3,3,3,128,128]{4,3,2,1,0:T(8,128)(2,1)} %weight_a.1) | copy-start | bytes 2654212
  2.4 17.0 %copy-start = (bf16[3,3,3,128,256]{4,3,2,1,0:T(8,128)(2,1)S(1)}, bf16[3,3,3,128,256]{4,3,2,1,0:T(8,128)(2,1)}, u32[]{:S(2)}) copy-start(bf16[3,3,3,128,256]{4,3,2,1,0:T(8,128)(2,1)} %refs_3_.1) | copy-start | bytes 5308420
  2.5 3.1 %collective-permute-start.2 = (bf16[2,3,32,128]{3,2,1,0:T(8,128)(2,1)}, bf16[2,3,32,128]{3,2,1,0:T(8,128)(2,1)S(1)}, u32[]{:S(2)}, u32[]{:S(2)}) collective-permute-start(bf16[2,3,32,128]{3,2,1,0:T(8,128)(2,1)} %get-tuple-element.40), channel_id=1, source_target_pairs={{0,1},{1,0},{2,3},{3,2},{4,5},{5,4},{6,7},{7,6},{8,9},{9,8},{10,11... | collective-permute-start | bytes 147464 | tf_op jit(solution)/shard_map/ppermute | solution.py:407
  3.0 8.3 %collective-permute-start.1 = (bf16[2,12,32,128]{3,2,1,0:T(8,128)(2,1)}, bf16[2,12,32,128]{3,2,1,0:T(8,128)(2,1)S(1)}, u32[]{:S(2)}, u32[]{:S(2)}) collective-permute-start(bf16[2,12,32,128]{3,2,1,0:T(8,128)(2,1)} %get-tuple-element.39), channel_id=1, source_target_pairs={{0,2},{1,3},{2,0},{3,1},{4,6},{5,7},{6,4},{7,5},{8,10},{9,11},{10,... | collective-permute-start | bytes 589832 | tf_op jit(solution)/shard_map/ppermute | solution.py:407
  6.4 0.7 %collective-permute-start.3 = (bf16[2,3,32,128]{3,2,1,0:T(8,128)(2,1)S(1)}, bf16[2,3,32,128]{3,2,1,0:T(8,128)(2,1)S(1)}, u32[]{:S(2)}, u32[]{:S(2)}) collective-permute-start(bf16[2,3,32,128]{3,2,1,0:T(8,128)(2,1)S(1)} %broadcast_select_fusion), channel_id=1, source_target_pairs={{2,6},{3,4},{4,3},{5,1},{6,10},{7,8},{8,7},{9,5},{10,14},{11,12},{... | collective-permute-start | bytes 147464 | tf_op jit(solution)/shard_map/ppermute | solution.py:407
  7.0 5.8 %collective-permute-start = (bf16[2,12,32,128]{3,2,1,0:T(8,128)(2,1)}, bf16[2,12,32,128]{3,2,1,0:T(8,128)(2,1)S(1)}, u32[]{:S(2)}, u32[]{:S(2)}) collective-permute-start(bf16[2,12,32,128]{3,2,1,0:T(8,128)(2,1)} %get-tuple-element.39), channel_id=1, source_target_pairs={{0,1},{1,0},{2,3},{3,2},{4,5},{5,4},{6,7},{7,6},{8,9},{9,8},{10,11... | collective-permute-start | bytes 589832 | tf_op jit(solution)/shard_map/ppermute | solution.py:407
  11.3 1.5 %collective-permute-start.4 = (bf16[2,12,32,128]{3,2,1,0:T(8,128)(2,1)S(1)}, bf16[2,12,32,128]{3,2,1,0:T(8,128)(2,1)S(1)}, u32[]{:S(2)}, u32[]{:S(2)}) collective-permute-start(bf16[2,12,32,128]{3,2,1,0:T(8,128)(2,1)S(1)} %collective-permute-done.1.refs_3_), channel_id=1, source_target_pairs={{0,1},{1,0},{2,3},{3,2},{4,5},{5,4},{6,7},{7,6},{8,9},{9,8},{10,11... | collective-permute-start | bytes 589832 | tf_op jit(solution)/shard_map/ppermute | solution.py:407
  11.3 1.5 %collective-permute-start.5 = (bf16[2,3,32,128]{3,2,1,0:T(8,128)(2,1)S(1)}, bf16[2,3,32,128]{3,2,1,0:T(8,128)(2,1)S(1)}, u32[]{:S(2)}, u32[]{:S(2)}) collective-permute-start(bf16[2,3,32,128]{3,2,1,0:T(8,128)(2,1)S(1)} %collective-permute-done.3.refs_5_), channel_id=1, source_target_pairs={{0,1},{1,0},{2,3},{3,2},{4,5},{5,4},{6,7},{7,6},{8,9},{9,8},{10,11... | collective-permute-start | bytes 147464 | tf_op jit(solution)/shard_map/ppermute | solution.py:407
  15.2 10.7 %collective-permute-start.6 = (bf16[9,16,256]{2,1,0:T(8,128)(2,1)S(1)}, bf16[9,16,256]{2,1,0:T(8,128)(2,1)S(1)}, u32[]{:S(2)}, u32[]{:S(2)}) collective-permute-start(bf16[9,16,256]{2,1,0:T(8,128)(2,1)S(1)} %get-tuple-element.56), channel_id=1, source_target_pairs={{0,8},{1,9},{2,10},{3,11},{4,12},{5,13},{6,14},{7,15},{8,0},{9,1},... | collective-permute-start | bytes 221192 | tf_op jit(solution)/shard_map/ppermute | solution.py:407
  22.0 7.8 %collective-permute-start.8 = (bf16[9,16,384]{2,1,0:T(8,128)(2,1)S(1)}, bf16[9,16,384]{2,1,0:T(8,128)(2,1)S(1)}, u32[]{:S(2)}, u32[]{:S(2)}) collective-permute-start(bf16[9,16,384]{2,1,0:T(8,128)(2,1)S(1)} %get-tuple-element.61), channel_id=1, source_target_pairs={{0,4},{1,5},{2,6},{3,7},{4,8},{5,9},{6,10},{7,11},{8,12},{9,13},{1... | collective-permute-start | bytes 331784 | tf_op jit(solution)/shard_map/ppermute | solution.py:407
  23.6 7.4 %collective-permute-start.9 = (bf16[9,16,384]{2,1,0:T(8,128)(2,1)S(1)}, bf16[9,16,384]{2,1,0:T(8,128)(2,1)S(1)}, u32[]{:S(2)}, u32[]{:S(2)}) collective-permute-start(bf16[9,16,384]{2,1,0:T(8,128)(2,1)S(1)} %get-tuple-element.62), channel_id=1, source_target_pairs={{0,12},{1,13},{2,14},{3,15},{4,0},{5,1},{6,2},{7,3},{8,4},{9,5},{1... | collective-permute-start | bytes 331784 | tf_op jit(solution)/shard_map/ppermute | solution.py:407
  25.9 5.7 %collective-permute-start.7 = (bf16[9,16,128]{2,1,0:T(8,128)(2,1)S(1)}, bf16[9,16,128]{2,1,0:T(8,128)(2,1)S(1)}, u32[]{:S(2)}, u32[]{:S(2)}) collective-permute-start(bf16[9,16,128]{2,1,0:T(8,128)(2,1)S(1)} %get-tuple-element.58), channel_id=1, source_target_pairs={{0,8},{1,9},{2,10},{3,11},{4,12},{5,13},{6,14},{7,15},{8,0},{9,1},... | collective-permute-start | bytes 110600 | tf_op jit(solution)/shard_map/ppermute | solution.py:407
  31.7 6.2 %collective-permute-start.11 = (bf16[9,16,384]{2,1,0:T(8,128)(2,1)S(1)}, bf16[9,16,384]{2,1,0:T(8,128)(2,1)S(1)}, u32[]{:S(2)}, u32[]{:S(2)}) collective-permute-start(bf16[9,16,384]{2,1,0:T(8,128)(2,1)S(1)} %shard_map.79.refs_0_), channel_id=1, source_target_pairs={{0,12},{1,13},{2,14},{3,15},{4,0},{5,1},{6,2},{7,3},{8,4},{9,5},{1... | collective-permute-start | bytes 331784 | tf_op jit(solution)/shard_map/ppermute | solution.py:407
  34.4 5.3 %collective-permute-start.15 = (bf16[9,16,384]{2,1,0:T(8,128)(2,1)S(1)}, bf16[9,16,384]{2,1,0:T(8,128)(2,1)S(1)}, u32[]{:S(2)}, u32[]{:S(2)}) collective-permute-start(bf16[9,16,384]{2,1,0:T(8,128)(2,1)S(1)} %shard_map.79.refs_0_), channel_id=1, source_target_pairs={{0,2},{1,3},{2,0},{3,1},{4,6},{5,7},{6,4},{7,5},{8,10},{9,11},{10,... | collective-permute-start | bytes 331784 | tf_op jit(solution)/shard_map/ppermute | solution.py:407
  34.7 7.5 %collective-permute-start.14 = (bf16[9,16,384]{2,1,0:T(8,128)(2,1)S(1)}, bf16[9,16,384]{2,1,0:T(8,128)(2,1)S(1)}, u32[]{:S(2)}, u32[]{:S(2)}) collective-permute-start(bf16[9,16,384]{2,1,0:T(8,128)(2,1)S(1)} %shard_map.79.refs_0_), channel_id=1, source_target_pairs={{0,4},{1,5},{2,6},{3,7},{4,8},{5,9},{6,10},{7,11},{8,12},{9,13},{1... | collective-permute-start | bytes 331784 | tf_op jit(solution)/shard_map/ppermute | solution.py:407
  34.7 10.1 %collective-permute-start.10 = (bf16[9,16,384]{2,1,0:T(8,128)(2,1)S(1)}, bf16[9,16,384]{2,1,0:T(8,128)(2,1)S(1)}, u32[]{:S(2)}, u32[]{:S(2)}) collective-permute-start(bf16[9,16,384]{2,1,0:T(8,128)(2,1)S(1)} %shard_map.79.refs_0_), channel_id=1, source_target_pairs={{0,8},{1,9},{2,10},{3,11},{4,12},{5,13},{6,14},{7,15},{8,0},{9,1},... | collective-permute-start | bytes 331784 | tf_op jit(solution)/shard_map/ppermute | solution.py:407
  37.8 6.9 %collective-permute-start.12 = (bf16[9,16,384]{2,1,0:T(8,128)(2,1)S(1)}, bf16[9,16,384]{2,1,0:T(8,128)(2,1)S(1)}, u32[]{:S(2)}, u32[]{:S(2)}) collective-permute-start(bf16[9,16,384]{2,1,0:T(8,128)(2,1)S(1)} %collective-permute-done.11.refs_1_), channel_id=1, source_target_pairs={{0,2},{1,3},{2,0},{3,1},{4,6},{5,7},{6,4},{7,5},{8,10},{9,11},{10,... | collective-permute-start | bytes 331784 | tf_op jit(solution)/shard_map/ppermute | solution.py:407
  37.8 7.4 %collective-permute-start.16 = (bf16[9,16,384]{2,1,0:T(8,128)(2,1)S(1)}, bf16[9,16,384]{2,1,0:T(8,128)(2,1)S(1)}, u32[]{:S(2)}, u32[]{:S(2)}) collective-permute-start(bf16[9,16,384]{2,1,0:T(8,128)(2,1)S(1)} %shard_map.79.refs_0_), channel_id=1, source_target_pairs={{0,1},{1,0},{2,3},{3,2},{4,5},{5,4},{6,7},{7,6},{8,9},{9,8},{10,11... | collective-permute-start | bytes 331784 | tf_op jit(solution)/shard_map/ppermute | solution.py:407
  39.7 5.7 %collective-permute-start.20 = (bf16[9,16,384]{2,1,0:T(8,128)(2,1)S(1)}, bf16[9,16,384]{2,1,0:T(8,128)(2,1)S(1)}, u32[]{:S(2)}, u32[]{:S(2)}) collective-permute-start(bf16[9,16,384]{2,1,0:T(8,128)(2,1)S(1)} %collective-permute-done.15.refs_4_), channel_id=1, source_target_pairs={{0,1},{1,0},{2,3},{3,2},{4,5},{5,4},{6,7},{7,6},{8,9},{9,8},{10,11... | collective-permute-start | bytes 331784 | tf_op jit(solution)/shard_map/ppermute | solution.py:407
  42.2 4.9 %collective-permute-start.21 = (bf16[9,16,384]{2,1,0:T(8,128)(2,1)S(1)}, bf16[9,16,384]{2,1,0:T(8,128)(2,1)S(1)}, u32[]{:S(2)}, u32[]{:S(2)}) collective-permute-start(bf16[9,16,384]{2,1,0:T(8,128)(2,1)S(1)} %collective-permute-done.14.refs_2_), channel_id=1, source_target_pairs={{0,2},{1,3},{2,0},{3,1},{4,6},{5,7},{6,4},{7,5},{8,10},{9,11},{10,... | collective-permute-start | bytes 331784 | tf_op jit(solution)/shard_map/ppermute | solution.py:407
  44.7 2.5 %collective-permute-start.18 = (bf16[9,16,384]{2,1,0:T(8,128)(2,1)S(1)}, bf16[9,16,384]{2,1,0:T(8,128)(2,1)S(1)}, u32[]{:S(2)}, u32[]{:S(2)}) collective-permute-start(bf16[9,16,384]{2,1,0:T(8,128)(2,1)S(1)} %collective-permute-done.14.refs_2_), channel_id=1, source_target_pairs={{0,1},{1,0},{2,3},{3,2},{4,5},{5,4},{6,7},{7,6},{8,9},{9,8},{10,11... | collective-permute-start | bytes 331784 | tf_op jit(solution)/shard_map/ppermute | solution.py:407
  44.7 2.9 %collective-permute-start.17 = (bf16[9,16,384]{2,1,0:T(8,128)(2,1)S(1)}, bf16[9,16,384]{2,1,0:T(8,128)(2,1)S(1)}, u32[]{:S(2)}, u32[]{:S(2)}) collective-permute-start(bf16[9,16,384]{2,1,0:T(8,128)(2,1)S(1)} %collective-permute-done.11.refs_1_), channel_id=1, source_target_pairs={{0,1},{1,0},{2,3},{3,2},{4,5},{5,4},{6,7},{7,6},{8,9},{9,8},{10,11... | collective-permute-start | bytes 331784 | tf_op jit(solution)/shard_map/ppermute | solution.py:407
  45.3 2.3 %collective-permute-start.19 = (bf16[9,16,384]{2,1,0:T(8,128)(2,1)S(1)}, bf16[9,16,384]{2,1,0:T(8,128)(2,1)S(1)}, u32[]{:S(2)}, u32[]{:S(2)}) collective-permute-start(bf16[9,16,384]{2,1,0:T(8,128)(2,1)S(1)} %collective-permute-done.10.refs_3_), channel_id=1, source_target_pairs={{0,1},{1,0},{2,3},{3,2},{4,5},{5,4},{6,7},{7,6},{8,9},{9,8},{10,11... | collective-permute-start | bytes 331784 | tf_op jit(solution)/shard_map/ppermute | solution.py:407
  45.3 5.4 %collective-permute-start.13 = (bf16[9,16,384]{2,1,0:T(8,128)(2,1)S(1)}, bf16[9,16,384]{2,1,0:T(8,128)(2,1)S(1)}, u32[]{:S(2)}, u32[]{:S(2)}) collective-permute-start(bf16[9,16,384]{2,1,0:T(8,128)(2,1)S(1)} %collective-permute-done.10.refs_3_), channel_id=1, source_target_pairs={{0,2},{1,3},{2,0},{3,1},{4,6},{5,7},{6,4},{7,5},{8,10},{9,11},{10,... | collective-permute-start | bytes 331784 | tf_op jit(solution)/shard_map/ppermute | solution.py:407
  47.1 2.2 %collective-permute-start.22 = (bf16[9,16,384]{2,1,0:T(8,128)(2,1)S(1)}, bf16[9,16,384]{2,1,0:T(8,128)(2,1)S(1)}, u32[]{:S(2)}, u32[]{:S(2)}) collective-permute-start(bf16[9,16,384]{2,1,0:T(8,128)(2,1)S(1)} %collective-permute-done.12.refs_2_), channel_id=1, source_target_pairs={{0,1},{1,0},{2,3},{3,2},{4,5},{5,4},{6,7},{7,6},{8,9},{9,8},{10,11... | collective-permute-start | bytes 331784 | tf_op jit(solution)/shard_map/ppermute | solution.py:407
  47.2 2.0 %collective-permute-start.23 = (bf16[9,16,384]{2,1,0:T(8,128)(2,1)S(1)}, bf16[9,16,384]{2,1,0:T(8,128)(2,1)S(1)}, u32[]{:S(2)}, u32[]{:S(2)}) collective-permute-start(bf16[9,16,384]{2,1,0:T(8,128)(2,1)S(1)} %collective-permute-done.21.refs_3_), channel_id=1, source_target_pairs={{0,1},{1,0},{2,3},{3,2},{4,5},{5,4},{6,7},{7,6},{8,9},{9,8},{10,11... | collective-permute-start | bytes 331784 | tf_op jit(solution)/shard_map/ppermute | solution.py:407
  50.7 1.3 %collective-permute-start.24 = (bf16[9,16,384]{2,1,0:T(8,128)(2,1)S(1)}, bf16[9,16,384]{2,1,0:T(8,128)(2,1)S(1)}, u32[]{:S(2)}, u32[]{:S(2)}) collective-permute-start(bf16[9,16,384]{2,1,0:T(8,128)(2,1)S(1)} %collective-permute-done.13.refs_2_), channel_id=1, source_target_pairs={{0,1},{1,0},{2,3},{3,2},{4,5},{5,4},{6,7},{7,6},{8,9},{9,8},{10,11... | collective-permute-start | bytes 331784 | tf_op jit(solution)/shard_map/ppermute | solution.py:407
